TPU v7x, 32 devices: a whole 2x2x4 slice. The times are simulated.
32 devices in a mesh: rep: 16 (over z, y, x), opt: 2 (over core).
Axes of the slice: x: 2, y: 2, z: 4, core: 2. Of those that a mesh axis runs over, the one named last changes fastest.
Arguments:
- tokens: bfloat16 [65536, 512], P(('rep', 'opt')), may hold values from -40 to 40
- out_grad: bfloat16 [65536, 512], P(('rep', 'opt')), may hold values from -5 to 5
- vectors: bfloat16 [6, 512], P(None, 'opt'), may hold values from -2 to 2
- qkv_weight: bfloat16 [512, 1536], P('opt'), may hold values from -0.25 to 0.25
- qkv_bias: bfloat16 [1536], P('opt'), may hold values from -1.5 to 1.5
- out_weight: bfloat16 [512, 512], P('opt'), may hold values from -1 to 1
- fc_weight: bfloat16 [512, 2048], P('opt'), may hold values from -0.25 to 0.25
- fc_bias: bfloat16 [2048], P('opt'), may hold values from -2.5 to 2.5
- proj_weight: bfloat16 [2048, 512], P('opt'), may hold values from -0.125 to 0.125
- mean_vectors: float32 [6, 512], P(None, 'opt'), may hold values from -24 to 24
- mean_qkv_weight: float32 [512, 1536], P('opt'), may hold values from -24 to 24
- mean_qkv_bias: float32 [1536], P('opt'), may hold values from -24 to 24
- mean_out_weight: float32 [512, 512], P('opt'), may hold values from -24 to 24
- mean_fc_weight: float32 [512, 2048], P('opt'), may hold values from -24 to 24
- mean_fc_bias: float32 [2048], P('opt'), may hold values from -24 to 24
- mean_proj_weight: float32 [2048, 512], P('opt'), may hold values from -24 to 24
- square_vectors: float32 [6, 512], P(None, 'opt'), may hold values from 32 to 512
- square_qkv_weight: float32 [512, 1536], P('opt'), may hold values from 32 to 512
- square_qkv_bias: float32 [1536], P('opt'), may hold values from 32 to 512
- square_out_weight: float32 [512, 512], P('opt'), may hold values from 32 to 512
- square_fc_weight: float32 [512, 2048], P('opt'), may hold values from 32 to 512
- square_fc_bias: float32 [2048], P('opt'), may hold values from 32 to 512
- square_proj_weight: float32 [2048, 512], P('opt'), may hold values from 32 to 512
Outputs:
- layer_out: bfloat16 [65536, 512], P(('rep', 'opt'))
- tokens_grad: bfloat16 [65536, 512], P(('rep', 'opt'))
- grad_vectors: float32 [6, 512], P(None, 'opt')
- grad_qkv_weight: float32 [512, 1536], P('opt')
- grad_qkv_bias: float32 [1536], P('opt')
- grad_out_weight: float32 [512, 512], P('opt')
- grad_fc_weight: float32 [512, 2048], P('opt')
- grad_fc_bias: float32 [2048], P('opt')
- grad_proj_weight: float32 [2048, 512], P('opt')
- step_vectors: float32 [6, 512], P(None, 'opt')
- step_qkv_weight: float32 [512, 1536], P('opt')
- step_qkv_bias: float32 [1536], P('opt')
- step_out_weight: float32 [512, 512], P('opt')
- step_fc_weight: float32 [512, 2048], P('opt')
- step_fc_bias: float32 [2048], P('opt')
- step_proj_weight: float32 [2048, 512], P('opt')
- new_mean_vectors: float32 [6, 512], P(None, 'opt')
- new_mean_qkv_weight: float32 [512, 1536], P('opt')
- new_mean_qkv_bias: float32 [1536], P('opt')
- new_mean_out_weight: float32 [512, 512], P('opt')
- new_mean_fc_weight: float32 [512, 2048], P('opt')
- new_mean_fc_bias: float32 [2048], P('opt')
- new_mean_proj_weight: float32 [2048, 512], P('opt')
- new_square_vectors: float32 [6, 512], P(None, 'opt')
- new_square_qkv_weight: float32 [512, 1536], P('opt')
- new_square_qkv_bias: float32 [1536], P('opt')
- new_square_out_weight: float32 [512, 512], P('opt')
- new_square_fc_weight: float32 [512, 2048], P('opt')
- new_square_fc_bias: float32 [2048], P('opt')
- new_square_proj_weight: float32 [2048, 512], P('opt')
All inputs are finite; a program needn't handle non-finite values.
Results may differ from a plain program's by a relative error of at most 0.015.
The roundings to bfloat16 on the way count: a program that leaves them out, or rounds other values in their place, can miss the bound.
Values may be sent and summed in bfloat16 or wider, within the bound.
No kernel may reach another device: no remote copies, remote signals or barrier semaphores. Data moves between devices by JAX's collectives and lax.ppermute only.
A program may use at most 256 MiB of HBM per device.

v0:
```python
import jax
import jax.numpy as jnp
from jax import lax
from jax.sharding import PartitionSpec as P

H = 8
ROT = 16
LEN = 512
ADAM_STEP = 10


LN_EPS = 1e-05
ADAM_EPS = 1e-08
BETA_ONE = 0.9
BETA_TWO = 0.95
LEARN_RATE = 0.02
WEIGHT_DECAY = 0.01
SHARD_DIMS = (1, 0, 0, 0, 0, 0, 0)
INV_ROOT_TWO = 0.7071067811865476
INV_ROOT_TWO_PI = 0.3989422804014327


def rotary_tables():
    freqs = jnp.power(10000.0, -jnp.arange(0, ROT, 2).astype(jnp.float32) / ROT)
    angles = jnp.arange(LEN).astype(jnp.float32)[:, None] * freqs[None, :]
    angles = jnp.concatenate([angles, angles], -1)[:, None, :]
    return (jnp.cos(angles), jnp.sin(angles))


def rotate(inputs, cosine, sine):
    half_rot = ROT // 2
    leading = inputs[..., :ROT]
    turned = jnp.concatenate([-leading[..., half_rot:], leading[..., :half_rot]], -1)
    return jnp.concatenate([leading * cosine + turned * sine, inputs[..., ROT:]], -1)


def rotate_back(grads_in, cosine, sine):
    half_rot = ROT // 2
    leading = grads_in[..., :ROT]
    shifted = leading * sine
    turned = jnp.concatenate([shifted[..., half_rot:], -shifted[..., :half_rot]], -1)
    return jnp.concatenate([leading * cosine + turned, grads_in[..., ROT:]], -1)


def causal_mask():
    return jnp.arange(LEN)[:, None] >= jnp.arange(LEN)[None, :]


def score_block(queries, keys_rot):
    scale = queries.shape[-1] ** (-0.5)
    scores = (
        jnp.einsum("qhd,khd->hqk", queries, keys_rot, preferred_element_type=jnp.float32) * scale
    )
    return jnp.where(causal_mask()[None], scores, -1e30)


def attend(block):
    queries, keys_rot, values = block
    scores = score_block(queries, keys_rot)
    row_top = jnp.max(scores, -1, keepdims=True)
    exps = jnp.exp(scores - row_top)
    row_total = jnp.sum(exps, -1, keepdims=True)
    probs = (exps / row_total).astype(jnp.bfloat16)
    attended = jnp.einsum("hqk,khd->qhd", probs, values, preferred_element_type=jnp.float32)
    return (attended.reshape(attended.shape[0], -1).astype(jnp.bfloat16), row_top, row_total)


def attend_back(block):
    queries, keys_rot, values, row_top, row_total, attended_grad = block
    scale = queries.shape[-1] ** (-0.5)
    probs_f = jnp.exp(score_block(queries, keys_rot) - row_top) / row_total
    probs = probs_f.astype(jnp.bfloat16)
    prob_grad = jnp.einsum(
        "qhd,khd->hqk", attended_grad, values, preferred_element_type=jnp.float32
    )
    value_grad = jnp.einsum(
        "hqk,qhd->khd", probs, attended_grad, preferred_element_type=jnp.float32
    )
    score_grad = (probs_f * (prob_grad - jnp.sum(prob_grad * probs_f, -1, keepdims=True))).astype(
        jnp.bfloat16
    )
    query_grad = (
        jnp.einsum("hqk,khd->qhd", score_grad, keys_rot, preferred_element_type=jnp.float32) * scale
    )
    key_grad = (
        jnp.einsum("hqk,qhd->khd", score_grad, queries, preferred_element_type=jnp.float32) * scale
    )
    return (query_grad, key_grad, value_grad)


def local_pass(tokens, out_grad, full):
    vectors, qkv_weight, qkv_bias, out_weight, fc_weight, fc_bias, proj_weight = full
    row_count, model_width = tokens.shape
    seq_count = row_count // LEN
    head_size = model_width // H
    tokens_f = tokens.astype(jnp.float32)
    centre = tokens_f - jnp.mean(tokens_f, -1, keepdims=True)
    inv_dev = lax.rsqrt(jnp.mean(centre * centre, -1, keepdims=True) + LN_EPS)
    normed = centre * inv_dev
    vec_f = vectors.astype(jnp.float32)
    first_in = (normed * vec_f[0] + vec_f[1]).astype(jnp.bfloat16)
    second_in = (normed * vec_f[2] + vec_f[3]).astype(jnp.bfloat16)
    mixed = jnp.dot(first_in, qkv_weight, preferred_element_type=jnp.float32) + qkv_bias.astype(
        jnp.float32
    )
    mixed = mixed.reshape(seq_count, LEN, 3, H, head_size)
    cosine, sine = rotary_tables()
    queries = rotate(mixed[:, :, 0], cosine, sine).astype(jnp.bfloat16)
    keys_rot = rotate(mixed[:, :, 1], cosine, sine).astype(jnp.bfloat16)
    values = mixed[:, :, 2].astype(jnp.bfloat16)
    attended, row_top, row_total = lax.map(attend, (queries, keys_rot, values))
    attended = attended.reshape(row_count, model_width)
    attn_out = jnp.dot(attended, out_weight, preferred_element_type=jnp.float32) + vec_f[4]
    hidden = jnp.dot(second_in, fc_weight, preferred_element_type=jnp.float32) + fc_bias.astype(
        jnp.float32
    )
    activated = jax.nn.gelu(hidden, approximate=False).astype(jnp.bfloat16)
    mlp_out = jnp.dot(activated, proj_weight, preferred_element_type=jnp.float32) + vec_f[5]
    layer_out = (tokens_f + attn_out + mlp_out).astype(jnp.bfloat16)
    grad_out_weight = jnp.einsum(
        "ti,to->io", attended, out_grad, preferred_element_type=jnp.float32
    )
    grad_proj_weight = jnp.einsum(
        "tf,to->fo", activated, out_grad, preferred_element_type=jnp.float32
    )
    out_sum = jnp.sum(out_grad, 0, dtype=jnp.float32)
    attended_grad = jnp.einsum(
        "to,io->ti", out_grad, out_weight, preferred_element_type=jnp.float32
    ).astype(jnp.bfloat16)
    act_grad = jnp.einsum("to,fo->tf", out_grad, proj_weight, preferred_element_type=jnp.float32)
    slope = (
        0.5 * lax.erfc(-hidden * INV_ROOT_TWO)
        + hidden * jnp.exp(-0.5 * hidden * hidden) * INV_ROOT_TWO_PI
    )
    hidden_grad = (act_grad * slope).astype(jnp.bfloat16)
    grad_fc_weight = jnp.einsum(
        "ti,tf->if", second_in, hidden_grad, preferred_element_type=jnp.float32
    )
    grad_fc_bias = jnp.sum(hidden_grad, 0, dtype=jnp.float32)
    second_grad = jnp.einsum(
        "tf,if->ti", hidden_grad, fc_weight, preferred_element_type=jnp.float32
    )
    query_grad, key_grad, value_grad = lax.map(
        attend_back,
        (
            queries,
            keys_rot,
            values,
            row_top,
            row_total,
            attended_grad.reshape(seq_count, LEN, H, head_size),
        ),
    )
    qkv_grad = jnp.stack(
        [rotate_back(query_grad, cosine, sine), rotate_back(key_grad, cosine, sine), value_grad], 2
    )
    qkv_grad = qkv_grad.reshape(row_count, 3 * model_width).astype(jnp.bfloat16)
    grad_qkv_weight = jnp.einsum(
        "ti,tj->ij", first_in, qkv_grad, preferred_element_type=jnp.float32
    )
    grad_qkv_bias = jnp.sum(qkv_grad, 0, dtype=jnp.float32)
    first_grad = jnp.einsum("tj,ij->ti", qkv_grad, qkv_weight, preferred_element_type=jnp.float32)
    grad_vectors = jnp.stack(
        [
            jnp.sum(first_grad * normed, 0),
            jnp.sum(first_grad, 0),
            jnp.sum(second_grad * normed, 0),
            jnp.sum(second_grad, 0),
            out_sum,
            out_sum,
        ]
    )
    normed_grad = first_grad * vec_f[0] + second_grad * vec_f[2]
    ln_grad = inv_dev * (
        normed_grad
        - jnp.mean(normed_grad, -1, keepdims=True)
        - normed * jnp.mean(normed_grad * normed, -1, keepdims=True)
    )
    tokens_grad = (out_grad.astype(jnp.float32) + ln_grad).astype(jnp.bfloat16)
    grads = (
        grad_vectors,
        grad_qkv_weight,
        grad_qkv_bias,
        grad_out_weight,
        grad_fc_weight,
        grad_fc_bias,
        grad_proj_weight,
    )
    return (layer_out, tokens_grad, grads)


def owner_major(gradient, shard_dim, group_size):
    shape = gradient.shape
    split_shape = (
        shape[:shard_dim] + (group_size, shape[shard_dim] // group_size) + shape[shard_dim + 1 :]
    )
    return jnp.moveaxis(gradient.reshape(split_shape), shard_dim, 0).reshape(group_size, -1)


def body(
    tokens,
    out_grad,
    vectors,
    qkv_weight,
    qkv_bias,
    out_weight,
    fc_weight,
    fc_bias,
    proj_weight,
    mean_vectors,
    mean_qkv_weight,
    mean_qkv_bias,
    mean_out_weight,
    mean_fc_weight,
    mean_fc_bias,
    mean_proj_weight,
    square_vectors,
    square_qkv_weight,
    square_qkv_bias,
    square_out_weight,
    square_fc_weight,
    square_fc_bias,
    square_proj_weight,
):
    own_shards = (vectors, qkv_weight, qkv_bias, out_weight, fc_weight, fc_bias, proj_weight)
    means = (
        mean_vectors,
        mean_qkv_weight,
        mean_qkv_bias,
        mean_out_weight,
        mean_fc_weight,
        mean_fc_bias,
        mean_proj_weight,
    )
    squares = (
        square_vectors,
        square_qkv_weight,
        square_qkv_bias,
        square_out_weight,
        square_fc_weight,
        square_fc_bias,
        square_proj_weight,
    )
    full = (
        lax.all_gather(vectors, "opt", axis=1, tiled=True),
        lax.all_gather(qkv_weight, "opt", axis=0, tiled=True),
        lax.all_gather(qkv_bias, "opt", axis=0, tiled=True),
        lax.all_gather(out_weight, "opt", axis=0, tiled=True),
        lax.all_gather(fc_weight, "opt", axis=0, tiled=True),
        lax.all_gather(fc_bias, "opt", axis=0, tiled=True),
        lax.all_gather(proj_weight, "opt", axis=0, tiled=True),
    )
    layer_out, tokens_grad, grads = local_pass(tokens, out_grad, full)
    group_size = lax.axis_size("opt")
    buffer = jnp.concatenate(
        [
            owner_major(gradient, shard_dim, group_size)
            for gradient, shard_dim in zip(grads, SHARD_DIMS)
        ],
        1,
    )
    owner_part = lax.psum_scatter(buffer, "opt", scatter_dimension=0, tiled=True)
    summed = lax.psum(owner_part, "rep").reshape(-1)
    fix_one = 1.0 - BETA_ONE**ADAM_STEP
    fix_two = 1.0 - BETA_TWO**ADAM_STEP
    grad_shards = []
    steps = []
    new_means = []
    new_squares = []
    offset = 0
    for index in range(7):
        own_shard = own_shards[index]
        length = own_shard.size
        gradient = summed[offset : offset + length].reshape(own_shard.shape)
        offset = offset + length
        new_mean = BETA_ONE * means[index] + (1.0 - BETA_ONE) * gradient
        new_square = BETA_TWO * squares[index] + (1.0 - BETA_TWO) * gradient * gradient
        update = -LEARN_RATE * (
            new_mean / fix_one / (jnp.sqrt(new_square / fix_two) + ADAM_EPS)
            + WEIGHT_DECAY * own_shard.astype(jnp.float32)
        )
        grad_shards.append(gradient)
        steps.append(update)
        new_means.append(new_mean)
        new_squares.append(new_square)
    return (layer_out, tokens_grad, *grad_shards, *steps, *new_means, *new_squares)


def solution(mesh):
    in_specs = (
        P(("rep", "opt"), None),
        P(("rep", "opt"), None),
        P(None, "opt"),
        P("opt", None),
        P("opt"),
        P("opt", None),
        P("opt", None),
        P("opt"),
        P("opt", None),
        P(None, "opt"),
        P("opt", None),
        P("opt"),
        P("opt", None),
        P("opt", None),
        P("opt"),
        P("opt", None),
        P(None, "opt"),
        P("opt", None),
        P("opt"),
        P("opt", None),
        P("opt", None),
        P("opt"),
        P("opt", None),
    )
    out_specs = (
        P(("rep", "opt"), None),
        P(("rep", "opt"), None),
        P(None, "opt"),
        P("opt", None),
        P("opt"),
        P("opt", None),
        P("opt", None),
        P("opt"),
        P("opt", None),
        P(None, "opt"),
        P("opt", None),
        P("opt"),
        P("opt", None),
        P("opt", None),
        P("opt"),
        P("opt", None),
        P(None, "opt"),
        P("opt", None),
        P("opt"),
        P("opt", None),
        P("opt", None),
        P("opt"),
        P("opt", None),
        P(None, "opt"),
        P("opt", None),
        P("opt"),
        P("opt", None),
        P("opt", None),
        P("opt"),
        P("opt", None),
    )
    return jax.shard_map(body, mesh=mesh, in_specs=in_specs, out_specs=out_specs, check_vma=False)
```

profile of v0, /device:TPU:0, one launch (start us, length us, event | category | flops | bytes accessed | tf_op | source)
XLA Modules:
  0.0 784.0 jit_solution(1261395857112050772)
XLA Ops:
  22.5 2.6 convolution_convert_fusion
  25.1 6.2 reshape.277
  31.2 5.5 copy.92
  36.8 8.1 %convolution_add_fusion = f32[2048,1536]{1,0:T(8,128)} fusion(bf16[512,1536]{1,0:T(8,128)(2,1)} %all-gather.5.cloned.1.call-done, f32[1536]{0:T(1024)S(1)} %reshape.276, bf16[2048,512]{1,0:T(8,128)(2,1)S(1)} %copy-done.2, f32[512]{0:T(512)S(1)} %bitcast.182, f32[512]{0:T(512)S(1)} %bitcast.174, f32[2048]{0:T(1024)S(1)} %add_rsqrt_fusion, ...), kind=kOutput, calls=%fused_computation.85 | convolution fusion | flops 3230662656 | bytes 16279552 | tf_op jit(solution)/shard_map/dot_general | solution.py:103
  44.9 12.8 %copy.84 = f32[2048,1536]{0,1:T(8,128)} copy(f32[2048,1536]{1,0:T(8,128)} %convolution_add_fusion) | data formatting | bytes 25165824 | tf_op jit(solution)/shard_map/add | solution.py:103
  57.7 16.2 %reshape.263 = f32[4,512,3,8,64]{1,0,4,3,2:T(4,128)} reshape(f32[2048,1536]{0,1:T(8,128)} %copy.84) | data formatting | bytes 25165824 | tf_op jit(solution)/shard_map/reshape | solution.py:106
  73.9 2.9 fusion.83
  76.8 5.2 slice_bitcast_fusion
  91.3 43.0 %while.28 = (s32[]{:T(128)}, bf16[4,512,512]{2,1,0:T(8,128)(2,1)}, f32[4,8,512,1]{2,1,3,0:T(8,128)S(1)}, f32[4,8,512,1]{2,1,3,0:T(8,128)S(1)}, bf16[4,512,8,64]{...) while((s32[]{:T(128)}, bf16[4,512,512]{2,1,0:T(8,128)(2,1)}, ...), condition=%wide.region_5.6_spmd, body=%wide.region_2.5_spmd.sunk | while | flops 562552832 | bytes 30557288 | solution.py:111
  91.5 2.5 fusion.158
  95.8 4.3 fusion.160
  106.5 4.3 fusion.160
  112.9 2.5 fusion.158
  117.2 4.3 fusion.160
  127.9 4.3 fusion.160
  134.3 105.6 %while.29 = (s32[]{:T(128)}, f32[4,512,8,64]{1,3,2,0:T(8,128)}, f32[4,512,8,64]{1,3,2,0:T(8,128)}, bf16[4,512,8,64]{1,3,2,0:T(8,128)(2,1)}, bf16[4,512,8,64]{1,3...) while((s32[]{:T(128)}, f32[4,512,8,64]{1,3,2,0:T(8,128)}, ...), condition=%wide.region_8.9_spmd, body=%wide.region_6.8_spmd.sunk | while | flops 1363931136 | bytes 129111272 | solution.py:143
  134.4 3.7 exponential_divide_fusion.2
  141.4 6.0 multiply_reduce_fusion.2
  147.4 8.1 %multiply_convert_fusion.3 = bf16[8,512,512]{1,2,0:T(8,128)(2,1)S(1)} fusion(f32[8,512,512]{1,2,0:T(8,128)} %copy-done, f32[8,512,512]{1,2,0:T(8,128)} %get-tuple-element.403, f32[8,512]{1,0:T(8,128)S(1)} %get-tuple-element.404), kind=kLoop, calls=%fused_computation.22.clone.1 | loop fusion | flops 6291456 | bytes 20987904 | tf_op jit(solution)/shard_map/while/body/eval_jaxpr/convert_element_type | solution.py:79
  155.5 3.4 fusion.170
  160.7 3.7 exponential_divide_fusion.2
  167.7 6.0 multiply_reduce_fusion.2
  173.7 8.1 %multiply_convert_fusion.3 = bf16[8,512,512]{1,2,0:T(8,128)(2,1)S(1)} fusion(f32[8,512,512]{1,2,0:T(8,128)} %copy-done, f32[8,512,512]{1,2,0:T(8,128)} %get-tuple-element.403, f32[8,512]{1,0:T(8,128)S(1)} %get-tuple-element.404), kind=kLoop, calls=%fused_computation.22.clone.1 | loop fusion | flops 6291456 | bytes 20987904 | tf_op jit(solution)/shard_map/while/body/eval_jaxpr/convert_element_type | solution.py:79
  181.8 3.4 fusion.170
  187.1 3.7 exponential_divide_fusion.2
  194.1 6.0 multiply_reduce_fusion.2
  200.1 8.1 %multiply_convert_fusion.3 = bf16[8,512,512]{1,2,0:T(8,128)(2,1)S(1)} fusion(f32[8,512,512]{1,2,0:T(8,128)} %copy-done, f32[8,512,512]{1,2,0:T(8,128)} %get-tuple-element.403, f32[8,512]{1,0:T(8,128)S(1)} %get-tuple-element.404), kind=kLoop, calls=%fused_computation.22.clone.1 | loop fusion | flops 6291456 | bytes 20987904 | tf_op jit(solution)/shard_map/while/body/eval_jaxpr/convert_element_type | solution.py:79
  208.1 3.4 fusion.170
  213.4 3.7 exponential_divide_fusion.2
  220.4 6.0 multiply_reduce_fusion.2
  226.4 8.1 %multiply_convert_fusion.3 = bf16[8,512,512]{1,2,0:T(8,128)(2,1)S(1)} fusion(f32[8,512,512]{1,2,0:T(8,128)} %copy-done, f32[8,512,512]{1,2,0:T(8,128)} %get-tuple-element.403, f32[8,512]{1,0:T(8,128)S(1)} %get-tuple-element.404), kind=kLoop, calls=%fused_computation.22.clone.1 | loop fusion | flops 6291456 | bytes 20987904 | tf_op jit(solution)/shard_map/while/body/eval_jaxpr/convert_element_type | solution.py:79
  234.4 3.4 fusion.170
  242.0 7.0 copy.94
  249.3 4.7 copy.96
  256.3 3.1 reshape_reshape.13
  265.9 3.8 convert_reduce_fusion.1
  270.3 8.5 %copy.98 = bf16[4,512,3,8,64]{1,0,4,3,2:T(4,128)(2,1)S(1)} copy(bf16[4,512,3,8,64]{1,4,3,0,2:T(8,128)(2,1)} %get-tuple-element.237) | data formatting | bytes 12582912 | tf_op jit(solution)/shard_map/convert_element_type | solution.py:157
  278.9 2.7 copy.107
  281.7 2.6 copy-done.10
  284.3 4.5 fusion.99
  288.9 4.3 reshape_reshape.12
  293.2 8.9 %fusion.117 = f32[2048,512]{1,0:T(8,128)} fusion(bf16[2048,1536]{0,1:T(8,128)(2,1)} %bitcast.160, bf16[512,1536]{1,0:T(8,128)(2,1)} %all-gather.5.cloned.1.call-done), kind=kOutput, calls=%fused_computation.203 | convolution fusion | flops 3221225472 | bytes 12058624 | tf_op jit(solution)/shard_map/tj,ij->ti/dot_general | solution.py:162
  302.1 44.8 %multiply_convert_fusion.1 = (bf16[2048,2048]{1,0:T(8,128)(2,1)}, f32[2048,2048]{1,0:T(8,128)}, f32[2048,2048]{1,0:T(8,128)}) fusion(f32[2048]{0:T(1024)S(1)} %copy-done.43, bf16[512,2048]{1,0:T(8,128)(2,1)} %all-gather.7.cloned.1.call-done, bf16[2048,512]{1,0:T(8,128)(2,1)S(1)} %copy-done.4, f32[512]{0:T(512)S(1)} %bitcast.180, f32[512]{0:T(512)S(1)} %bitcast.177, ...), kind=kOutput, calls=%fused_computation.68 | convolution fusion | flops 4578082816 | bytes 46166016 | tf_op jit(solution)/shard_map/dot_general | solution.py:114
  346.9 20.2 %convert_reduce_fusion = (f32[2048]{0:T(1024)S(1)}, bf16[2048,2048]{1,0:T(8,128)(2,1)}) fusion(f32[2048,2048]{1,0:T(8,128)} %get-tuple-element.280, f32[2048]{0:T(1024)S(1)} %copy-done.43, f32[2048,2048]{1,0:T(8,128)} %get-tuple-element.240, bf16[2048,512]{1,0:T(8,128)(2,1)} %param.28, bf16[2048,512]{1,0:T(8,128)(2,1)} %all-gather.9.cloned.1.call-done), kind=kOutput, calls=%fused_computation.67 | convolution fusion | flops 4341102592 | bytes 46153728 | tf_op jit(solution)/shard_map/to,fo->tf/dot_general | solution.py:130
  367.2 10.3 %fusion.95 = f32[512,2048]{1,0:T(8,128)} fusion(bf16[2048,2048]{1,0:T(8,128)(2,1)} %get-tuple-element.282, bf16[2048,512]{1,0:T(8,128)(2,1)S(1)} %copy-done.4, f32[512]{0:T(512)S(1)} %bitcast.181, f32[512]{0:T(512)S(1)} %bitcast.178, f32[2048]{0:T(1024)S(1)} %copy-done.38, f32[2048]{0:T(1024)S(1)} %copy-done.35), kind=kOutput, calls=%fused_computation.193 | convolution fusion | flops 4301258752 | bytes 14700544 | tf_op jit(solution)/shard_map/ti,tf->if/dot_general | solution.py:136
  377.5 7.7 fusion.102
  385.2 7.7 reshape_reshape.14
  393.0 4.9 convert_reduce_fusion.3
  397.9 10.6 %fusion.119 = f32[2048,512]{1,0:T(8,128)} fusion(bf16[2048,2048]{1,0:T(8,128)(2,1)} %get-tuple-element.239, bf16[2048,512]{1,0:T(8,128)(2,1)} %param.28), kind=kOutput, calls=%fused_computation.205 | convolution fusion | flops 4294967296 | bytes 14680064 | tf_op jit(solution)/shard_map/tf,to->fo/dot_general | solution.py:123
  408.5 7.8 reshape_reshape.15
  416.9 4.7 constant_dynamic-update-slice_fusion.6
  427.0 2.6 constant_dynamic-update-slice_fusion.1
  430.8 51.4 %all-reduce.6.cloned.1.call-done = f32[2,1576192]{1,0:T(2,128)} async-done(((f32[2,1576192]{1,0:T(2,128)}), f32[2,1576192]{1,0:T(2,128)}) %all-reduce.6.cloned.1.call-update) | async-done | bytes 12609552
  482.2 8.7 %constant_dynamic-slice_fusion = f32[1,1576192]{1,0:T(1,128)} fusion(f32[2,1576192]{1,0:T(2,128)} %all-reduce.6.cloned.1.call-done, u32[]{:T(128)} %bitcast.43), kind=kLoop, calls=%fused_computation.191 | loop fusion | bytes 12609540
  490.9 7.7 fusion.116
  498.7 3.0 fusion.80
  501.6 203.1 %all-reduce.4.cloned.1.call-done = f32[1,1576192]{1,0:T(1,128)} async-done(((f32[1,1576192]{1,0:T(1,128)}), f32[1,1576192]{1,0:T(1,128)}) %all-reduce.4.cloned.1.call-update) | async-done | bytes 6304784 | tf_op jit(solution)/shard_map/psum | solution.py:263
  707.9 17.4 %slice_reduce_fusion.2 = f32[393216]{0:T(1024)S(1)} fusion(f32[1,1576192]{1,0:T(1,128)} %all-reduce.4.cloned.1.call-done), kind=kLoop, calls=%fused_computation.136 | loop fusion | bytes 3145728 | tf_op jit(solution)/shard_map/slice | solution.py:274
  726.7 25.3 %slice_reduce_fusion = (f32[524288]{0:T(1024)}, f32[524288]{0:T(1024)}) fusion(f32[1,1576192]{1,0:T(1,128)} %all-reduce.4.cloned.1.call-done), kind=kLoop, calls=%fused_computation.127 | loop fusion | bytes 8388608 | tf_op jit(solution)/shard_map/slice | solution.py:274
  753.9 3.7 reshape.272
  761.2 2.7 add_multiply_fusion.3
  763.9 4.6 add_multiply_fusion.2
  768.6 3.8 add_multiply_fusion.1
  773.1 3.9 add_multiply_fusion
  (274 shorter events, 95.0 us)
Async XLA Ops:
  7.2 10.3 %copy-start.2 = (bf16[2048,512]{1,0:T(8,128)(2,1)S(1)}, bf16[2048,512]{1,0:T(8,128)(2,1)}, u32[]{:S(2)}) copy-start(bf16[2048,512]{1,0:T(8,128)(2,1)} %param.27) | copy-start | bytes 6291460
  7.2 11.9 %copy-start.27 = (bf16[256,512]{1,0:T(8,128)(2,1)S(1)}, bf16[256,512]{1,0:T(8,128)(2,1)}, u32[]{:S(2)}) copy-start(bf16[256,512]{1,0:T(8,128)(2,1)} %param.32) | copy-start | bytes 786436
  7.2 29.5 %all-gather.5.cloned.1.call-start = ((), (), s32[]{:S(2)}) async-start(), calls=%async_computation | async-start | bytes 2359296 | tf_op jit(solution)/shard_map/all_gather | solution.py:246
  8.0 294.1 %all-gather.7.cloned.1.call-start = ((), (), s32[]{:S(2)}) async-start(), calls=%async_computation.1 | async-start | bytes 3145728 | tf_op jit(solution)/shard_map/all_gather | solution.py:249
  8.7 338.2 %all-gather.9.cloned.1.call-start = ((), (), s32[]{:S(2)}) async-start(), calls=%async_computation.2 | async-start | bytes 3145728 | tf_op jit(solution)/shard_map/all_gather | solution.py:251
  9.4 472.7 %all-reduce.6.cloned.1.call-start = ((), (), s32[]{:S(2)}) async-start(), calls=%async_computation.4 | async-start | bytes 25219072
  12.3 10.2 %copy-start.20 = (bf16[2048,512]{1,0:T(8,128)(2,1)S(1)}, bf16[2048,512]{1,0:T(8,128)(2,1)}, u32[]{:S(2)}) copy-start(bf16[2048,512]{1,0:T(8,128)(2,1)} %param.28) | copy-start | bytes 6291460
  17.5 19.2 %copy-start.54 = (f32[1,512]{1,0:T(1,128)}, f32[1,512]{1,0:T(1,128)S(1)}, u32[]{:S(2)}) copy-start(f32[1,512]{1,0:T(1,128)S(1)} %get-tuple-element.276) | copy-start | bytes 6148
  17.5 19.2 %copy-start.59 = (f32[1,512]{1,0:T(1,128)}, f32[1,512]{1,0:T(1,128)S(1)}, u32[]{:S(2)}) copy-start(f32[1,512]{1,0:T(1,128)S(1)} %get-tuple-element.277) | copy-start | bytes 6148
  17.9 18.9 %copy-start.34 = (f32[2048]{0:T(1024)}, f32[2048]{0:T(1024)S(1)}, u32[]{:S(2)}) copy-start(f32[2048]{0:T(1024)S(1)} %broadcast_multiply_fusion.3) | copy-start | bytes 24580
  19.0 17.8 %copy-start.37 = (f32[2048]{0:T(1024)}, f32[2048]{0:T(1024)S(1)}, u32[]{:S(2)}) copy-start(f32[2048]{0:T(1024)S(1)} %add_rsqrt_fusion) | copy-start | bytes 24580
  19.1 66.3 %copy-start.30 = (f32[512,16]{0,1:T(8,128)}, f32[512,16]{0,1:T(8,128)S(1)}, u32[]{:S(2)}) copy-start(f32[512,16]{0,1:T(8,128)S(1)} %get-tuple-element.272) | copy-start | bytes 98308
  19.1 66.3 %copy-start.32 = (f32[512,16]{0,1:T(8,128)}, f32[512,16]{0,1:T(8,128)S(1)}, u32[]{:S(2)}) copy-start(f32[512,16]{0,1:T(8,128)S(1)} %get-tuple-element.273) | copy-start | bytes 98308
  141.4 6.0 copy-start.17
  167.7 6.0 copy-start.17
  194.1 6.0 copy-start.17
  220.4 6.0 copy-start.17
  242.0 7.0 copy-start.9
  249.3 4.8 copy-start.21
  249.3 4.8 copy-start.62
  254.0 5.3 copy-start.33
  278.9 5.4 copy-start.3
  278.9 5.4 copy-start.35
  278.9 5.4 copy-start.38
  278.9 5.4 copy-start.55
  278.9 5.4 copy-start.60
  293.2 8.9 %copy-start.4 = (bf16[2048,512]{1,0:T(8,128)(2,1)S(1)}, bf16[2048,512]{1,0:T(8,128)(2,1)}, u32[]{:S(2)}) copy-start(bf16[2048,512]{1,0:T(8,128)(2,1)} %param.27) | copy-start | bytes 6291460
  293.2 8.9 %copy-start.43 = (f32[2048]{0:T(1024)S(1)}, f32[2048]{0:T(1024)}, u32[]{:S(2)}) copy-start(f32[2048]{0:T(1024)} %convert_element_type.129) | copy-start | bytes 24580
  293.2 8.9 %copy-start.57 = (f32[1,512]{1,0:T(1,128)S(1)}, f32[1,512]{1,0:T(1,128)}, u32[]{:S(2)}) copy-start(f32[1,512]{1,0:T(1,128)} %get-tuple-element.278) | copy-start | bytes 6148
  293.2 8.9 %copy-start.58 = (f32[1,512]{1,0:T(1,128)S(1)}, f32[1,512]{1,0:T(1,128)}, u32[]{:S(2)}) copy-start(f32[1,512]{1,0:T(1,128)} %get-tuple-element.279) | copy-start | bytes 6148
  367.1 10.4 %copy-start.56 = (f32[1,512]{1,0:T(1,128)S(1)}, f32[1,512]{1,0:T(1,128)}, u32[]{:S(2)}) copy-start(f32[1,512]{1,0:T(1,128)} %copy-done.54) | copy-start | bytes 6148
  367.1 10.4 %copy-start.61 = (bf16[512,2048]{1,0:T(8,128)(2,1)S(1)}, bf16[512,2048]{1,0:T(8,128)(2,1)}, u32[]{:S(2)}) copy-start(bf16[512,2048]{1,0:T(8,128)(2,1)} %all-gather.7.cloned.1.call-done) | copy-start | bytes 6291460
  367.2 10.4 %copy-start.65 = (bf16[2048,2048]{1,0:T(8,128)(2,1)S(1)}, bf16[2048,2048]{1,0:T(8,128)(2,1)}, u32[]{:S(2)}) copy-start(bf16[2048,2048]{1,0:T(8,128)(2,1)} %get-tuple-element.282) | copy-start | bytes 25165828
  367.2 10.3 %copy-start.66 = (f32[2048,512]{1,0:T(8,128)S(1)}, f32[2048,512]{1,0:T(8,128)}, u32[]{:S(2)}) copy-start(f32[2048,512]{1,0:T(8,128)} %fusion.117) | copy-start | bytes 12582916
  416.3 5.3 copy-start.39
  416.3 5.9 copy-start.12
  416.9 6.4 copy-start.5
  429.6 275.1 %all-reduce.4.cloned.1.call-start = ((), (), s32[]{:S(2)}) async-start(), calls=%async_computation.3 | async-start | bytes 12609536 | tf_op jit(solution)/shard_map/psum | solution.py:263
  490.9 7.7 copy-start.29
  490.9 7.7 copy-start.52
  490.9 7.7 copy-start.53
  490.9 7.7 copy-start.63
  705.4 55.1 %copy-start.36 = (f32[6,256]{1,0:T(8,128)}, f32[6,256]{1,0:T(8,128)S(1)}, u32[]{:S(2)}) copy-start(f32[6,256]{1,0:T(8,128)S(1)} %reshape.269) | copy-start | bytes 18436
  707.9 53.2 %copy-start.19 = (f32[256,512]{1,0:T(8,128)}, f32[256,512]{1,0:T(8,128)S(1)}, u32[]{:S(2)}) copy-start(f32[256,512]{1,0:T(8,128)S(1)} %reshape.271) | copy-start | bytes 1572868
  752.0 6.5 copy-start.46
  752.0 6.5 copy-start.48
  752.0 6.5 copy-start.49
  752.0 7.8 copy-start.47
  752.0 7.8 copy-start.50
  752.0 7.8 %copy-start.51 = (f32[768]{0:T(1024)S(1)}, f32[768]{0:T(1024)}, u32[]{:S(2)}) copy-start(f32[768]{0:T(1024)} %param.45) | copy-start | bytes 9220
  752.0 8.5 %copy-start.42 = (bf16[6,256]{1,0:T(8,128)(2,1)S(1)}, bf16[6,256]{1,0:T(8,128)(2,1)}, u32[]{:S(2)}) copy-start(bf16[6,256]{1,0:T(8,128)(2,1)} %param.29) | copy-start | bytes 9220
  752.0 8.5 %copy-start.44 = (f32[6,256]{1,0:T(8,128)S(1)}, f32[6,256]{1,0:T(8,128)}, u32[]{:S(2)}) copy-start(f32[6,256]{1,0:T(8,128)} %param.36) | copy-start | bytes 18436
  752.1 8.5 %copy-start.45 = (f32[6,256]{1,0:T(8,128)S(1)}, f32[6,256]{1,0:T(8,128)}, u32[]{:S(2)}) copy-start(f32[6,256]{1,0:T(8,128)} %param.43) | copy-start | bytes 18436
  753.9 18.6 %copy-start.7 = (f32[1024,512]{1,0:T(8,128)}, f32[1024,512]{1,0:T(8,128)S(1)}, u32[]{:S(2)}) copy-start(f32[1024,512]{1,0:T(8,128)S(1)} %reshape.273) | copy-start | bytes 6291460
  753.9 9.9 %copy-start.15 = (bf16[256,1536]{1,0:T(8,128)(2,1)S(1)}, bf16[256,1536]{1,0:T(8,128)(2,1)}, u32[]{:S(2)}) copy-start(bf16[256,1536]{1,0:T(8,128)(2,1)} %param.30) | copy-start | bytes 2359300
  757.7 6.2 copy-start.11
  757.7 6.2 copy-start.26
  758.5 10.0 %copy-start.41 = (f32[1,1024]{1,0:T(1,128)}, f32[1,1024]{1,0:T(1,128)S(1)}, u32[]{:S(2)}) copy-start(f32[1,1024]{1,0:T(1,128)S(1)} %slice.178) | copy-start | bytes 12292
  759.9 8.6 %copy-start.40 = (f32[768]{0:T(1024)}, f32[768]{0:T(1024)S(1)}, u32[]{:S(2)}) copy-start(f32[768]{0:T(1024)S(1)} %slice_reduce_fusion.5) | copy-start | bytes 9220
  763.9 4.7 copy-start.8
  763.9 4.6 copy-start.13
  763.9 4.6 copy-start.22
  763.9 4.7 copy-start.23
  768.6 4.5 copy-start.25
  (20 other events, 62.7 us)
Sparse Core Ops, SparseCore 0:
  9.6 12.8 all-gather.4
  24.0 11.4 all-gather.6
  37.0 11.7 all-gather.8
  429.7 52.4 all-reduce.5
  491.0 213.6 all-reduce.3
where the time goes:
time: 792 us; the launch traced here: 784 us
  waiting for transfers between devices  257 us (32%)
  matrix products  223 us (28%)
  local copies, waits for them, and re-layouts  204 us (26%)
  other arithmetic  76.4 us (10%)
  between operations  15.2 us (2%)
  blocking collectives  8.52 us (1%)
    psum x1, waiting for transfers between devices, body(): summed = lax.psum(owner_part, 'rep').reshape(-1)  203 us
    unnamed x6, waiting for transfers between devices  53.5 us
    slice x6, local copies, waits for them, and re-layouts, body(): gradient = summed[offset:offset + length].reshape(own_shard.shape)  47.3 us
    dot_general x1, matrix products, local_pass(): jnp.dot(second_in, fc_weight, preferred_element_type=jnp.float32)  44.8 us
    convert_element_type x4, other arithmetic, attend_back(): (probs_f * (prob_grad - jnp.sum(prob_grad * probs_f, -1, keepdims=True)))...  32.2 us
    unnamed x137, local copies, waits for them, and re-layouts  29.6 us
    dot_general x8, matrix products, score_block(): jnp.einsum('qhd,khd->hqk', queries, keys_rot, preferred_element_type=jnp....  25 us
    dot_general x4, matrix products, attend_back(): jnp.einsum('qhd,khd->hqk', attended_grad, values, preferred_element_type=...  23.9 us
  transfers between devices with their start and end apart: 5, of which 2 were waited for; matrix products, arithmetic and copies ran while one was open for 42% of the time, Pallas kernels for 0%

commit v1 on v0

v1 whole, which is shorter than its diff:
```python
import functools

import jax
import jax.numpy as jnp
import numpy as np
from jax import lax
from jax.experimental import pallas as pl
from jax.experimental.pallas import tpu as pltpu
from jax.sharding import PartitionSpec as P

H = 8
ROT = 16
LEN = 512
ADAM_STEP = 10

LN_EPS = 1e-05
ADAM_EPS = 1e-08
BETA_ONE = 0.9
BETA_TWO = 0.95
LEARN_RATE = 0.02
WEIGHT_DECAY = 0.01
FIX_ONE = 1.0 - BETA_ONE**ADAM_STEP
FIX_TWO = 1.0 - BETA_TWO**ADAM_STEP
INV_ROOT_TWO = 0.7071067811865476
INV_ROOT_TWO_PI = 0.3989422804014327

bf16 = jnp.bfloat16
f32 = jnp.float32
SMALL_ROWS = 26


def dot_nn(a, b):
    return lax.dot_general(a, b, (((1,), (0,)), ((), ())), preferred_element_type=f32)


def dot_nt(a, b):
    return lax.dot_general(a, b, (((1,), (1,)), ((), ())), preferred_element_type=f32)


def dot_tn(a, b):
    return lax.dot_general(a, b, (((0,), (0,)), ((), ())), preferred_element_type=f32)


def full_spec(shape):
    zeros = (0,) * len(shape)
    return pl.BlockSpec(shape, lambda *_: zeros)


def cost(flops, moved, transcendentals=0):
    return pl.CostEstimate(
        flops=int(flops), bytes_accessed=int(moved), transcendentals=int(transcendentals)
    )


def vec_row(small_ref, i):
    n = SMALL_ROWS
    rows = [small_ref[o * n + 2 * i + k] for o in range(2) for k in range(2)]
    return jnp.concatenate(rows, 1)


def normalise(x):
    centre = x - jnp.mean(x, -1, keepdims=True)
    inv_dev = lax.rsqrt(jnp.mean(centre * centre, -1, keepdims=True) + LN_EPS)
    return centre * inv_dev, inv_dev


def norm_kernel(tok_ref, small_ref, first_ref, second_ref):
    normed, _ = normalise(tok_ref[...].astype(f32))
    first_ref[...] = (normed * vec_row(small_ref, 0) + vec_row(small_ref, 1)).astype(bf16)
    second_ref[...] = (normed * vec_row(small_ref, 2) + vec_row(small_ref, 3)).astype(bf16)


def norm_call(tokens, small):
    rows, width = tokens.shape
    tile = 512
    spec = pl.BlockSpec((tile, width), lambda i: (i, 0))
    out = jax.ShapeDtypeStruct((rows, width), bf16)
    return pl.pallas_call(
        norm_kernel,
        grid=(rows // tile,),
        in_specs=[spec, full_spec(small.shape)],
        out_specs=[spec, spec],
        out_shape=[out, out],
        cost_estimate=cost(20 * rows * width, 6 * rows * width),
        name="norm",
    )(tokens, small)


def ff_kernel(j, reps, meta, second_ref, grad_ref, fco_ref, fcx_ref, pro_ref, prx_ref, small_ref,
              own_ref, send_ref, act_ref, hg_ref, bias_ref):
    rel = pl.program_id(0)
    c = meta[0]
    idx = meta[1]
    o = rel ^ c
    rows, width = second_ref.shape
    half = width // 2
    cols = act_ref.shape[1]
    rr = own_ref.shape[2]
    proj = jnp.where(rel == 0, pro_ref[...], prx_ref[...])
    fco = fco_ref[...]
    fcx = fcx_ref[...]
    base = o * SMALL_ROWS + 18 + 4 * j
    bias = jnp.concatenate([small_ref[base + k] for k in range(cols // 128)], 1)
    own_lanes = pl.ds(pl.multiple_of(c * half, half), half)
    far_lanes = pl.ds(pl.multiple_of((1 - c) * half, half), half)
    tile = 256

    def block(i, total):
        r = pl.ds(pl.multiple_of(i * tile, tile), tile)
        hidden = dot_nn(second_ref[r, own_lanes], fco) + dot_nn(second_ref[r, far_lanes], fcx) + bias
        act_grad = dot_nt(grad_ref[r, :], proj)
        phi_cap = 0.5 + 0.5 * lax.erf(hidden * INV_ROOT_TWO)
        slope = phi_cap + hidden * (jnp.exp(-0.5 * hidden * hidden) * INV_ROOT_TWO_PI)
        act_ref[r, :] = (hidden * phi_cap).astype(bf16)
        hg = (act_grad * slope).astype(bf16)
        hg_ref[r, :] = hg
        return total + jnp.sum(hg.astype(f32).reshape(tile // 8, 8, cols), 0)

    total = lax.fori_loop(0, rows // tile, block, jnp.zeros((8, cols), f32))
    bias_ref[...] = jnp.sum(total, 0, keepdims=True)[None]

    gp = dot_tn(act_ref[...], grad_ref[...])

    def put_proj(ref):
        for a in range(reps):
            piece = gp[a * 2 * rr : (a + 1) * 2 * rr]
            ref[0, a ^ idx] = jnp.concatenate([piece[:rr], piece[rr:]], 1).astype(bf16)

    pl.when(rel == 0)(lambda: put_proj(own_ref))
    pl.when(rel == 1)(lambda: put_proj(send_ref))
    lanes = pl.ds(pl.multiple_of(o * cols, cols), cols)
    for ref, side in ((own_ref, own_lanes), (send_ref, far_lanes)):
        gf = dot_tn(second_ref[:, side], hg_ref[...])
        for a in range(reps):
            ref[1, a ^ idx, :, lanes] = gf[a * rr : (a + 1) * rr].astype(bf16)


def ff_call(j, reps, meta, second, grad, fc_own, fc_far, proj_own, proj_far, small):
    rows, width = second.shape
    ff = fc_own.shape[1]
    half = width // 2
    cols = ff // 4
    rr = half // reps
    buf = (2, reps, rr, 2 * cols)
    fc_spec = pl.BlockSpec((half, cols), lambda i, m: (0, (i ^ m[0]) * 2 + j))
    proj_spec = pl.BlockSpec((cols, width), lambda i, m: (j, 0))
    grid_spec = pltpu.PrefetchScalarGridSpec(
        num_scalar_prefetch=1,
        grid=(2,),
        in_specs=[
            full_spec((rows, width)),
            full_spec((rows, width)),
            fc_spec,
            fc_spec,
            proj_spec,
            proj_spec,
            full_spec(small.shape),
        ],
        out_specs=[
            full_spec(buf),
            full_spec(buf),
            pl.BlockSpec((rows, cols), lambda i, m: (0, i)),
            pl.BlockSpec((rows, cols), lambda i, m: (0, i)),
            pl.BlockSpec((1, 1, cols), lambda i, m: (i, 0, 0)),
        ],
    )
    return pl.pallas_call(
        functools.partial(ff_kernel, j, reps),
        grid_spec=grid_spec,
        out_shape=[
            jax.ShapeDtypeStruct(buf, bf16),
            jax.ShapeDtypeStruct(buf, bf16),
            jax.ShapeDtypeStruct((rows, 2 * cols), bf16),
            jax.ShapeDtypeStruct((rows, 2 * cols), bf16),
            jax.ShapeDtypeStruct((2, 1, cols), f32),
        ],
        cost_estimate=cost(8 * rows * width * 2 * cols, 4 * rows * width + 8 * rows * cols),
        name=f"feed_forward_{j}",
    )(meta, second, grad, fc_own, fc_far, proj_own, proj_far, small)


def rotate_rows(x, cosine, sine):
    parts = []
    for h in range(2):
        low, high = x[64 * h : 64 * h + 8], x[64 * h + 8 : 64 * h + 16]
        parts += [low * cosine - high * sine, high * cosine + low * sine, x[64 * h + 16 : 64 * h + 64]]
    return jnp.concatenate(parts, 0)


def attention_kernel(j, reps, meta, first_ref, grad_ref, wq_ref, wk_ref, wv_ref, xq_ref, xk_ref, xv_ref,
                     oo_ref, ox_ref, small_ref, trig_ref,
                     own_ref, send_ref, qg_ref, att_ref, bias_ref,
                     wt_ref, bcol_ref, qgs_ref, attt_ref, btot_ref):
    rel = pl.program_id(0)
    s = pl.program_id(1)
    c = meta[0]
    idx = meta[1]
    o = rel ^ c
    rows, width = first_ref.shape
    half = width // 2
    rr = own_ref.shape[2]
    own_lanes = pl.ds(pl.multiple_of(c * half, half), half)
    far_lanes = pl.ds(pl.multiple_of((1 - c) * half, half), half)

    @pl.when(s == 0)
    def _():
        for p, (own, far) in enumerate(((wq_ref, xq_ref), (wk_ref, xk_ref), (wv_ref, xv_ref))):
            wt_ref[128 * p : 128 * (p + 1), own_lanes] = own[...].T
            wt_ref[128 * p : 128 * (p + 1), far_lanes] = far[...].T
            row = p * 4 + o * 2 + j
            owner = row // 6
            bias = small_ref[owner * SMALL_ROWS + 12 + row - 6 * owner]
            bcol_ref[128 * p : 128 * (p + 1), :] = jnp.broadcast_to(bias, (128, 128)).T
        btot_ref[...] = jnp.zeros_like(btot_ref)

    seq = pl.ds(pl.multiple_of(s * LEN, LEN), LEN)
    first = first_ref[seq, :]
    grad = grad_ref[seq, :]
    out_w = jnp.where(rel == 0, oo_ref[...], ox_ref[...])
    mixed = dot_nt(wt_ref[...], first) + bcol_ref[:, :1]
    da_t = dot_nt(out_w, grad).astype(bf16)
    cosine, sine = trig_ref[0], trig_ref[1]
    q_t = rotate_rows(mixed[:128], cosine, sine).astype(bf16) * jnp.asarray(0.125, bf16)
    k_t = rotate_rows(mixed[128:256], cosine, sine).astype(bf16)
    v_t = mixed[256:].astype(bf16)
    k_tok = k_t.T
    v_tok = v_t.T
    hl = LEN // 2
    row_id = lax.broadcasted_iota(jnp.int32, (hl, hl), 0)
    col_id = lax.broadcasted_iota(jnp.int32, (hl, hl), 1)
    keep = row_id <= col_id
    zeros = jnp.zeros((64, LEN), bf16)
    att, dq, dk, dv = [], [], [], []
    for h in range(2):
        hs = slice(64 * h, 64 * h + 64)
        qh, kh, vh, dah = q_t[hs], k_t[hs], v_t[hs], da_t[hs]
        pad = (lambda u: jnp.concatenate([u, zeros], 0)) if h == 0 else (lambda u: jnp.concatenate([zeros, u], 0))
        qz, daz = pad(qh), pad(dah)
        att_h, dq_h = [], []
        dk_h = dv_h = None
        for t in range(2):
            ts = slice(hl * t, hl * t + hl)
            n = hl * (t + 1)
            score = dot_nn(k_tok[:n], qz[:, ts])
            diag = jnp.where(keep, score[n - hl :], -1e30)
            score = diag if t == 0 else jnp.concatenate([score[:hl], diag], 0)
            exps = jnp.exp(score - jnp.max(score, 0, keepdims=True))
            prob = exps * (1.0 / jnp.sum(exps, 0, keepdims=True))
            prob_b = prob.astype(bf16)
            att_h.append(dot_nn(vh[:, :n], prob_b))
            pg = dot_nn(v_tok[:n], daz[:, ts])
            sg = (prob * (pg - jnp.sum(pg * prob, 0, keepdims=True))).astype(bf16)
            dq_h.append(dot_nn(kh[:, :n], sg))
            dv_t = dot_nt(dah[:, ts], prob_b)
            dk_t = dot_nt(qh[:, ts], sg)
            if t == 0:
                dv_h, dk_h = dv_t, dk_t
            else:
                dv_h = jnp.concatenate([dv_h + dv_t[:, :hl], dv_t[:, hl:]], 1)
                dk_h = jnp.concatenate([dk_h + dk_t[:, :hl], dk_t[:, hl:]], 1)
        att.append(jnp.concatenate(att_h, 1))
        dq.append(jnp.concatenate(dq_h, 1) * 0.125)
        dk.append(dk_h)
        dv.append(dv_h)
    att_t = jnp.concatenate(att, 0).astype(bf16)
    dq_t = rotate_rows(jnp.concatenate(dq, 0), cosine, -sine)
    dk_t = rotate_rows(jnp.concatenate(dk, 0), cosine, -sine)
    qkv_t = jnp.concatenate([dq_t, dk_t, jnp.concatenate(dv, 0)], 0).astype(bf16)
    qkv_g = qkv_t.T
    qg_ref[...] = qkv_g
    qgs_ref[seq, :] = qkv_g
    att_ref[...] = att_t.T
    attt_ref[:, seq] = att_t
    btot_ref[...] += jnp.sum(qkv_g.astype(f32).reshape(LEN // 8, 8, 384), 0)

    @pl.when(s == pl.num_programs(1) - 1)
    def _():
        bias_ref[...] = jnp.sum(btot_ref[...], 0, keepdims=True)[None]
        for ref, side in ((own_ref, own_lanes), (send_ref, far_lanes)):
            gw = dot_tn(first_ref[:, side], qgs_ref[...])
            for a in range(reps):
                ref[o, a ^ idx, :, 0:384] = gw[a * rr : (a + 1) * rr].astype(bf16)
        go = dot_nn(attt_ref[...], grad_ref[...])
        hr = rr // 2

        def put_out(ref):
            for a in range(reps):
                piece = go[a * hr : (a + 1) * hr]
                for part in range(2):
                    both = [piece[:, 256 * part + 128 * k : 256 * part + 128 * (k + 1)] for k in range(2)]
                    ref[part, a ^ idx, :, 384:512] = jnp.concatenate(both, 0).astype(bf16)

        pl.when(rel == 0)(lambda: put_out(own_ref))
        pl.when(rel == 1)(lambda: put_out(send_ref))


def trig_tables():
    freqs = np.power(np.float32(10000.0), -np.arange(0, ROT, 2).astype(np.float32) / np.float32(ROT))
    angles = (np.arange(LEN).astype(np.float32)[None, :] * freqs[:, None]).astype(np.float32)
    return np.stack([np.cos(angles), np.sin(angles)]).astype(np.float32)


def attention_call(j, reps, meta, first, grad, qkv_own, qkv_far, out_own, out_far, small, trig):
    rows, width = first.shape
    half = width // 2
    rr = half // reps
    buf = (2, reps, rr, 512)
    w_specs = [
        pl.BlockSpec((half, 128), functools.partial(lambda p, r, s, m: (0, p * 4 + (r ^ m[0]) * 2 + j), p))
        for p in range(3)
    ]
    o_spec = pl.BlockSpec((128, width), lambda r, s, m: (j, 0))
    grid_spec = pltpu.PrefetchScalarGridSpec(
        num_scalar_prefetch=1,
        grid=(2, rows // LEN),
        in_specs=[
            full_spec((rows, width)),
            full_spec((rows, width)),
            *w_specs,
            *w_specs,
            o_spec,
            o_spec,
            full_spec(small.shape),
            full_spec(trig.shape),
        ],
        out_specs=[
            full_spec(buf),
            full_spec(buf),
            pl.BlockSpec((LEN, 384), lambda r, s, m: (s, r)),
            pl.BlockSpec((LEN, 128), lambda r, s, m: (s, r)),
            pl.BlockSpec((1, 1, 384), lambda r, s, m: (r, 0, 0)),
        ],
        scratch_shapes=[
            pltpu.VMEM((384, width), bf16),
            pltpu.VMEM((384, 128), f32),
            pltpu.VMEM((rows, 384), bf16),
            pltpu.VMEM((128, rows), bf16),
            pltpu.VMEM((8, 384), f32),
        ],
    )
    flops = 2 * rows * width * (2 * 768 + 2 * 256) + 4 * 6 * 2 * rows * LEN * 128
    return pl.pallas_call(
        functools.partial(attention_kernel, j, reps),
        grid_spec=grid_spec,
        out_shape=[
            jax.ShapeDtypeStruct(buf, bf16),
            jax.ShapeDtypeStruct(buf, bf16),
            jax.ShapeDtypeStruct((rows, 768), bf16),
            jax.ShapeDtypeStruct((rows, 256), bf16),
            jax.ShapeDtypeStruct((2, 1, 384), f32),
        ],
        cost_estimate=cost(flops, 4 * rows * width + 2 * rows * 1024),
        name=f"attention_{j}",
    )(meta, first, grad, *[qkv_own] * 3, *[qkv_far] * 3, out_own, out_far, small, trig)


def output_kernel(meta, tok_ref, grad_ref, at0_ref, at1_ref, ac0_ref, ac1_ref, hg0_ref, hg1_ref, qg0_ref, qg1_ref,
                  oo_ref, ox_ref, po_ref, px_ref, fo_ref, fx_ref, wo_ref, wx_ref, small_ref,
                  qb0_ref, qb1_ref, fb0_ref, fb1_ref,
                  lay_ref, tg_ref, own_ref, send_ref,
                  wgo_ref, wgx_ref, sg_ref, fg_ref, tot_ref, qb_ref):
    i = pl.program_id(0)
    c = meta[0]
    tile, width = tok_ref.shape
    half = width // 2
    own_lanes = pl.ds(pl.multiple_of(c * half, half), half)
    far_lanes = pl.ds(pl.multiple_of((1 - c) * half, half), half)

    @pl.when(i == 0)
    def _():
        for w_ref, g_ref in ((wo_ref, wgo_ref), (wx_ref, wgx_ref)):
            for j in range(2):
                for rel in range(2):
                    for p in range(3):
                        src = pl.ds(pl.multiple_of((p * 4 + (rel ^ c) * 2 + j) * 128, 128), 128)
                        dst = (j * 6 + rel * 3 + p) * 128
                        g_ref[:, dst : dst + 128] = w_ref[:, src]
        tot_ref[...] = jnp.zeros_like(tot_ref)

    x = tok_ref[...].astype(f32)
    grad = grad_ref[...].astype(f32)
    normed, inv_dev = normalise(x)
    at0, at1 = at0_ref[...], at1_ref[...]
    acc = dot_nn(jnp.concatenate([at0[:, :128], at1[:, :128]], 1), oo_ref[...])
    acc += dot_nn(jnp.concatenate([at0[:, 128:], at1[:, 128:]], 1), ox_ref[...])
    for j, ac_ref in enumerate((ac0_ref, ac1_ref)):
        acc += dot_nn(ac_ref[:, :512], po_ref[512 * j : 512 * (j + 1), :])
        acc += dot_nn(ac_ref[:, 512:], px_ref[512 * j : 512 * (j + 1), :])
    lay_ref[...] = (x + acc + (vec_row(small_ref, 4) + vec_row(small_ref, 5))).astype(bf16)

    for f_ref, wg_ref, lanes in ((fo_ref, wgo_ref, own_lanes), (fx_ref, wgx_ref, far_lanes)):
        total = None
        for j, hg_ref in enumerate((hg0_ref, hg1_ref)):
            for rel in range(2):
                cols = pl.ds(pl.multiple_of((rel ^ c) * 1024 + 512 * j, 512), 512)
                term = dot_nt(hg_ref[:, 512 * rel : 512 * (rel + 1)], f_ref[:, cols])
                total = term if total is None else total + term
        sg_ref[:, lanes] = total
        fg_ref[:, lanes] = dot_nt(qg0_ref[...], wg_ref[:, :768]) + dot_nt(qg1_ref[...], wg_ref[:, 768:])
    second_g = sg_ref[...]
    first_g = fg_ref[...]
    e = first_g * vec_row(small_ref, 0) + second_g * vec_row(small_ref, 2)
    ln = inv_dev * (
        e - jnp.mean(e, -1, keepdims=True) - normed * jnp.mean(e * normed, -1, keepdims=True)
    )
    tg_ref[...] = (grad + ln).astype(bf16)
    for k, term in enumerate((first_g * normed, first_g, second_g * normed, second_g, grad)):
        tot_ref[k] += jnp.sum(term.reshape(tile // 8, 8, width), 0)

    @pl.when(i == pl.num_programs(0) - 1)
    def _():
        for j, b_ref in enumerate((qb0_ref, qb1_ref)):
            for rel in range(2):
                for p in range(3):
                    qb_ref[p * 4 + (rel ^ c) * 2 + j] = b_ref[rel][:, 128 * p : 128 * (p + 1)]
        sums = [jnp.sum(tot_ref[k], 0, keepdims=True) for k in range(5)]
        sums.append(sums[4])
        for ref, rel in ((own_ref, 0), (send_ref, 1)):
            owner = rel ^ c
            for k in range(6):
                for part in range(2):
                    low = sums[k][:, 128 * part : 128 * (part + 1)]
                    high = sums[k][:, 256 + 128 * part : 256 + 128 * (part + 1)]
                    ref[2 * k + part] = jnp.where(owner == 0, low, high)
            for k in range(6):
                ref[12 + k] = qb_ref[owner * 6 + k]
            for j, b_ref in enumerate((fb0_ref, fb1_ref)):
                for k in range(4):
                    ref[18 + 4 * j + k] = b_ref[rel][:, 128 * k : 128 * (k + 1)]
            for k in range(SMALL_ROWS, 32):
                ref[k] = jnp.zeros((1, 128), f32)


def output_call(meta, tokens, grad, atts, acts, hgs, qgs, out_w, proj_w, fc_w, qkv_w, small, qbs, fbs):
    rows, width = tokens.shape
    tile = 256
    blk = lambda n: pl.BlockSpec((tile, n), lambda i, m: (i, 0))
    weights = [*out_w, *proj_w, *fc_w, *qkv_w]
    tail = [small, *qbs, *fbs]
    packed = (32, 1, 128)
    grid_spec = pltpu.PrefetchScalarGridSpec(
        num_scalar_prefetch=1,
        grid=(rows // tile,),
        in_specs=[
            blk(width),
            blk(width),
            *[blk(a.shape[1]) for a in (*atts, *acts, *hgs, *qgs)],
            *[full_spec(w.shape) for w in weights],
            *[full_spec(w.shape) for w in tail],
        ],
        out_specs=[blk(width), blk(width), full_spec(packed), full_spec(packed)],
        scratch_shapes=[
            pltpu.VMEM(qkv_w[0].shape, bf16),
            pltpu.VMEM(qkv_w[0].shape, bf16),
            pltpu.VMEM((tile, width), f32),
            pltpu.VMEM((tile, width), f32),
            pltpu.VMEM((5, 8, width), f32),
            pltpu.VMEM((12, 1, 128), f32),
        ],
    )
    return pl.pallas_call(
        output_kernel,
        grid_spec=grid_spec,
        out_shape=[
            jax.ShapeDtypeStruct((rows, width), bf16),
            jax.ShapeDtypeStruct((rows, width), bf16),
            jax.ShapeDtypeStruct(packed, f32),
            jax.ShapeDtypeStruct(packed, f32),
        ],
        cost_estimate=cost(2 * rows * width * (512 + 2048 * 2 + 1536), 2 * rows * (4 * 512 + 4 * 2048)),
        name="outputs",
    )(meta, tokens, grad, *atts, *acts, *hgs, *qgs, *weights, *tail)


def sum_kernel(n_in, groups_out, *refs):
    parts = len(groups_out)
    ins, outs = refs[: parts * n_in], refs[parts * n_in :]
    k = 0
    for part, count in enumerate(groups_out):
        terms = [r for r in ins[part * n_in : (part + 1) * n_in]]
        rows = terms[0].shape[0] // count
        for piece in range(count):
            sl = slice(piece * rows, (piece + 1) * rows)
            total = terms[0][sl].astype(f32)
            for t in terms[1:]:
                total += t[sl].astype(f32)
            outs[k][...] = total.astype(outs[k].dtype)
            k += 1


def sum_call(parts, count, name):
    n_in = len(parts[0])
    ins = [a for part in parts for a in part]
    outs = []
    for part in parts:
        a = part[0]
        outs += [jax.ShapeDtypeStruct((a.shape[0] // count, *a.shape[1:]), a.dtype)] * count
    moved = sum(a.size * a.dtype.itemsize for a in ins)
    got = pl.pallas_call(
        functools.partial(sum_kernel, n_in, [count] * len(parts)),
        out_shape=outs,
        cost_estimate=cost(moved, 2 * moved),
        name=name,
    )(*ins)
    return [got[i * count : (i + 1) * count] for i in range(len(parts))]


def join_kernel(n_in, *refs):
    parts = len(refs) // (n_in + 1)
    for part in range(parts):
        out = refs[parts * n_in + part]
        rows = out.shape[0] // n_in
        for k in range(n_in):
            out[k * rows : (k + 1) * rows] = refs[part * n_in + k][...]


def join_call(parts, name):
    n_in = len(parts[0])
    ins = [a for part in parts for a in part]
    outs = [
        jax.ShapeDtypeStruct((part[0].shape[0] * n_in, *part[0].shape[1:]), part[0].dtype) for part in parts
    ]
    moved = sum(a.size * a.dtype.itemsize for a in ins)
    return pl.pallas_call(
        functools.partial(join_kernel, n_in),
        out_shape=outs,
        cost_estimate=cost(0, 2 * moved),
        name=name,
    )(*ins)


def exchange(a, reps, mask):
    return lax.ppermute(a, "rep", [(i, i ^ mask) for i in range(reps)])


def swap(a):
    return lax.ppermute(a, "opt", [(0, 1), (1, 0)])


def bit_groups(reps):
    bits = reps.bit_length() - 1
    return [(lo, min(2, bits - lo)) for lo in range(0, bits, 2)]


def relative_base(index, reps):
    out = 0
    for lo, n in bit_groups(reps):
        out = (out << n) | ((index >> lo) & ((1 << n) - 1))
    return out


def reduce_set(own, received, reps, tag):
    groups = bit_groups(reps)
    parts = None
    n = 1 << groups[0][1]
    w = own.shape[1:]
    own2, rec2 = own.reshape(2 * w[0], *w[1:]), received.reshape(2 * w[0], *w[1:])
    (pieces,) = sum_call([[own2, rec2]], 2 * n, f"{tag}_pair")
    pieces = [pieces[:n], pieces[n:]]
    for g, (lo, bits) in enumerate(groups):
        terms = [
            [part[0], *[exchange(part[k], reps, k << lo) for k in range(1, 1 << bits)]] for part in pieces
        ]
        n = 1 << groups[g + 1][1] if g + 1 < len(groups) else 1
        pieces = sum_call(terms, n, f"{tag}_sum{g}")
    parts = [part[0] for part in pieces]
    for g, (lo, bits) in reversed(list(enumerate(groups))):
        pieces = [
            [part, *[exchange(part, reps, k << lo) for k in range(1, 1 << bits)]] for part in parts
        ]
        if g:
            parts = join_call(pieces, f"{tag}_join{g}")
    return pieces


def adamw(grad, mean, square, weight):
    new_mean = BETA_ONE * mean + (1.0 - BETA_ONE) * grad
    new_square = BETA_TWO * square + (1.0 - BETA_TWO) * grad * grad
    step = -LEARN_RATE * (
        new_mean * (1.0 / FIX_ONE) / (jnp.sqrt(new_square * (1.0 / FIX_TWO)) + ADAM_EPS)
        + WEIGHT_DECAY * weight.astype(f32)
    )
    return step, new_mean, new_square


def pick(refs, which, row, cols):
    out = refs[0][row, :, cols]
    for k in range(1, len(refs)):
        out = jnp.where(which == k, refs[k][row, :, cols], out)
    return out.astype(f32)


def adam_block(grad, m_ref, s_ref, w_ref, g_out, st_out, m_out, s_out, at):
    step, mean, square = adamw(grad, m_ref[at], s_ref[at], w_ref[at])
    g_out[at] = grad
    st_out[at] = step
    m_out[at] = mean
    s_out[at] = square


def adam_ff_kernel(n, low, meta, *refs):
    pieces, refs = refs[: 4 * n], refs[4 * n :]
    proj, fc = refs[0:3], refs[3:6]
    proj_out, fc_out = refs[6:10], refs[10:14]
    q = pl.program_id(0)
    idx = meta[1]
    which = q ^ (idx // low)
    idx_low = idx % low
    for j in range(2):
        p_refs = pieces[2 * n * j : 2 * n * j + n]
        f_refs = pieces[2 * n * j + n : 2 * n * j + 2 * n]
        rr = p_refs[0].shape[1]
        for z in range(low):
            row = z ^ idx_low
            for k in range(2):
                grad = pick(p_refs, which, row, slice(512 * k, 512 * k + 512))
                at = (j, slice((2 * z + k) * rr, (2 * z + k + 1) * rr), slice(None))
                adam_block(grad, *proj, *proj_out, at)
                grad = pick(f_refs, which, row, slice(512 * k, 512 * k + 512))
                at = (slice(z * rr, (z + 1) * rr), slice(1024 * k + 512 * j, 1024 * k + 512 * j + 512))
                adam_block(grad, *fc, *fc_out, at)


def adam_qkv_kernel(n, low, meta, *refs):
    pieces, refs = refs[: 4 * n], refs[4 * n :]
    qkv, out = refs[0:3], refs[3:6]
    qkv_out, out_out = refs[6:10], refs[10:14]
    q = pl.program_id(0)
    idx = meta[1]
    which = q ^ (idx // low)
    idx_low = idx % low
    for j in range(2):
        for part in range(2):
            g_refs = pieces[2 * n * j + n * part : 2 * n * j + n * part + n]
            rr = g_refs[0].shape[1]
            hr = rr // 2
            for z in range(low):
                grad = pick(g_refs, which, z ^ idx_low, slice(None))
                for p in range(3):
                    col = (p * 4 + part * 2 + j) * 128
                    at = (slice(z * rr, (z + 1) * rr), slice(col, col + 128))
                    adam_block(grad[:, 128 * p : 128 * (p + 1)], *qkv, *qkv_out, at)
                for k in range(2):
                    col = 256 * part + 128 * k
                    at = (j, slice(z * hr, (z + 1) * hr), slice(col, col + 128))
                    adam_block(grad[k * hr : (k + 1) * hr, 384:], *out, *out_out, at)


def adam_call(kernel, reps, meta, sets, first, second, first_spec, second_spec, name):
    pieces = [a for pair in sets for part in pair for a in part]
    n = len(sets[0][0])
    low = reps // n
    ins = [*pieces, *first, *second]
    outs = [jax.ShapeDtypeStruct(first[0].shape, f32)] * 4 + [jax.ShapeDtypeStruct(second[0].shape, f32)] * 4
    grid_spec = pltpu.PrefetchScalarGridSpec(
        num_scalar_prefetch=1,
        grid=(n,),
        in_specs=[*[full_spec(a.shape) for a in pieces], *[first_spec] * 3, *[second_spec] * 3],
        out_specs=[*[first_spec] * 4, *[second_spec] * 4],
    )
    size = first[0].size + second[0].size
    return pl.pallas_call(
        functools.partial(kernel, n, low),
        grid_spec=grid_spec,
        out_shape=outs,
        cost_estimate=cost(20 * size, 28 * size),
        name=name,
    )(meta, *ins)


def body(
    tokens,
    out_grad,
    vectors,
    qkv_weight,
    qkv_bias,
    out_weight,
    fc_weight,
    fc_bias,
    proj_weight,
    mean_vectors,
    mean_qkv_weight,
    mean_qkv_bias,
    mean_out_weight,
    mean_fc_weight,
    mean_fc_bias,
    mean_proj_weight,
    square_vectors,
    square_qkv_weight,
    square_qkv_bias,
    square_out_weight,
    square_fc_weight,
    square_fc_bias,
    square_proj_weight,
):
    reps = lax.axis_size("rep")
    c = lax.axis_index("opt")
    idx = relative_base(lax.axis_index("rep"), reps)
    meta = jnp.stack([c, idx]).astype(jnp.int32)
    trig = jnp.asarray(trig_tables())

    packed = jnp.concatenate(
        [vectors.reshape(12, 128), qkv_bias.reshape(6, 128), fc_bias.reshape(8, 128)], 0
    )
    small = lax.all_gather(packed, "opt", axis=0, tiled=True).astype(f32).reshape(2 * SMALL_ROWS, 1, 128)
    fc_far = swap(fc_weight)
    proj_far = swap(proj_weight)
    qkv_far = swap(qkv_weight)
    out_far = swap(out_weight)

    first, second = norm_call(tokens, small)
    ff = [
        ff_call(j, reps, meta, second, out_grad, fc_weight, fc_far, proj_weight, proj_far, small)
        for j in range(2)
    ]
    ff_sets = [reduce_set(r[0], swap(r[1]), reps, f"ff{j}") for j, r in enumerate(ff)]
    att = [
        attention_call(j, reps, meta, first, out_grad, qkv_weight, qkv_far, out_weight, out_far, small, trig)
        for j in range(2)
    ]
    att_sets = [reduce_set(r[0], swap(r[1]), reps, f"att{j}") for j, r in enumerate(att)]
    layer_out, tokens_grad, small_own, small_send = output_call(
        meta,
        tokens,
        out_grad,
        [r[3] for r in att],
        [r[2] for r in ff],
        [r[3] for r in ff],
        [r[2] for r in att],
        (out_weight, out_far),
        (proj_weight, proj_far),
        (fc_weight, fc_far),
        (qkv_weight, qkv_far),
        small,
        [r[4] for r in att],
        [r[4] for r in ff],
    )

    ((total,),) = sum_call([[small_own, swap(small_send)]], 1, "small_pair")
    for g, (lo, bits) in enumerate(bit_groups(reps)):
        terms = [total, *[exchange(total, reps, k << lo) for k in range(1, 1 << bits)]]
        ((total,),) = sum_call([terms], 1, f"small_sum{g}")
    flat = total.reshape(32, 128)
    g_vec = flat[:12].reshape(6, 256)
    g_qb = flat[12:18].reshape(768)
    g_fb = flat[18:26].reshape(1024)

    n = 1 << bit_groups(reps)[0][1]
    view = lambda a: a.reshape(2, 512, 512)
    fq = proj_weight.shape[0] // 2 // n
    proj_adam = adam_call(
        adam_ff_kernel,
        reps,
        meta,
        ff_sets,
        [view(a) for a in (mean_proj_weight, square_proj_weight, proj_weight)],
        [mean_fc_weight, square_fc_weight, fc_weight],
        pl.BlockSpec((2, fq, 512), lambda q, m: (0, q, 0)),
        pl.BlockSpec((256 // n, 2048), lambda q, m: (q, 0)),
        "adam_ff",
    )
    a_proj = [a.reshape(1024, 512) for a in proj_adam[:4]]
    a_fc = proj_adam[4:]
    view_o = lambda a: a.reshape(2, 128, 512)
    qkv_adam = adam_call(
        adam_qkv_kernel,
        reps,
        meta,
        att_sets,
        [mean_qkv_weight, square_qkv_weight, qkv_weight],
        [view_o(a) for a in (mean_out_weight, square_out_weight, out_weight)],
        pl.BlockSpec((256 // n, 1536), lambda q, m: (q, 0)),
        pl.BlockSpec((2, 128 // n, 512), lambda q, m: (0, q, 0)),
        "adam_qkv",
    )
    a_qkv = qkv_adam[:4]
    a_out = [a.reshape(256, 512) for a in qkv_adam[4:]]
    a_vec = (g_vec, *adamw(g_vec, mean_vectors, square_vectors, vectors))
    a_qb = (g_qb, *adamw(g_qb, mean_qkv_bias, square_qkv_bias, qkv_bias))
    a_fb = (g_fb, *adamw(g_fb, mean_fc_bias, square_fc_bias, fc_bias))
    order = (a_vec, a_qkv, a_qb, a_out, a_fc, a_fb, a_proj)
    return (layer_out, tokens_grad, *[a[k] for k in range(4) for a in order])


def solution(mesh):
    rows = P(("rep", "opt"), None)
    weights = (P(None, "opt"), P("opt", None), P("opt"), P("opt", None), P("opt", None), P("opt"), P("opt", None))
    in_specs = (rows, rows, *weights, *weights, *weights)
    out_specs = (rows, rows, *weights, *weights, *weights, *weights)
    return jax.shard_map(body, mesh=mesh, in_specs=in_specs, out_specs=out_specs, check_vma=False)
```

time: 792 us -> 389 us (0.49)
  waiting for transfers between devices: 257 us -> 26.3 us
  matrix products: 223 us -> 0 us
  Pallas kernels: 0 us -> 201 us
  local copies, waits for them, and re-layouts: 204 us -> 8.79 us
  starting transfers between devices: 0.19 us -> 143 us
  other arithmetic: 76.4 us -> 3.18 us
  between operations: 15.2 us -> 2.04 us
    dot_general x40 -> x0, matrix products: 223 us -> none  [the longest x1 44.8 us: local_pass(): jnp.dot(second_in, fc_weight, preferred_element_type=jnp.float32)]
    psum x1 -> x0, waiting for transfers between devices: 203 us -> none  [body(): summed = lax.psum(owner_part, 'rep').reshape(-1)]
    pallas_call x0 -> x27, Pallas kernels: none -> 201 us  [the longest x2 78.1 us: attention_call(): pl.pallas_call(functools.partial(attention_kernel, j, reps), grid_spec=gr...]
    ppermute x0 -> x111, starting transfers between devices: none -> 143 us  [the longest x102 140 us: exchange(): return lax.ppermute(a, 'rep', [(i, i ^ mask) for i in range(reps)])]
    unnamed x6 -> x0, waiting for transfers between devices: 53.5 us -> none
    slice x11 -> x3, local copies, waits for them, and re-layouts: 51.4 us -> 2.07 us  [the longest x1 0.71 us: body(): g_vec = flat[:12].reshape(6, 256)]
    convert_element_type x7 -> x0, other arithmetic: 32.9 us -> none  [the longest x4 32.2 us: attend_back(): (probs_f * (prob_grad - jnp.sum(prob_grad * probs_f, -1, keepdims=True)))...]
    while x38 -> x0, local copies, waits for them, and re-layouts: 29 us -> none  [the longest x3 17.3 us: local_pass(): lax.map(attend_back, (queries, keys_rot, values, row_top, row_total, atte...]
  transfers between devices with their start and end apart: 5 -> 111, of which waited for: 2 -> 20; matrix products, arithmetic and copies ran while one was open for 42% -> 2% of each run, Pallas kernels for 0% -> 49%
where the time goes in v1:
time: 389 us; the launch traced here: 388 us
  Pallas kernels  201 us (52%)
  starting transfers between devices  143 us (37%)
  waiting for transfers between devices  26.3 us (7%)
  local copies, waits for them, and re-layouts  8.79 us (2%)
    ppermute x102, starting transfers between devices, exchange(): return lax.ppermute(a, 'rep', [(i, i ^ mask) for i in range(reps)])  140 us
    pallas_call x2, Pallas kernels, attention_call(): pl.pallas_call(functools.partial(attention_kernel, j, reps), grid_spec=gr...  78.1 us
    pallas_call x2, Pallas kernels, ff_call(): pl.pallas_call(functools.partial(ff_kernel, j, reps), grid_spec=grid_spec...  40.6 us
    pallas_call x15, Pallas kernels, sum_call(): pl.pallas_call(functools.partial(sum_kernel, n_in, [count] * len(parts)),...  26.7 us
    ppermute x102, waiting for transfers between devices, exchange(): return lax.ppermute(a, 'rep', [(i, i ^ mask) for i in range(reps)])  25.2 us
    pallas_call x1, Pallas kernels, output_call(): pl.pallas_call(output_kernel, grid_spec=grid_spec, out_shape=[jax.ShapeDt...  24.8 us
    pallas_call x2, Pallas kernels, adam_call(): pl.pallas_call(functools.partial(kernel, n, low), grid_spec=grid_spec, ou...  19.9 us
  transfers between devices with their start and end apart: 111, of which 20 were waited for; matrix products, arithmetic and copies ran while one was open for 2% of the time, Pallas kernels for 49%

profile of v1, /device:TPU:0, one launch (start us, length us, event | category | flops | bytes accessed | tf_op | source)
XLA Modules:
  0.0 387.7 jit_solution(13494974006572883730)
XLA Ops:
  3.2 3.5 all-gather
  7.4 5.0 %norm.1 = (bf16[2048,512]{1,0:T(8,128)(2,1)}, bf16[2048,512]{1,0:T(8,128)(2,1)}) custom-call(bf16[2048,512]{1,0:T(8,128)(2,1)} %tok_ref.3, f32[52,1,128]{2,1,0:T(1,128)} %reshape.193.small_ref), custom_call_target="tpu_custom_call" | custom-call | flops 20971520 | bytes 6291456 | tf_op jit(solution)/shard_map/norm/pallas_call | solution.py:78
  13.9 39.0 %attention_0.1 = (bf16[2,16,16,512]{3,2,1,0:T(8,128)(2,1)}, bf16[2,16,16,512]{3,2,1,0:T(8,128)(2,1)}, bf16[2048,768]{1,0:T(8,128)(2,1)}, bf16[2048,256]{1,0:T(8,128)(2,1)}, f32[2,1,384]{2,1,0:T(1,128)}) custom-call(s32[2]{0:T(128)} %pad_add_fusion.meta, bf16[2048,512]{1,0:T(8,128)(2,1)} %get-tuple-element.152.first_ref, bf16[2048,512]{1,0:T(8,128)(2,1)} %grad_ref.9, ...), custom_call_target="tpu_custom_call" | custom-call | flops 10737418240 | bytes 8388608 | tf_op jit(solution)/shard_map/attention_0/pallas_call | solution.py:342
  53.4 39.0 %attention_1.1 = (bf16[2,16,16,512]{3,2,1,0:T(8,128)(2,1)}, bf16[2,16,16,512]{3,2,1,0:T(8,128)(2,1)}, bf16[2048,768]{1,0:T(8,128)(2,1)}, bf16[2048,256]{1,0:T(8,128)(2,1)}, f32[2,1,384]{2,1,0:T(1,128)}) custom-call(s32[2]{0:T(128)} %pad_add_fusion.meta, bf16[2048,512]{1,0:T(8,128)(2,1)} %get-tuple-element.152.first_ref, bf16[2048,512]{1,0:T(8,128)(2,1)} %grad_ref.9, ...), custom_call_target="tpu_custom_call" | custom-call | flops 10737418240 | bytes 8388608 | tf_op jit(solution)/shard_map/attention_1/pallas_call | solution.py:342
  94.0 20.3 %feed_forward_0.1 = (bf16[2,16,16,1024]{3,2,1,0:T(8,128)(2,1)}, bf16[2,16,16,1024]{3,2,1,0:T(8,128)(2,1)}, bf16[2048,1024]{1,0:T(8,128)(2,1)}, bf16[2048,1024]{1,0:T(8,128)(2,1)}, f32[2,1,512]{2,1,0:T(1,128)}) custom-call(s32[2]{0:T(128)} %pad_add_fusion.meta, bf16[2048,512]{1,0:T(8,128)(2,1)} %get-tuple-element.155.second_ref, bf16[2048,512]{1,0:T(8,128)(2,1)} %grad_ref.9, ...), custom_call_target="tpu_custom_call" | custom-call | flops 8589934592 | bytes 12582912 | tf_op jit(solution)/shard_map/feed_forward_0/pallas_call | solution.py:167
  114.7 20.3 %feed_forward_1.1 = (bf16[2,16,16,1024]{3,2,1,0:T(8,128)(2,1)}, bf16[2,16,16,1024]{3,2,1,0:T(8,128)(2,1)}, bf16[2048,1024]{1,0:T(8,128)(2,1)}, bf16[2048,1024]{1,0:T(8,128)(2,1)}, f32[2,1,512]{2,1,0:T(1,128)}) custom-call(s32[2]{0:T(128)} %pad_add_fusion.meta, bf16[2048,512]{1,0:T(8,128)(2,1)} %get-tuple-element.155.second_ref, bf16[2048,512]{1,0:T(8,128)(2,1)} %grad_ref.9, ...), custom_call_target="tpu_custom_call" | custom-call | flops 8589934592 | bytes 12582912 | tf_op jit(solution)/shard_map/feed_forward_1/pallas_call | solution.py:167
  135.2 24.8 %outputs.1 = (bf16[2048,512]{1,0:T(8,128)(2,1)}, bf16[2048,512]{1,0:T(8,128)(2,1)}, f32[32,1,128]{2,1,0:T(1,128)}, f32[32,1,128]{2,1,0:T(1,128)}) custom-call(s32[2]{0:T(128)} %pad_add_fusion.meta, bf16[2048,512]{1,0:T(8,128)(2,1)} %tok_ref.3, bf16[2048,512]{1,0:T(8,128)(2,1)} %grad_ref.9, bf16[2048,256]{1,0:T(8,128)(2,1)} %get-tuple-element.153.at0_ref, ...), custom_call_target="tpu_custom_call" | custom-call | flops 12884901888 | bytes 41943040 | tf_op jit(solution)/shard_map/outputs/pallas_call | solution.py:461
  163.4 2.8 collective-permute-start.5
  166.3 1.9 collective-permute-done.5.refs_1_
  168.2 2.1 collective-permute-start.6
  170.3 1.9 collective-permute-done.6.refs_2_
  172.2 2.9 collective-permute-start.7
  175.1 1.9 collective-permute-done.7.refs_3_
  179.1 2.1 collective-permute-start.8
  181.1 2.2 collective-permute-done.8.refs_1_
  183.3 2.9 collective-permute-start.9
  187.6 2.0 att0_pair.1
  199.1 1.7 collective-permute-start.17
  200.8 2.0 att1_pair.1
  204.7 1.7 collective-permute-start.39
  210.0 1.7 collective-permute-start.42
  211.7 1.7 att0_sum0.1
  215.4 2.6 collective-permute-start.20
  218.5 1.7 collective-permute-start.22
  221.2 2.6 collective-permute-start.23
  223.7 1.7 att1_sum0.1
  225.6 1.8 collective-permute-start.44
  227.4 2.6 collective-permute-start.45
  233.2 2.6 collective-permute-start.48
  237.3 1.8 collective-permute-start.25
  239.1 2.6 collective-permute-start.26
  242.2 1.7 collective-permute-start.28
  244.9 2.6 collective-permute-start.29
  249.1 1.8 collective-permute-start.50
  250.9 2.6 collective-permute-start.51
  255.0 1.9 collective-permute-start.53
  256.9 1.9 collective-permute-start.30
  259.8 2.5 ff0_pair.1
  263.3 2.6 collective-permute-start.54
  265.9 3.0 collective-permute-done.54.refs_7_
  269.8 1.8 collective-permute-start.32
  272.5 2.6 collective-permute-done.32.refs_3_
  275.1 1.7 collective-permute-start.64
  278.6 1.7 collective-permute-start.67
  280.3 2.5 ff1_pair.1
  284.8 1.7 collective-permute-start.89
  288.3 1.7 collective-permute-start.92
  290.0 2.0 ff0_sum0.1
  292.2 2.5 collective-permute-start.69
  294.7 1.9 collective-permute-start.70
  301.7 2.5 collective-permute-start.72
  304.2 1.9 collective-permute-start.73
  306.1 2.0 ff1_sum0.1
  312.3 1.9 collective-permute-start.95
  316.8 1.9 collective-permute-start.98
  318.7 2.4 collective-permute-start.75
  321.2 1.9 collective-permute-start.76
  323.0 2.5 collective-permute-start.78
  325.6 1.9 collective-permute-start.79
  332.8 3.1 collective-permute-start.100
  339.6 3.1 collective-permute-start.103
  349.5 1.7 collective-permute-start.60
  366.7 7.8 %adam_qkv.1 = (f32[256,1536]{1,0:T(8,128)}, f32[256,1536]{1,0:T(8,128)}, f32[256,1536]{1,0:T(8,128)}, f32[256,1536]{1,0:T(8,128)}, f32[2,128,512]{2,1,0:T(8,128)...) custom-call(s32[2]{0:T(128)} %pad_add_fusion.meta, ...), custom_call_target="tpu_custom_call" | custom-call | flops 10485760 | bytes 14680064 | tf_op jit(solution)/shard_map/adam_qkv/pallas_call | solution.py:662
  375.4 12.1 %adam_ff.1 = (f32[2,512,512]{2,1,0:T(8,128)}, f32[2,512,512]{2,1,0:T(8,128)}, f32[2,512,512]{2,1,0:T(8,128)}, f32[2,512,512]{2,1,0:T(8,128)}, f32[256,2048]{1,0:...) custom-call(s32[2]{0:T(128)} %pad_add_fusion.meta, ...), custom_call_target="tpu_custom_call" | custom-call | flops 20971520 | bytes 29360128 | tf_op jit(solution)/shard_map/adam_ff/pallas_call | solution.py:662
  (445 shorter events, 95.2 us)
Async XLA Ops:
  0.7 12.3 %collective-permute-start = (bf16[256,1536]{1,0:T(8,128)(2,1)}, bf16[256,1536]{1,0:T(8,128)(2,1)S(1)}, u32[]{:S(2)}, u32[]{:S(2)}) collective-permute-start(bf16[256,1536]{1,0:T(8,128)(2,1)} %refs_18_.1), channel_id=1, source_target_pairs={{0,1},{1,0},{2,3},{3,2},{4,5},{5,4},{6,7},{7,6},{8,9},{9,8},{10,11... | collective-permute-start | bytes 2359304 | tf_op jit(solution)/shard_map/ppermute | solution.py:537
  1.2 11.7 %collective-permute-start.1 = (bf16[256,512]{1,0:T(8,128)(2,1)}, bf16[256,512]{1,0:T(8,128)(2,1)S(1)}, u32[]{:S(2)}, u32[]{:S(2)}) collective-permute-start(bf16[256,512]{1,0:T(8,128)(2,1)} %oo_ref.5), channel_id=1, source_target_pairs={{0,1},{1,0},{2,3},{3,2},{4,5},{5,4},{6,7},{7,6},{8,9},{9,8},{10,11... | collective-permute-start | bytes 786440 | tf_op jit(solution)/shard_map/ppermute | solution.py:537
  1.3 91.4 %collective-permute-start.2 = (bf16[256,2048]{1,0:T(8,128)(2,1)}, bf16[256,2048]{1,0:T(8,128)(2,1)S(1)}, u32[]{:S(2)}, u32[]{:S(2)}) collective-permute-start(bf16[256,2048]{1,0:T(8,128)(2,1)} %refs_21_.1), channel_id=1, source_target_pairs={{0,1},{1,0},{2,3},{3,2},{4,5},{5,4},{6,7},{7,6},{8,9},{9,8},{10,11... | collective-permute-start | bytes 3145736 | tf_op jit(solution)/shard_map/ppermute | solution.py:537
  1.7 90.9 %collective-permute-start.3 = (bf16[1024,512]{1,0:T(8,128)(2,1)}, bf16[1024,512]{1,0:T(8,128)(2,1)S(1)}, u32[]{:S(2)}, u32[]{:S(2)}) collective-permute-start(bf16[1024,512]{1,0:T(8,128)(2,1)} %po_ref.1), channel_id=1, source_target_pairs={{0,1},{1,0},{2,3},{3,2},{4,5},{5,4},{6,7},{7,6},{8,9},{9,8},{10,11... | collective-permute-start | bytes 3145736 | tf_op jit(solution)/shard_map/ppermute | solution.py:537
  53.0 133.2 %collective-permute-start.11 = (bf16[2,16,16,512]{3,2,1,0:T(8,128)(2,1)}, bf16[2,16,16,512]{3,2,1,0:T(8,128)(2,1)S(1)}, u32[]{:S(2)}, u32[]{:S(2)}) collective-permute-start(bf16[2,16,16,512]{3,2,1,0:T(8,128)(2,1)} %get-tuple-element.171), channel_id=1, source_target_pairs={{0,1},{1,0},{2,3},{3,2},{4,5},{5,4},{6,7},{7,6},{8,9},{9,8},{10,11... | collective-permute-start | bytes 1572872 | tf_op jit(solution)/shard_map/ppermute | solution.py:537
  92.5 101.1 %collective-permute-start.36 = (bf16[2,16,16,512]{3,2,1,0:T(8,128)(2,1)}, bf16[2,16,16,512]{3,2,1,0:T(8,128)(2,1)S(1)}, u32[]{:S(2)}, u32[]{:S(2)}) collective-permute-start(bf16[2,16,16,512]{3,2,1,0:T(8,128)(2,1)} %get-tuple-element.193), channel_id=1, source_target_pairs={{0,1},{1,0},{2,3},{3,2},{4,5},{5,4},{6,7},{7,6},{8,9},{9,8},{10,11... | collective-permute-start | bytes 1572872 | tf_op jit(solution)/shard_map/ppermute | solution.py:537
  114.3 144.5 %collective-permute-start.61 = (bf16[2,16,16,1024]{3,2,1,0:T(8,128)(2,1)}, bf16[2,16,16,1024]{3,2,1,0:T(8,128)(2,1)S(1)}, u32[]{:S(2)}, u32[]{:S(2)}) collective-permute-start(bf16[2,16,16,1024]{3,2,1,0:T(8,128)(2,1)} %get-tuple-element.217), channel_id=1, source_target_pairs={{0,1},{1,0},{2,3},{3,2},{4,5},{5,4},{6,7},{7,6},{8,9},{9,8},{10,11... | collective-permute-start | bytes 3145736 | tf_op jit(solution)/shard_map/ppermute | solution.py:537
  135.0 142.6 %collective-permute-start.86 = (bf16[2,16,16,1024]{3,2,1,0:T(8,128)(2,1)}, bf16[2,16,16,1024]{3,2,1,0:T(8,128)(2,1)S(1)}, u32[]{:S(2)}, u32[]{:S(2)}) collective-permute-start(bf16[2,16,16,1024]{3,2,1,0:T(8,128)(2,1)} %get-tuple-element.239), channel_id=1, source_target_pairs={{0,1},{1,0},{2,3},{3,2},{4,5},{5,4},{6,7},{7,6},{8,9},{9,8},{10,11... | collective-permute-start | bytes 3145736 | tf_op jit(solution)/shard_map/ppermute | solution.py:537
  195.0 7.7 %collective-permute-start.15 = (bf16[4,16,512]{2,1,0:T(8,128)(2,1)}, bf16[4,16,512]{2,1,0:T(8,128)(2,1)S(1)}, u32[]{:S(2)}, u32[]{:S(2)}) collective-permute-start(bf16[4,16,512]{2,1,0:T(8,128)(2,1)} %get-tuple-element.177), channel_id=1, source_target_pairs={{0,2},{2,0},{4,6},{6,4},{8,10},{10,8},{12,14},{14,12},{16,18},{18,... | collective-permute-start | bytes 196616 | tf_op jit(solution)/shard_map/ppermute | solution.py:533
  218.0 7.5 %collective-permute-start.21 = (bf16[1,16,512]{2,1,0:T(8,128)(2,1)}, bf16[1,16,512]{2,1,0:T(8,128)(2,1)S(1)}, u32[]{:S(2)}, u32[]{:S(2)}) collective-permute-start(bf16[1,16,512]{2,1,0:T(8,128)(2,1)} %get-tuple-element.185), channel_id=1, source_target_pairs={{0,8},{2,10},{4,12},{6,14},{8,0},{10,2},{12,4},{14,6},{16,24},{18,... | collective-permute-start | bytes 49160 | tf_op jit(solution)/shard_map/ppermute | solution.py:533
  218.5 7.1 %collective-permute-start.22 = (bf16[1,16,512]{2,1,0:T(8,128)(2,1)}, bf16[1,16,512]{2,1,0:T(8,128)(2,1)S(1)}, u32[]{:S(2)}, u32[]{:S(2)}) collective-permute-start(bf16[1,16,512]{2,1,0:T(8,128)(2,1)} %get-tuple-element.186), channel_id=1, source_target_pairs={{0,16},{2,18},{4,20},{6,22},{8,24},{10,26},{12,28},{14,30},{16,0},... | collective-permute-start | bytes 49160 | tf_op jit(solution)/shard_map/ppermute | solution.py:533
  230.0 7.2 %collective-permute-start.46 = (bf16[1,16,512]{2,1,0:T(8,128)(2,1)}, bf16[1,16,512]{2,1,0:T(8,128)(2,1)S(1)}, u32[]{:S(2)}, u32[]{:S(2)}) collective-permute-start(bf16[1,16,512]{2,1,0:T(8,128)(2,1)} %get-tuple-element.207), channel_id=1, source_target_pairs={{0,8},{2,10},{4,12},{6,14},{8,0},{10,2},{12,4},{14,6},{16,24},{18,... | collective-permute-start | bytes 49160 | tf_op jit(solution)/shard_map/ppermute | solution.py:533
  230.6 6.7 %collective-permute-start.47 = (bf16[1,16,512]{2,1,0:T(8,128)(2,1)}, bf16[1,16,512]{2,1,0:T(8,128)(2,1)S(1)}, u32[]{:S(2)}, u32[]{:S(2)}) collective-permute-start(bf16[1,16,512]{2,1,0:T(8,128)(2,1)} %get-tuple-element.208), channel_id=1, source_target_pairs={{0,16},{2,18},{4,20},{6,22},{8,24},{10,26},{12,28},{14,30},{16,0},... | collective-permute-start | bytes 49160 | tf_op jit(solution)/shard_map/ppermute | solution.py:533
  241.7 7.2 %collective-permute-start.27 = (bf16[1,16,512]{2,1,0:T(8,128)(2,1)}, bf16[1,16,512]{2,1,0:T(8,128)(2,1)S(1)}, u32[]{:S(2)}, u32[]{:S(2)}) collective-permute-start(bf16[1,16,512]{2,1,0:T(8,128)(2,1)} %get-tuple-element.189.refs_4_), channel_id=1, source_target_pairs={{0,8},{2,10},{4,12},{6,14},{8,0},{10,2},{12,4},{14,6},{16,24},{18,... | collective-permute-start | bytes 49160 | tf_op jit(solution)/shard_map/ppermute | solution.py:533
  242.2 6.8 %collective-permute-start.28 = (bf16[1,16,512]{2,1,0:T(8,128)(2,1)}, bf16[1,16,512]{2,1,0:T(8,128)(2,1)S(1)}, u32[]{:S(2)}, u32[]{:S(2)}) collective-permute-start(bf16[1,16,512]{2,1,0:T(8,128)(2,1)} %get-tuple-element.189.refs_4_), channel_id=1, source_target_pairs={{0,16},{2,18},{4,20},{6,22},{8,24},{10,26},{12,28},{14,30},{16,0},... | collective-permute-start | bytes 49160 | tf_op jit(solution)/shard_map/ppermute | solution.py:533
  253.4 8.9 %collective-permute-start.52 = (bf16[1,16,512]{2,1,0:T(8,128)(2,1)}, bf16[1,16,512]{2,1,0:T(8,128)(2,1)S(1)}, u32[]{:S(2)}, u32[]{:S(2)}) collective-permute-start(bf16[1,16,512]{2,1,0:T(8,128)(2,1)} %get-tuple-element.211.refs_4_), channel_id=1, source_target_pairs={{0,8},{2,10},{4,12},{6,14},{8,0},{10,2},{12,4},{14,6},{16,24},{18,... | collective-permute-start | bytes 49160 | tf_op jit(solution)/shard_map/ppermute | solution.py:533
  255.0 8.2 %collective-permute-start.53 = (bf16[1,16,512]{2,1,0:T(8,128)(2,1)}, bf16[1,16,512]{2,1,0:T(8,128)(2,1)S(1)}, u32[]{:S(2)}, u32[]{:S(2)}) collective-permute-start(bf16[1,16,512]{2,1,0:T(8,128)(2,1)} %get-tuple-element.211.refs_4_), channel_id=1, source_target_pairs={{0,16},{2,18},{4,20},{6,22},{8,24},{10,26},{12,28},{14,30},{16,0},... | collective-permute-start | bytes 49160 | tf_op jit(solution)/shard_map/ppermute | solution.py:533
  256.9 12.9 %collective-permute-start.30 = (bf16[4,16,512]{2,1,0:T(8,128)(2,1)}, bf16[4,16,512]{2,1,0:T(8,128)(2,1)S(1)}, u32[]{:S(2)}, u32[]{:S(2)}) collective-permute-start(bf16[4,16,512]{2,1,0:T(8,128)(2,1)} %get-tuple-element.190.refs_0_), channel_id=1, source_target_pairs={{0,2},{2,0},{4,6},{6,4},{8,10},{10,8},{12,14},{14,12},{16,18},{18,... | collective-permute-start | bytes 196616 | tf_op jit(solution)/shard_map/ppermute | solution.py:533
  258.8 12.8 %collective-permute-start.31 = (bf16[4,16,512]{2,1,0:T(8,128)(2,1)}, bf16[4,16,512]{2,1,0:T(8,128)(2,1)S(1)}, u32[]{:S(2)}, u32[]{:S(2)}) collective-permute-start(bf16[4,16,512]{2,1,0:T(8,128)(2,1)} %get-tuple-element.190.refs_0_), channel_id=1, source_target_pairs={{0,4},{2,6},{4,0},{6,2},{8,12},{10,14},{12,8},{14,10},{16,20},{18,... | collective-permute-start | bytes 196616 | tf_op jit(solution)/shard_map/ppermute | solution.py:533
  262.4 16.2 %collective-permute-start.62 = (bf16[4,16,1024]{2,1,0:T(8,128)(2,1)}, bf16[4,16,1024]{2,1,0:T(8,128)(2,1)S(1)}, u32[]{:S(2)}, u32[]{:S(2)}) collective-permute-start(bf16[4,16,1024]{2,1,0:T(8,128)(2,1)} %get-tuple-element.219), channel_id=1, source_target_pairs={{0,2},{2,0},{4,6},{6,4},{8,10},{10,8},{12,14},{14,12},{16,18},{18,... | collective-permute-start | bytes 393224 | tf_op jit(solution)/shard_map/ppermute | solution.py:533
  268.9 14.0 %collective-permute-start.63 = (bf16[4,16,1024]{2,1,0:T(8,128)(2,1)}, bf16[4,16,1024]{2,1,0:T(8,128)(2,1)S(1)}, u32[]{:S(2)}, u32[]{:S(2)}) collective-permute-start(bf16[4,16,1024]{2,1,0:T(8,128)(2,1)} %get-tuple-element.220), channel_id=1, source_target_pairs={{0,4},{2,6},{4,0},{6,2},{8,12},{10,14},{12,8},{14,10},{16,20},{18,... | collective-permute-start | bytes 393224 | tf_op jit(solution)/shard_map/ppermute | solution.py:533
  275.1 8.8 %collective-permute-start.64 = (bf16[4,16,1024]{2,1,0:T(8,128)(2,1)}, bf16[4,16,1024]{2,1,0:T(8,128)(2,1)S(1)}, u32[]{:S(2)}, u32[]{:S(2)}) collective-permute-start(bf16[4,16,1024]{2,1,0:T(8,128)(2,1)} %get-tuple-element.221), channel_id=1, source_target_pairs={{0,6},{2,4},{4,2},{6,0},{8,14},{10,12},{12,10},{14,8},{16,22},{18,... | collective-permute-start | bytes 393224 | tf_op jit(solution)/shard_map/ppermute | solution.py:533
  276.8 8.0 %collective-permute-start.65 = (bf16[4,16,1024]{2,1,0:T(8,128)(2,1)}, bf16[4,16,1024]{2,1,0:T(8,128)(2,1)S(1)}, u32[]{:S(2)}, u32[]{:S(2)}) collective-permute-start(bf16[4,16,1024]{2,1,0:T(8,128)(2,1)} %get-tuple-element.223), channel_id=1, source_target_pairs={{0,2},{2,0},{4,6},{6,4},{8,10},{10,8},{12,14},{14,12},{16,18},{18,... | collective-permute-start | bytes 393224 | tf_op jit(solution)/shard_map/ppermute | solution.py:533
  277.6 8.9 %collective-permute-start.66 = (bf16[4,16,1024]{2,1,0:T(8,128)(2,1)}, bf16[4,16,1024]{2,1,0:T(8,128)(2,1)S(1)}, u32[]{:S(2)}, u32[]{:S(2)}) collective-permute-start(bf16[4,16,1024]{2,1,0:T(8,128)(2,1)} %get-tuple-element.224), channel_id=1, source_target_pairs={{0,4},{2,6},{4,0},{6,2},{8,12},{10,14},{12,8},{14,10},{16,20},{18,... | collective-permute-start | bytes 393224 | tf_op jit(solution)/shard_map/ppermute | solution.py:533
  278.6 8.8 %collective-permute-start.67 = (bf16[4,16,1024]{2,1,0:T(8,128)(2,1)}, bf16[4,16,1024]{2,1,0:T(8,128)(2,1)S(1)}, u32[]{:S(2)}, u32[]{:S(2)}) collective-permute-start(bf16[4,16,1024]{2,1,0:T(8,128)(2,1)} %get-tuple-element.225), channel_id=1, source_target_pairs={{0,6},{2,4},{4,2},{6,0},{8,14},{10,12},{12,10},{14,8},{16,22},{18,... | collective-permute-start | bytes 393224 | tf_op jit(solution)/shard_map/ppermute | solution.py:533
  283.8 8.2 %collective-permute-start.88 = (bf16[4,16,1024]{2,1,0:T(8,128)(2,1)}, bf16[4,16,1024]{2,1,0:T(8,128)(2,1)S(1)}, u32[]{:S(2)}, u32[]{:S(2)}) collective-permute-start(bf16[4,16,1024]{2,1,0:T(8,128)(2,1)} %get-tuple-element.242), channel_id=1, source_target_pairs={{0,4},{2,6},{4,0},{6,2},{8,12},{10,14},{12,8},{14,10},{16,20},{18,... | collective-permute-start | bytes 393224 | tf_op jit(solution)/shard_map/ppermute | solution.py:533
  284.8 7.4 %collective-permute-start.89 = (bf16[4,16,1024]{2,1,0:T(8,128)(2,1)}, bf16[4,16,1024]{2,1,0:T(8,128)(2,1)S(1)}, u32[]{:S(2)}, u32[]{:S(2)}) collective-permute-start(bf16[4,16,1024]{2,1,0:T(8,128)(2,1)} %get-tuple-element.243), channel_id=1, source_target_pairs={{0,6},{2,4},{4,2},{6,0},{8,14},{10,12},{12,10},{14,8},{16,22},{18,... | collective-permute-start | bytes 393224 | tf_op jit(solution)/shard_map/ppermute | solution.py:533
  286.5 8.2 %collective-permute-start.90 = (bf16[4,16,1024]{2,1,0:T(8,128)(2,1)}, bf16[4,16,1024]{2,1,0:T(8,128)(2,1)S(1)}, u32[]{:S(2)}, u32[]{:S(2)}) collective-permute-start(bf16[4,16,1024]{2,1,0:T(8,128)(2,1)} %get-tuple-element.245), channel_id=1, source_target_pairs={{0,2},{2,0},{4,6},{6,4},{8,10},{10,8},{12,14},{14,12},{16,18},{18,... | collective-permute-start | bytes 393224 | tf_op jit(solution)/shard_map/ppermute | solution.py:533
  287.3 9.2 %collective-permute-start.91 = (bf16[4,16,1024]{2,1,0:T(8,128)(2,1)}, bf16[4,16,1024]{2,1,0:T(8,128)(2,1)S(1)}, u32[]{:S(2)}, u32[]{:S(2)}) collective-permute-start(bf16[4,16,1024]{2,1,0:T(8,128)(2,1)} %get-tuple-element.246), channel_id=1, source_target_pairs={{0,4},{2,6},{4,0},{6,2},{8,12},{10,14},{12,8},{14,10},{16,20},{18,... | collective-permute-start | bytes 393224 | tf_op jit(solution)/shard_map/ppermute | solution.py:533
  288.3 9.8 %collective-permute-start.92 = (bf16[4,16,1024]{2,1,0:T(8,128)(2,1)}, bf16[4,16,1024]{2,1,0:T(8,128)(2,1)S(1)}, u32[]{:S(2)}, u32[]{:S(2)}) collective-permute-start(bf16[4,16,1024]{2,1,0:T(8,128)(2,1)} %get-tuple-element.247), channel_id=1, source_target_pairs={{0,6},{2,4},{4,2},{6,0},{8,14},{10,12},{12,10},{14,8},{16,22},{18,... | collective-permute-start | bytes 393224 | tf_op jit(solution)/shard_map/ppermute | solution.py:533
  292.1 7.2 %collective-permute-start.68 = (bf16[1,16,1024]{2,1,0:T(8,128)(2,1)}, bf16[1,16,1024]{2,1,0:T(8,128)(2,1)S(1)}, u32[]{:S(2)}, u32[]{:S(2)}) collective-permute-start(bf16[1,16,1024]{2,1,0:T(8,128)(2,1)} %get-tuple-element.227), channel_id=1, source_target_pairs={{0,8},{2,10},{4,12},{6,14},{8,0},{10,2},{12,4},{14,6},{16,24},{18,... | collective-permute-start | bytes 98312 | tf_op jit(solution)/shard_map/ppermute | solution.py:533
  292.2 8.3 %collective-permute-start.69 = (bf16[1,16,1024]{2,1,0:T(8,128)(2,1)}, bf16[1,16,1024]{2,1,0:T(8,128)(2,1)S(1)}, u32[]{:S(2)}, u32[]{:S(2)}) collective-permute-start(bf16[1,16,1024]{2,1,0:T(8,128)(2,1)} %get-tuple-element.228), channel_id=1, source_target_pairs={{0,16},{2,18},{4,20},{6,22},{8,24},{10,26},{12,28},{14,30},{16,0},... | collective-permute-start | bytes 98312 | tf_op jit(solution)/shard_map/ppermute | solution.py:533
  294.7 7.0 %collective-permute-start.70 = (bf16[1,16,1024]{2,1,0:T(8,128)(2,1)}, bf16[1,16,1024]{2,1,0:T(8,128)(2,1)S(1)}, u32[]{:S(2)}, u32[]{:S(2)}) collective-permute-start(bf16[1,16,1024]{2,1,0:T(8,128)(2,1)} %get-tuple-element.229), channel_id=1, source_target_pairs={{0,24},{2,26},{4,28},{6,30},{8,16},{10,18},{12,20},{14,22},{16,8},... | collective-permute-start | bytes 98312 | tf_op jit(solution)/shard_map/ppermute | solution.py:533
  296.5 7.6 %collective-permute-start.71 = (bf16[1,16,1024]{2,1,0:T(8,128)(2,1)}, bf16[1,16,1024]{2,1,0:T(8,128)(2,1)S(1)}, u32[]{:S(2)}, u32[]{:S(2)}) collective-permute-start(bf16[1,16,1024]{2,1,0:T(8,128)(2,1)} %get-tuple-element.231), channel_id=1, source_target_pairs={{0,8},{2,10},{4,12},{6,14},{8,0},{10,2},{12,4},{14,6},{16,24},{18,... | collective-permute-start | bytes 98312 | tf_op jit(solution)/shard_map/ppermute | solution.py:533
  298.1 14.2 %collective-permute-start.34 = (bf16[4,16,512]{2,1,0:T(8,128)(2,1)S(1)}, bf16[4,16,512]{2,1,0:T(8,128)(2,1)S(1)}, u32[]{:S(2)}, u32[]{:S(2)}) collective-permute-start(bf16[4,16,512]{2,1,0:T(8,128)(2,1)S(1)} %copy-done.29), channel_id=1, source_target_pairs={{0,4},{2,6},{4,0},{6,2},{8,12},{10,14},{12,8},{14,10},{16,20},{18,... | collective-permute-start | bytes 196616 | tf_op jit(solution)/shard_map/ppermute | solution.py:533
  299.2 15.0 %collective-permute-start.35 = (bf16[4,16,512]{2,1,0:T(8,128)(2,1)S(1)}, bf16[4,16,512]{2,1,0:T(8,128)(2,1)S(1)}, u32[]{:S(2)}, u32[]{:S(2)}) collective-permute-start(bf16[4,16,512]{2,1,0:T(8,128)(2,1)S(1)} %copy-done.29), channel_id=1, source_target_pairs={{0,6},{2,4},{4,2},{6,0},{8,14},{10,12},{12,10},{14,8},{16,22},{18,... | collective-permute-start | bytes 196616 | tf_op jit(solution)/shard_map/ppermute | solution.py:533
  300.5 14.8 %collective-permute-start.55 = (bf16[4,16,512]{2,1,0:T(8,128)(2,1)}, bf16[4,16,512]{2,1,0:T(8,128)(2,1)S(1)}, u32[]{:S(2)}, u32[]{:S(2)}) collective-permute-start(bf16[4,16,512]{2,1,0:T(8,128)(2,1)} %get-tuple-element.212.refs_8_), channel_id=1, source_target_pairs={{0,2},{2,0},{4,6},{6,4},{8,10},{10,8},{12,14},{14,12},{16,18},{18,... | collective-permute-start | bytes 196616 | tf_op jit(solution)/shard_map/ppermute | solution.py:533
  308.1 8.6 %collective-permute-start.93 = (bf16[1,16,1024]{2,1,0:T(8,128)(2,1)}, bf16[1,16,1024]{2,1,0:T(8,128)(2,1)S(1)}, u32[]{:S(2)}, u32[]{:S(2)}) collective-permute-start(bf16[1,16,1024]{2,1,0:T(8,128)(2,1)} %get-tuple-element.249), channel_id=1, source_target_pairs={{0,8},{2,10},{4,12},{6,14},{8,0},{10,2},{12,4},{14,6},{16,24},{18,... | collective-permute-start | bytes 98312 | tf_op jit(solution)/shard_map/ppermute | solution.py:533
  310.1 8.5 %collective-permute-start.94 = (bf16[1,16,1024]{2,1,0:T(8,128)(2,1)}, bf16[1,16,1024]{2,1,0:T(8,128)(2,1)S(1)}, u32[]{:S(2)}, u32[]{:S(2)}) collective-permute-start(bf16[1,16,1024]{2,1,0:T(8,128)(2,1)} %get-tuple-element.250), channel_id=1, source_target_pairs={{0,16},{2,18},{4,20},{6,22},{8,24},{10,26},{12,28},{14,30},{16,0},... | collective-permute-start | bytes 98312 | tf_op jit(solution)/shard_map/ppermute | solution.py:533
  314.2 6.9 %collective-permute-start.96 = (bf16[1,16,1024]{2,1,0:T(8,128)(2,1)}, bf16[1,16,1024]{2,1,0:T(8,128)(2,1)S(1)}, u32[]{:S(2)}, u32[]{:S(2)}) collective-permute-start(bf16[1,16,1024]{2,1,0:T(8,128)(2,1)} %get-tuple-element.253), channel_id=1, source_target_pairs={{0,8},{2,10},{4,12},{6,14},{8,0},{10,2},{12,4},{14,6},{16,24},{18,... | collective-permute-start | bytes 98312 | tf_op jit(solution)/shard_map/ppermute | solution.py:533
  315.2 7.8 %collective-permute-start.97 = (bf16[1,16,1024]{2,1,0:T(8,128)(2,1)}, bf16[1,16,1024]{2,1,0:T(8,128)(2,1)S(1)}, u32[]{:S(2)}, u32[]{:S(2)}) collective-permute-start(bf16[1,16,1024]{2,1,0:T(8,128)(2,1)} %get-tuple-element.254), channel_id=1, source_target_pairs={{0,16},{2,18},{4,20},{6,22},{8,24},{10,26},{12,28},{14,30},{16,0},... | collective-permute-start | bytes 98312 | tf_op jit(solution)/shard_map/ppermute | solution.py:533
  318.6 6.9 %collective-permute-start.74 = (bf16[1,16,1024]{2,1,0:T(8,128)(2,1)}, bf16[1,16,1024]{2,1,0:T(8,128)(2,1)S(1)}, u32[]{:S(2)}, u32[]{:S(2)}) collective-permute-start(bf16[1,16,1024]{2,1,0:T(8,128)(2,1)} %get-tuple-element.234.refs_0_), channel_id=1, source_target_pairs={{0,8},{2,10},{4,12},{6,14},{8,0},{10,2},{12,4},{14,6},{16,24},{18,... | collective-permute-start | bytes 98312 | tf_op jit(solution)/shard_map/ppermute | solution.py:533
  318.7 11.6 %collective-permute-start.75 = (bf16[1,16,1024]{2,1,0:T(8,128)(2,1)}, bf16[1,16,1024]{2,1,0:T(8,128)(2,1)S(1)}, u32[]{:S(2)}, u32[]{:S(2)}) collective-permute-start(bf16[1,16,1024]{2,1,0:T(8,128)(2,1)} %get-tuple-element.234.refs_0_), channel_id=1, source_target_pairs={{0,16},{2,18},{4,20},{6,22},{8,24},{10,26},{12,28},{14,30},{16,0},... | collective-permute-start | bytes 98312 | tf_op jit(solution)/shard_map/ppermute | solution.py:533
  321.2 10.4 %collective-permute-start.76 = (bf16[1,16,1024]{2,1,0:T(8,128)(2,1)}, bf16[1,16,1024]{2,1,0:T(8,128)(2,1)S(1)}, u32[]{:S(2)}, u32[]{:S(2)}) collective-permute-start(bf16[1,16,1024]{2,1,0:T(8,128)(2,1)} %get-tuple-element.234.refs_0_), channel_id=1, source_target_pairs={{0,24},{2,26},{4,28},{6,30},{8,16},{10,18},{12,20},{14,22},{16,8},... | collective-permute-start | bytes 98312 | tf_op jit(solution)/shard_map/ppermute | solution.py:533
  323.0 9.7 %collective-permute-start.77 = (bf16[1,16,1024]{2,1,0:T(8,128)(2,1)}, bf16[1,16,1024]{2,1,0:T(8,128)(2,1)S(1)}, u32[]{:S(2)}, u32[]{:S(2)}) collective-permute-start(bf16[1,16,1024]{2,1,0:T(8,128)(2,1)} %get-tuple-element.235.refs_4_), channel_id=1, source_target_pairs={{0,8},{2,10},{4,12},{6,14},{8,0},{10,2},{12,4},{14,6},{16,24},{18,... | collective-permute-start | bytes 98312 | tf_op jit(solution)/shard_map/ppermute | solution.py:533
  323.0 9.7 %collective-permute-start.78 = (bf16[1,16,1024]{2,1,0:T(8,128)(2,1)}, bf16[1,16,1024]{2,1,0:T(8,128)(2,1)S(1)}, u32[]{:S(2)}, u32[]{:S(2)}) collective-permute-start(bf16[1,16,1024]{2,1,0:T(8,128)(2,1)} %get-tuple-element.235.refs_4_), channel_id=1, source_target_pairs={{0,16},{2,18},{4,20},{6,22},{8,24},{10,26},{12,28},{14,30},{16,0},... | collective-permute-start | bytes 98312 | tf_op jit(solution)/shard_map/ppermute | solution.py:533
  325.6 10.3 %collective-permute-start.79 = (bf16[1,16,1024]{2,1,0:T(8,128)(2,1)}, bf16[1,16,1024]{2,1,0:T(8,128)(2,1)S(1)}, u32[]{:S(2)}, u32[]{:S(2)}) collective-permute-start(bf16[1,16,1024]{2,1,0:T(8,128)(2,1)} %get-tuple-element.235.refs_4_), channel_id=1, source_target_pairs={{0,24},{2,26},{4,28},{6,30},{8,16},{10,18},{12,20},{14,22},{16,8},... | collective-permute-start | bytes 98312 | tf_op jit(solution)/shard_map/ppermute | solution.py:533
  330.4 9.1 %collective-permute-start.56 = (bf16[4,16,512]{2,1,0:T(8,128)(2,1)}, bf16[4,16,512]{2,1,0:T(8,128)(2,1)S(1)}, u32[]{:S(2)}, u32[]{:S(2)}) collective-permute-start(bf16[4,16,512]{2,1,0:T(8,128)(2,1)} %get-tuple-element.212.refs_8_), channel_id=1, source_target_pairs={{0,4},{2,6},{4,0},{6,2},{8,12},{10,14},{12,8},{14,10},{16,20},{18,... | collective-permute-start | bytes 196616 | tf_op jit(solution)/shard_map/ppermute | solution.py:533
  331.5 8.1 %collective-permute-start.57 = (bf16[4,16,512]{2,1,0:T(8,128)(2,1)}, bf16[4,16,512]{2,1,0:T(8,128)(2,1)S(1)}, u32[]{:S(2)}, u32[]{:S(2)}) collective-permute-start(bf16[4,16,512]{2,1,0:T(8,128)(2,1)} %get-tuple-element.212.refs_8_), channel_id=1, source_target_pairs={{0,6},{2,4},{4,2},{6,0},{8,14},{10,12},{12,10},{14,8},{16,22},{18,... | collective-permute-start | bytes 196616 | tf_op jit(solution)/shard_map/ppermute | solution.py:533
  332.8 10.0 %collective-permute-start.99 = (bf16[1,16,1024]{2,1,0:T(8,128)(2,1)}, bf16[1,16,1024]{2,1,0:T(8,128)(2,1)S(1)}, u32[]{:S(2)}, u32[]{:S(2)}) collective-permute-start(bf16[1,16,1024]{2,1,0:T(8,128)(2,1)} %get-tuple-element.256.refs_0_), channel_id=1, source_target_pairs={{0,8},{2,10},{4,12},{6,14},{8,0},{10,2},{12,4},{14,6},{16,24},{18,... | collective-permute-start | bytes 98312 | tf_op jit(solution)/shard_map/ppermute | solution.py:533
  332.8 11.2 %collective-permute-start.100 = (bf16[1,16,1024]{2,1,0:T(8,128)(2,1)}, bf16[1,16,1024]{2,1,0:T(8,128)(2,1)S(1)}, u32[]{:S(2)}, u32[]{:S(2)}) collective-permute-start(bf16[1,16,1024]{2,1,0:T(8,128)(2,1)} %get-tuple-element.256.refs_0_), channel_id=1, source_target_pairs={{0,16},{2,18},{4,20},{6,22},{8,24},{10,26},{12,28},{14,30},{16,0},... | collective-permute-start | bytes 98312 | tf_op jit(solution)/shard_map/ppermute | solution.py:533
  335.9 9.3 %collective-permute-start.101 = (bf16[1,16,1024]{2,1,0:T(8,128)(2,1)}, bf16[1,16,1024]{2,1,0:T(8,128)(2,1)S(1)}, u32[]{:S(2)}, u32[]{:S(2)}) collective-permute-start(bf16[1,16,1024]{2,1,0:T(8,128)(2,1)} %get-tuple-element.256.refs_0_), channel_id=1, source_target_pairs={{0,24},{2,26},{4,28},{6,30},{8,16},{10,18},{12,20},{14,22},{16,8},... | collective-permute-start | bytes 98312 | tf_op jit(solution)/shard_map/ppermute | solution.py:533
  339.5 8.1 %collective-permute-start.102 = (bf16[1,16,1024]{2,1,0:T(8,128)(2,1)}, bf16[1,16,1024]{2,1,0:T(8,128)(2,1)S(1)}, u32[]{:S(2)}, u32[]{:S(2)}) collective-permute-start(bf16[1,16,1024]{2,1,0:T(8,128)(2,1)} %get-tuple-element.257.refs_4_), channel_id=1, source_target_pairs={{0,8},{2,10},{4,12},{6,14},{8,0},{10,2},{12,4},{14,6},{16,24},{18,... | collective-permute-start | bytes 98312 | tf_op jit(solution)/shard_map/ppermute | solution.py:533
  339.6 8.7 %collective-permute-start.103 = (bf16[1,16,1024]{2,1,0:T(8,128)(2,1)}, bf16[1,16,1024]{2,1,0:T(8,128)(2,1)S(1)}, u32[]{:S(2)}, u32[]{:S(2)}) collective-permute-start(bf16[1,16,1024]{2,1,0:T(8,128)(2,1)} %get-tuple-element.257.refs_4_), channel_id=1, source_target_pairs={{0,16},{2,18},{4,20},{6,22},{8,24},{10,26},{12,28},{14,30},{16,0},... | collective-permute-start | bytes 98312 | tf_op jit(solution)/shard_map/ppermute | solution.py:533
  342.8 6.7 %collective-permute-start.104 = (bf16[1,16,1024]{2,1,0:T(8,128)(2,1)}, bf16[1,16,1024]{2,1,0:T(8,128)(2,1)S(1)}, u32[]{:S(2)}, u32[]{:S(2)}) collective-permute-start(bf16[1,16,1024]{2,1,0:T(8,128)(2,1)} %get-tuple-element.257.refs_4_), channel_id=1, source_target_pairs={{0,24},{2,26},{4,28},{6,30},{8,16},{10,18},{12,20},{14,22},{16,8},... | collective-permute-start | bytes 98312 | tf_op jit(solution)/shard_map/ppermute | solution.py:533
  344.0 13.1 %collective-permute-start.80 = (bf16[4,16,1024]{2,1,0:T(8,128)(2,1)}, bf16[4,16,1024]{2,1,0:T(8,128)(2,1)S(1)}, u32[]{:S(2)}, u32[]{:S(2)}) collective-permute-start(bf16[4,16,1024]{2,1,0:T(8,128)(2,1)} %get-tuple-element.236.refs_0_), channel_id=1, source_target_pairs={{0,2},{2,0},{4,6},{6,4},{8,10},{10,8},{12,14},{14,12},{16,18},{18,... | collective-permute-start | bytes 393224 | tf_op jit(solution)/shard_map/ppermute | solution.py:533
  345.2 13.1 %collective-permute-start.81 = (bf16[4,16,1024]{2,1,0:T(8,128)(2,1)}, bf16[4,16,1024]{2,1,0:T(8,128)(2,1)S(1)}, u32[]{:S(2)}, u32[]{:S(2)}) collective-permute-start(bf16[4,16,1024]{2,1,0:T(8,128)(2,1)} %get-tuple-element.236.refs_0_), channel_id=1, source_target_pairs={{0,4},{2,6},{4,0},{6,2},{8,12},{10,14},{12,8},{14,10},{16,20},{18,... | collective-permute-start | bytes 393224 | tf_op jit(solution)/shard_map/ppermute | solution.py:533
  353.5 6.6 %collective-permute-start.82 = (bf16[4,16,1024]{2,1,0:T(8,128)(2,1)}, bf16[4,16,1024]{2,1,0:T(8,128)(2,1)S(1)}, u32[]{:S(2)}, u32[]{:S(2)}) collective-permute-start(bf16[4,16,1024]{2,1,0:T(8,128)(2,1)} %get-tuple-element.236.refs_0_), channel_id=1, source_target_pairs={{0,6},{2,4},{4,2},{6,0},{8,14},{10,12},{12,10},{14,8},{16,22},{18,... | collective-permute-start | bytes 393224 | tf_op jit(solution)/shard_map/ppermute | solution.py:533
  357.1 6.6 %collective-permute-start.85 = (bf16[4,16,1024]{2,1,0:T(8,128)(2,1)}, bf16[4,16,1024]{2,1,0:T(8,128)(2,1)S(1)}, u32[]{:S(2)}, u32[]{:S(2)}) collective-permute-start(bf16[4,16,1024]{2,1,0:T(8,128)(2,1)} %get-tuple-element.237.refs_4_), channel_id=1, source_target_pairs={{0,6},{2,4},{4,2},{6,0},{8,14},{10,12},{12,10},{14,8},{16,22},{18,... | collective-permute-start | bytes 393224 | tf_op jit(solution)/shard_map/ppermute | solution.py:533
  360.1 14.4 %collective-permute-start.106 = (bf16[4,16,1024]{2,1,0:T(8,128)(2,1)}, bf16[4,16,1024]{2,1,0:T(8,128)(2,1)S(1)}, u32[]{:S(2)}, u32[]{:S(2)}) collective-permute-start(bf16[4,16,1024]{2,1,0:T(8,128)(2,1)} %get-tuple-element.258.refs_8_), channel_id=1, source_target_pairs={{0,4},{2,6},{4,0},{6,2},{8,12},{10,14},{12,8},{14,10},{16,20},{18,... | collective-permute-start | bytes 393224 | tf_op jit(solution)/shard_map/ppermute | solution.py:533
  361.2 13.4 %collective-permute-start.107 = (bf16[4,16,1024]{2,1,0:T(8,128)(2,1)}, bf16[4,16,1024]{2,1,0:T(8,128)(2,1)S(1)}, u32[]{:S(2)}, u32[]{:S(2)}) collective-permute-start(bf16[4,16,1024]{2,1,0:T(8,128)(2,1)} %get-tuple-element.258.refs_8_), channel_id=1, source_target_pairs={{0,6},{2,4},{4,2},{6,0},{8,14},{10,12},{12,10},{14,8},{16,22},{18,... | collective-permute-start | bytes 393224 | tf_op jit(solution)/shard_map/ppermute | solution.py:533
  362.4 12.2 %collective-permute-start.108 = (bf16[4,16,1024]{2,1,0:T(8,128)(2,1)}, bf16[4,16,1024]{2,1,0:T(8,128)(2,1)S(1)}, u32[]{:S(2)}, u32[]{:S(2)}) collective-permute-start(bf16[4,16,1024]{2,1,0:T(8,128)(2,1)} %get-tuple-element.259.refs_12_), channel_id=1, source_target_pairs={{0,2},{2,0},{4,6},{6,4},{8,10},{10,8},{12,14},{14,12},{16,18},{18,... | collective-permute-start | bytes 393224 | tf_op jit(solution)/shard_map/ppermute | solution.py:533
  363.7 11.0 %collective-permute-start.109 = (bf16[4,16,1024]{2,1,0:T(8,128)(2,1)}, bf16[4,16,1024]{2,1,0:T(8,128)(2,1)S(1)}, u32[]{:S(2)}, u32[]{:S(2)}) collective-permute-start(bf16[4,16,1024]{2,1,0:T(8,128)(2,1)} %get-tuple-element.259.refs_12_), channel_id=1, source_target_pairs={{0,4},{2,6},{4,0},{6,2},{8,12},{10,14},{12,8},{14,10},{16,20},{18,... | collective-permute-start | bytes 393224 | tf_op jit(solution)/shard_map/ppermute | solution.py:533
  364.7 9.9 %collective-permute-start.110 = (bf16[4,16,1024]{2,1,0:T(8,128)(2,1)}, bf16[4,16,1024]{2,1,0:T(8,128)(2,1)S(1)}, u32[]{:S(2)}, u32[]{:S(2)}) collective-permute-start(bf16[4,16,1024]{2,1,0:T(8,128)(2,1)} %get-tuple-element.259.refs_12_), channel_id=1, source_target_pairs={{0,6},{2,4},{4,2},{6,0},{8,14},{10,12},{12,10},{14,8},{16,22},{18,... | collective-permute-start | bytes 393224 | tf_op jit(solution)/shard_map/ppermute | solution.py:533
  (171 other events, 2715.5 us)

commit v2 on v1

v2 whole, which is shorter than its diff:
```python
import functools

import jax
import jax.numpy as jnp
import numpy as np
from jax import lax
from jax.experimental import pallas as pl
from jax.experimental.pallas import tpu as pltpu
from jax.sharding import PartitionSpec as P

H = 8
ROT = 16
LEN = 512
ADAM_STEP = 10

LN_EPS = 1e-05
ADAM_EPS = 1e-08
BETA_ONE = 0.9
BETA_TWO = 0.95
LEARN_RATE = 0.02
WEIGHT_DECAY = 0.01
FIX_ONE = 1.0 - BETA_ONE**ADAM_STEP
FIX_TWO = 1.0 - BETA_TWO**ADAM_STEP
INV_ROOT_TWO = 0.7071067811865476
INV_ROOT_TWO_PI = 0.3989422804014327

bf16 = jnp.bfloat16
f32 = jnp.float32
SMALL_ROWS = 26


def dot_nn(a, b):
    return lax.dot_general(a, b, (((1,), (0,)), ((), ())), preferred_element_type=f32)


def dot_nt(a, b):
    return lax.dot_general(a, b, (((1,), (1,)), ((), ())), preferred_element_type=f32)


def dot_tn(a, b):
    return lax.dot_general(a, b, (((0,), (0,)), ((), ())), preferred_element_type=f32)


def full_spec(shape):
    zeros = (0,) * len(shape)
    return pl.BlockSpec(shape, lambda *_: zeros)


def cost(flops, moved, transcendentals=0):
    return pl.CostEstimate(
        flops=int(flops), bytes_accessed=int(moved), transcendentals=int(transcendentals)
    )


def vec_row(small_ref, i):
    n = SMALL_ROWS
    rows = [small_ref[o * n + 2 * i + k] for o in range(2) for k in range(2)]
    return jnp.concatenate(rows, 1)


def normalise(x):
    centre = x - jnp.mean(x, -1, keepdims=True)
    inv_dev = lax.rsqrt(jnp.mean(centre * centre, -1, keepdims=True) + LN_EPS)
    return centre * inv_dev, inv_dev


def norm_kernel(tok_ref, small_ref, first_ref, second_ref):
    normed, _ = normalise(tok_ref[...].astype(f32))
    first_ref[...] = (normed * vec_row(small_ref, 0) + vec_row(small_ref, 1)).astype(bf16)
    second_ref[...] = (normed * vec_row(small_ref, 2) + vec_row(small_ref, 3)).astype(bf16)


def norm_call(tokens, small):
    rows, width = tokens.shape
    tile = 512
    spec = pl.BlockSpec((tile, width), lambda i: (i, 0))
    out = jax.ShapeDtypeStruct((rows, width), bf16)
    return pl.pallas_call(
        norm_kernel,
        grid=(rows // tile,),
        in_specs=[spec, full_spec(small.shape)],
        out_specs=[spec, spec],
        out_shape=[out, out],
        cost_estimate=cost(20 * rows * width, 6 * rows * width),
        name="norm",
        compiler_params=pltpu.CompilerParams(vmem_limit_bytes=12 << 20),
    )(tokens, small)


def ff_kernel(meta, second_ref, grad_ref, fco_ref, fcx_ref, pro_ref, prx_ref, small_ref,
              own_ref, send_ref, act_ref, hg_ref, bias_ref, fc_ref):
    j = pl.program_id(0)
    rel = pl.program_id(1)
    c = meta[0]
    rank, far_rank = meta[1], meta[2]
    o = rel ^ c
    rows, width = second_ref.shape
    half = width // 2
    cols = act_ref.shape[1]
    quarter = half // 4
    proj = jnp.where(rel == 0, pro_ref[...], prx_ref[...])
    own_lanes = pl.ds(pl.multiple_of(c * half, half), half)
    far_lanes = pl.ds(pl.multiple_of((1 - c) * half, half), half)
    fc_ref[own_lanes, :] = fco_ref[...]
    fc_ref[far_lanes, :] = fcx_ref[...]
    fc = fc_ref[...]
    base = o * SMALL_ROWS + 18 + 4 * j
    bias = jnp.concatenate([small_ref[base + k] for k in range(cols // 128)], 1)
    tile = 256

    def block(i, total):
        r = pl.ds(pl.multiple_of(i * tile, tile), tile)
        hidden = dot_nn(second_ref[r, :], fc) + bias
        act_grad = dot_nt(grad_ref[r, :], proj)
        phi_cap = 0.5 + 0.5 * lax.erf(hidden * INV_ROOT_TWO)
        slope = phi_cap + hidden * (jnp.exp(-0.5 * hidden * hidden) * INV_ROOT_TWO_PI)
        act_ref[r, :] = (hidden * phi_cap).astype(bf16)
        hg = (act_grad * slope).astype(bf16)
        hg_ref[r, :] = hg
        return total + jnp.sum(hg.astype(f32).reshape(tile // 8, 8, cols), 0)

    total = lax.fori_loop(0, rows // tile, block, jnp.zeros((8, cols), f32))
    bias_ref[...] = jnp.sum(total, 0, keepdims=True)[None]

    gp = dot_tn(act_ref[...], grad_ref[...])
    pcols = pl.ds(pl.multiple_of(j * 1024, 1024), 1024)

    def put_proj(ref, number):
        for a in range(4):
            piece = gp[a * 2 * quarter : (a + 1) * 2 * quarter]
            ref[a ^ number, :, pcols] = jnp.concatenate([piece[:quarter], piece[quarter:]], 1).astype(bf16)

    pl.when(rel == 0)(lambda: put_proj(own_ref, rank))
    pl.when(rel == 1)(lambda: put_proj(send_ref, far_rank))
    lanes = pl.ds(pl.multiple_of(2048 + o * 1024 + j * cols, cols), cols)
    for ref, side, number in ((own_ref, own_lanes, rank), (send_ref, far_lanes, far_rank)):
        gf = dot_tn(second_ref[:, side], hg_ref[...])
        for a in range(4):
            ref[a ^ number, :, lanes] = gf[a * quarter : (a + 1) * quarter].astype(bf16)


def ff_call(meta, second, grad, fc_own, fc_far, proj_own, proj_far, small):
    rows, width = second.shape
    ff = fc_own.shape[1]
    half = width // 2
    cols = ff // 4
    buf = (4, half // 4, 2 * ff)
    fc_spec = pl.BlockSpec((half, cols), lambda j, r, m: (0, (r ^ m[0]) * 2 + j))
    proj_spec = pl.BlockSpec((cols, width), lambda j, r, m: (j, 0))
    act_spec = pl.BlockSpec((rows, cols), lambda j, r, m: (0, 2 * j + r))
    grid_spec = pltpu.PrefetchScalarGridSpec(
        num_scalar_prefetch=1,
        grid=(2, 2),
        in_specs=[
            full_spec((rows, width)),
            full_spec((rows, width)),
            fc_spec,
            fc_spec,
            proj_spec,
            proj_spec,
            full_spec(small.shape),
        ],
        out_specs=[
            full_spec(buf),
            full_spec(buf),
            act_spec,
            act_spec,
            pl.BlockSpec((1, 1, cols), lambda j, r, m: (2 * j + r, 0, 0)),
        ],
        scratch_shapes=[pltpu.VMEM((width, cols), bf16)],
    )
    return pl.pallas_call(
        ff_kernel,
        grid_spec=grid_spec,
        out_shape=[
            jax.ShapeDtypeStruct(buf, bf16),
            jax.ShapeDtypeStruct(buf, bf16),
            jax.ShapeDtypeStruct((rows, ff), bf16),
            jax.ShapeDtypeStruct((rows, ff), bf16),
            jax.ShapeDtypeStruct((4, 1, cols), f32),
        ],
        cost_estimate=cost(8 * rows * width * ff, 4 * rows * width + 4 * rows * ff),
        name="feed_forward",
        compiler_params=pltpu.CompilerParams(vmem_limit_bytes=40 << 20),
    )(meta, second, grad, fc_own, fc_far, proj_own, proj_far, small)


def rotate_rows(x, cosine, sine):
    parts = []
    for h in range(2):
        low, high = x[64 * h : 64 * h + 8], x[64 * h + 8 : 64 * h + 16]
        parts += [low * cosine - high * sine, high * cosine + low * sine, x[64 * h + 16 : 64 * h + 64]]
    return jnp.concatenate(parts, 0)


def attention_kernel(j, rel, meta, first_ref, grad_ref, wq_ref, wk_ref, wv_ref, xq_ref, xk_ref, xv_ref,
                     ow_ref, small_ref, trig_ref,
                     own_ref, send_ref, og_ref, qg_ref, att_ref, bias_ref,
                     wt_ref, bcol_ref, qgs_ref, attt_ref, btot_ref):
    s = pl.program_id(0)
    c = meta[0]
    rank, far_rank = meta[1], meta[2]
    o = rel ^ c
    rows, width = first_ref.shape
    half = width // 2
    quarter = half // 4
    own_lanes = pl.ds(pl.multiple_of(c * half, half), half)
    far_lanes = pl.ds(pl.multiple_of((1 - c) * half, half), half)

    @pl.when(s == 0)
    def _():
        for p, (own, far) in enumerate(((wq_ref, xq_ref), (wk_ref, xk_ref), (wv_ref, xv_ref))):
            wt_ref[128 * p : 128 * (p + 1), own_lanes] = own[...].T
            wt_ref[128 * p : 128 * (p + 1), far_lanes] = far[...].T
            row = p * 4 + o * 2 + j
            owner = row // 6
            bias = small_ref[owner * SMALL_ROWS + 12 + row - 6 * owner]
            bcol_ref[128 * p : 128 * (p + 1), :] = jnp.broadcast_to(bias, (128, 128)).T
        btot_ref[...] = jnp.zeros_like(btot_ref)

    seq = pl.ds(pl.multiple_of(s * LEN, LEN), LEN)
    first = first_ref[seq, :]
    grad = grad_ref[seq, :]
    mixed = dot_nt(wt_ref[...], first) + bcol_ref[:, :1]
    da_t = dot_nt(ow_ref[...], grad).astype(bf16)
    cosine, sine = trig_ref[0], trig_ref[1]
    q_t = rotate_rows(mixed[:128], cosine, sine).astype(bf16) * jnp.asarray(0.125, bf16)
    k_t = rotate_rows(mixed[128:256], cosine, sine).astype(bf16)
    v_t = mixed[256:].astype(bf16)
    k_tok = k_t.T
    v_tok = v_t.T
    hl = LEN // 2
    row_id = lax.broadcasted_iota(jnp.int32, (hl, hl), 0)
    col_id = lax.broadcasted_iota(jnp.int32, (hl, hl), 1)
    keep = row_id <= col_id
    zeros = jnp.zeros((64, LEN), bf16)
    att, dq, dk, dv = [], [], [], []
    for h in range(2):
        hs = slice(64 * h, 64 * h + 64)
        qh, kh, vh, dah = q_t[hs], k_t[hs], v_t[hs], da_t[hs]
        pad = (lambda u: jnp.concatenate([u, zeros], 0)) if h == 0 else (lambda u: jnp.concatenate([zeros, u], 0))
        qz, daz = pad(qh), pad(dah)
        att_h, dq_h = [], []
        dk_h = dv_h = None
        for t in range(2):
            ts = slice(hl * t, hl * t + hl)
            n = hl * (t + 1)
            score = dot_nn(k_tok[:n], qz[:, ts])
            diag = jnp.where(keep, score[n - hl :], -1e30)
            score = diag if t == 0 else jnp.concatenate([score[:hl], diag], 0)
            exps = jnp.exp(score - jnp.max(score, 0, keepdims=True))
            prob = exps * (1.0 / jnp.sum(exps, 0, keepdims=True))
            prob_b = prob.astype(bf16)
            att_h.append(dot_nn(vh[:, :n], prob_b))
            pg = dot_nn(v_tok[:n], daz[:, ts])
            sg = (prob * (pg - jnp.sum(pg * prob, 0, keepdims=True))).astype(bf16)
            dq_h.append(dot_nn(kh[:, :n], sg))
            dv_t = dot_nt(dah[:, ts], prob_b)
            dk_t = dot_nt(qh[:, ts], sg)
            if t == 0:
                dv_h, dk_h = dv_t, dk_t
            else:
                dv_h = jnp.concatenate([dv_h + dv_t[:, :hl], dv_t[:, hl:]], 1)
                dk_h = jnp.concatenate([dk_h + dk_t[:, :hl], dk_t[:, hl:]], 1)
        att.append(jnp.concatenate(att_h, 1))
        dq.append(jnp.concatenate(dq_h, 1) * 0.125)
        dk.append(dk_h)
        dv.append(dv_h)
    att_t = jnp.concatenate(att, 0).astype(bf16)
    dq_t = rotate_rows(jnp.concatenate(dq, 0), cosine, -sine)
    dk_t = rotate_rows(jnp.concatenate(dk, 0), cosine, -sine)
    qkv_t = jnp.concatenate([dq_t, dk_t, jnp.concatenate(dv, 0)], 0).astype(bf16)
    qkv_g = qkv_t.T
    qg_ref[...] = qkv_g
    qgs_ref[seq, :] = qkv_g
    att_ref[...] = att_t.T
    attt_ref[:, seq] = att_t
    btot_ref[...] += jnp.sum(qkv_g.astype(f32).reshape(LEN // 8, 8, 384), 0)

    @pl.when(s == pl.num_programs(0) - 1)
    def _():
        bias_ref[...] = jnp.sum(btot_ref[...], 0, keepdims=True)
        for ref, side, number in ((own_ref, own_lanes, rank), (send_ref, far_lanes, far_rank)):
            gw = dot_tn(first_ref[:, side], qgs_ref[...])
            for a in range(4):
                ref[a ^ number] = gw[a * quarter : (a + 1) * quarter].astype(bf16)
        go = dot_nn(attt_ref[...], grad_ref[...])
        hq = quarter // 2
        for a in range(4):
            piece = go[a * hq : (a + 1) * hq]
            og_ref[a ^ (far_rank if rel else rank)] = jnp.concatenate([piece[:, :256], piece[:, 256:]], 0).astype(bf16)


def trig_tables():
    freqs = np.power(np.float32(10000.0), -np.arange(0, ROT, 2).astype(np.float32) / np.float32(ROT))
    angles = (np.arange(LEN).astype(np.float32)[None, :] * freqs[:, None]).astype(np.float32)
    return np.stack([np.cos(angles), np.sin(angles)]).astype(np.float32)


def attention_call(j, rel, meta, first, grad, qkv_own, qkv_far, out_w, small, trig):
    rows, width = first.shape
    half = width // 2
    qbuf = (4, half // 4, 384)
    obuf = (4, half // 4, 256)
    w_specs = [
        pl.BlockSpec((half, 128), functools.partial(lambda p, s, m: (0, p * 4 + (rel ^ m[0]) * 2 + j), p))
        for p in range(3)
    ]
    grid_spec = pltpu.PrefetchScalarGridSpec(
        num_scalar_prefetch=1,
        grid=(rows // LEN,),
        in_specs=[
            full_spec((rows, width)),
            full_spec((rows, width)),
            *w_specs,
            *w_specs,
            pl.BlockSpec((128, width), lambda s, m: (j, 0)),
            full_spec(small.shape),
            full_spec(trig.shape),
        ],
        out_specs=[
            full_spec(qbuf),
            full_spec(qbuf),
            full_spec(obuf),
            pl.BlockSpec((LEN, 384), lambda s, m: (s, 0)),
            pl.BlockSpec((LEN, 128), lambda s, m: (s, 0)),
            full_spec((1, 384)),
        ],
        scratch_shapes=[
            pltpu.VMEM((384, width), bf16),
            pltpu.VMEM((384, 128), f32),
            pltpu.VMEM((rows, 384), bf16),
            pltpu.VMEM((128, rows), bf16),
            pltpu.VMEM((8, 384), f32),
        ],
    )
    flops = 2 * rows * width * (2 * 384 + 2 * 128) + 2 * 6 * 2 * rows * LEN * 128
    return pl.pallas_call(
        functools.partial(attention_kernel, j, rel),
        grid_spec=grid_spec,
        out_shape=[
            jax.ShapeDtypeStruct(qbuf, bf16),
            jax.ShapeDtypeStruct(qbuf, bf16),
            jax.ShapeDtypeStruct(obuf, bf16),
            jax.ShapeDtypeStruct((rows, 384), bf16),
            jax.ShapeDtypeStruct((rows, 128), bf16),
            jax.ShapeDtypeStruct((1, 384), f32),
        ],
        cost_estimate=cost(flops, 4 * rows * width + 2 * rows * 512),
        name=f"attention_{j}{rel}",
        compiler_params=pltpu.CompilerParams(vmem_limit_bytes=26 << 20),
    )(meta, first, grad, *[qkv_own] * 3, *[qkv_far] * 3, out_w, small, trig)


def output_kernel(meta, tok_ref, grad_ref, act_ref, hg_ref, *refs):
    at_refs, qg_refs, refs = refs[0:4], refs[4:8], refs[8:]
    oo_ref, ox_ref, po_ref, px_ref, fo_ref, fx_ref, wo_ref, wx_ref, small_ref = refs[:9]
    qb_refs, fb_ref, refs = refs[9:13], refs[13], refs[14:]
    lay_ref, tg_ref, own_ref, send_ref, wgo_ref, wgx_ref, sg_ref, fg_ref, tot_ref, qb_ref = refs
    i = pl.program_id(0)
    c = meta[0]
    tile, width = tok_ref.shape
    half = width // 2
    own_lanes = pl.ds(pl.multiple_of(c * half, half), half)
    far_lanes = pl.ds(pl.multiple_of((1 - c) * half, half), half)

    @pl.when(i == 0)
    def _():
        for w_ref, g_ref in ((wo_ref, wgo_ref), (wx_ref, wgx_ref)):
            for j in range(2):
                for rel in range(2):
                    for p in range(3):
                        src = pl.ds(pl.multiple_of((p * 4 + (rel ^ c) * 2 + j) * 128, 128), 128)
                        dst = (j * 6 + rel * 3 + p) * 128
                        g_ref[:, dst : dst + 128] = w_ref[:, src]
        tot_ref[...] = jnp.zeros_like(tot_ref)

    x = tok_ref[...].astype(f32)
    grad = grad_ref[...].astype(f32)
    normed, inv_dev = normalise(x)
    acc = dot_nn(jnp.concatenate([at_refs[0][...], at_refs[2][...]], 1), oo_ref[...])
    acc += dot_nn(jnp.concatenate([at_refs[1][...], at_refs[3][...]], 1), ox_ref[...])
    for j in range(2):
        for rel, p_ref in enumerate((po_ref, px_ref)):
            k = 512 * (2 * j + rel)
            acc += dot_nn(act_ref[:, k : k + 512], p_ref[512 * j : 512 * (j + 1), :])
    lay_ref[...] = (x + acc + (vec_row(small_ref, 4) + vec_row(small_ref, 5))).astype(bf16)

    for f_ref, wg_ref, lanes in ((fo_ref, wgo_ref, own_lanes), (fx_ref, wgx_ref, far_lanes)):
        total = None
        for j in range(2):
            for rel in range(2):
                k = 512 * (2 * j + rel)
                cols = pl.ds(pl.multiple_of((rel ^ c) * 1024 + 512 * j, 512), 512)
                term = dot_nt(hg_ref[:, k : k + 512], f_ref[:, cols])
                total = term if total is None else total + term
        sg_ref[:, lanes] = total
        qg = [jnp.concatenate([qg_refs[2 * j][...], qg_refs[2 * j + 1][...]], 1) for j in range(2)]
        fg_ref[:, lanes] = dot_nt(qg[0], wg_ref[:, :768]) + dot_nt(qg[1], wg_ref[:, 768:])
    second_g = sg_ref[...]
    first_g = fg_ref[...]
    e = first_g * vec_row(small_ref, 0) + second_g * vec_row(small_ref, 2)
    ln = inv_dev * (
        e - jnp.mean(e, -1, keepdims=True) - normed * jnp.mean(e * normed, -1, keepdims=True)
    )
    tg_ref[...] = (grad + ln).astype(bf16)
    for k, term in enumerate((first_g * normed, first_g, second_g * normed, second_g, grad)):
        tot_ref[k] += jnp.sum(term.reshape(tile // 8, 8, width), 0)

    @pl.when(i == pl.num_programs(0) - 1)
    def _():
        for j in range(2):
            for rel in range(2):
                for p in range(3):
                    qb_ref[p * 4 + (rel ^ c) * 2 + j] = qb_refs[2 * j + rel][:, 128 * p : 128 * (p + 1)]
        sums = [jnp.sum(tot_ref[k], 0, keepdims=True) for k in range(5)]
        sums.append(sums[4])
        for ref, rel in ((own_ref, 0), (send_ref, 1)):
            owner = rel ^ c
            for k in range(6):
                for part in range(2):
                    low = sums[k][:, 128 * part : 128 * (part + 1)]
                    high = sums[k][:, 256 + 128 * part : 256 + 128 * (part + 1)]
                    ref[2 * k + part] = jnp.where(owner == 0, low, high)
            for k in range(6):
                ref[12 + k] = qb_ref[owner * 6 + k]
            for j in range(2):
                for k in range(4):
                    ref[18 + 4 * j + k] = fb_ref[2 * j + rel][:, 128 * k : 128 * (k + 1)]
            for k in range(SMALL_ROWS, 32):
                ref[k] = jnp.zeros((1, 128), f32)


def output_call(meta, tokens, grad, act, hg, atts, qgs, out_w, proj_w, fc_w, qkv_w, small, qbs, fb):
    rows, width = tokens.shape
    tile = 256
    blk = lambda n: pl.BlockSpec((tile, n), lambda i, m: (i, 0))
    weights = [*out_w, *proj_w, *fc_w, *qkv_w]
    tail = [small, *qbs, fb]
    packed = (32, 1, 128)
    grid_spec = pltpu.PrefetchScalarGridSpec(
        num_scalar_prefetch=1,
        grid=(rows // tile,),
        in_specs=[
            blk(width),
            blk(width),
            *[blk(a.shape[1]) for a in (act, hg, *atts, *qgs)],
            *[full_spec(w.shape) for w in weights],
            *[full_spec(w.shape) for w in tail],
        ],
        out_specs=[blk(width), blk(width), full_spec(packed), full_spec(packed)],
        scratch_shapes=[
            pltpu.VMEM(qkv_w[0].shape, bf16),
            pltpu.VMEM(qkv_w[0].shape, bf16),
            pltpu.VMEM((tile, width), f32),
            pltpu.VMEM((tile, width), f32),
            pltpu.VMEM((5, 8, width), f32),
            pltpu.VMEM((12, 1, 128), f32),
        ],
    )
    return pl.pallas_call(
        output_kernel,
        grid_spec=grid_spec,
        out_shape=[
            jax.ShapeDtypeStruct((rows, width), bf16),
            jax.ShapeDtypeStruct((rows, width), bf16),
            jax.ShapeDtypeStruct(packed, f32),
            jax.ShapeDtypeStruct(packed, f32),
        ],
        cost_estimate=cost(2 * rows * width * (512 + 2048 * 2 + 1536), 2 * rows * (4 * 512 + 4 * 2048)),
        name="outputs",
        compiler_params=pltpu.CompilerParams(vmem_limit_bytes=44 << 20),
    )(meta, tokens, grad, act, hg, *atts, *qgs, *weights, *tail)


def sum_kernel(n_in, *refs):
    ins, outs = refs[:n_in], refs[n_in:]
    for k, out in enumerate(outs):
        rows = out.shape[0]
        for i in range(rows):
            total = ins[0][k * rows + i].astype(f32)
            for term in ins[1:]:
                total += term[k * rows + i].astype(f32)
            out[i] = total.astype(out.dtype)


def sum_call(terms, count, name):
    shape, dtype = terms[0].shape, terms[0].dtype
    moved = len(terms) * terms[0].size * terms[0].dtype.itemsize
    return pl.pallas_call(
        functools.partial(sum_kernel, len(terms)),
        out_shape=[jax.ShapeDtypeStruct((shape[0] // count, *shape[1:]), dtype)] * count,
        compiler_params=pltpu.CompilerParams(vmem_limit_bytes=(moved * 3) // 2 + (4 << 20)),
        cost_estimate=cost(moved, 2 * moved),
        name=name,
    )(*terms)


def pair_kernel(*refs):
    own, got, outs = refs[:6], refs[6:12], refs[12:]
    col = 0
    for mine, other in zip(own, got):
        w = mine.shape[2]
        for k, out in enumerate(outs):
            for i in range(2):
                total = mine[2 * k + i].astype(f32) + other[2 * k + i].astype(f32)
                out[i, :, col : col + w] = total.astype(bf16)
        col += w


def pair_call(own, got, name):
    rows = own[0].shape[1]
    width = sum(a.shape[2] for a in own)
    return pl.pallas_call(
        pair_kernel,
        out_shape=[jax.ShapeDtypeStruct((2, rows, width), bf16)] * 2,
        compiler_params=pltpu.CompilerParams(vmem_limit_bytes=12 << 20),
        cost_estimate=cost(8 * rows * width, 24 * rows * width),
        name=name,
    )(*own, *got)


def exchange(a, reps, far, near):
    pairs = [(2 * i + c, 2 * (i ^ (near if c else far)) + c) for i in range(reps) for c in range(2)]
    return lax.ppermute(a, ("rep", "opt"), pairs)


def swap(a):
    return lax.ppermute(a, "opt", [(0, 1), (1, 0)])


def tie(value, *others):
    return lax.optimization_barrier((value, *others))[0]


def rest_bits(reps):
    return [1 << b for b in range(2, reps.bit_length() - 1)]


def spread(total, reps):
    return [total, exchange(total, reps, 2, 1), exchange(total, reps, 1, 2), exchange(total, reps, 3, 3)]


def adamw(grad, mean, square, weight):
    new_mean = BETA_ONE * mean + (1.0 - BETA_ONE) * grad
    new_square = BETA_TWO * square + (1.0 - BETA_TWO) * grad * grad
    step = -LEARN_RATE * (
        new_mean * (1.0 / FIX_ONE) / (jnp.sqrt(new_square * (1.0 / FIX_TWO)) + ADAM_EPS)
        + WEIGHT_DECAY * weight.astype(f32)
    )
    return step, new_mean, new_square


def pick(refs, which, cols, rows=slice(None)):
    out = refs[0][0, rows, cols]
    for k in range(1, len(refs)):
        out = jnp.where(which == k, refs[k][0, rows, cols], out)
    return out.astype(f32)


def adam_block(grad, m_ref, s_ref, w_ref, g_out, st_out, m_out, s_out, at):
    step, mean, square = adamw(grad, m_ref[at], s_ref[at], w_ref[at])
    g_out[at] = grad
    st_out[at] = step
    m_out[at] = mean
    s_out[at] = square


def adam_ff_kernel(meta, *refs):
    pieces, proj, fc, proj_out, fc_out = refs[:4], refs[4:7], refs[7:10], refs[10:14], refs[14:18]
    which = pl.program_id(0) ^ meta[1]
    quarter = fc[0].shape[0]
    for j in range(2):
        for k in range(2):
            at = (j, slice(k * quarter, (k + 1) * quarter), slice(None))
            col = 1024 * j + 512 * k
            adam_block(pick(pieces, which, slice(col, col + 512)), *proj, *proj_out, at)
            at = (slice(None), slice(col, col + 512))
            adam_block(pick(pieces, which, slice(2048 + col, 2048 + col + 512)), *fc, *fc_out, at)


def adam_qkv_kernel(meta, *refs):
    pieces, qkv, out, qkv_out, out_out = refs[:4], refs[4:7], refs[7:10], refs[10:14], refs[14:18]
    c = meta[0]
    which = pl.program_id(0) ^ meta[1]
    quarter = qkv[0].shape[0]
    hq = quarter // 2
    for j in range(2):
        for slot in range(2):
            for p in range(3):
                col = 384 * (2 * j + slot) + 128 * p
                grad = pick(pieces, which, slice(col, col + 128))
                lanes = pl.ds(pl.multiple_of((p * 4 + (slot ^ c) * 2 + j) * 128, 128), 128)
                adam_block(grad, *qkv, *qkv_out, (slice(None), lanes))
        for k in range(2):
            col = 1536 + 256 * j
            grad = pick(pieces, which, slice(col, col + 256), slice(k * hq, (k + 1) * hq))
            adam_block(grad, *out, *out_out, (j, slice(None), slice(256 * k, 256 * k + 256)))


def adam_call(kernel, meta, pieces, first, second, first_spec, second_spec, name):
    outs = [jax.ShapeDtypeStruct(first[0].shape, f32)] * 4 + [jax.ShapeDtypeStruct(second[0].shape, f32)] * 4
    grid_spec = pltpu.PrefetchScalarGridSpec(
        num_scalar_prefetch=1,
        grid=(4,),
        in_specs=[*[full_spec(a.shape) for a in pieces], *[first_spec] * 3, *[second_spec] * 3],
        out_specs=[*[first_spec] * 4, *[second_spec] * 4],
    )
    size = first[0].size + second[0].size
    return pl.pallas_call(
        kernel,
        grid_spec=grid_spec,
        out_shape=outs,
        compiler_params=pltpu.CompilerParams(vmem_limit_bytes=32 << 20),
        cost_estimate=cost(20 * size, 28 * size),
        name=name,
    )(meta, *pieces, *first, *second)


def body(
    tokens,
    out_grad,
    vectors,
    qkv_weight,
    qkv_bias,
    out_weight,
    fc_weight,
    fc_bias,
    proj_weight,
    mean_vectors,
    mean_qkv_weight,
    mean_qkv_bias,
    mean_out_weight,
    mean_fc_weight,
    mean_fc_bias,
    mean_proj_weight,
    square_vectors,
    square_qkv_weight,
    square_qkv_bias,
    square_out_weight,
    square_fc_weight,
    square_fc_bias,
    square_proj_weight,
):
    reps = lax.axis_size("rep")
    c = lax.axis_index("opt")
    place = lax.axis_index("rep")
    low, high = place & 1, (place >> 1) & 1
    ranks = jnp.stack([2 * low + high, 2 * high + low])
    meta = jnp.stack([c, ranks[c], ranks[1 - c]]).astype(jnp.int32)
    trig = jnp.asarray(trig_tables())

    packed = jnp.concatenate(
        [vectors.reshape(12, 128), qkv_bias.reshape(6, 128), fc_bias.reshape(8, 128)], 0
    )
    small = lax.all_gather(packed, "opt", axis=0, tiled=True).astype(f32).reshape(2 * SMALL_ROWS, 1, 128)
    fc_far = swap(fc_weight)
    proj_far = swap(proj_weight)
    qkv_far = swap(qkv_weight)
    out_far = swap(out_weight)

    first, second = norm_call(tokens, small)
    own, send, act, hg, fb = ff_call(meta, second, out_grad, fc_weight, fc_far, proj_weight, proj_far, small)

    ff_got = swap(send)
    att = {}
    last = own
    order = [(0, 1), (0, 0), (1, 1), (1, 0)]

    def attend(k, *wait):
        j, rel = order[k]
        out_w = out_far if rel else out_weight
        att[j, rel] = attention_call(
            j, rel, tie(meta, *wait), first, out_grad, qkv_weight, qkv_far, out_w, small, trig
        )
        return att[j, rel][5]

    mark = attend(0, own)
    keep, send = sum_call([tie(own, mark), ff_got], 2, "ff_pair")
    got = exchange(send, reps, 1, 2)
    mark = attend(1, keep)
    keep, send = sum_call([tie(keep, mark), got], 2, "ff_sum0")
    got = exchange(send, reps, 2, 1)
    mark = attend(2, keep)
    (ff_total,) = sum_call([tie(keep, mark), got], 1, "ff_sum1")
    bits = rest_bits(reps)
    got = exchange(ff_total, reps, bits[0], bits[0])
    mark = attend(3, ff_total)

    keys = [(0, 0), (0, 1), (1, 0), (1, 1)]
    q_own = [att[k][0] for k in keys]
    q_got = [swap(att[j, 1 - rel][1]) for j, rel in keys]
    o_own = [att[j, 0][2] for j in range(2)]
    o_got = [swap(att[j, 1][2]) for j in range(2)]
    (ff_total,) = sum_call([tie(ff_total, mark), got], 1, "ff_sum2")
    keep, send = pair_call([*q_own, *o_own], [*q_got, *o_got], "att_pair")
    att_got = exchange(send, reps, 1, 2)
    for bit in bits[1:]:
        got = exchange(ff_total, reps, bit, bit)
        (ff_total,) = sum_call([ff_total, got], 1, "ff_sum3")
    ff_pieces = spread(ff_total, reps)

    layer_out, tokens_grad, small_own, small_send = output_call(
        tie(meta, keep),
        tokens,
        out_grad,
        act,
        hg,
        [att[k][4] for k in keys],
        [att[k][3] for k in keys],
        (out_weight, out_far),
        (proj_weight, proj_far),
        (fc_weight, fc_far),
        (qkv_weight, qkv_far),
        small,
        [att[k][5] for k in keys],
        fb,
    )
    keep, send = sum_call([keep, att_got], 2, "att_sum0")
    got = exchange(send, reps, 2, 1)
    (att_total,) = sum_call([keep, got], 1, "att_sum1")
    for bit in bits:
        got = exchange(att_total, reps, bit, bit)
        (att_total,) = sum_call([att_total, got], 1, "att_sum2")
    att_pieces = spread(att_total, reps)

    (total,) = sum_call([small_own, swap(small_send)], 1, "small_pair")
    for bit in (1, 2, *bits):
        (total,) = sum_call([total, exchange(total, reps, bit, bit)], 1, "small_sum")
    flat = total.reshape(32, 128)
    g_vec = flat[:12].reshape(6, 256)
    g_qb = flat[12:18].reshape(768)
    g_fb = flat[18:26].reshape(1024)

    view = lambda a: a.reshape(2, 512, 512)
    proj_adam = adam_call(
        adam_ff_kernel,
        meta,
        ff_pieces,
        [view(a) for a in (mean_proj_weight, square_proj_weight, proj_weight)],
        [mean_fc_weight, square_fc_weight, fc_weight],
        pl.BlockSpec((2, 128, 512), lambda q, m: (0, q, 0)),
        pl.BlockSpec((64, 2048), lambda q, m: (q, 0)),
        "adam_ff",
    )
    a_proj = [a.reshape(1024, 512) for a in proj_adam[:4]]
    a_fc = proj_adam[4:]
    view_o = lambda a: a.reshape(2, 128, 512)
    qkv_adam = adam_call(
        adam_qkv_kernel,
        meta,
        att_pieces,
        [mean_qkv_weight, square_qkv_weight, qkv_weight],
        [view_o(a) for a in (mean_out_weight, square_out_weight, out_weight)],
        pl.BlockSpec((64, 1536), lambda q, m: (q, 0)),
        pl.BlockSpec((2, 32, 512), lambda q, m: (0, q, 0)),
        "adam_qkv",
    )
    a_qkv = qkv_adam[:4]
    a_out = [a.reshape(256, 512) for a in qkv_adam[4:]]
    a_vec = (g_vec, *adamw(g_vec, mean_vectors, square_vectors, vectors))
    a_qb = (g_qb, *adamw(g_qb, mean_qkv_bias, square_qkv_bias, qkv_bias))
    a_fb = (g_fb, *adamw(g_fb, mean_fc_bias, square_fc_bias, fc_bias))
    order = (a_vec, a_qkv, a_qb, a_out, a_fc, a_fb, a_proj)
    return (layer_out, tokens_grad, *[a[k] for k in range(4) for a in order])


def solution(mesh):
    rows = P(("rep", "opt"), None)
    weights = (P(None, "opt"), P("opt", None), P("opt"), P("opt", None), P("opt", None), P("opt"), P("opt", None))
    in_specs = (rows, rows, *weights, *weights, *weights)
    out_specs = (rows, rows, *weights, *weights, *weights, *weights)
    return jax.shard_map(body, mesh=mesh, in_specs=in_specs, out_specs=out_specs, check_vma=False)
```

time: 389 us -> 238 us (0.61)
  starting transfers between devices: 143 us -> 26.5 us
  Pallas kernels: 201 us -> 144 us
  waiting for transfers between devices: 26.3 us -> 45.5 us
  local copies, waits for them, and re-layouts: 8.79 us -> 13.6 us
    ppermute x102 -> x18, starting transfers between devices: 140 us -> 23.2 us  [exchange(): return lax.ppermute(a, ('rep', 'opt'), pairs)]
    pallas_call x25 -> x22, Pallas kernels: 171 us -> 120 us  [the longest x4 70.7 us: attention_call(): pl.pallas_call(functools.partial(attention_kernel, j, rel), grid_spec=gri...]
    ppermute x102 -> x18, waiting for transfers between devices: 25.2 us -> 39.5 us  [exchange(): return lax.ppermute(a, ('rep', 'opt'), pairs)]
    unnamed x248 -> x68, local copies, waits for them, and re-layouts: 5.38 us -> 12.2 us
    ppermute x9 -> x12, waiting for transfers between devices: 1.07 us -> 5.97 us  [swap(): return lax.ppermute(a, 'opt', [(0, 1), (1, 0)])]
  transfers between devices with their start and end apart: 111 -> 30, of which waited for: 20 -> 10; matrix products, arithmetic and copies ran while one was open for 2% -> 2% of each run, Pallas kernels for 49% -> 44%
where the time goes in v2:
time: 238 us; the launch traced here: 237 us
  Pallas kernels  144 us (61%)
  waiting for transfers between devices  45.5 us (19%)
  starting transfers between devices  26.5 us (11%)
  local copies, waits for them, and re-layouts  13.6 us (6%)
  other arithmetic  4.01 us (2%)
  blocking collectives  2.53 us (1%)
    pallas_call x4, Pallas kernels, attention_call(): pl.pallas_call(functools.partial(attention_kernel, j, rel), grid_spec=gri...  70.7 us
    ppermute x18, waiting for transfers between devices, exchange(): return lax.ppermute(a, ('rep', 'opt'), pairs)  39.5 us
    pallas_call x1, Pallas kernels, ff_call(): pl.pallas_call(ff_kernel, grid_spec=grid_spec, out_shape=[jax.ShapeDtypeS...  31.5 us
    ppermute x18, starting transfers between devices, exchange(): return lax.ppermute(a, ('rep', 'opt'), pairs)  23.2 us
    pallas_call x1, Pallas kernels, output_call(): pl.pallas_call(output_kernel, grid_spec=grid_spec, out_shape=[jax.ShapeDt...  22.1 us
    pallas_call x2, Pallas kernels, adam_call(): pl.pallas_call(kernel, grid_spec=grid_spec, out_shape=outs, compiler_para...  16 us
    unnamed x68, local copies, waits for them, and re-layouts  12.2 us
    ppermute x12, waiting for transfers between devices, swap(): return lax.ppermute(a, 'opt', [(0, 1), (1, 0)])  5.97 us
  transfers between devices with their start and end apart: 30, of which 10 were waited for; matrix products, arithmetic and copies ran while one was open for 2% of the time, Pallas kernels for 44%

profile of v2, /device:TPU:0, one launch (start us, length us, event | category | flops | bytes accessed | tf_op | source)
XLA Modules:
  0.0 237.3 jit_solution(280892708405064721)
XLA Ops:
  0.7 0.6 collective-permute-start
  1.3 0.7 reshape.132
  2.0 0.7 maximum_bitcast_fusion
  2.7 2.5 %all-gather = bf16[2,26,128]{2,1,0:T(8,128)(2,1)S(1)} all-gather(bf16[1,26,128]{2,1,0:T(8,128)(2,1)S(1)} %maximum_bitcast_fusion), channel_id=1, replica_groups=mesh['rep'=16,'opt'=2] {'opt'}, dimensions={0}, use_global_device_ids=true | all-gather | bytes 19968 | tf_op jit(solution)/shard_map/all_gather | solution.py:656
  5.3 0.6 fusion.6
  5.9 1.6 copy-done.4
  7.5 1.9 norm.1
  9.4 1.4 pad_add_fusion.1.meta
  10.8 1.6 copy-done.17
  12.4 31.5 %feed_forward.1 = (bf16[4,64,4096]{2,1,0:T(8,128)(2,1)S(1)}, bf16[4,64,4096]{2,1,0:T(8,128)(2,1)S(1)}, bf16[2048,2048]{1,0:T(8,128)(2,1)}, bf16[2048,2048]{1,0:T(8,128)(2,1)}, f32[4,1,512]{2,1,0:T(1,128)S(1)}) custom-call(s32[3]{0:T(128)S(1)} %pad_add_fusion.1.meta, bf16[2048,512]{1,0:T(8,128)(2,1)S(1)} %get-tuple-element.98.second_ref, ...), custom_call_target="tpu_custom_call" | custom-call | flops 17179869184 | bytes 20971520 | tf_op jit(solution)/shard_map/feed_forward/pallas_call | solution.py:172
  43.9 0.4 collective-permute-start.4
  44.4 0.4 collective-permute-start.3
  44.9 4.8 %collective-permute-done.3.ow_ref.refs_9_ = bf16[256,512]{1,0:T(8,128)(2,1)S(1)} collective-permute-done((bf16[256,512]{1,0:T(8,128)(2,1)S(1)}, bf16[256,512]{1,0:T(8,128)(2,1)S(1)}, u32[]{:S(2)}, u32[]{:S(2)}) %collective-permute-start.3) | collective-permute-done | bytes 262176 | tf_op jit(solution)/shard_map/ppermute | solution.py:529
  49.6 17.6 %attention_01.1 = (bf16[4,64,384]{2,1,0:T(8,128)(2,1)S(1)}, bf16[4,64,384]{2,1,0:T(8,128)(2,1)S(1)}, bf16[4,64,256]{2,1,0:T(8,128)(2,1)S(1)}, bf16[2048,384]{1,0...) custom-call(s32[3]{0:T(128)S(1)} %pad_add_fusion.1.meta, ...), custom_call_target="tpu_custom_call" | custom-call | flops 5368709120 | bytes 6291456 | tf_op jit(solution)/shard_map/attention_01/pallas_call | solution.py:338
  67.3 0.5 ff_pair.1
  67.8 0.6 copy-done.19
  68.4 2.8 %collective-permute-start.5 = (bf16[2,64,4096]{2,1,0:T(8,128)(2,1)S(1)}, bf16[2,64,4096]{2,1,0:T(8,128)(2,1)S(1)}, u32[]{:S(2)}, u32[]{:S(2)}) collective-permute-start(bf16[2,64,4096]{2,1,0:T(8,128)(2,1)S(1)} %get-tuple-element.111), channel_id=1, source_target_pairs={{0,2},{1,5},{2,0},{3,7},{4,6},{5,1},{6,4},{7,3},{8,10},{9,13},{10,... | collective-permute-start | bytes 3145736 | tf_op jit(solution)/shard_map/ppermute | solution.py:525
  71.2 17.8 %attention_00.1 = (bf16[4,64,384]{2,1,0:T(8,128)(2,1)S(1)}, bf16[4,64,384]{2,1,0:T(8,128)(2,1)S(1)}, bf16[4,64,256]{2,1,0:T(8,128)(2,1)S(1)}, bf16[2048,384]{1,0...) custom-call(s32[3]{0:T(128)S(1)} %pad_add_fusion.1.meta, ...), custom_call_target="tpu_custom_call" | custom-call | flops 5368709120 | bytes 6291456 | tf_op jit(solution)/shard_map/attention_00/pallas_call | solution.py:338
  89.0 0.2 ff_sum0.1
  89.2 1.6 collective-permute-start.6
  90.8 0.5 collective-permute-start.7
  91.3 17.6 %attention_11.1 = (bf16[4,64,384]{2,1,0:T(8,128)(2,1)S(1)}, bf16[4,64,384]{2,1,0:T(8,128)(2,1)S(1)}, bf16[4,64,256]{2,1,0:T(8,128)(2,1)S(1)}, bf16[2048,384]{1,0...) custom-call(s32[3]{0:T(128)S(1)} %pad_add_fusion.1.meta, ...), custom_call_target="tpu_custom_call" | custom-call | flops 5368709120 | bytes 6291456 | tf_op jit(solution)/shard_map/attention_11/pallas_call | solution.py:338
  108.9 1.1 copy-done.20
  110.0 0.5 collective-permute-start.9
  110.7 17.8 %attention_10.1 = (bf16[4,64,384]{2,1,0:T(8,128)(2,1)S(1)}, bf16[4,64,384]{2,1,0:T(8,128)(2,1)S(1)}, bf16[4,64,256]{2,1,0:T(8,128)(2,1)S(1)}, bf16[2048,384]{1,0...) custom-call(s32[3]{0:T(128)S(1)} %pad_add_fusion.1.meta, ...), custom_call_target="tpu_custom_call" | custom-call | flops 5368709120 | bytes 6291456 | tf_op jit(solution)/shard_map/attention_10/pallas_call | solution.py:338
  128.6 0.5 collective-permute-start.12
  129.1 1.6 collective-permute-start.25
  130.7 0.3 att_pair.1
  131.0 0.6 collective-permute-start.18
  131.6 11.5 %collective-permute-done.25.refs_1_ = bf16[1,64,4096]{2,1,0:T(8,128)(2,1)S(1)} collective-permute-done((bf16[1,64,4096]{2,1,0:T(8,128)(2,1)S(1)}, bf16[1,64,4096]{2,1,0:T(8,128)(2,1)S(1)}, u32[]{:S(2)}, u32[]{:S(2)}) %collective-permute-start.25) | collective-permute-done | bytes 524320 | tf_op jit(solution)/shard_map/ppermute | solution.py:525
  143.1 2.6 %collective-permute-start.26 = (bf16[1,64,4096]{2,1,0:T(8,128)(2,1)S(1)}, bf16[1,64,4096]{2,1,0:T(8,128)(2,1)S(1)}, u32[]{:S(2)}, u32[]{:S(2)}) collective-permute-start(bf16[1,64,4096]{2,1,0:T(8,128)(2,1)S(1)} %ff_sum2.1.refs_0_), channel_id=1, source_target_pairs={{0,16},{1,17},{2,18},{3,19},{4,20},{5,21},{6,22},{7,23},{8,24},{9,... | collective-permute-start | bytes 1572872 | tf_op jit(solution)/shard_map/ppermute | solution.py:525
  145.9 0.6 collective-permute-start.19
  146.5 22.1 %outputs.1 = (bf16[2048,512]{1,0:T(8,128)(2,1)}, bf16[2048,512]{1,0:T(8,128)(2,1)}, f32[32,1,128]{2,1,0:T(1,128)S(1)}, f32[32,1,128]{2,1,0:T(1,128)S(1)}) custom-call(s32[3]{0:T(128)S(1)} %pad_add_fusion.1.meta, bf16[2048,512]{1,0:T(8,128)(2,1)} %tok_ref.3, bf16[2048,512]{1,0:T(8,128)(2,1)} %grad_ref.11, bf16[2048,2048]{1,0:T(8,128)(2,1)} %get-tuple-element.130.act_ref, ...), custom_call_target="tpu_custom_call" | custom-call | flops 12884901888 | bytes 41943040 | tf_op jit(solution)/shard_map/outputs/pallas_call | solution.py:461
  168.8 1.2 collective-permute-done.13.refs_1_
  169.9 0.6 collective-permute-start.14
  170.5 3.2 %collective-permute-done.14.refs_1_ = f32[32,1,128]{2,1,0:T(1,128)S(1)} collective-permute-done((f32[32,1,128]{2,1,0:T(1,128)S(1)}, f32[32,1,128]{2,1,0:T(1,128)S(1)}, u32[]{:S(2)}, u32[]{:S(2)}) %collective-permute-start.14) | collective-permute-done | bytes 16416 | tf_op jit(solution)/shard_map/ppermute | solution.py:525
  173.8 1.5 collective-permute-start.15
  175.4 1.7 collective-permute-start.20
  177.1 0.5 collective-permute-done.15.refs_1_
  177.6 1.6 collective-permute-start.16
  179.2 3.5 %collective-permute-done.16.refs_1_ = f32[32,1,128]{2,1,0:T(1,128)S(1)} collective-permute-done((f32[32,1,128]{2,1,0:T(1,128)S(1)}, f32[32,1,128]{2,1,0:T(1,128)S(1)}, u32[]{:S(2)}, u32[]{:S(2)}) %collective-permute-start.16) | collective-permute-done | bytes 16416 | tf_op jit(solution)/shard_map/ppermute | solution.py:525
  182.8 0.4 collective-permute-start.17
  183.2 4.3 %collective-permute-done.17.refs_1_ = f32[32,1,128]{2,1,0:T(1,128)S(1)} collective-permute-done((f32[32,1,128]{2,1,0:T(1,128)S(1)}, f32[32,1,128]{2,1,0:T(1,128)S(1)}, u32[]{:S(2)}, u32[]{:S(2)}) %collective-permute-start.17) | collective-permute-done | bytes 16416 | tf_op jit(solution)/shard_map/ppermute | solution.py:525
  187.6 0.1 ff_sum3.1.refs_0_
  187.7 0.5 collective-permute-start.29
  188.3 0.6 add_multiply_fusion.1
  188.9 0.2 collective-permute-start.21
  189.2 1.8 collective-permute-start.28
  191.0 1.5 collective-permute-start.27
  192.5 0.6 add_multiply_fusion.2
  193.1 7.1 %collective-permute-done.21.refs_1_ = bf16[1,64,2048]{2,1,0:T(8,128)(2,1)S(1)} collective-permute-done((bf16[1,64,2048]{2,1,0:T(8,128)(2,1)S(1)}, bf16[1,64,2048]{2,1,0:T(8,128)(2,1)S(1)}, u32[]{:S(2)}, u32[]{:S(2)}) %collective-permute-start.21) | collective-permute-done | bytes 262176 | tf_op jit(solution)/shard_map/ppermute | solution.py:525
  200.3 2.5 %collective-permute-start.24 = (bf16[1,64,2048]{2,1,0:T(8,128)(2,1)S(1)}, bf16[1,64,2048]{2,1,0:T(8,128)(2,1)}, u32[]{:S(2)}, u32[]{:S(2)}) collective-permute-start(bf16[1,64,2048]{2,1,0:T(8,128)(2,1)S(1)} %att_sum2.3.refs_0_), channel_id=1, source_target_pairs={{0,6},{1,7},{2,4},{3,5},{4,2},{5,3},{6,0},{7,1},{8,14},{9,15},{10,... | collective-permute-start | bytes 786440 | tf_op jit(solution)/shard_map/ppermute | solution.py:525
  202.8 0.5 collective-permute-start.23
  203.3 0.2 collective-permute-done.29.refs_3_
  203.5 0.5 collective-permute-start.22
  204.1 0.6 add_multiply_fusion
  204.7 9.2 %collective-permute-done.28.refs_2_ = bf16[1,64,4096]{2,1,0:T(8,128)(2,1)} collective-permute-done((bf16[1,64,4096]{2,1,0:T(8,128)(2,1)S(1)}, bf16[1,64,4096]{2,1,0:T(8,128)(2,1)}, u32[]{:S(2)}, u32[]{:S(2)}) %collective-permute-start.28) | collective-permute-done | bytes 524320 | tf_op jit(solution)/shard_map/ppermute | solution.py:525
  213.9 1.6 copy-done.1
  215.5 1.6 copy-done.2
  217.1 1.6 copy-done.3
  218.7 1.2 copy-done.8
  219.9 1.2 copy-done.10
  221.2 9.7 %adam_ff.1 = (f32[2,512,512]{2,1,0:T(8,128)}, f32[2,512,512]{2,1,0:T(8,128)}, f32[2,512,512]{2,1,0:T(8,128)}, f32[2,512,512]{2,1,0:T(8,128)}, f32[256,2048]{1,0:...) custom-call(s32[3]{0:T(128)S(1)} %pad_add_fusion.1.meta, ...), custom_call_target="tpu_custom_call" | custom-call | flops 20971520 | bytes 29360128 | tf_op jit(solution)/shard_map/adam_ff/pallas_call | solution.py:610
  230.9 6.3 %adam_qkv.1 = (f32[256,1536]{1,0:T(8,128)}, f32[256,1536]{1,0:T(8,128)}, f32[256,1536]{1,0:T(8,128)}, f32[256,1536]{1,0:T(8,128)}, f32[2,128,512]{2,1,0:T(8,128)...) custom-call(s32[3]{0:T(128)S(1)} %pad_add_fusion.1.meta, ...), custom_call_target="tpu_custom_call" | custom-call | flops 10485760 | bytes 14680064 | tf_op jit(solution)/shard_map/adam_qkv/pallas_call | solution.py:610
  (102 shorter events, 1.3 us)
Async XLA Ops:
  0.7 10.1 %collective-permute-start = (bf16[256,2048]{1,0:T(8,128)(2,1)}, bf16[256,2048]{1,0:T(8,128)(2,1)S(1)}, u32[]{:S(2)}, u32[]{:S(2)}) collective-permute-start(bf16[256,2048]{1,0:T(8,128)(2,1)} %refs_9_.1), channel_id=1, source_target_pairs={{0,1},{1,0},{2,3},{3,2},{4,5},{5,4},{6,7},{7,6},{8,9},{9,8},{10,11... | collective-permute-start | bytes 3145736 | tf_op jit(solution)/shard_map/ppermute | solution.py:529
  1.2 9.6 %collective-permute-start.1 = (bf16[1024,512]{1,0:T(8,128)(2,1)}, bf16[1024,512]{1,0:T(8,128)(2,1)S(1)}, u32[]{:S(2)}, u32[]{:S(2)}) collective-permute-start(bf16[1024,512]{1,0:T(8,128)(2,1)} %refs_10_.1), channel_id=1, source_target_pairs={{0,1},{1,0},{2,3},{3,2},{4,5},{5,4},{6,7},{7,6},{8,9},{9,8},{10,11... | collective-permute-start | bytes 3145736 | tf_op jit(solution)/shard_map/ppermute | solution.py:529
  5.9 1.6 copy-start.4
  7.5 3.3 %copy-start.7 = (bf16[256,2048]{1,0:T(8,128)(2,1)S(1)}, bf16[256,2048]{1,0:T(8,128)(2,1)}, u32[]{:S(2)}) copy-start(bf16[256,2048]{1,0:T(8,128)(2,1)} %refs_9_.1) | copy-start | bytes 3145732
  7.5 3.3 %copy-start.9 = (bf16[1024,512]{1,0:T(8,128)(2,1)S(1)}, bf16[1024,512]{1,0:T(8,128)(2,1)}, u32[]{:S(2)}) copy-start(bf16[1024,512]{1,0:T(8,128)(2,1)} %refs_10_.1) | copy-start | bytes 3145732
  10.8 1.6 copy-start.17
  12.4 31.9 %copy-start.11 = (bf16[256,1536]{1,0:T(8,128)(2,1)S(1)}, bf16[256,1536]{1,0:T(8,128)(2,1)}, u32[]{:S(2)}) copy-start(bf16[256,1536]{1,0:T(8,128)(2,1)} %refs_6_.1) | copy-start | bytes 2359300
  12.4 32.0 %copy-start.15 = (bf16[256,512]{1,0:T(8,128)(2,1)S(1)}, bf16[256,512]{1,0:T(8,128)(2,1)}, u32[]{:S(2)}) copy-start(bf16[256,512]{1,0:T(8,128)(2,1)} %refs_8_.2) | copy-start | bytes 786436
  12.4 37.2 %copy-start.18 = (f32[2,8,512]{2,1,0:T(8,128)S(1)}, f32[2,8,512]{2,1,0:T(8,128)}, u32[]{:S(2)}) copy-start(f32[2,8,512]{2,1,0:T(8,128)} %constant.31.clone.trig_ref) | copy-start | bytes 98308
  43.9 23.3 %collective-permute-start.4 = (bf16[4,64,4096]{2,1,0:T(8,128)(2,1)S(1)}, bf16[4,64,4096]{2,1,0:T(8,128)(2,1)S(1)}, u32[]{:S(2)}, u32[]{:S(2)}) collective-permute-start(bf16[4,64,4096]{2,1,0:T(8,128)(2,1)S(1)} %get-tuple-element.104), channel_id=1, source_target_pairs={{0,1},{1,0},{2,3},{3,2},{4,5},{5,4},{6,7},{7,6},{8,9},{9,8},{10,11... | collective-permute-start | bytes 6291464 | tf_op jit(solution)/shard_map/ppermute | solution.py:529
  44.3 5.3 %collective-permute-start.2 = (bf16[256,1536]{1,0:T(8,128)(2,1)S(1)}, bf16[256,1536]{1,0:T(8,128)(2,1)S(1)}, u32[]{:S(2)}, u32[]{:S(2)}) collective-permute-start(bf16[256,1536]{1,0:T(8,128)(2,1)S(1)} %copy-done.11), channel_id=1, source_target_pairs={{0,1},{1,0},{2,3},{3,2},{4,5},{5,4},{6,7},{7,6},{8,9},{9,8},{10,11... | collective-permute-start | bytes 2359304 | tf_op jit(solution)/shard_map/ppermute | solution.py:529
  44.4 5.2 %collective-permute-start.3 = (bf16[256,512]{1,0:T(8,128)(2,1)S(1)}, bf16[256,512]{1,0:T(8,128)(2,1)S(1)}, u32[]{:S(2)}, u32[]{:S(2)}) collective-permute-start(bf16[256,512]{1,0:T(8,128)(2,1)S(1)} %copy-done.15), channel_id=1, source_target_pairs={{0,1},{1,0},{2,3},{3,2},{4,5},{5,4},{6,7},{7,6},{8,9},{9,8},{10,11... | collective-permute-start | bytes 786440 | tf_op jit(solution)/shard_map/ppermute | solution.py:529
  67.2 1.1 copy-start.19
  68.4 20.6 %collective-permute-start.5 = (bf16[2,64,4096]{2,1,0:T(8,128)(2,1)S(1)}, bf16[2,64,4096]{2,1,0:T(8,128)(2,1)S(1)}, u32[]{:S(2)}, u32[]{:S(2)}) collective-permute-start(bf16[2,64,4096]{2,1,0:T(8,128)(2,1)S(1)} %get-tuple-element.111), channel_id=1, source_target_pairs={{0,2},{1,5},{2,0},{3,7},{4,6},{5,1},{6,4},{7,3},{8,10},{9,13},{10,... | collective-permute-start | bytes 3145736 | tf_op jit(solution)/shard_map/ppermute | solution.py:525
  89.2 21.3 %collective-permute-start.6 = (bf16[1,64,4096]{2,1,0:T(8,128)(2,1)S(1)}, bf16[1,64,4096]{2,1,0:T(8,128)(2,1)S(1)}, u32[]{:S(2)}, u32[]{:S(2)}) collective-permute-start(bf16[1,64,4096]{2,1,0:T(8,128)(2,1)S(1)} %get-tuple-element.116), channel_id=1, source_target_pairs={{0,4},{1,3},{2,6},{3,1},{4,0},{5,7},{6,2},{7,5},{8,12},{9,11},{10,... | collective-permute-start | bytes 1572872 | tf_op jit(solution)/shard_map/ppermute | solution.py:525
  90.8 37.8 %collective-permute-start.11 = (bf16[4,64,256]{2,1,0:T(8,128)(2,1)S(1)}, bf16[4,64,256]{2,1,0:T(8,128)(2,1)S(1)}, u32[]{:S(2)}, u32[]{:S(2)}) collective-permute-start(bf16[4,64,256]{2,1,0:T(8,128)(2,1)S(1)} %get-tuple-element.126), channel_id=1, source_target_pairs={{0,1},{1,0},{2,3},{3,2},{4,5},{5,4},{6,7},{7,6},{8,9},{9,8},{10,11... | collective-permute-start | bytes 393224 | tf_op jit(solution)/shard_map/ppermute | solution.py:529
  90.8 38.3 %collective-permute-start.7 = (bf16[4,64,384]{2,1,0:T(8,128)(2,1)S(1)}, bf16[4,64,384]{2,1,0:T(8,128)(2,1)S(1)}, u32[]{:S(2)}, u32[]{:S(2)}) collective-permute-start(bf16[4,64,384]{2,1,0:T(8,128)(2,1)S(1)} %get-tuple-element.122), channel_id=1, source_target_pairs={{0,1},{1,0},{2,3},{3,2},{4,5},{5,4},{6,7},{7,6},{8,9},{9,8},{10,11... | collective-permute-start | bytes 589832 | tf_op jit(solution)/shard_map/ppermute | solution.py:529
  91.3 39.4 %collective-permute-start.8 = (bf16[4,64,384]{2,1,0:T(8,128)(2,1)S(1)}, bf16[4,64,384]{2,1,0:T(8,128)(2,1)S(1)}, u32[]{:S(2)}, u32[]{:S(2)}) collective-permute-start(bf16[4,64,384]{2,1,0:T(8,128)(2,1)S(1)} %get-tuple-element.123), channel_id=1, source_target_pairs={{0,1},{1,0},{2,3},{3,2},{4,5},{5,4},{6,7},{7,6},{8,9},{9,8},{10,11... | collective-permute-start | bytes 589832 | tf_op jit(solution)/shard_map/ppermute | solution.py:529
  108.9 1.1 copy-start.20
  110.0 20.7 %collective-permute-start.9 = (bf16[4,64,384]{2,1,0:T(8,128)(2,1)S(1)}, bf16[4,64,384]{2,1,0:T(8,128)(2,1)S(1)}, u32[]{:S(2)}, u32[]{:S(2)}) collective-permute-start(bf16[4,64,384]{2,1,0:T(8,128)(2,1)S(1)} %get-tuple-element.124), channel_id=1, source_target_pairs={{0,1},{1,0},{2,3},{3,2},{4,5},{5,4},{6,7},{7,6},{8,9},{9,8},{10,11... | collective-permute-start | bytes 589832 | tf_op jit(solution)/shard_map/ppermute | solution.py:529
  128.5 17.4 %copy-start.21 = (bf16[2048,384]{1,0:T(8,128)(2,1)}, bf16[2048,384]{1,0:T(8,128)(2,1)S(1)}, u32[]{:S(2)}) copy-start(bf16[2048,384]{1,0:T(8,128)(2,1)S(1)} %get-tuple-element.138.refs_6_) | copy-start | bytes 4718596
  128.5 2.2 collective-permute-start.10
  128.6 2.1 collective-permute-start.12
  129.1 13.9 %collective-permute-start.25 = (bf16[1,64,4096]{2,1,0:T(8,128)(2,1)S(1)}, bf16[1,64,4096]{2,1,0:T(8,128)(2,1)S(1)}, u32[]{:S(2)}, u32[]{:S(2)}) collective-permute-start(bf16[1,64,4096]{2,1,0:T(8,128)(2,1)S(1)} %ff_sum1.1.refs_0_), channel_id=1, source_target_pairs={{0,8},{1,9},{2,10},{3,11},{4,12},{5,13},{6,14},{7,15},{8,0},{9,1},... | collective-permute-start | bytes 1572872 | tf_op jit(solution)/shard_map/ppermute | solution.py:525
  131.0 14.8 %collective-permute-start.18 = (bf16[2,64,2048]{2,1,0:T(8,128)(2,1)S(1)}, bf16[2,64,2048]{2,1,0:T(8,128)(2,1)S(1)}, u32[]{:S(2)}, u32[]{:S(2)}) collective-permute-start(bf16[2,64,2048]{2,1,0:T(8,128)(2,1)S(1)} %get-tuple-element.146), channel_id=1, source_target_pairs={{0,2},{1,5},{2,0},{3,7},{4,6},{5,1},{6,4},{7,3},{8,10},{9,13},{10,... | collective-permute-start | bytes 1572872 | tf_op jit(solution)/shard_map/ppermute | solution.py:525
  143.1 44.4 %collective-permute-start.26 = (bf16[1,64,4096]{2,1,0:T(8,128)(2,1)S(1)}, bf16[1,64,4096]{2,1,0:T(8,128)(2,1)S(1)}, u32[]{:S(2)}, u32[]{:S(2)}) collective-permute-start(bf16[1,64,4096]{2,1,0:T(8,128)(2,1)S(1)} %ff_sum2.1.refs_0_), channel_id=1, source_target_pairs={{0,16},{1,17},{2,18},{3,19},{4,20},{5,21},{6,22},{7,23},{8,24},{9,... | collective-permute-start | bytes 1572872 | tf_op jit(solution)/shard_map/ppermute | solution.py:525
  145.9 29.4 %collective-permute-start.19 = (bf16[1,64,2048]{2,1,0:T(8,128)(2,1)S(1)}, bf16[1,64,2048]{2,1,0:T(8,128)(2,1)S(1)}, u32[]{:S(2)}, u32[]{:S(2)}) collective-permute-start(bf16[1,64,2048]{2,1,0:T(8,128)(2,1)S(1)} %get-tuple-element.148), channel_id=1, source_target_pairs={{0,4},{1,3},{2,6},{3,1},{4,0},{5,7},{6,2},{7,5},{8,12},{9,11},{10,... | collective-permute-start | bytes 786440 | tf_op jit(solution)/shard_map/ppermute | solution.py:525
  168.6 19.6 %copy-start.28 = (bf16[1024]{0:T(1024)(128)(2,1)S(1)}, bf16[1024]{0:T(1024)(128)(2,1)}, u32[]{:S(2)}) copy-start(bf16[1024]{0:T(1024)(128)(2,1)} %param.31) | copy-start | bytes 6148
  168.6 19.6 %copy-start.30 = (f32[1024]{0:T(1024)S(1)}, f32[1024]{0:T(1024)}, u32[]{:S(2)}) copy-start(f32[1024]{0:T(1024)} %param.38) | copy-start | bytes 12292
  168.6 19.6 %copy-start.31 = (f32[1024]{0:T(1024)S(1)}, f32[1024]{0:T(1024)}, u32[]{:S(2)}) copy-start(f32[1024]{0:T(1024)} %param.45) | copy-start | bytes 12292
  168.6 23.8 %copy-start.29 = (bf16[768]{0:T(1024)(128)(2,1)S(1)}, bf16[768]{0:T(1024)(128)(2,1)}, u32[]{:S(2)}) copy-start(bf16[768]{0:T(1024)(128)(2,1)} %param.28) | copy-start | bytes 4612
  168.7 23.8 %copy-start.32 = (f32[768]{0:T(1024)S(1)}, f32[768]{0:T(1024)}, u32[]{:S(2)}) copy-start(f32[768]{0:T(1024)} %param.35) | copy-start | bytes 9220
  168.7 23.8 %copy-start.33 = (f32[768]{0:T(1024)S(1)}, f32[768]{0:T(1024)}, u32[]{:S(2)}) copy-start(f32[768]{0:T(1024)} %param.42) | copy-start | bytes 9220
  168.7 1.2 collective-permute-start.13
  169.9 3.8 %collective-permute-start.14 = (f32[32,1,128]{2,1,0:T(1,128)S(1)}, f32[32,1,128]{2,1,0:T(1,128)S(1)}, u32[]{:S(2)}, u32[]{:S(2)}) collective-permute-start(f32[32,1,128]{2,1,0:T(1,128)S(1)} %small_pair.1.refs_0_), channel_id=1, source_target_pairs={{0,2},{1,3},{2,0},{3,1},{4,6},{5,7},{6,4},{7,5},{8,10},{9,11},{10,... | collective-permute-start | bytes 49160 | tf_op jit(solution)/shard_map/ppermute | solution.py:525
  173.8 30.3 %copy-start.25 = (bf16[6,256]{1,0:T(8,128)(2,1)S(1)}, bf16[6,256]{1,0:T(8,128)(2,1)}, u32[]{:S(2)}) copy-start(bf16[6,256]{1,0:T(8,128)(2,1)} %param.26) | copy-start | bytes 9220
  173.8 30.3 %copy-start.26 = (f32[6,256]{1,0:T(8,128)S(1)}, f32[6,256]{1,0:T(8,128)}, u32[]{:S(2)}) copy-start(f32[6,256]{1,0:T(8,128)} %param.33) | copy-start | bytes 18436
  173.8 30.3 %copy-start.27 = (f32[6,256]{1,0:T(8,128)S(1)}, f32[6,256]{1,0:T(8,128)}, u32[]{:S(2)}) copy-start(f32[6,256]{1,0:T(8,128)} %param.40) | copy-start | bytes 18436
  173.8 3.8 %collective-permute-start.15 = (f32[32,1,128]{2,1,0:T(1,128)S(1)}, f32[32,1,128]{2,1,0:T(1,128)S(1)}, u32[]{:S(2)}, u32[]{:S(2)}) collective-permute-start(f32[32,1,128]{2,1,0:T(1,128)S(1)} %small_sum.4.refs_0_), channel_id=1, source_target_pairs={{0,4},{1,5},{2,6},{3,7},{4,0},{5,1},{6,2},{7,3},{8,12},{9,13},{10,... | collective-permute-start | bytes 49160 | tf_op jit(solution)/shard_map/ppermute | solution.py:525
  175.4 38.5 %copy-start = (f32[1024,512]{1,0:T(8,128)S(1)}, f32[1024,512]{1,0:T(8,128)}, u32[]{:S(2)}) copy-start(f32[1024,512]{1,0:T(8,128)} %param.39) | copy-start | bytes 6291460
  175.4 13.4 %collective-permute-start.20 = (bf16[1,64,2048]{2,1,0:T(8,128)(2,1)S(1)}, bf16[1,64,2048]{2,1,0:T(8,128)(2,1)S(1)}, u32[]{:S(2)}, u32[]{:S(2)}) collective-permute-start(bf16[1,64,2048]{2,1,0:T(8,128)(2,1)S(1)} %att_sum1.1.refs_0_), channel_id=1, source_target_pairs={{0,8},{1,9},{2,10},{3,11},{4,12},{5,13},{6,14},{7,15},{8,0},{9,1},... | collective-permute-start | bytes 786440 | tf_op jit(solution)/shard_map/ppermute | solution.py:525
  177.6 5.2 %collective-permute-start.16 = (f32[32,1,128]{2,1,0:T(1,128)S(1)}, f32[32,1,128]{2,1,0:T(1,128)S(1)}, u32[]{:S(2)}, u32[]{:S(2)}) collective-permute-start(f32[32,1,128]{2,1,0:T(1,128)S(1)} %small_sum.5.refs_0_), channel_id=1, source_target_pairs={{0,8},{1,9},{2,10},{3,11},{4,12},{5,13},{6,14},{7,15},{8,0},{9,1},... | collective-permute-start | bytes 49160 | tf_op jit(solution)/shard_map/ppermute | solution.py:525
  182.8 4.7 %collective-permute-start.17 = (f32[32,1,128]{2,1,0:T(1,128)S(1)}, f32[32,1,128]{2,1,0:T(1,128)S(1)}, u32[]{:S(2)}, u32[]{:S(2)}) collective-permute-start(f32[32,1,128]{2,1,0:T(1,128)S(1)} %small_sum.6.refs_0_), channel_id=1, source_target_pairs={{0,16},{1,17},{2,18},{3,19},{4,20},{5,21},{6,22},{7,23},{8,24},{9,... | collective-permute-start | bytes 49160 | tf_op jit(solution)/shard_map/ppermute | solution.py:525
  187.6 43.3 %copy-start.24 = (f32[8,1,128]{2,1,0:T(1,128)}, f32[8,1,128]{2,1,0:T(1,128)S(1)}, u32[]{:S(2)}) copy-start(f32[8,1,128]{2,1,0:T(1,128)S(1)} %slice.17) | copy-start | bytes 12292
  187.7 15.8 %collective-permute-start.29 = (bf16[1,64,4096]{2,1,0:T(8,128)(2,1)S(1)}, bf16[1,64,4096]{2,1,0:T(8,128)(2,1)S(1)}, u32[]{:S(2)}, u32[]{:S(2)}) collective-permute-start(bf16[1,64,4096]{2,1,0:T(8,128)(2,1)S(1)} %ff_sum3.1.refs_0_), channel_id=1, source_target_pairs={{0,6},{1,7},{2,4},{3,5},{4,2},{5,3},{6,0},{7,1},{8,14},{9,15},{10,... | collective-permute-start | bytes 1572872 | tf_op jit(solution)/shard_map/ppermute | solution.py:525
  188.9 11.2 %collective-permute-start.21 = (bf16[1,64,2048]{2,1,0:T(8,128)(2,1)S(1)}, bf16[1,64,2048]{2,1,0:T(8,128)(2,1)S(1)}, u32[]{:S(2)}, u32[]{:S(2)}) collective-permute-start(bf16[1,64,2048]{2,1,0:T(8,128)(2,1)S(1)} %att_sum2.2.refs_0_), channel_id=1, source_target_pairs={{0,16},{1,17},{2,18},{3,19},{4,20},{5,21},{6,22},{7,23},{8,24},{9,... | collective-permute-start | bytes 786440 | tf_op jit(solution)/shard_map/ppermute | solution.py:525
  189.2 41.6 %copy-start.23 = (f32[6,128]{1,0:T(8,128)}, f32[6,128]{1,0:T(8,128)S(1)}, u32[]{:S(2)}) copy-start(f32[6,128]{1,0:T(8,128)S(1)} %slice_reduce_fusion.1) | copy-start | bytes 9220
  189.2 24.7 %collective-permute-start.28 = (bf16[1,64,4096]{2,1,0:T(8,128)(2,1)S(1)}, bf16[1,64,4096]{2,1,0:T(8,128)(2,1)}, u32[]{:S(2)}, u32[]{:S(2)}) collective-permute-start(bf16[1,64,4096]{2,1,0:T(8,128)(2,1)S(1)} %ff_sum3.1.refs_0_), channel_id=1, source_target_pairs={{0,2},{1,5},{2,0},{3,7},{4,6},{5,1},{6,4},{7,3},{8,10},{9,13},{10,... | collective-permute-start | bytes 1572872 | tf_op jit(solution)/shard_map/ppermute | solution.py:525
  191.0 22.9 %collective-permute-start.27 = (bf16[1,64,4096]{2,1,0:T(8,128)(2,1)S(1)}, bf16[1,64,4096]{2,1,0:T(8,128)(2,1)}, u32[]{:S(2)}, u32[]{:S(2)}) collective-permute-start(bf16[1,64,4096]{2,1,0:T(8,128)(2,1)S(1)} %ff_sum3.1.refs_0_), channel_id=1, source_target_pairs={{0,4},{1,3},{2,6},{3,1},{4,0},{5,7},{6,2},{7,5},{8,12},{9,11},{10,... | collective-permute-start | bytes 1572872 | tf_op jit(solution)/shard_map/ppermute | solution.py:525
  200.3 30.6 %collective-permute-start.24 = (bf16[1,64,2048]{2,1,0:T(8,128)(2,1)S(1)}, bf16[1,64,2048]{2,1,0:T(8,128)(2,1)}, u32[]{:S(2)}, u32[]{:S(2)}) collective-permute-start(bf16[1,64,2048]{2,1,0:T(8,128)(2,1)S(1)} %att_sum2.3.refs_0_), channel_id=1, source_target_pairs={{0,6},{1,7},{2,4},{3,5},{4,2},{5,3},{6,0},{7,1},{8,14},{9,15},{10,... | collective-permute-start | bytes 786440 | tf_op jit(solution)/shard_map/ppermute | solution.py:525
  202.8 28.1 %collective-permute-start.23 = (bf16[1,64,2048]{2,1,0:T(8,128)(2,1)S(1)}, bf16[1,64,2048]{2,1,0:T(8,128)(2,1)}, u32[]{:S(2)}, u32[]{:S(2)}) collective-permute-start(bf16[1,64,2048]{2,1,0:T(8,128)(2,1)S(1)} %att_sum2.3.refs_0_), channel_id=1, source_target_pairs={{0,2},{1,5},{2,0},{3,7},{4,6},{5,1},{6,4},{7,3},{8,10},{9,13},{10,... | collective-permute-start | bytes 786440 | tf_op jit(solution)/shard_map/ppermute | solution.py:525
  203.5 27.4 %collective-permute-start.22 = (bf16[1,64,2048]{2,1,0:T(8,128)(2,1)S(1)}, bf16[1,64,2048]{2,1,0:T(8,128)(2,1)}, u32[]{:S(2)}, u32[]{:S(2)}) collective-permute-start(bf16[1,64,2048]{2,1,0:T(8,128)(2,1)S(1)} %att_sum2.3.refs_0_), channel_id=1, source_target_pairs={{0,4},{1,3},{2,6},{3,1},{4,0},{5,7},{6,2},{7,5},{8,12},{9,11},{10,... | collective-permute-start | bytes 786440 | tf_op jit(solution)/shard_map/ppermute | solution.py:525
  204.1 26.8 %copy-start.22 = (f32[6,256]{1,0:T(8,128)}, f32[6,256]{1,0:T(8,128)S(1)}, u32[]{:S(2)}) copy-start(f32[6,256]{1,0:T(8,128)S(1)} %reshape.137) | copy-start | bytes 18436
  213.9 1.6 copy-start.1
  215.5 1.6 copy-start.2
  217.1 1.6 copy-start.3
  218.7 1.2 copy-start.8
  219.9 1.2 copy-start.10
  221.1 9.8 %copy-start.5 = (f32[256,1536]{1,0:T(8,128)S(1)}, f32[256,1536]{1,0:T(8,128)}, u32[]{:S(2)}) copy-start(f32[256,1536]{1,0:T(8,128)} %refs_4_.1) | copy-start | bytes 4718596
  221.1 9.8 %copy-start.6 = (f32[256,1536]{1,0:T(8,128)S(1)}, f32[256,1536]{1,0:T(8,128)}, u32[]{:S(2)}) copy-start(f32[256,1536]{1,0:T(8,128)} %refs_5_.1) | copy-start | bytes 4718596
  221.1 9.8 %copy-start.12 = (bf16[256,1536]{1,0:T(8,128)(2,1)S(1)}, bf16[256,1536]{1,0:T(8,128)(2,1)}, u32[]{:S(2)}) copy-start(bf16[256,1536]{1,0:T(8,128)(2,1)} %refs_6_.1) | copy-start | bytes 2359300
  221.1 9.8 %copy-start.13 = (f32[256,512]{1,0:T(8,128)S(1)}, f32[256,512]{1,0:T(8,128)}, u32[]{:S(2)}) copy-start(f32[256,512]{1,0:T(8,128)} %param.36) | copy-start | bytes 1572868
  221.1 9.8 %copy-start.14 = (f32[256,512]{1,0:T(8,128)S(1)}, f32[256,512]{1,0:T(8,128)}, u32[]{:S(2)}) copy-start(f32[256,512]{1,0:T(8,128)} %param.43) | copy-start | bytes 1572868
  221.1 9.8 %copy-start.16 = (bf16[256,512]{1,0:T(8,128)(2,1)S(1)}, bf16[256,512]{1,0:T(8,128)(2,1)}, u32[]{:S(2)}) copy-start(bf16[256,512]{1,0:T(8,128)(2,1)} %refs_8_.2) | copy-start | bytes 786436

commit v3 on v2

--- a/solution.py
+++ b/solution.py
@@ -26,6 +26,7 @@
 
 bf16 = jnp.bfloat16
 f32 = jnp.float32
+PARTS = 2
 SMALL_ROWS = 26
 
 
@@ -88,11 +89,11 @@
 
 
 def ff_kernel(meta, second_ref, grad_ref, fco_ref, fcx_ref, pro_ref, prx_ref, small_ref,
-              own_ref, send_ref, act_ref, hg_ref, bias_ref, fc_ref):
+              send_ref, act_ref, hg_ref, bias_ref, fc_ref):
     j = pl.program_id(0)
     rel = pl.program_id(1)
     c = meta[0]
-    rank, far_rank = meta[1], meta[2]
+    far_rank = meta[2]
     o = rel ^ c
     rows, width = second_ref.shape
     half = width // 2
@@ -121,22 +122,35 @@
 
     total = lax.fori_loop(0, rows // tile, block, jnp.zeros((8, cols), f32))
     bias_ref[...] = jnp.sum(total, 0, keepdims=True)[None]
-
-    gp = dot_tn(act_ref[...], grad_ref[...])
-    pcols = pl.ds(pl.multiple_of(j * 1024, 1024), 1024)
-
-    def put_proj(ref, number):
-        for a in range(4):
-            piece = gp[a * 2 * quarter : (a + 1) * 2 * quarter]
-            ref[a ^ number, :, pcols] = jnp.concatenate([piece[:quarter], piece[quarter:]], 1).astype(bf16)
-
-    pl.when(rel == 0)(lambda: put_proj(own_ref, rank))
-    pl.when(rel == 1)(lambda: put_proj(send_ref, far_rank))
+    pl.when(rel == 1)(lambda: put_proj(send_ref, dot_tn(act_ref[...], grad_ref[...]), j, far_rank))
+    put_fc(send_ref, dot_tn(second_ref[:, far_lanes], hg_ref[...]), o, j, far_rank)
+
+
+def put_proj(ref, grad, j, rank):
+    quarter = ref.shape[1]
+    lanes = pl.ds(pl.multiple_of(j * 1024, 1024), 1024)
+    for a in range(4):
+        piece = grad[a * 2 * quarter : (a + 1) * 2 * quarter]
+        ref[a ^ rank, :, lanes] = jnp.concatenate([piece[:quarter], piece[quarter:]], 1).astype(bf16)
+
+
+def put_fc(ref, grad, o, j, rank):
+    quarter = ref.shape[1]
+    cols = grad.shape[1]
     lanes = pl.ds(pl.multiple_of(2048 + o * 1024 + j * cols, cols), cols)
-    for ref, side, number in ((own_ref, own_lanes, rank), (send_ref, far_lanes, far_rank)):
-        gf = dot_tn(second_ref[:, side], hg_ref[...])
-        for a in range(4):
-            ref[a ^ number, :, lanes] = gf[a * quarter : (a + 1) * quarter].astype(bf16)
+    for a in range(4):
+        ref[a ^ rank, :, lanes] = grad[a * quarter : (a + 1) * quarter].astype(bf16)
+
+
+def ff_own_kernel(meta, second_ref, grad_ref, act_ref, hg_ref, own_ref):
+    j = pl.program_id(0)
+    rel = pl.program_id(1)
+    c = meta[0]
+    rank = meta[1]
+    half = second_ref.shape[1] // 2
+    own_lanes = pl.ds(pl.multiple_of(c * half, half), half)
+    pl.when(rel == 0)(lambda: put_proj(own_ref, dot_tn(act_ref[...], grad_ref[...]), j, rank))
+    put_fc(own_ref, dot_tn(second_ref[:, own_lanes], hg_ref[...]), rel ^ c, j, rank)
 
 
 def ff_call(meta, second, grad, fc_own, fc_far, proj_own, proj_far, small):
@@ -162,7 +176,6 @@
         ],
         out_specs=[
             full_spec(buf),
-            full_spec(buf),
             act_spec,
             act_spec,
             pl.BlockSpec((1, 1, cols), lambda j, r, m: (2 * j + r, 0, 0)),
@@ -174,15 +187,40 @@
         grid_spec=grid_spec,
         out_shape=[
             jax.ShapeDtypeStruct(buf, bf16),
-            jax.ShapeDtypeStruct(buf, bf16),
             jax.ShapeDtypeStruct((rows, ff), bf16),
             jax.ShapeDtypeStruct((rows, ff), bf16),
             jax.ShapeDtypeStruct((4, 1, cols), f32),
         ],
-        cost_estimate=cost(8 * rows * width * ff, 4 * rows * width + 4 * rows * ff),
+        cost_estimate=cost(6 * rows * width * ff, 4 * rows * width + 4 * rows * ff),
         name="feed_forward",
         compiler_params=pltpu.CompilerParams(vmem_limit_bytes=40 << 20),
     )(meta, second, grad, fc_own, fc_far, proj_own, proj_far, small)
+
+
+def ff_own_call(meta, second, grad, act, hg):
+    rows, width = second.shape
+    ff = act.shape[1]
+    cols = ff // 4
+    buf = (4, width // 8, 2 * ff)
+    grid_spec = pltpu.PrefetchScalarGridSpec(
+        num_scalar_prefetch=1,
+        grid=(2, 2),
+        in_specs=[
+            full_spec((rows, width)),
+            full_spec((rows, width)),
+            pl.BlockSpec((rows, cols), lambda j, r, m: (0, 2 * j)),
+            pl.BlockSpec((rows, cols), lambda j, r, m: (0, 2 * j + r)),
+        ],
+        out_specs=full_spec(buf),
+    )
+    return pl.pallas_call(
+        ff_own_kernel,
+        grid_spec=grid_spec,
+        out_shape=jax.ShapeDtypeStruct(buf, bf16),
+        cost_estimate=cost(2 * rows * width * ff, 4 * rows * width + 3 * rows * ff),
+        name="feed_forward_own",
+        compiler_params=pltpu.CompilerParams(vmem_limit_bytes=30 << 20),
+    )(meta, second, grad, act, hg)
 
 
 def rotate_rows(x, cosine, sine):
@@ -194,9 +232,10 @@
 
 
 def attention_kernel(j, rel, meta, first_ref, grad_ref, wq_ref, wk_ref, wv_ref, xq_ref, xk_ref, xv_ref,
-                     ow_ref, small_ref, trig_ref,
-                     own_ref, send_ref, og_ref, qg_ref, att_ref, bias_ref,
-                     wt_ref, bcol_ref, qgs_ref, attt_ref, btot_ref):
+                     ow_ref, small_ref, trig_ref, *refs):
+    if rel == 0:
+        own_first_ref, send_first_ref, refs = refs[0], refs[1], refs[2:]
+    own_ref, send_ref, qg_ref, att_ref, bias_ref, wt_ref, bcol_ref, qgs_ref, attt_ref, btot_ref = refs
     s = pl.program_id(0)
     c = meta[0]
     rank, far_rank = meta[1], meta[2]
@@ -280,15 +319,24 @@
     @pl.when(s == pl.num_programs(0) - 1)
     def _():
         bias_ref[...] = jnp.sum(btot_ref[...], 0, keepdims=True)
-        for ref, side, number in ((own_ref, own_lanes, rank), (send_ref, far_lanes, far_rank)):
+        at_own, at_send = (0, 384) if rel == 0 else (0, 0)
+        if rel == 0:
+            own_ref[:, :, 384:768] = own_first_ref[...]
+            send_ref[:, :, :384] = send_first_ref[:, :, :384]
+            send_ref[:, :, 768:] = send_first_ref[:, :, 384:]
+        for ref, side, number, at in ((own_ref, own_lanes, rank, at_own), (send_ref, far_lanes, far_rank, at_send)):
             gw = dot_tn(first_ref[:, side], qgs_ref[...])
             for a in range(4):
-                ref[a ^ number] = gw[a * quarter : (a + 1) * quarter].astype(bf16)
+                ref[a ^ number, :, at : at + 384] = gw[a * quarter : (a + 1) * quarter].astype(bf16)
         go = dot_nn(attt_ref[...], grad_ref[...])
         hq = quarter // 2
         for a in range(4):
             piece = go[a * hq : (a + 1) * hq]
-            og_ref[a ^ (far_rank if rel else rank)] = jnp.concatenate([piece[:, :256], piece[:, 256:]], 0).astype(bf16)
+            piece = jnp.concatenate([piece[:, :256], piece[:, 256:]], 0).astype(bf16)
+            if rel == 0:
+                own_ref[a ^ rank, :, 768:] = piece
+            else:
+                send_ref[a ^ far_rank, :, 384:] = piece
 
 
 def trig_tables():
@@ -297,11 +345,10 @@
     return np.stack([np.cos(angles), np.sin(angles)]).astype(np.float32)
 
 
-def attention_call(j, rel, meta, first, grad, qkv_own, qkv_far, out_w, small, trig):
+def attention_call(j, rel, meta, first, grad, qkv_own, qkv_far, out_w, small, trig, before=()):
     rows, width = first.shape
     half = width // 2
-    qbuf = (4, half // 4, 384)
-    obuf = (4, half // 4, 256)
+    bufs = [(4, half // 4, w) for w in ((1024, 1024) if rel == 0 else (384, 640))]
     w_specs = [
         pl.BlockSpec((half, 128), functools.partial(lambda p, s, m: (0, p * 4 + (rel ^ m[0]) * 2 + j), p))
         for p in range(3)
@@ -317,11 +364,10 @@
             pl.BlockSpec((128, width), lambda s, m: (j, 0)),
             full_spec(small.shape),
             full_spec(trig.shape),
+            *[full_spec(a.shape) for a in before],
         ],
         out_specs=[
-            full_spec(qbuf),
-            full_spec(qbuf),
-            full_spec(obuf),
+            *[full_spec(b) for b in bufs],
             pl.BlockSpec((LEN, 384), lambda s, m: (s, 0)),
             pl.BlockSpec((LEN, 128), lambda s, m: (s, 0)),
             full_spec((1, 384)),
@@ -339,9 +385,7 @@
         functools.partial(attention_kernel, j, rel),
         grid_spec=grid_spec,
         out_shape=[
-            jax.ShapeDtypeStruct(qbuf, bf16),
-            jax.ShapeDtypeStruct(qbuf, bf16),
-            jax.ShapeDtypeStruct(obuf, bf16),
+            *[jax.ShapeDtypeStruct(b, bf16) for b in bufs],
             jax.ShapeDtypeStruct((rows, 384), bf16),
             jax.ShapeDtypeStruct((rows, 128), bf16),
             jax.ShapeDtypeStruct((1, 384), f32),
@@ -349,14 +393,20 @@
         cost_estimate=cost(flops, 4 * rows * width + 2 * rows * 512),
         name=f"attention_{j}{rel}",
         compiler_params=pltpu.CompilerParams(vmem_limit_bytes=26 << 20),
-    )(meta, first, grad, *[qkv_own] * 3, *[qkv_far] * 3, out_w, small, trig)
-
-
-def output_kernel(meta, tok_ref, grad_ref, act_ref, hg_ref, *refs):
+    )(meta, first, grad, *[qkv_own] * 3, *[qkv_far] * 3, out_w, small, trig, *before)
+
+
+def output_kernel(part, parts, meta, tok_ref, grad_ref, act_ref, hg_ref, *refs):
     at_refs, qg_refs, refs = refs[0:4], refs[4:8], refs[8:]
     oo_ref, ox_ref, po_ref, px_ref, fo_ref, fx_ref, wo_ref, wx_ref, small_ref = refs[:9]
     qb_refs, fb_ref, refs = refs[9:13], refs[13], refs[14:]
-    lay_ref, tg_ref, own_ref, send_ref, wgo_ref, wgx_ref, sg_ref, fg_ref, tot_ref, qb_ref = refs
+    if part > 0:
+        before_ref, refs = refs[0], refs[3:]
+    lay_ref, tg_ref, refs = refs[0], refs[1], refs[2:]
+    if part < parts - 1:
+        tot_ref, wgo_ref, wgx_ref, sg_ref, fg_ref = refs
+    else:
+        own_ref, send_ref, wgo_ref, wgx_ref, sg_ref, fg_ref, tot_ref, qb_ref = refs
     i = pl.program_id(0)
     c = meta[0]
     tile, width = tok_ref.shape
@@ -373,7 +423,7 @@
                         src = pl.ds(pl.multiple_of((p * 4 + (rel ^ c) * 2 + j) * 128, 128), 128)
                         dst = (j * 6 + rel * 3 + p) * 128
                         g_ref[:, dst : dst + 128] = w_ref[:, src]
-        tot_ref[...] = jnp.zeros_like(tot_ref)
+        tot_ref[...] = jnp.zeros_like(tot_ref) if part == 0 else before_ref[...]
 
     x = tok_ref[...].astype(f32)
     grad = grad_ref[...].astype(f32)
@@ -406,6 +456,9 @@
     tg_ref[...] = (grad + ln).astype(bf16)
     for k, term in enumerate((first_g * normed, first_g, second_g * normed, second_g, grad)):
         tot_ref[k] += jnp.sum(term.reshape(tile // 8, 8, width), 0)
+
+    if part < parts - 1:
+        return
 
     @pl.when(i == pl.num_programs(0) - 1)
     def _():
@@ -431,46 +484,61 @@
                 ref[k] = jnp.zeros((1, 128), f32)
 
 
-def output_call(meta, tokens, grad, act, hg, atts, qgs, out_w, proj_w, fc_w, qkv_w, small, qbs, fb):
+def output_call(part, parts, meta, tokens, grad, act, hg, atts, qgs, out_w, proj_w, fc_w, qkv_w, small, qbs, fb,
+                before=None):
     rows, width = tokens.shape
     tile = 256
-    blk = lambda n: pl.BlockSpec((tile, n), lambda i, m: (i, 0))
+    tiles = rows // tile // parts
+    blk = lambda n: pl.BlockSpec((tile, n), lambda i, m: (part * tiles + i, 0))
     weights = [*out_w, *proj_w, *fc_w, *qkv_w]
     tail = [small, *qbs, fb]
+    sums = (5, 8, width)
     packed = (32, 1, 128)
+    last = part == parts - 1
+    extra, extra_specs, aliases = [], [], {}
+    count = 5 + len(atts) + len(qgs) + len(weights) + len(tail)
+    if before is not None:
+        extra = [before[2], before[0], before[1]]
+        extra_specs = [full_spec(sums), pl.BlockSpec(memory_space=pl.ANY), pl.BlockSpec(memory_space=pl.ANY)]
+        aliases = {count + 1: 0, count + 2: 1}
+    scratch = [
+        pltpu.VMEM(qkv_w[0].shape, bf16),
+        pltpu.VMEM(qkv_w[0].shape, bf16),
+        pltpu.VMEM((tile, width), f32),
+        pltpu.VMEM((tile, width), f32),
+    ]
+    if last:
+        scratch += [pltpu.VMEM(sums, f32), pltpu.VMEM((12, 1, 128), f32)]
+    given = [packed, packed] if last else [sums]
     grid_spec = pltpu.PrefetchScalarGridSpec(
         num_scalar_prefetch=1,
-        grid=(rows // tile,),
+        grid=(tiles,),
         in_specs=[
             blk(width),
             blk(width),
             *[blk(a.shape[1]) for a in (act, hg, *atts, *qgs)],
             *[full_spec(w.shape) for w in weights],
             *[full_spec(w.shape) for w in tail],
-        ],
-        out_specs=[blk(width), blk(width), full_spec(packed), full_spec(packed)],
-        scratch_shapes=[
-            pltpu.VMEM(qkv_w[0].shape, bf16),
-            pltpu.VMEM(qkv_w[0].shape, bf16),
-            pltpu.VMEM((tile, width), f32),
-            pltpu.VMEM((tile, width), f32),
-            pltpu.VMEM((5, 8, width), f32),
-            pltpu.VMEM((12, 1, 128), f32),
-        ],
+            *extra_specs,
+        ],
+        out_specs=[blk(width), blk(width), *[full_spec(g) for g in given]],
+        scratch_shapes=scratch,
     )
     return pl.pallas_call(
-        output_kernel,
+        functools.partial(output_kernel, part, parts),
         grid_spec=grid_spec,
         out_shape=[
             jax.ShapeDtypeStruct((rows, width), bf16),
             jax.ShapeDtypeStruct((rows, width), bf16),
-            jax.ShapeDtypeStruct(packed, f32),
-            jax.ShapeDtypeStruct(packed, f32),
-        ],
-        cost_estimate=cost(2 * rows * width * (512 + 2048 * 2 + 1536), 2 * rows * (4 * 512 + 4 * 2048)),
-        name="outputs",
+            *[jax.ShapeDtypeStruct(g, f32) for g in given],
+        ],
+        input_output_aliases=aliases,
+        cost_estimate=cost(
+            2 * rows * width * (512 + 2048 * 2 + 1536) // parts, 2 * rows * (4 * 512 + 4 * 2048) // parts
+        ),
+        name=f"outputs_{part}",
         compiler_params=pltpu.CompilerParams(vmem_limit_bytes=44 << 20),
-    )(meta, tokens, grad, act, hg, *atts, *qgs, *weights, *tail)
+    )(meta, tokens, grad, act, hg, *atts, *qgs, *weights, *tail, *extra)
 
 
 def sum_kernel(n_in, *refs):
@@ -496,28 +564,36 @@
     )(*terms)
 
 
-def pair_kernel(*refs):
-    own, got, outs = refs[:6], refs[6:12], refs[12:]
-    col = 0
-    for mine, other in zip(own, got):
-        w = mine.shape[2]
-        for k, out in enumerate(outs):
-            for i in range(2):
-                total = mine[2 * k + i].astype(f32) + other[2 * k + i].astype(f32)
-                out[i, :, col : col + w] = total.astype(bf16)
-        col += w
-
-
-def pair_call(own, got, name):
-    rows = own[0].shape[1]
-    width = sum(a.shape[2] for a in own)
+def along_kernel(n_in, meta, *refs):
+    ins, outs = refs[:n_in], refs[n_in:]
+    rows = outs[0].shape[1]
+    for k, out in enumerate(outs):
+        at = pl.ds(pl.multiple_of((meta[3] ^ k) * rows, rows), rows)
+        total = ins[0][0, at, :].astype(f32)
+        for term in ins[1:]:
+            total += term[0, at, :].astype(f32)
+        out[0] = total.astype(bf16)
+
+
+def join_kernel(meta, *refs):
+    ins, out = refs[:4], refs[4]
+    rows = ins[0].shape[1]
+    for k, piece in enumerate(ins):
+        out[0, pl.ds(pl.multiple_of((meta[3] ^ k) * rows, rows), rows), :] = piece[0]
+
+
+def along_call(kernel, meta, terms, outs, name):
+    moved = 2 * sum(a.size for a in terms)
+    whole = pl.BlockSpec(memory_space=pltpu.VMEM)
     return pl.pallas_call(
-        pair_kernel,
-        out_shape=[jax.ShapeDtypeStruct((2, rows, width), bf16)] * 2,
-        compiler_params=pltpu.CompilerParams(vmem_limit_bytes=12 << 20),
-        cost_estimate=cost(8 * rows * width, 24 * rows * width),
+        kernel,
+        in_specs=[pl.BlockSpec(memory_space=pltpu.SMEM), *[whole] * len(terms)],
+        out_specs=[whole] * len(outs),
+        out_shape=[jax.ShapeDtypeStruct(o, bf16) for o in outs],
+        compiler_params=pltpu.CompilerParams(vmem_limit_bytes=(moved * 3) // 2 + (4 << 20)),
+        cost_estimate=cost(moved, 2 * moved),
         name=name,
-    )(*own, *got)
+    )(meta, *terms)
 
 
 def exchange(a, reps, far, near):
@@ -537,8 +613,13 @@
     return [1 << b for b in range(2, reps.bit_length() - 1)]
 
 
-def spread(total, reps):
-    return [total, exchange(total, reps, 2, 1), exchange(total, reps, 1, 2), exchange(total, reps, 3, 3)]
+def crosses(pieces, reps):
+    steps = ((2, 1), (1, 2), (3, 3))
+    return [exchange(a, reps, *step) for a, step in zip(pieces, steps)]
+
+
+def along(pieces, reps):
+    return [exchange(a, reps, 4 * k, 4 * k) for k, a in enumerate(pieces, 1)]
 
 
 def adamw(grad, mean, square, weight):
@@ -580,21 +661,20 @@
 
 
 def adam_qkv_kernel(meta, *refs):
-    pieces, qkv, out, qkv_out, out_out = refs[:4], refs[4:7], refs[7:10], refs[10:14], refs[14:18]
+    sets, qkv, out, qkv_out, out_out = (refs[:4], refs[4:8]), refs[8:11], refs[11:14], refs[14:18], refs[18:22]
     c = meta[0]
     which = pl.program_id(0) ^ meta[1]
     quarter = qkv[0].shape[0]
     hq = quarter // 2
-    for j in range(2):
+    for j, pieces in enumerate(sets):
         for slot in range(2):
             for p in range(3):
-                col = 384 * (2 * j + slot) + 128 * p
+                col = 384 * slot + 128 * p
                 grad = pick(pieces, which, slice(col, col + 128))
                 lanes = pl.ds(pl.multiple_of((p * 4 + (slot ^ c) * 2 + j) * 128, 128), 128)
                 adam_block(grad, *qkv, *qkv_out, (slice(None), lanes))
         for k in range(2):
-            col = 1536 + 256 * j
-            grad = pick(pieces, which, slice(col, col + 256), slice(k * hq, (k + 1) * hq))
+            grad = pick(pieces, which, slice(768, 1024), slice(k * hq, (k + 1) * hq))
             adam_block(grad, *out, *out_out, (j, slice(None), slice(256 * k, 256 * k + 256)))
 
 
@@ -611,7 +691,7 @@
         kernel,
         grid_spec=grid_spec,
         out_shape=outs,
-        compiler_params=pltpu.CompilerParams(vmem_limit_bytes=32 << 20),
+        compiler_params=pltpu.CompilerParams(vmem_limit_bytes=56 << 20),
         cost_estimate=cost(20 * size, 28 * size),
         name=name,
     )(meta, *pieces, *first, *second)
@@ -647,7 +727,7 @@
     place = lax.axis_index("rep")
     low, high = place & 1, (place >> 1) & 1
     ranks = jnp.stack([2 * low + high, 2 * high + low])
-    meta = jnp.stack([c, ranks[c], ranks[1 - c]]).astype(jnp.int32)
+    meta = jnp.stack([c, ranks[c], ranks[1 - c], (place >> 2) & 3]).astype(jnp.int32)
     trig = jnp.asarray(trig_tables())
 
     packed = jnp.concatenate(
@@ -660,96 +740,124 @@
     out_far = swap(out_weight)
 
     first, second = norm_call(tokens, small)
-    own, send, act, hg, fb = ff_call(meta, second, out_grad, fc_weight, fc_far, proj_weight, proj_far, small)
-
-    ff_got = swap(send)
+    send, act, hg, fb = ff_call(meta, second, out_grad, fc_weight, fc_far, proj_weight, proj_far, small)
+    got = swap(send)
+    own = ff_own_call(tie(meta, send), second, out_grad, act, hg)
+
     att = {}
-    last = own
-    order = [(0, 1), (0, 0), (1, 1), (1, 0)]
-
-    def attend(k, *wait):
-        j, rel = order[k]
+    sets = {}
+    bits = rest_bits(reps)
+
+    def attend(j, rel, *wait):
         out_w = out_far if rel else out_weight
+        before = att[j, 1][:2] if rel == 0 else ()
         att[j, rel] = attention_call(
-            j, rel, tie(meta, *wait), first, out_grad, qkv_weight, qkv_far, out_w, small, trig
+            j, rel, tie(meta, *wait), first, out_grad, qkv_weight, qkv_far, out_w, small, trig, before
         )
-        return att[j, rel][5]
-
-    mark = attend(0, own)
-    keep, send = sum_call([tie(own, mark), ff_got], 2, "ff_pair")
+        return att[j, rel][4]
+
+    def rest(total, name):
+        for bit in bits[2:]:
+            (total,) = sum_call([total, exchange(total, reps, bit, bit)], 1, name)
+        return total
+
+    keep, send = sum_call([own, got], 2, "ff_pair")
     got = exchange(send, reps, 1, 2)
-    mark = attend(1, keep)
+    mark = attend(0, 1, keep)
     keep, send = sum_call([tie(keep, mark), got], 2, "ff_sum0")
     got = exchange(send, reps, 2, 1)
-    mark = attend(2, keep)
-    (ff_total,) = sum_call([tie(keep, mark), got], 1, "ff_sum1")
-    bits = rest_bits(reps)
-    got = exchange(ff_total, reps, bits[0], bits[0])
-    mark = attend(3, ff_total)
+    mark = attend(0, 0, keep)
+    rows = keep.shape[1]
+    part = (1, rows // 4, keep.shape[2])
+    pieces = along_call(functools.partial(along_kernel, 2), meta, [tie(keep, mark), got], [part] * 4, "ff_sum1")
+    got = along(pieces[1:], reps)
+    c_own, c_got = att[0, 0][0], swap(att[0, 0][1])
+    mark = attend(1, 1, *pieces)
+    (piece,) = sum_call([tie(pieces[0], mark), *got], 1, "ff_sum2")
+    piece = rest(piece, "ff_sum3")
+    pieces = [piece, *along([piece] * 3, reps)]
+    c_keep, c_send = sum_call([tie(c_own, mark), c_got], 2, "att_pair")
+    c_got = exchange(c_send, reps, 1, 2)
+    mark = attend(1, 0, piece, c_keep)
+
+    d_own, d_got = att[1, 0][0], swap(att[1, 0][1])
+    (ff_total,) = along_call(join_kernel, meta, [tie(pieces[0], mark), *pieces[1:]], [keep[:1].shape], "ff_join")
+    ff_pieces = [ff_total, exchange(ff_total, reps, 2, 1), exchange(ff_total, reps, 1, 2)]
+    c_keep, c_send = sum_call([tie(c_keep, mark), c_got], 2, "att_sum0")
+    c_got = exchange(c_send, reps, 2, 1)
 
     keys = [(0, 0), (0, 1), (1, 0), (1, 1)]
-    q_own = [att[k][0] for k in keys]
-    q_got = [swap(att[j, 1 - rel][1]) for j, rel in keys]
-    o_own = [att[j, 0][2] for j in range(2)]
-    o_got = [swap(att[j, 1][2]) for j in range(2)]
-    (ff_total,) = sum_call([tie(ff_total, mark), got], 1, "ff_sum2")
-    keep, send = pair_call([*q_own, *o_own], [*q_got, *o_got], "att_pair")
-    att_got = exchange(send, reps, 1, 2)
-    for bit in bits[1:]:
-        got = exchange(ff_total, reps, bit, bit)
-        (ff_total,) = sum_call([ff_total, got], 1, "ff_sum3")
-    ff_pieces = spread(ff_total, reps)
-
-    layer_out, tokens_grad, small_own, small_send = output_call(
-        tie(meta, keep),
+    give = lambda part, before, *wait: output_call(
+        part,
+        PARTS,
+        tie(meta, *wait),
         tokens,
         out_grad,
         act,
         hg,
-        [att[k][4] for k in keys],
         [att[k][3] for k in keys],
+        [att[k][2] for k in keys],
         (out_weight, out_far),
         (proj_weight, proj_far),
         (fc_weight, fc_far),
         (qkv_weight, qkv_far),
         small,
-        [att[k][5] for k in keys],
+        [att[k][4] for k in keys],
         fb,
-    )
-    keep, send = sum_call([keep, att_got], 2, "att_sum0")
-    got = exchange(send, reps, 2, 1)
-    (att_total,) = sum_call([keep, got], 1, "att_sum1")
-    for bit in bits:
-        got = exchange(att_total, reps, bit, bit)
-        (att_total,) = sum_call([att_total, got], 1, "att_sum2")
-    att_pieces = spread(att_total, reps)
-
-    (total,) = sum_call([small_own, swap(small_send)], 1, "small_pair")
+        before,
+    )
+    done = give(0, None, ff_total, c_keep)
+    mark = done[2]
+    d_keep, d_send = sum_call([tie(d_own, mark), d_got], 2, "att_pair")
+    d_got = exchange(d_send, reps, 1, 2)
+    (c_total,) = sum_call([tie(c_keep, mark), c_got], 1, "att_sum1")
+    c_got = along([c_total] * 3, reps)
+    ff_pieces.append(exchange(tie(ff_pieces[2], mark), reps, 2, 1))
+    layer_out, tokens_grad, small_own, small_send = give(1, done, d_keep, c_total, *ff_pieces[1:3])
+
+    (c_total,) = sum_call([tie(c_total, small_own), *c_got], 1, "att_sum2")
+    c_total = rest(c_total, "att_sum3")
+    d_keep, d_send = sum_call([tie(d_keep, c_total), d_got], 2, "att_sum0")
+    d_got = exchange(d_send, reps, 2, 1)
+    (total,) = sum_call([tie(small_own, d_keep), swap(small_send)], 1, "small_pair")
+    (d_total,) = sum_call([tie(d_keep, total), d_got], 1, "att_sum1")
+    d_got = along([d_total] * 3, reps)
+    ff_last = tie(ff_pieces[3], d_total)
+    c_pieces = [c_total, exchange(tie(c_total, ff_last), reps, 2, 1), exchange(tie(c_total, ff_last), reps, 1, 2)]
+
+    view = lambda a: a.reshape(2, 512, 512)
+    proj_adam = adam_call(
+        adam_ff_kernel,
+        tie(meta, total, d_total, ff_last),
+        [*ff_pieces[:3], ff_last],
+        [view(a) for a in (mean_proj_weight, square_proj_weight, proj_weight)],
+        [mean_fc_weight, square_fc_weight, fc_weight],
+        pl.BlockSpec((2, 128, 512), lambda q, m: (0, q, 0)),
+        pl.BlockSpec((64, 2048), lambda q, m: (q, 0)),
+        "adam_ff",
+    )
+    a_proj = [a.reshape(1024, 512) for a in proj_adam[:4]]
+    a_fc = proj_adam[4:]
+
+    (d_total,) = sum_call([tie(d_total, a_fc[0], *c_pieces[1:]), *d_got], 1, "att_sum4")
+    d_total = rest(d_total, "att_sum5")
+    d_pieces = [d_total, *crosses([d_total] * 3, reps)]
+    c_pieces.append(exchange(tie(c_pieces[2], d_total), reps, 2, 1))
+    total = tie(total, d_total)
     for bit in (1, 2, *bits):
+        if bit == bits[-1]:
+            total = tie(total, *c_pieces[1:], *d_pieces[1:])
         (total,) = sum_call([total, exchange(total, reps, bit, bit)], 1, "small_sum")
     flat = total.reshape(32, 128)
     g_vec = flat[:12].reshape(6, 256)
     g_qb = flat[12:18].reshape(768)
     g_fb = flat[18:26].reshape(1024)
 
-    view = lambda a: a.reshape(2, 512, 512)
-    proj_adam = adam_call(
-        adam_ff_kernel,
-        meta,
-        ff_pieces,
-        [view(a) for a in (mean_proj_weight, square_proj_weight, proj_weight)],
-        [mean_fc_weight, square_fc_weight, fc_weight],
-        pl.BlockSpec((2, 128, 512), lambda q, m: (0, q, 0)),
-        pl.BlockSpec((64, 2048), lambda q, m: (q, 0)),
-        "adam_ff",
-    )
-    a_proj = [a.reshape(1024, 512) for a in proj_adam[:4]]
-    a_fc = proj_adam[4:]
     view_o = lambda a: a.reshape(2, 128, 512)
     qkv_adam = adam_call(
         adam_qkv_kernel,
         meta,
-        att_pieces,
+        [*c_pieces, *d_pieces],
         [mean_qkv_weight, square_qkv_weight, qkv_weight],
         [view_o(a) for a in (mean_out_weight, square_out_weight, out_weight)],
         pl.BlockSpec((64, 1536), lambda q, m: (q, 0)),

time: 238 us -> 237 us (level)
  waiting for transfers between devices: 45.5 us -> 13.5 us
  starting transfers between devices: 26.5 us -> 43.3 us
  Pallas kernels: 144 us -> 157 us
    ppermute x18 -> x31, waiting for transfers between devices: 39.5 us -> 10.7 us  [exchange(): return lax.ppermute(a, ('rep', 'opt'), pairs)]
    ppermute x18 -> x31, starting transfers between devices: 23.2 us -> 42.1 us  [exchange(): return lax.ppermute(a, ('rep', 'opt'), pairs)]
    pallas_call x2 -> x5, Pallas kernels: 22.3 us -> 35.5 us  [the longest x2 27 us: output_call(): pl.pallas_call(functools.partial(output_kernel, part, parts), grid_spec=g...]
    pallas_call x2, Pallas kernels: 16 us -> 20.6 us  [adam_call(): pl.pallas_call(kernel, grid_spec=grid_spec, out_shape=outs, compiler_para...]
    pallas_call x1, Pallas kernels: 31.5 us -> 27.1 us  [ff_call(): pl.pallas_call(ff_kernel, grid_spec=grid_spec, out_shape=[jax.ShapeDtypeS...]
    ppermute x12 -> x8, waiting for transfers between devices: 5.97 us -> 2.73 us  [swap(): return lax.ppermute(a, 'opt', [(0, 1), (1, 0)])]
    unnamed x68 -> x78, local copies, waits for them, and re-layouts: 12.2 us -> 13.2 us
  transfers between devices with their start and end apart: 30 -> 39, of which waited for: 10 -> 6; matrix products, arithmetic and copies ran while one was open for 2% -> 1% of each run, Pallas kernels for 44% -> 55%
where the time goes in v3:
time: 237 us
  Pallas kernels  157 us (66%)
  starting transfers between devices  43.3 us (18%)
  local copies, waits for them, and re-layouts  14.6 us (6%)
  waiting for transfers between devices  13.5 us (6%)
  other arithmetic  4.02 us (2%)
  blocking collectives  2.64 us (1%)
    pallas_call x4, Pallas kernels, attention_call(): pl.pallas_call(functools.partial(attention_kernel, j, rel), grid_spec=gri...  70.7 us
    ppermute x31, starting transfers between devices, exchange(): return lax.ppermute(a, ('rep', 'opt'), pairs)  42.1 us
    pallas_call x1, Pallas kernels, ff_call(): pl.pallas_call(ff_kernel, grid_spec=grid_spec, out_shape=[jax.ShapeDtypeS...  27.1 us
    pallas_call x2, Pallas kernels, output_call(): pl.pallas_call(functools.partial(output_kernel, part, parts), grid_spec=g...  27 us
    pallas_call x2, Pallas kernels, adam_call(): pl.pallas_call(kernel, grid_spec=grid_spec, out_shape=outs, compiler_para...  20.6 us
    unnamed x78, local copies, waits for them, and re-layouts  13.2 us
    ppermute x31, waiting for transfers between devices, exchange(): return lax.ppermute(a, ('rep', 'opt'), pairs)  10.7 us
    pallas_call x1, Pallas kernels, ff_own_call(): pl.pallas_call(ff_own_kernel, grid_spec=grid_spec, out_shape=jax.ShapeDty...  7.17 us
  transfers between devices with their start and end apart: 39, of which 6 were waited for; matrix products, arithmetic and copies ran while one was open for 1% of the time, Pallas kernels for 55%

profile of v3, /device:TPU:0, one launch (start us, length us, event | category | flops | bytes accessed | tf_op | source)
XLA Modules:
  0.0 236.8 jit_solution(17301078205175272296)
XLA Ops:
  0.7 0.6 collective-permute-start
  1.3 0.7 reshape.132
  2.0 0.7 maximum_bitcast_fusion
  2.7 2.6 %all-gather = bf16[2,26,128]{2,1,0:T(8,128)(2,1)S(1)} all-gather(bf16[1,26,128]{2,1,0:T(8,128)(2,1)S(1)} %maximum_bitcast_fusion), channel_id=1, replica_groups=mesh['rep'=16,'opt'=2] {'opt'}, dimensions={0}, use_global_device_ids=true | all-gather | bytes 19968 | tf_op jit(solution)/shard_map/all_gather | solution.py:736
  5.5 0.6 fusion.6
  6.1 1.6 copy-done.3
  7.7 1.9 norm.1
  9.6 1.4 pad_add_fusion.1.meta
  11.0 1.2 copy-done.4
  12.2 1.2 copy-done.6
  13.4 27.1 %feed_forward.1 = (bf16[4,64,4096]{2,1,0:T(8,128)(2,1)S(1)}, bf16[2048,2048]{1,0:T(8,128)(2,1)}, bf16[2048,2048]{1,0:T(8,128)(2,1)}, f32[4,1,512]{2,1,0:T(1,128)S(1)}) custom-call(s32[4]{0:T(128)S(1)} %pad_add_fusion.1.meta, bf16[2048,512]{1,0:T(8,128)(2,1)S(1)} %get-tuple-element.122.second_ref, bf16[2048,512]{1,0:T(8,128)(2,1)S(1)} %copy-done.2, ...), custom_call_target="tpu_custom_call" | custom-call | flops 12884901888 | bytes 20971520 | tf_op jit(solution)/shard_map/feed_forward/pallas_call | solution.py:185
  40.5 0.5 collective-permute-start.2
  41.1 3.4 %copy-done = bf16[2048,2048]{1,0:T(8,128)(2,1)S(1)} copy-done((bf16[2048,2048]{1,0:T(8,128)(2,1)S(1)}, bf16[2048,2048]{1,0:T(8,128)(2,1)}, u32[]{:S(2)}) %copy-start) | copy-done | bytes 8388632
  44.4 3.4 %copy-done.1 = bf16[2048,2048]{1,0:T(8,128)(2,1)S(1)} copy-done((bf16[2048,2048]{1,0:T(8,128)(2,1)S(1)}, bf16[2048,2048]{1,0:T(8,128)(2,1)}, u32[]{:S(2)}) %copy-start.1) | copy-done | bytes 8388632
  47.8 7.2 %feed_forward_own.1.refs_0_ = bf16[4,64,4096]{2,1,0:T(8,128)(2,1)S(1)} custom-call(s32[4]{0:T(128)S(1)} %pad_add_fusion.1.meta, bf16[2048,512]{1,0:T(8,128)(2,1)S(1)} %get-tuple-element.122.second_ref, bf16[2048,512]{1,0:T(8,128)(2,1)S(1)} %copy-done.2, bf16[2048,2048]{1,0:T(8,128)(2,1)S(1)} %copy-done, bf16[2048,2048]{1,0:T(8,128)(2,1)S(1)} %copy-done.1), custom_call_target="tpu_custom_call" | custom-call | flops 4294967296 | bytes 16777216 | tf_op jit(solution)/shard_map/feed_forward_own/pallas_call | solution.py:216
  55.0 0.5 ff_pair.1
  55.5 2.9 %collective-permute-start.5 = (bf16[2,64,4096]{2,1,0:T(8,128)(2,1)S(1)}, bf16[2,64,4096]{2,1,0:T(8,128)(2,1)S(1)}, u32[]{:S(2)}, u32[]{:S(2)}) collective-permute-start(bf16[2,64,4096]{2,1,0:T(8,128)(2,1)S(1)} %get-tuple-element.132), channel_id=1, source_target_pairs={{0,2},{1,5},{2,0},{3,7},{4,6},{5,1},{6,4},{7,3},{8,10},{9,13},{10,... | collective-permute-start | bytes 3145736 | tf_op jit(solution)/shard_map/ppermute | solution.py:601
  58.4 1.5 collective-permute-done.4.ow_ref.refs_9_
  60.0 17.6 %attention_01.1 = (bf16[4,64,384]{2,1,0:T(8,128)(2,1)S(1)}, bf16[4,64,640]{2,1,0:T(8,128)(2,1)S(1)}, bf16[2048,384]{1,0:T(8,128)(2,1)S(1)}, bf16[2048,128]{1,0:T(8,128)(2,1)S(1)}, f32[1,384]{1,0:T(1,128)S(1)}) custom-call(s32[4]{0:T(128)S(1)} %pad_add_fusion.1.meta, bf16[2048,512]{1,0:T(8,128)(2,1)S(1)} %get-tuple-element.129.first_ref, ...), custom_call_target="tpu_custom_call" | custom-call | flops 5368709120 | bytes 6291456 | tf_op jit(solution)/shard_map/attention_01/pallas_call | solution.py:384
  77.6 1.1 copy-done.9
  78.9 1.6 collective-permute-start.6
  80.5 17.7 %attention_00.1 = (bf16[4,64,1024]{2,1,0:T(8,128)(2,1)S(1)}, bf16[4,64,1024]{2,1,0:T(8,128)(2,1)S(1)}, bf16[2048,384]{1,0:T(8,128)(2,1)S(1)}, bf16[2048,128]{1,0:T(8,128)(2,1)S(1)}, f32[1,384]{1,0:T(1,128)S(1)}) custom-call(s32[4]{0:T(128)S(1)} %pad_add_fusion.1.meta, bf16[2048,512]{1,0:T(8,128)(2,1)S(1)} %get-tuple-element.129.first_ref, ...), custom_call_target="tpu_custom_call" | custom-call | flops 5368709120 | bytes 6291456 | tf_op jit(solution)/shard_map/attention_00/pallas_call | solution.py:384
  98.3 0.7 ff_sum1.1
  99.0 1.7 collective-permute-start.7
  100.7 2.6 %collective-permute-start.8 = (bf16[1,16,4096]{2,1,0:T(8,128)(2,1)S(1)}, bf16[1,16,4096]{2,1,0:T(8,128)(2,1)S(1)}, u32[]{:S(2)}, u32[]{:S(2)}) collective-permute-start(bf16[1,16,4096]{2,1,0:T(8,128)(2,1)S(1)} %get-tuple-element.142), channel_id=1, source_target_pairs={{0,16},{1,17},{2,18},{3,19},{4,20},{5,21},{6,22},{7,23},{8,24},{9,... | collective-permute-start | bytes 393224 | tf_op jit(solution)/shard_map/ppermute | solution.py:601
  103.5 17.6 %attention_11.1 = (bf16[4,64,384]{2,1,0:T(8,128)(2,1)S(1)}, bf16[4,64,640]{2,1,0:T(8,128)(2,1)S(1)}, bf16[2048,384]{1,0:T(8,128)(2,1)S(1)}, bf16[2048,128]{1,0:T(8,128)(2,1)S(1)}, f32[1,384]{1,0:T(1,128)S(1)}) custom-call(s32[4]{0:T(128)S(1)} %pad_add_fusion.1.meta, bf16[2048,512]{1,0:T(8,128)(2,1)S(1)} %get-tuple-element.129.first_ref, ...), custom_call_target="tpu_custom_call" | custom-call | flops 5368709120 | bytes 6291456 | tf_op jit(solution)/shard_map/attention_11/pallas_call | solution.py:384
  121.2 0.6 collective-permute-start.14
  121.9 3.7 %collective-permute-start.13 = (bf16[1,16,4096]{2,1,0:T(8,128)(2,1)S(1)}, bf16[1,16,4096]{2,1,0:T(8,128)(2,1)S(1)}, u32[]{:S(2)}, u32[]{:S(2)}) collective-permute-start(bf16[1,16,4096]{2,1,0:T(8,128)(2,1)S(1)} %ff_sum2.1.refs_0_), channel_id=1, source_target_pairs={{0,24},{1,25},{2,26},{3,27},{4,28},{5,29},{6,30},{7,31},{8,16},{9,... | collective-permute-start | bytes 393224 | tf_op jit(solution)/shard_map/ppermute | solution.py:601
  125.6 0.8 collective-permute-start.11
  126.3 17.8 %attention_10.1 = (bf16[4,64,1024]{2,1,0:T(8,128)(2,1)S(1)}, bf16[4,64,1024]{2,1,0:T(8,128)(2,1)S(1)}, bf16[2048,384]{1,0:T(8,128)(2,1)S(1)}, bf16[2048,128]{1,0:T(8,128)(2,1)S(1)}, f32[1,384]{1,0:T(1,128)S(1)}) custom-call(s32[4]{0:T(128)S(1)} %pad_add_fusion.1.meta, bf16[2048,512]{1,0:T(8,128)(2,1)S(1)} %get-tuple-element.129.first_ref, ...), custom_call_target="tpu_custom_call" | custom-call | flops 5368709120 | bytes 6291456 | tf_op jit(solution)/shard_map/attention_10/pallas_call | solution.py:384
  144.2 1.1 copy-done.11
  145.3 0.6 ff_join.1.refs_0_
  145.9 1.5 collective-permute-start.18
  147.5 0.5 collective-permute-start.17
  148.1 1.5 collective-permute-start.16
  149.6 13.4 %outputs_0.1 = (bf16[2048,512]{1,0:T(8,128)(2,1)}, bf16[2048,512]{1,0:T(8,128)(2,1)}, f32[5,8,512]{2,1,0:T(8,128)S(1)}) custom-call(s32[4]{0:T(128)S(1)} %pad_add_fusion.1.meta, bf16[2048,512]{1,0:T(8,128)(2,1)} %tok_ref.5, bf16[2048,512]{1,0:T(8,128)(2,1)} %grad_ref.15, bf16[2048,2048]{1,0:T(8,128)(2,1)} %get-tuple-element.125.act_ref, ...), custom_call_target="tpu_custom_call" | custom-call | flops 6442450944 | bytes 20971520 | tf_op jit(solution)/shard_map/outputs_0/pallas_call | solution.py:527
  163.1 3.7 %collective-permute-start.21 = (bf16[1,64,1024]{2,1,0:T(8,128)(2,1)S(1)}, bf16[1,64,1024]{2,1,0:T(8,128)(2,1)S(1)}, u32[]{:S(2)}, u32[]{:S(2)}) collective-permute-start(bf16[1,64,1024]{2,1,0:T(8,128)(2,1)S(1)} %att_sum1.2.refs_0_), channel_id=1, source_target_pairs={{0,24},{1,25},{2,26},{3,27},{4,28},{5,29},{6,30},{7,31},{8,16},{9,... | collective-permute-start | bytes 393224 | tf_op jit(solution)/shard_map/ppermute | solution.py:601
  166.8 0.8 collective-permute-start.19
  167.7 0.6 collective-permute-start.22
  168.3 1.3 collective-permute-start.25
  169.7 13.6 %outputs_1.1 = (bf16[2048,512]{1,0:T(8,128)(2,1)}, bf16[2048,512]{1,0:T(8,128)(2,1)}, f32[32,1,128]{2,1,0:T(1,128)S(1)}, f32[32,1,128]{2,1,0:T(1,128)S(1)}) custom-call(s32[4]{0:T(128)S(1)} %pad_add_fusion.1.meta, bf16[2048,512]{1,0:T(8,128)(2,1)} %tok_ref.5, bf16[2048,512]{1,0:T(8,128)(2,1)} %grad_ref.15, ...), custom_call_target="tpu_custom_call", output_to_operand_aliasing={{0}: (28, {}), {1}: (29, {})} | custom-call | flops 6442450944 | bytes 20971520 | tf_op jit(solution)/shard_map/outputs_1/pallas_call | solution.py:527
  183.5 0.8 collective-permute-start.24
  184.3 1.2 collective-permute-done.23.refs_1_
  185.5 3.0 %collective-permute-done.24.refs_1_ = bf16[1,64,1024]{2,1,0:T(8,128)(2,1)S(1)} collective-permute-done((bf16[1,64,1024]{2,1,0:T(8,128)(2,1)S(1)}, bf16[1,64,1024]{2,1,0:T(8,128)(2,1)S(1)}, u32[]{:S(2)}, u32[]{:S(2)}) %collective-permute-start.24) | collective-permute-done | bytes 131104 | tf_op jit(solution)/shard_map/ppermute | solution.py:601
  188.6 0.8 collective-permute-start.27
  189.4 1.7 collective-permute-start.26
  191.0 3.8 %collective-permute-start.30 = (bf16[1,64,1024]{2,1,0:T(8,128)(2,1)S(1)}, bf16[1,64,1024]{2,1,0:T(8,128)(2,1)S(1)}, u32[]{:S(2)}, u32[]{:S(2)}) collective-permute-start(bf16[1,64,1024]{2,1,0:T(8,128)(2,1)S(1)} %att_sum1.3.refs_0_), channel_id=1, source_target_pairs={{0,24},{1,25},{2,26},{3,27},{4,28},{5,29},{6,30},{7,31},{8,16},{9,... | collective-permute-start | bytes 393224 | tf_op jit(solution)/shard_map/ppermute | solution.py:601
  194.8 0.6 collective-permute-start.28
  195.4 12.4 %adam_ff.1 = (f32[2,512,512]{2,1,0:T(8,128)}, f32[2,512,512]{2,1,0:T(8,128)}, f32[2,512,512]{2,1,0:T(8,128)}, f32[2,512,512]{2,1,0:T(8,128)}, f32[256,2048]{1,0:...) custom-call(s32[4]{0:T(128)} %copy-done.16, bf16[1,64,4096]{2,1,0:T(8,128)(2,1)} %copy-done.13, ...), custom_call_target="tpu_custom_call" | custom-call | flops 20971520 | bytes 29360128 | tf_op jit(solution)/shard_map/adam_ff/pallas_call | solution.py:690
  208.0 0.4 collective-permute-start.34
  208.5 1.5 collective-permute-start.37
  209.9 1.6 collective-permute-start.36
  211.6 0.4 collective-permute-start.35
  212.0 1.3 collective-permute-start.31
  213.3 2.8 %collective-permute-done.31.refs_1_ = f32[32,1,128]{2,1,0:T(1,128)S(1)} collective-permute-done((f32[32,1,128]{2,1,0:T(1,128)S(1)}, f32[32,1,128]{2,1,0:T(1,128)S(1)}, u32[]{:S(2)}, u32[]{:S(2)}) %collective-permute-start.31) | collective-permute-done | bytes 16416 | tf_op jit(solution)/shard_map/ppermute | solution.py:601
  216.1 1.3 collective-permute-start.32
  217.4 2.5 %collective-permute-done.32.refs_1_ = f32[32,1,128]{2,1,0:T(1,128)S(1)} collective-permute-done((f32[32,1,128]{2,1,0:T(1,128)S(1)}, f32[32,1,128]{2,1,0:T(1,128)S(1)}, u32[]{:S(2)}, u32[]{:S(2)}) %collective-permute-start.32) | collective-permute-done | bytes 16416 | tf_op jit(solution)/shard_map/ppermute | solution.py:601
  220.0 1.5 collective-permute-start.33
  221.5 2.3 collective-permute-done.33.refs_1_
  223.9 2.4 %collective-permute-start.38 = (f32[32,1,128]{2,1,0:T(1,128)S(1)}, f32[32,1,128]{2,1,0:T(1,128)S(1)}, u32[]{:S(2)}, u32[]{:S(2)}) collective-permute-start(f32[32,1,128]{2,1,0:T(1,128)S(1)} %small_sum.6.refs_0_), channel_id=1, source_target_pairs={{0,16},{1,17},{2,18},{3,19},{4,20},{5,21},{6,22},{7,23},{8,24},{9,... | collective-permute-start | bytes 49160 | tf_op jit(solution)/shard_map/ppermute | solution.py:601
  226.4 8.2 %adam_qkv.1 = (f32[256,1536]{1,0:T(8,128)}, f32[256,1536]{1,0:T(8,128)}, f32[256,1536]{1,0:T(8,128)}, f32[256,1536]{1,0:T(8,128)}, f32[2,128,512]{2,1,0:T(8,128)...) custom-call(s32[4]{0:T(128)} %copy-done.16, bf16[1,64,1024]{2,1,0:T(8,128)(2,1)} %copy-done.14, ...), custom_call_target="tpu_custom_call" | custom-call | flops 10485760 | bytes 14680064 | tf_op jit(solution)/shard_map/adam_qkv/pallas_call | solution.py:690
  234.8 0.6 add_multiply_fusion.1
  235.4 0.6 add_multiply_fusion.2
  236.0 0.6 add_multiply_fusion
  (135 shorter events, 1.9 us)
Async XLA Ops:
  0.7 10.3 %copy-start.2 = (bf16[2048,512]{1,0:T(8,128)(2,1)S(1)}, bf16[2048,512]{1,0:T(8,128)(2,1)}, u32[]{:S(2)}) copy-start(bf16[2048,512]{1,0:T(8,128)(2,1)} %grad_ref.15) | copy-start | bytes 6291460
  0.7 10.3 %collective-permute-start = (bf16[256,2048]{1,0:T(8,128)(2,1)}, bf16[256,2048]{1,0:T(8,128)(2,1)S(1)}, u32[]{:S(2)}, u32[]{:S(2)}) collective-permute-start(bf16[256,2048]{1,0:T(8,128)(2,1)} %refs_9_.2), channel_id=1, source_target_pairs={{0,1},{1,0},{2,3},{3,2},{4,5},{5,4},{6,7},{7,6},{8,9},{9,8},{10,11... | collective-permute-start | bytes 3145736 | tf_op jit(solution)/shard_map/ppermute | solution.py:605
  1.2 9.7 %collective-permute-start.1 = (bf16[1024,512]{1,0:T(8,128)(2,1)}, bf16[1024,512]{1,0:T(8,128)(2,1)}, u32[]{:S(2)}, u32[]{:S(2)}) collective-permute-start(bf16[1024,512]{1,0:T(8,128)(2,1)} %refs_10_.4), channel_id=1, source_target_pairs={{0,1},{1,0},{2,3},{3,2},{4,5},{5,4},{6,7},{7,6},{8,9},{9,8},{10,11... | collective-permute-start | bytes 3145736 | tf_op jit(solution)/shard_map/ppermute | solution.py:605
  10.9 158.7 %copy-start.16 = (s32[4]{0:T(128)}, s32[4]{0:T(128)S(1)}, u32[]{:S(2)}) copy-start(s32[4]{0:T(128)S(1)} %pad_add_fusion.1.meta) | copy-start | bytes 52
  13.4 27.6 %copy-start.8 = (bf16[256,1536]{1,0:T(8,128)(2,1)S(1)}, bf16[256,1536]{1,0:T(8,128)(2,1)}, u32[]{:S(2)}) copy-start(bf16[256,1536]{1,0:T(8,128)(2,1)} %refs_10_.5) | copy-start | bytes 2359300
  40.5 14.5 %collective-permute-start.2 = (bf16[4,64,4096]{2,1,0:T(8,128)(2,1)S(1)}, bf16[4,64,4096]{2,1,0:T(8,128)(2,1)S(1)}, u32[]{:S(2)}, u32[]{:S(2)}) collective-permute-start(bf16[4,64,4096]{2,1,0:T(8,128)(2,1)S(1)} %get-tuple-element.123), channel_id=1, source_target_pairs={{0,1},{1,0},{2,3},{3,2},{4,5},{5,4},{6,7},{7,6},{8,9},{9,8},{10,11... | collective-permute-start | bytes 6291464 | tf_op jit(solution)/shard_map/ppermute | solution.py:605
  41.0 19.0 %collective-permute-start.3 = (bf16[256,1536]{1,0:T(8,128)(2,1)S(1)}, bf16[256,1536]{1,0:T(8,128)(2,1)S(1)}, u32[]{:S(2)}, u32[]{:S(2)}) collective-permute-start(bf16[256,1536]{1,0:T(8,128)(2,1)S(1)} %copy-done.8), channel_id=1, source_target_pairs={{0,1},{1,0},{2,3},{3,2},{4,5},{5,4},{6,7},{7,6},{8,9},{9,8},{10,11... | collective-permute-start | bytes 2359304 | tf_op jit(solution)/shard_map/ppermute | solution.py:605
  55.0 3.4 %copy-start.12 = (bf16[256,512]{1,0:T(8,128)(2,1)S(1)}, bf16[256,512]{1,0:T(8,128)(2,1)}, u32[]{:S(2)}) copy-start(bf16[256,512]{1,0:T(8,128)(2,1)} %refs_8_.5) | copy-start | bytes 786436
  55.0 5.0 %copy-start.17 = (f32[2,8,512]{2,1,0:T(8,128)S(1)}, f32[2,8,512]{2,1,0:T(8,128)}, u32[]{:S(2)}) copy-start(f32[2,8,512]{2,1,0:T(8,128)} %constant.31.clone.trig_ref) | copy-start | bytes 98308
  55.5 23.2 %collective-permute-start.5 = (bf16[2,64,4096]{2,1,0:T(8,128)(2,1)S(1)}, bf16[2,64,4096]{2,1,0:T(8,128)(2,1)S(1)}, u32[]{:S(2)}, u32[]{:S(2)}) collective-permute-start(bf16[2,64,4096]{2,1,0:T(8,128)(2,1)S(1)} %get-tuple-element.132), channel_id=1, source_target_pairs={{0,2},{1,5},{2,0},{3,7},{4,6},{5,1},{6,4},{7,3},{8,10},{9,13},{10,... | collective-permute-start | bytes 3145736 | tf_op jit(solution)/shard_map/ppermute | solution.py:601
  58.4 1.5 collective-permute-start.4
  78.9 19.4 %collective-permute-start.6 = (bf16[1,64,4096]{2,1,0:T(8,128)(2,1)S(1)}, bf16[1,64,4096]{2,1,0:T(8,128)(2,1)S(1)}, u32[]{:S(2)}, u32[]{:S(2)}) collective-permute-start(bf16[1,64,4096]{2,1,0:T(8,128)(2,1)S(1)} %get-tuple-element.139), channel_id=1, source_target_pairs={{0,4},{1,3},{2,6},{3,1},{4,0},{5,7},{6,2},{7,5},{8,12},{9,11},{10,... | collective-permute-start | bytes 1572872 | tf_op jit(solution)/shard_map/ppermute | solution.py:601
  98.2 22.8 %collective-permute-start.10 = (bf16[4,64,1024]{2,1,0:T(8,128)(2,1)S(1)}, bf16[4,64,1024]{2,1,0:T(8,128)(2,1)S(1)}, u32[]{:S(2)}, u32[]{:S(2)}) collective-permute-start(bf16[4,64,1024]{2,1,0:T(8,128)(2,1)S(1)} %get-tuple-element.149), channel_id=1, source_target_pairs={{0,1},{1,0},{2,3},{3,2},{4,5},{5,4},{6,7},{7,6},{8,9},{9,8},{10,11... | collective-permute-start | bytes 1572872 | tf_op jit(solution)/shard_map/ppermute | solution.py:605
  99.0 22.8 %collective-permute-start.7 = (bf16[1,16,4096]{2,1,0:T(8,128)(2,1)S(1)}, bf16[1,16,4096]{2,1,0:T(8,128)(2,1)S(1)}, u32[]{:S(2)}, u32[]{:S(2)}) collective-permute-start(bf16[1,16,4096]{2,1,0:T(8,128)(2,1)S(1)} %get-tuple-element.141), channel_id=1, source_target_pairs={{0,8},{1,9},{2,10},{3,11},{4,12},{5,13},{6,14},{7,15},{8,0},{9,1},... | collective-permute-start | bytes 393224 | tf_op jit(solution)/shard_map/ppermute | solution.py:601
  100.7 21.1 %collective-permute-start.8 = (bf16[1,16,4096]{2,1,0:T(8,128)(2,1)S(1)}, bf16[1,16,4096]{2,1,0:T(8,128)(2,1)S(1)}, u32[]{:S(2)}, u32[]{:S(2)}) collective-permute-start(bf16[1,16,4096]{2,1,0:T(8,128)(2,1)S(1)} %get-tuple-element.142), channel_id=1, source_target_pairs={{0,16},{1,17},{2,18},{3,19},{4,20},{5,21},{6,22},{7,23},{8,24},{9,... | collective-permute-start | bytes 393224 | tf_op jit(solution)/shard_map/ppermute | solution.py:601
  103.3 18.6 %collective-permute-start.9 = (bf16[1,16,4096]{2,1,0:T(8,128)(2,1)S(1)}, bf16[1,16,4096]{2,1,0:T(8,128)(2,1)S(1)}, u32[]{:S(2)}, u32[]{:S(2)}) collective-permute-start(bf16[1,16,4096]{2,1,0:T(8,128)(2,1)S(1)} %get-tuple-element.143), channel_id=1, source_target_pairs={{0,24},{1,25},{2,26},{3,27},{4,28},{5,29},{6,30},{7,31},{8,16},{9,... | collective-permute-start | bytes 393224 | tf_op jit(solution)/shard_map/ppermute | solution.py:601
  121.0 5.3 %copy-start.10 = (bf16[2048,384]{1,0:T(8,128)(2,1)}, bf16[2048,384]{1,0:T(8,128)(2,1)S(1)}, u32[]{:S(2)}) copy-start(bf16[2048,384]{1,0:T(8,128)(2,1)S(1)} %get-tuple-element.168.refs_7_) | copy-start | bytes 4718596
  121.2 26.8 %collective-permute-start.14 = (bf16[2,64,1024]{2,1,0:T(8,128)(2,1)S(1)}, bf16[2,64,1024]{2,1,0:T(8,128)(2,1)S(1)}, u32[]{:S(2)}, u32[]{:S(2)}) collective-permute-start(bf16[2,64,1024]{2,1,0:T(8,128)(2,1)S(1)} %get-tuple-element.158), channel_id=1, source_target_pairs={{0,2},{1,5},{2,0},{3,7},{4,6},{5,1},{6,4},{7,3},{8,10},{9,13},{10,... | collective-permute-start | bytes 786440 | tf_op jit(solution)/shard_map/ppermute | solution.py:601
  121.9 23.4 %collective-permute-start.13 = (bf16[1,16,4096]{2,1,0:T(8,128)(2,1)S(1)}, bf16[1,16,4096]{2,1,0:T(8,128)(2,1)S(1)}, u32[]{:S(2)}, u32[]{:S(2)}) collective-permute-start(bf16[1,16,4096]{2,1,0:T(8,128)(2,1)S(1)} %ff_sum2.1.refs_0_), channel_id=1, source_target_pairs={{0,24},{1,25},{2,26},{3,27},{4,28},{5,29},{6,30},{7,31},{8,16},{9,... | collective-permute-start | bytes 393224 | tf_op jit(solution)/shard_map/ppermute | solution.py:601
  125.6 19.7 %collective-permute-start.12 = (bf16[1,16,4096]{2,1,0:T(8,128)(2,1)S(1)}, bf16[1,16,4096]{2,1,0:T(8,128)(2,1)S(1)}, u32[]{:S(2)}, u32[]{:S(2)}) collective-permute-start(bf16[1,16,4096]{2,1,0:T(8,128)(2,1)S(1)} %ff_sum2.1.refs_0_), channel_id=1, source_target_pairs={{0,16},{1,17},{2,18},{3,19},{4,20},{5,21},{6,22},{7,23},{8,24},{9,... | collective-permute-start | bytes 393224 | tf_op jit(solution)/shard_map/ppermute | solution.py:601
  125.6 19.8 %collective-permute-start.11 = (bf16[1,16,4096]{2,1,0:T(8,128)(2,1)S(1)}, bf16[1,16,4096]{2,1,0:T(8,128)(2,1)S(1)}, u32[]{:S(2)}, u32[]{:S(2)}) collective-permute-start(bf16[1,16,4096]{2,1,0:T(8,128)(2,1)S(1)} %ff_sum2.1.refs_0_), channel_id=1, source_target_pairs={{0,8},{1,9},{2,10},{3,11},{4,12},{5,13},{6,14},{7,15},{8,0},{9,1},... | collective-permute-start | bytes 393224 | tf_op jit(solution)/shard_map/ppermute | solution.py:601
  126.3 23.3 %copy-start.7 = (bf16[1024,512]{1,0:T(8,128)(2,1)S(1)}, bf16[1024,512]{1,0:T(8,128)(2,1)}, u32[]{:S(2)}) copy-start(bf16[1024,512]{1,0:T(8,128)(2,1)} %refs_10_.4) | copy-start | bytes 3145732
  145.3 4.3 %copy-start.5 = (bf16[256,2048]{1,0:T(8,128)(2,1)S(1)}, bf16[256,2048]{1,0:T(8,128)(2,1)}, u32[]{:S(2)}) copy-start(bf16[256,2048]{1,0:T(8,128)(2,1)} %refs_9_.2) | copy-start | bytes 3145732
  145.3 21.5 %collective-permute-start.15 = (bf16[4,64,1024]{2,1,0:T(8,128)(2,1)S(1)}, bf16[4,64,1024]{2,1,0:T(8,128)(2,1)S(1)}, u32[]{:S(2)}, u32[]{:S(2)}) collective-permute-start(bf16[4,64,1024]{2,1,0:T(8,128)(2,1)S(1)} %get-tuple-element.172), channel_id=1, source_target_pairs={{0,1},{1,0},{2,3},{3,2},{4,5},{5,4},{6,7},{7,6},{8,9},{9,8},{10,11... | collective-permute-start | bytes 1572872 | tf_op jit(solution)/shard_map/ppermute | solution.py:605
  145.9 17.1 %copy-start.13 = (bf16[1,64,4096]{2,1,0:T(8,128)(2,1)}, bf16[1,64,4096]{2,1,0:T(8,128)(2,1)S(1)}, u32[]{:S(2)}) copy-start(bf16[1,64,4096]{2,1,0:T(8,128)(2,1)S(1)} %ff_join.1.refs_0_) | copy-start | bytes 1572868
  145.9 21.8 %collective-permute-start.18 = (bf16[1,64,4096]{2,1,0:T(8,128)(2,1)S(1)}, bf16[1,64,4096]{2,1,0:T(8,128)(2,1)S(1)}, u32[]{:S(2)}, u32[]{:S(2)}) collective-permute-start(bf16[1,64,4096]{2,1,0:T(8,128)(2,1)S(1)} %ff_join.1.refs_0_), channel_id=1, source_target_pairs={{0,2},{1,5},{2,0},{3,7},{4,6},{5,1},{6,4},{7,3},{8,10},{9,13},{10,... | collective-permute-start | bytes 1572872 | tf_op jit(solution)/shard_map/ppermute | solution.py:601
  147.5 20.9 %collective-permute-start.17 = (bf16[1,64,4096]{2,1,0:T(8,128)(2,1)S(1)}, bf16[1,64,4096]{2,1,0:T(8,128)(2,1)S(1)}, u32[]{:S(2)}, u32[]{:S(2)}) collective-permute-start(bf16[1,64,4096]{2,1,0:T(8,128)(2,1)S(1)} %ff_join.1.refs_0_), channel_id=1, source_target_pairs={{0,4},{1,3},{2,6},{3,1},{4,0},{5,7},{6,2},{7,5},{8,12},{9,11},{10,... | collective-permute-start | bytes 1572872 | tf_op jit(solution)/shard_map/ppermute | solution.py:601
  148.1 15.0 %collective-permute-start.16 = (bf16[1,64,1024]{2,1,0:T(8,128)(2,1)S(1)}, bf16[1,64,1024]{2,1,0:T(8,128)(2,1)S(1)}, u32[]{:S(2)}, u32[]{:S(2)}) collective-permute-start(bf16[1,64,1024]{2,1,0:T(8,128)(2,1)S(1)} %get-tuple-element.175), channel_id=1, source_target_pairs={{0,4},{1,3},{2,6},{3,1},{4,0},{5,7},{6,2},{7,5},{8,12},{9,11},{10,... | collective-permute-start | bytes 393224 | tf_op jit(solution)/shard_map/ppermute | solution.py:601
  163.1 20.2 %collective-permute-start.21 = (bf16[1,64,1024]{2,1,0:T(8,128)(2,1)S(1)}, bf16[1,64,1024]{2,1,0:T(8,128)(2,1)S(1)}, u32[]{:S(2)}, u32[]{:S(2)}) collective-permute-start(bf16[1,64,1024]{2,1,0:T(8,128)(2,1)S(1)} %att_sum1.2.refs_0_), channel_id=1, source_target_pairs={{0,24},{1,25},{2,26},{3,27},{4,28},{5,29},{6,30},{7,31},{8,16},{9,... | collective-permute-start | bytes 393224 | tf_op jit(solution)/shard_map/ppermute | solution.py:601
  166.8 16.5 %collective-permute-start.20 = (bf16[1,64,1024]{2,1,0:T(8,128)(2,1)S(1)}, bf16[1,64,1024]{2,1,0:T(8,128)(2,1)S(1)}, u32[]{:S(2)}, u32[]{:S(2)}) collective-permute-start(bf16[1,64,1024]{2,1,0:T(8,128)(2,1)S(1)} %att_sum1.2.refs_0_), channel_id=1, source_target_pairs={{0,16},{1,17},{2,18},{3,19},{4,20},{5,21},{6,22},{7,23},{8,24},{9,... | collective-permute-start | bytes 393224 | tf_op jit(solution)/shard_map/ppermute | solution.py:601
  166.8 16.5 %collective-permute-start.19 = (bf16[1,64,1024]{2,1,0:T(8,128)(2,1)S(1)}, bf16[1,64,1024]{2,1,0:T(8,128)(2,1)S(1)}, u32[]{:S(2)}, u32[]{:S(2)}) collective-permute-start(bf16[1,64,1024]{2,1,0:T(8,128)(2,1)S(1)} %att_sum1.2.refs_0_), channel_id=1, source_target_pairs={{0,8},{1,9},{2,10},{3,11},{4,12},{5,13},{6,14},{7,15},{8,0},{9,1},... | collective-permute-start | bytes 393224 | tf_op jit(solution)/shard_map/ppermute | solution.py:601
  167.7 15.6 %copy-start.18 = (bf16[1,64,4096]{2,1,0:T(8,128)(2,1)}, bf16[1,64,4096]{2,1,0:T(8,128)(2,1)S(1)}, u32[]{:S(2)}) copy-start(bf16[1,64,4096]{2,1,0:T(8,128)(2,1)S(1)} %collective-permute-done.18.refs_2_) | copy-start | bytes 1572868
  167.7 15.7 %collective-permute-start.22 = (bf16[2,64,1024]{2,1,0:T(8,128)(2,1)S(1)}, bf16[2,64,1024]{2,1,0:T(8,128)(2,1)S(1)}, u32[]{:S(2)}, u32[]{:S(2)}) collective-permute-start(bf16[2,64,1024]{2,1,0:T(8,128)(2,1)S(1)} %get-tuple-element.184), channel_id=1, source_target_pairs={{0,2},{1,5},{2,0},{3,7},{4,6},{5,1},{6,4},{7,3},{8,10},{9,13},{10,... | collective-permute-start | bytes 786440 | tf_op jit(solution)/shard_map/ppermute | solution.py:601
  168.3 14.9 %copy-start.19 = (bf16[1,64,4096]{2,1,0:T(8,128)(2,1)}, bf16[1,64,4096]{2,1,0:T(8,128)(2,1)S(1)}, u32[]{:S(2)}) copy-start(bf16[1,64,4096]{2,1,0:T(8,128)(2,1)S(1)} %collective-permute-done.17.refs_1_) | copy-start | bytes 1572868
  168.3 20.2 %collective-permute-start.25 = (bf16[1,64,4096]{2,1,0:T(8,128)(2,1)S(1)}, bf16[1,64,4096]{2,1,0:T(8,128)(2,1)S(1)}, u32[]{:S(2)}, u32[]{:S(2)}) collective-permute-start(bf16[1,64,4096]{2,1,0:T(8,128)(2,1)S(1)} %collective-permute-done.18.refs_2_), channel_id=1, source_target_pairs={{0,4},{1,3},{2,6},{3,1},{4,0},{5,7},{6,2},{7,5},{8,12},{9,11},{10,... | collective-permute-start | bytes 1572872 | tf_op jit(solution)/shard_map/ppermute | solution.py:601
  183.4 24.5 %copy-start.14 = (bf16[1,64,1024]{2,1,0:T(8,128)(2,1)}, bf16[1,64,1024]{2,1,0:T(8,128)(2,1)S(1)}, u32[]{:S(2)}) copy-start(bf16[1,64,1024]{2,1,0:T(8,128)(2,1)S(1)} %att_sum2.1.refs_0_) | copy-start | bytes 393220
  183.5 5.0 %collective-permute-start.24 = (bf16[1,64,1024]{2,1,0:T(8,128)(2,1)S(1)}, bf16[1,64,1024]{2,1,0:T(8,128)(2,1)S(1)}, u32[]{:S(2)}, u32[]{:S(2)}) collective-permute-start(bf16[1,64,1024]{2,1,0:T(8,128)(2,1)S(1)} %get-tuple-element.189), channel_id=1, source_target_pairs={{0,4},{1,3},{2,6},{3,1},{4,0},{5,7},{6,2},{7,5},{8,12},{9,11},{10,... | collective-permute-start | bytes 393224 | tf_op jit(solution)/shard_map/ppermute | solution.py:601
  184.3 1.2 collective-permute-start.23
  188.6 6.8 %copy-start.20 = (bf16[1,64,4096]{2,1,0:T(8,128)(2,1)}, bf16[1,64,4096]{2,1,0:T(8,128)(2,1)S(1)}, u32[]{:S(2)}) copy-start(bf16[1,64,4096]{2,1,0:T(8,128)(2,1)S(1)} %collective-permute-done.25.refs_3_) | copy-start | bytes 1572868
  188.6 19.3 %collective-permute-start.27 = (bf16[1,64,1024]{2,1,0:T(8,128)(2,1)S(1)}, bf16[1,64,1024]{2,1,0:T(8,128)(2,1)S(1)}, u32[]{:S(2)}, u32[]{:S(2)}) collective-permute-start(bf16[1,64,1024]{2,1,0:T(8,128)(2,1)S(1)} %att_sum2.1.refs_0_), channel_id=1, source_target_pairs={{0,2},{1,5},{2,0},{3,7},{4,6},{5,1},{6,4},{7,3},{8,10},{9,13},{10,... | collective-permute-start | bytes 393224 | tf_op jit(solution)/shard_map/ppermute | solution.py:601
  189.4 18.5 %collective-permute-start.26 = (bf16[1,64,1024]{2,1,0:T(8,128)(2,1)S(1)}, bf16[1,64,1024]{2,1,0:T(8,128)(2,1)S(1)}, u32[]{:S(2)}, u32[]{:S(2)}) collective-permute-start(bf16[1,64,1024]{2,1,0:T(8,128)(2,1)S(1)} %att_sum2.1.refs_0_), channel_id=1, source_target_pairs={{0,4},{1,3},{2,6},{3,1},{4,0},{5,7},{6,2},{7,5},{8,12},{9,11},{10,... | collective-permute-start | bytes 393224 | tf_op jit(solution)/shard_map/ppermute | solution.py:601
  191.0 16.9 %collective-permute-start.30 = (bf16[1,64,1024]{2,1,0:T(8,128)(2,1)S(1)}, bf16[1,64,1024]{2,1,0:T(8,128)(2,1)S(1)}, u32[]{:S(2)}, u32[]{:S(2)}) collective-permute-start(bf16[1,64,1024]{2,1,0:T(8,128)(2,1)S(1)} %att_sum1.3.refs_0_), channel_id=1, source_target_pairs={{0,24},{1,25},{2,26},{3,27},{4,28},{5,29},{6,30},{7,31},{8,16},{9,... | collective-permute-start | bytes 393224 | tf_op jit(solution)/shard_map/ppermute | solution.py:601
  194.8 13.1 %collective-permute-start.29 = (bf16[1,64,1024]{2,1,0:T(8,128)(2,1)S(1)}, bf16[1,64,1024]{2,1,0:T(8,128)(2,1)S(1)}, u32[]{:S(2)}, u32[]{:S(2)}) collective-permute-start(bf16[1,64,1024]{2,1,0:T(8,128)(2,1)S(1)} %att_sum1.3.refs_0_), channel_id=1, source_target_pairs={{0,16},{1,17},{2,18},{3,19},{4,20},{5,21},{6,22},{7,23},{8,24},{9,... | collective-permute-start | bytes 393224 | tf_op jit(solution)/shard_map/ppermute | solution.py:601
  194.8 13.1 %collective-permute-start.28 = (bf16[1,64,1024]{2,1,0:T(8,128)(2,1)S(1)}, bf16[1,64,1024]{2,1,0:T(8,128)(2,1)S(1)}, u32[]{:S(2)}, u32[]{:S(2)}) collective-permute-start(bf16[1,64,1024]{2,1,0:T(8,128)(2,1)S(1)} %att_sum1.3.refs_0_), channel_id=1, source_target_pairs={{0,8},{1,9},{2,10},{3,11},{4,12},{5,13},{6,14},{7,15},{8,0},{9,1},... | collective-permute-start | bytes 393224 | tf_op jit(solution)/shard_map/ppermute | solution.py:601
  207.9 18.4 %copy-start.21 = (bf16[1,64,1024]{2,1,0:T(8,128)(2,1)}, bf16[1,64,1024]{2,1,0:T(8,128)(2,1)S(1)}, u32[]{:S(2)}) copy-start(bf16[1,64,1024]{2,1,0:T(8,128)(2,1)S(1)} %collective-permute-done.27.refs_2_) | copy-start | bytes 393220
  207.9 18.4 %copy-start.22 = (bf16[1,64,1024]{2,1,0:T(8,128)(2,1)}, bf16[1,64,1024]{2,1,0:T(8,128)(2,1)S(1)}, u32[]{:S(2)}) copy-start(bf16[1,64,1024]{2,1,0:T(8,128)(2,1)S(1)} %collective-permute-done.26.refs_1_) | copy-start | bytes 393220
  208.0 18.3 %copy-start.15 = (bf16[1,64,1024]{2,1,0:T(8,128)(2,1)}, bf16[1,64,1024]{2,1,0:T(8,128)(2,1)S(1)}, u32[]{:S(2)}) copy-start(bf16[1,64,1024]{2,1,0:T(8,128)(2,1)S(1)} %att_sum4.1.refs_4_) | copy-start | bytes 393220
  208.0 15.8 %collective-permute-start.34 = (bf16[1,64,1024]{2,1,0:T(8,128)(2,1)S(1)}, bf16[1,64,1024]{2,1,0:T(8,128)(2,1)S(1)}, u32[]{:S(2)}, u32[]{:S(2)}) collective-permute-start(bf16[1,64,1024]{2,1,0:T(8,128)(2,1)S(1)} %collective-permute-done.27.refs_2_), channel_id=1, source_target_pairs={{0,4},{1,3},{2,6},{3,1},{4,0},{5,7},{6,2},{7,5},{8,12},{9,11},{10,... | collective-permute-start | bytes 393224 | tf_op jit(solution)/shard_map/ppermute | solution.py:601
  208.5 15.3 %collective-permute-start.37 = (bf16[1,64,1024]{2,1,0:T(8,128)(2,1)S(1)}, bf16[1,64,1024]{2,1,0:T(8,128)(2,1)S(1)}, u32[]{:S(2)}, u32[]{:S(2)}) collective-permute-start(bf16[1,64,1024]{2,1,0:T(8,128)(2,1)S(1)} %att_sum4.1.refs_4_), channel_id=1, source_target_pairs={{0,6},{1,7},{2,4},{3,5},{4,2},{5,3},{6,0},{7,1},{8,14},{9,15},{10,... | collective-permute-start | bytes 393224 | tf_op jit(solution)/shard_map/ppermute | solution.py:601
  209.9 13.9 %collective-permute-start.36 = (bf16[1,64,1024]{2,1,0:T(8,128)(2,1)S(1)}, bf16[1,64,1024]{2,1,0:T(8,128)(2,1)S(1)}, u32[]{:S(2)}, u32[]{:S(2)}) collective-permute-start(bf16[1,64,1024]{2,1,0:T(8,128)(2,1)S(1)} %att_sum4.1.refs_4_), channel_id=1, source_target_pairs={{0,2},{1,5},{2,0},{3,7},{4,6},{5,1},{6,4},{7,3},{8,10},{9,13},{10,... | collective-permute-start | bytes 393224 | tf_op jit(solution)/shard_map/ppermute | solution.py:601
  211.6 12.3 %collective-permute-start.35 = (bf16[1,64,1024]{2,1,0:T(8,128)(2,1)S(1)}, bf16[1,64,1024]{2,1,0:T(8,128)(2,1)S(1)}, u32[]{:S(2)}, u32[]{:S(2)}) collective-permute-start(bf16[1,64,1024]{2,1,0:T(8,128)(2,1)S(1)} %att_sum4.1.refs_4_), channel_id=1, source_target_pairs={{0,4},{1,3},{2,6},{3,1},{4,0},{5,7},{6,2},{7,5},{8,12},{9,11},{10,... | collective-permute-start | bytes 393224 | tf_op jit(solution)/shard_map/ppermute | solution.py:601
  212.0 4.2 %collective-permute-start.31 = (f32[32,1,128]{2,1,0:T(1,128)S(1)}, f32[32,1,128]{2,1,0:T(1,128)S(1)}, u32[]{:S(2)}, u32[]{:S(2)}) collective-permute-start(f32[32,1,128]{2,1,0:T(1,128)S(1)} %small_pair.1.refs_0_), channel_id=1, source_target_pairs={{0,2},{1,3},{2,0},{3,1},{4,6},{5,7},{6,4},{7,5},{8,10},{9,11},{10,... | collective-permute-start | bytes 49160 | tf_op jit(solution)/shard_map/ppermute | solution.py:601
  216.1 3.8 %collective-permute-start.32 = (f32[32,1,128]{2,1,0:T(1,128)S(1)}, f32[32,1,128]{2,1,0:T(1,128)S(1)}, u32[]{:S(2)}, u32[]{:S(2)}) collective-permute-start(f32[32,1,128]{2,1,0:T(1,128)S(1)} %small_sum.4.refs_0_), channel_id=1, source_target_pairs={{0,4},{1,5},{2,6},{3,7},{4,0},{5,1},{6,2},{7,3},{8,12},{9,13},{10,... | collective-permute-start | bytes 49160 | tf_op jit(solution)/shard_map/ppermute | solution.py:601
  220.0 3.8 %collective-permute-start.33 = (f32[32,1,128]{2,1,0:T(1,128)S(1)}, f32[32,1,128]{2,1,0:T(1,128)S(1)}, u32[]{:S(2)}, u32[]{:S(2)}) collective-permute-start(f32[32,1,128]{2,1,0:T(1,128)S(1)} %small_sum.5.refs_0_), channel_id=1, source_target_pairs={{0,8},{1,9},{2,10},{3,11},{4,12},{5,13},{6,14},{7,15},{8,0},{9,1},... | collective-permute-start | bytes 49160 | tf_op jit(solution)/shard_map/ppermute | solution.py:601
  223.9 10.7 %collective-permute-start.38 = (f32[32,1,128]{2,1,0:T(1,128)S(1)}, f32[32,1,128]{2,1,0:T(1,128)S(1)}, u32[]{:S(2)}, u32[]{:S(2)}) collective-permute-start(f32[32,1,128]{2,1,0:T(1,128)S(1)} %small_sum.6.refs_0_), channel_id=1, source_target_pairs={{0,16},{1,17},{2,18},{3,19},{4,20},{5,21},{6,22},{7,23},{8,24},{9,... | collective-permute-start | bytes 49160 | tf_op jit(solution)/shard_map/ppermute | solution.py:601
  226.3 8.4 %copy-start.33 = (bf16[1024]{0:T(1024)(128)(2,1)S(1)}, bf16[1024]{0:T(1024)(128)(2,1)}, u32[]{:S(2)}) copy-start(bf16[1024]{0:T(1024)(128)(2,1)} %param.31) | copy-start | bytes 6148
  226.3 8.4 %copy-start.35 = (f32[1024]{0:T(1024)S(1)}, f32[1024]{0:T(1024)}, u32[]{:S(2)}) copy-start(f32[1024]{0:T(1024)} %param.38) | copy-start | bytes 12292
  226.3 8.4 %copy-start.36 = (f32[1024]{0:T(1024)S(1)}, f32[1024]{0:T(1024)}, u32[]{:S(2)}) copy-start(f32[1024]{0:T(1024)} %param.45) | copy-start | bytes 12292
  226.3 9.0 %copy-start.34 = (bf16[768]{0:T(1024)(128)(2,1)S(1)}, bf16[768]{0:T(1024)(128)(2,1)}, u32[]{:S(2)}) copy-start(bf16[768]{0:T(1024)(128)(2,1)} %param.28) | copy-start | bytes 4612
  226.4 9.0 %copy-start.37 = (f32[768]{0:T(1024)S(1)}, f32[768]{0:T(1024)}, u32[]{:S(2)}) copy-start(f32[768]{0:T(1024)} %param.35) | copy-start | bytes 9220
  226.4 9.0 %copy-start.38 = (f32[768]{0:T(1024)S(1)}, f32[768]{0:T(1024)}, u32[]{:S(2)}) copy-start(f32[768]{0:T(1024)} %param.42) | copy-start | bytes 9220
  226.4 9.6 %copy-start.30 = (bf16[6,256]{1,0:T(8,128)(2,1)S(1)}, bf16[6,256]{1,0:T(8,128)(2,1)}, u32[]{:S(2)}) copy-start(bf16[6,256]{1,0:T(8,128)(2,1)} %param.26) | copy-start | bytes 9220
  226.4 9.6 %copy-start.31 = (f32[6,256]{1,0:T(8,128)S(1)}, f32[6,256]{1,0:T(8,128)}, u32[]{:S(2)}) copy-start(f32[6,256]{1,0:T(8,128)} %param.33) | copy-start | bytes 18436
  226.4 9.6 %copy-start.32 = (f32[6,256]{1,0:T(8,128)S(1)}, f32[6,256]{1,0:T(8,128)}, u32[]{:S(2)}) copy-start(f32[6,256]{1,0:T(8,128)} %param.40) | copy-start | bytes 18436
  (14 other events, 28.9 us)

commit v4 on v3

--- a/solution.py
+++ b/solution.py
@@ -219,7 +219,7 @@
         out_shape=jax.ShapeDtypeStruct(buf, bf16),
         cost_estimate=cost(2 * rows * width * ff, 4 * rows * width + 3 * rows * ff),
         name="feed_forward_own",
-        compiler_params=pltpu.CompilerParams(vmem_limit_bytes=30 << 20),
+        compiler_params=pltpu.CompilerParams(vmem_limit_bytes=44 << 20),
     )(meta, second, grad, act, hg)
 
 
@@ -392,7 +392,7 @@
         ],
         cost_estimate=cost(flops, 4 * rows * width + 2 * rows * 512),
         name=f"attention_{j}{rel}",
-        compiler_params=pltpu.CompilerParams(vmem_limit_bytes=26 << 20),
+        compiler_params=pltpu.CompilerParams(vmem_limit_bytes=18 << 20),
     )(meta, first, grad, *[qkv_own] * 3, *[qkv_far] * 3, out_w, small, trig, *before)
 
 
@@ -537,7 +537,7 @@
             2 * rows * width * (512 + 2048 * 2 + 1536) // parts, 2 * rows * (4 * 512 + 4 * 2048) // parts
         ),
         name=f"outputs_{part}",
-        compiler_params=pltpu.CompilerParams(vmem_limit_bytes=44 << 20),
+        compiler_params=pltpu.CompilerParams(vmem_limit_bytes=30 << 20),
     )(meta, tokens, grad, act, hg, *atts, *qgs, *weights, *tail, *extra)
 
 
@@ -564,30 +564,45 @@
     )(*terms)
 
 
-def along_kernel(n_in, meta, *refs):
-    ins, outs = refs[:n_in], refs[n_in:]
-    rows = outs[0].shape[1]
-    for k, out in enumerate(outs):
-        at = pl.ds(pl.multiple_of((meta[3] ^ k) * rows, rows), rows)
-        total = ins[0][0, at, :].astype(f32)
-        for term in ins[1:]:
-            total += term[0, at, :].astype(f32)
-        out[0] = total.astype(bf16)
-
-
-def join_kernel(meta, *refs):
-    ins, out = refs[:4], refs[4]
-    rows = ins[0].shape[1]
-    for k, piece in enumerate(ins):
-        out[0, pl.ds(pl.multiple_of((meta[3] ^ k) * rows, rows), rows), :] = piece[0]
-
-
-def along_call(kernel, meta, terms, outs, name):
+def pair_kernel(*refs):
+    own, got, outs = refs[:2], refs[2:4], refs[4:]
+    for j, (mine, other) in enumerate(zip(own, got)):
+        w = mine.shape[2]
+        for k, out in enumerate(outs):
+            total = mine[k].astype(f32) + other[k].astype(f32)
+            out[0, :, j * w : (j + 1) * w] = total.astype(bf16)
+
+
+def pair_call(own, got, name):
+    rows, width = own[0].shape[1], 2 * own[0].shape[2]
+    return pl.pallas_call(
+        pair_kernel,
+        out_shape=[jax.ShapeDtypeStruct((1, rows, width), bf16)] * 4,
+        compiler_params=pltpu.CompilerParams(vmem_limit_bytes=12 << 20),
+        cost_estimate=cost(8 * rows * width, 24 * rows * width),
+        name=name,
+    )(*own, *got)
+
+
+def half_kernel(meta, mine_ref, got_ref, keep_ref, send_ref):
+    rows = keep_ref.shape[1]
+    for out, number in ((keep_ref, meta[3]), (send_ref, 1 - meta[3])):
+        at = pl.ds(pl.multiple_of(number * rows, rows), rows)
+        out[0] = (mine_ref[0, at, :].astype(f32) + got_ref[0, at, :].astype(f32)).astype(bf16)
+
+
+def join_kernel(meta, mine_ref, got_ref, out_ref):
+    rows = mine_ref.shape[1]
+    for piece, number in ((mine_ref, meta[3]), (got_ref, 1 - meta[3])):
+        out_ref[0, pl.ds(pl.multiple_of(number * rows, rows), rows), :] = piece[0]
+
+
+def half_call(kernel, meta, terms, outs, name):
     moved = 2 * sum(a.size for a in terms)
     whole = pl.BlockSpec(memory_space=pltpu.VMEM)
     return pl.pallas_call(
         kernel,
-        in_specs=[pl.BlockSpec(memory_space=pltpu.SMEM), *[whole] * len(terms)],
+        in_specs=[pl.BlockSpec(memory_space=pltpu.SMEM), whole, whole],
         out_specs=[whole] * len(outs),
         out_shape=[jax.ShapeDtypeStruct(o, bf16) for o in outs],
         compiler_params=pltpu.CompilerParams(vmem_limit_bytes=(moved * 3) // 2 + (4 << 20)),
@@ -618,10 +633,6 @@
     return [exchange(a, reps, *step) for a, step in zip(pieces, steps)]
 
 
-def along(pieces, reps):
-    return [exchange(a, reps, 4 * k, 4 * k) for k, a in enumerate(pieces, 1)]
-
-
 def adamw(grad, mean, square, weight):
     new_mean = BETA_ONE * mean + (1.0 - BETA_ONE) * grad
     new_square = BETA_TWO * square + (1.0 - BETA_TWO) * grad * grad
@@ -648,8 +659,8 @@
 
 
 def adam_ff_kernel(meta, *refs):
-    pieces, proj, fc, proj_out, fc_out = refs[:4], refs[4:7], refs[7:10], refs[10:14], refs[14:18]
-    which = pl.program_id(0) ^ meta[1]
+    pieces, proj, fc, proj_out, fc_out = refs[:-14], refs[-14:-11], refs[-11:-8], refs[-8:-4], refs[-4:]
+    which = pl.program_id(0)
     quarter = fc[0].shape[0]
     for j in range(2):
         for k in range(2):
@@ -661,40 +672,56 @@
 
 
 def adam_qkv_kernel(meta, *refs):
-    sets, qkv, out, qkv_out, out_out = (refs[:4], refs[4:8]), refs[8:11], refs[11:14], refs[14:18], refs[18:22]
+    pieces, qkv, out, qkv_out, out_out = refs[:-14], refs[-14:-11], refs[-11:-8], refs[-8:-4], refs[-4:]
     c = meta[0]
-    which = pl.program_id(0) ^ meta[1]
+    which = pl.program_id(0)
     quarter = qkv[0].shape[0]
     hq = quarter // 2
-    for j, pieces in enumerate(sets):
+    for j in range(2):
         for slot in range(2):
             for p in range(3):
-                col = 384 * slot + 128 * p
+                col = 1024 * j + 384 * slot + 128 * p
                 grad = pick(pieces, which, slice(col, col + 128))
                 lanes = pl.ds(pl.multiple_of((p * 4 + (slot ^ c) * 2 + j) * 128, 128), 128)
                 adam_block(grad, *qkv, *qkv_out, (slice(None), lanes))
         for k in range(2):
-            grad = pick(pieces, which, slice(768, 1024), slice(k * hq, (k + 1) * hq))
+            col = 1024 * j + 768
+            grad = pick(pieces, which, slice(col, col + 256), slice(k * hq, (k + 1) * hq))
             adam_block(grad, *out, *out_out, (j, slice(None), slice(256 * k, 256 * k + 256)))
 
 
-def adam_call(kernel, meta, pieces, first, second, first_spec, second_spec, name):
+def adam_call(kernel, meta, start, pieces, first, second, first_spec, second_spec, name, before=()):
     outs = [jax.ShapeDtypeStruct(first[0].shape, f32)] * 4 + [jax.ShapeDtypeStruct(second[0].shape, f32)] * 4
+    specs = [
+        pl.BlockSpec(shape, functools.partial(lambda at, i, m: at((start + i) ^ m[1]), at))
+        for shape, at in (first_spec, second_spec)
+    ]
+    count = len(before)
+
+    def run(meta_ref, *refs):
+        kernel(meta_ref, *refs[count:])
+
     grid_spec = pltpu.PrefetchScalarGridSpec(
         num_scalar_prefetch=1,
-        grid=(4,),
-        in_specs=[*[full_spec(a.shape) for a in pieces], *[first_spec] * 3, *[second_spec] * 3],
-        out_specs=[*[first_spec] * 4, *[second_spec] * 4],
-    )
-    size = first[0].size + second[0].size
+        grid=(len(pieces),),
+        in_specs=[
+            *[pl.BlockSpec(memory_space=pl.ANY)] * count,
+            *[full_spec(a.shape) for a in pieces],
+            *[specs[0]] * 3,
+            *[specs[1]] * 3,
+        ],
+        out_specs=[*[specs[0]] * 4, *[specs[1]] * 4],
+    )
+    size = (first[0].size + second[0].size) * len(pieces) // 4
     return pl.pallas_call(
-        kernel,
+        run,
         grid_spec=grid_spec,
         out_shape=outs,
+        input_output_aliases={1 + k: k for k in range(count)},
         compiler_params=pltpu.CompilerParams(vmem_limit_bytes=56 << 20),
         cost_estimate=cost(20 * size, 28 * size),
         name=name,
-    )(meta, *pieces, *first, *second)
+    )(meta, *before, *pieces, *first, *second)
 
 
 def body(
@@ -726,8 +753,9 @@
     c = lax.axis_index("opt")
     place = lax.axis_index("rep")
     low, high = place & 1, (place >> 1) & 1
-    ranks = jnp.stack([2 * low + high, 2 * high + low])
-    meta = jnp.stack([c, ranks[c], ranks[1 - c], (place >> 2) & 3]).astype(jnp.int32)
+    slot = lax.iota(jnp.int32, 4)
+    ranks = jnp.where((slot == 1) == (c == 0), 2 * low + high, 2 * high + low)
+    meta = jnp.where(slot == 0, c, jnp.where(slot == 3, (place >> 2) & 1, ranks)).astype(jnp.int32)
     trig = jnp.asarray(trig_tables())
 
     packed = jnp.concatenate(
@@ -740,12 +768,12 @@
     out_far = swap(out_weight)
 
     first, second = norm_call(tokens, small)
-    send, act, hg, fb = ff_call(meta, second, out_grad, fc_weight, fc_far, proj_weight, proj_far, small)
-    got = swap(send)
+    send, act, hg, fb = ff_call(
+        meta, second, out_grad, fc_weight, fc_far, proj_weight, proj_far, small
+    )
+    ff_got = swap(send)
     own = ff_own_call(tie(meta, send), second, out_grad, act, hg)
-
     att = {}
-    sets = {}
     bits = rest_bits(reps)
 
     def attend(j, rel, *wait):
@@ -756,35 +784,34 @@
         )
         return att[j, rel][4]
 
-    def rest(total, name):
-        for bit in bits[2:]:
+    def rest(total, start, name):
+        for bit in bits[start:]:
             (total,) = sum_call([total, exchange(total, reps, bit, bit)], 1, name)
         return total
 
-    keep, send = sum_call([own, got], 2, "ff_pair")
+    keep, send = sum_call([own, ff_got], 2, "ff_pair")
     got = exchange(send, reps, 1, 2)
     mark = attend(0, 1, keep)
     keep, send = sum_call([tie(keep, mark), got], 2, "ff_sum0")
     got = exchange(send, reps, 2, 1)
     mark = attend(0, 0, keep)
-    rows = keep.shape[1]
-    part = (1, rows // 4, keep.shape[2])
-    pieces = along_call(functools.partial(along_kernel, 2), meta, [tie(keep, mark), got], [part] * 4, "ff_sum1")
-    got = along(pieces[1:], reps)
-    c_own, c_got = att[0, 0][0], swap(att[0, 0][1])
-    mark = attend(1, 1, *pieces)
-    (piece,) = sum_call([tie(pieces[0], mark), *got], 1, "ff_sum2")
-    piece = rest(piece, "ff_sum3")
-    pieces = [piece, *along([piece] * 3, reps)]
-    c_keep, c_send = sum_call([tie(c_own, mark), c_got], 2, "att_pair")
-    c_got = exchange(c_send, reps, 1, 2)
-    mark = attend(1, 0, piece, c_keep)
-
-    d_own, d_got = att[1, 0][0], swap(att[1, 0][1])
-    (ff_total,) = along_call(join_kernel, meta, [tie(pieces[0], mark), *pieces[1:]], [keep[:1].shape], "ff_join")
-    ff_pieces = [ff_total, exchange(ff_total, reps, 2, 1), exchange(ff_total, reps, 1, 2)]
-    c_keep, c_send = sum_call([tie(c_keep, mark), c_got], 2, "att_sum0")
-    c_got = exchange(c_send, reps, 2, 1)
+    whole = keep.shape
+    half = (1, whole[1] // 2, whole[2])
+    keep, send = half_call(half_kernel, meta, [tie(keep, mark), got], [half] * 2, "ff_sum1")
+    got = exchange(send, reps, bits[0], bits[0])
+    own, others = [att[0, 0][0]], [swap(att[0, 0][1])]
+    mark = attend(1, 1, keep)
+    (piece,) = sum_call([tie(keep, mark), got], 1, "ff_sum2")
+    ff_got = exchange(piece, reps, bits[1], bits[1])
+    mark = attend(1, 0, piece, others[0])
+
+    (piece,) = sum_call([tie(piece, mark), ff_got], 1, "ff_sum3")
+    piece = rest(piece, 2, "ff_sum4")
+    ff_got = exchange(piece, reps, bits[0], bits[0])
+    own.append(att[1, 0][0])
+    others.append(swap(tie(att[1, 0][1], piece)))
+    chunks = pair_call(own, others, "att_pair")
+    got = crosses(chunks[1:], reps)
 
     keys = [(0, 0), (0, 1), (1, 0), (1, 1)]
     give = lambda part, before, *wait: output_call(
@@ -806,66 +833,67 @@
         fb,
         before,
     )
-    done = give(0, None, ff_total, c_keep)
-    mark = done[2]
-    d_keep, d_send = sum_call([tie(d_own, mark), d_got], 2, "att_pair")
-    d_got = exchange(d_send, reps, 1, 2)
-    (c_total,) = sum_call([tie(c_keep, mark), c_got], 1, "att_sum1")
-    c_got = along([c_total] * 3, reps)
-    ff_pieces.append(exchange(tie(ff_pieces[2], mark), reps, 2, 1))
-    layer_out, tokens_grad, small_own, small_send = give(1, done, d_keep, c_total, *ff_pieces[1:3])
-
-    (c_total,) = sum_call([tie(c_total, small_own), *c_got], 1, "att_sum2")
-    c_total = rest(c_total, "att_sum3")
-    d_keep, d_send = sum_call([tie(d_keep, c_total), d_got], 2, "att_sum0")
-    d_got = exchange(d_send, reps, 2, 1)
-    (total,) = sum_call([tie(small_own, d_keep), swap(small_send)], 1, "small_pair")
-    (d_total,) = sum_call([tie(d_keep, total), d_got], 1, "att_sum1")
-    d_got = along([d_total] * 3, reps)
-    ff_last = tie(ff_pieces[3], d_total)
-    c_pieces = [c_total, exchange(tie(c_total, ff_last), reps, 2, 1), exchange(tie(c_total, ff_last), reps, 1, 2)]
+    done = give(0, None, piece, chunks[0])
+    (att_total,) = sum_call([tie(chunks[0], done[2]), *got], 1, "att_sum0")
+    got = exchange(att_total, reps, bits[0], bits[0])
+    (ff_total,) = half_call(join_kernel, meta, [tie(piece, att_total), ff_got], [whole], "ff_join")
+    ff_pieces = [ff_total, exchange(ff_total, reps, 2, 1), exchange(ff_total, reps, 1, 2)]
+    layer_out, tokens_grad, small_own, small_send = give(1, done, att_total, ff_total)
+
+    (att_total,) = sum_call([tie(att_total, small_own, *ff_pieces[1:]), got], 1, "att_sum1")
+    got = exchange(att_total, reps, bits[1], bits[1])
+    ff_pieces.append(exchange(tie(ff_pieces[2], att_total), reps, 2, 1))
+    (total,) = sum_call([tie(small_own, att_total), swap(small_send)], 1, "small_pair")
+    small_got = exchange(total, reps, 1, 1)
 
     view = lambda a: a.reshape(2, 512, 512)
-    proj_adam = adam_call(
+    adam_ff = lambda start, pieces, before, *wait: adam_call(
         adam_ff_kernel,
-        tie(meta, total, d_total, ff_last),
-        [*ff_pieces[:3], ff_last],
+        tie(meta, *wait),
+        start,
+        pieces,
         [view(a) for a in (mean_proj_weight, square_proj_weight, proj_weight)],
         [mean_fc_weight, square_fc_weight, fc_weight],
-        pl.BlockSpec((2, 128, 512), lambda q, m: (0, q, 0)),
-        pl.BlockSpec((64, 2048), lambda q, m: (q, 0)),
-        "adam_ff",
-    )
-    a_proj = [a.reshape(1024, 512) for a in proj_adam[:4]]
-    a_fc = proj_adam[4:]
-
-    (d_total,) = sum_call([tie(d_total, a_fc[0], *c_pieces[1:]), *d_got], 1, "att_sum4")
-    d_total = rest(d_total, "att_sum5")
-    d_pieces = [d_total, *crosses([d_total] * 3, reps)]
-    c_pieces.append(exchange(tie(c_pieces[2], d_total), reps, 2, 1))
-    total = tie(total, d_total)
-    for bit in (1, 2, *bits):
-        if bit == bits[-1]:
-            total = tie(total, *c_pieces[1:], *d_pieces[1:])
-        (total,) = sum_call([total, exchange(total, reps, bit, bit)], 1, "small_sum")
+        ((2, 128, 512), lambda q: (0, q, 0)),
+        ((64, 2048), lambda q: (q, 0)),
+        f"adam_ff_{start}",
+        before,
+    )
+    a_ff = adam_ff(0, ff_pieces[:3], (), total, att_total)
+    (total,) = sum_call([tie(total, a_ff[4]), small_got], 1, "small_sum")
+    small_got = exchange(total, reps, 2, 2)
+    (att_total,) = sum_call([tie(att_total, total), got], 1, "att_sum2")
+    att_total = rest(att_total, 2, "att_sum3")
+    att_pieces = [att_total, *crosses([att_total] * 3, reps)]
+    a_ff = adam_ff(3, ff_pieces[3:], a_ff, att_total)
+    (total,) = sum_call([tie(total, a_ff[4]), small_got], 1, "small_sum")
+    (total,) = sum_call([total, exchange(total, reps, bits[0], bits[0])], 1, "small_sum")
+    mark = tie(total, *att_pieces[1:])
+    small_got = exchange(mark, reps, bits[1], bits[1])
+
+    view_o = lambda a: a.reshape(2, 128, 512)
+    qkv_adam = adam_call(
+        adam_qkv_kernel,
+        tie(meta, mark),
+        0,
+        att_pieces,
+        [mean_qkv_weight, square_qkv_weight, qkv_weight],
+        [view_o(a) for a in (mean_out_weight, square_out_weight, out_weight)],
+        ((64, 1536), lambda q: (q, 0)),
+        ((2, 32, 512), lambda q: (0, q, 0)),
+        "adam_qkv",
+    )
+    a_proj = [a.reshape(1024, 512) for a in a_ff[:4]]
+    a_fc = a_ff[4:]
+    a_qkv = qkv_adam[:4]
+    a_out = [a.reshape(256, 512) for a in qkv_adam[4:]]
+    (total,) = sum_call([tie(mark, a_out[0]), small_got], 1, "small_sum")
+    total = rest(total, 2, "small_sum")
     flat = total.reshape(32, 128)
     g_vec = flat[:12].reshape(6, 256)
     g_qb = flat[12:18].reshape(768)
     g_fb = flat[18:26].reshape(1024)
 
-    view_o = lambda a: a.reshape(2, 128, 512)
-    qkv_adam = adam_call(
-        adam_qkv_kernel,
-        meta,
-        [*c_pieces, *d_pieces],
-        [mean_qkv_weight, square_qkv_weight, qkv_weight],
-        [view_o(a) for a in (mean_out_weight, square_out_weight, out_weight)],
-        pl.BlockSpec((64, 1536), lambda q, m: (q, 0)),
-        pl.BlockSpec((2, 32, 512), lambda q, m: (0, q, 0)),
-        "adam_qkv",
-    )
-    a_qkv = qkv_adam[:4]
-    a_out = [a.reshape(256, 512) for a in qkv_adam[4:]]
     a_vec = (g_vec, *adamw(g_vec, mean_vectors, square_vectors, vectors))
     a_qb = (g_qb, *adamw(g_qb, mean_qkv_bias, square_qkv_bias, qkv_bias))
     a_fb = (g_fb, *adamw(g_fb, mean_fc_bias, square_fc_bias, fc_bias))

time: 237 us -> 214 us (0.903)
  starting transfers between devices: 43.3 us -> 27.5 us
  local copies, waits for them, and re-layouts: 14.6 us -> 5.73 us
  Pallas kernels: 157 us -> 162 us
  waiting for transfers between devices: 13.5 us -> 11.1 us
    ppermute x31 -> x20, starting transfers between devices: 42.1 us -> 26.2 us  [exchange(): return lax.ppermute(a, ('rep', 'opt'), pairs)]
    unnamed x78 -> x60, local copies, waits for them, and re-layouts: 13.2 us -> 4.97 us
    pallas_call x4 -> x6, Pallas kernels: 21.8 us -> 26.2 us  [the longest x3 24.7 us: adam_call(): pl.pallas_call(run, grid_spec=grid_spec, out_shape=outs, input_output_ali...]
    ppermute x31 -> x20, waiting for transfers between devices: 10.7 us -> 6.98 us  [exchange(): return lax.ppermute(a, ('rep', 'opt'), pairs)]
    pallas_call x1, Pallas kernels: 7.17 us -> 9.85 us  [ff_own_call(): pl.pallas_call(ff_own_kernel, grid_spec=grid_spec, out_shape=jax.ShapeDty...]
  transfers between devices with their start and end apart: 39 -> 28, of which waited for: 6 -> 5; matrix products, arithmetic and copies ran while one was open for 1% -> 1% of each run, Pallas kernels for 55% -> 63%
where the time goes in v4:
time: 214 us; the launch traced here: 213 us
  Pallas kernels  162 us (76%)
  starting transfers between devices  27.5 us (13%)
  waiting for transfers between devices  11.1 us (5%)
  local copies, waits for them, and re-layouts  5.73 us (3%)
  blocking collectives  2.64 us (1%)
  other arithmetic  2.58 us (1%)
    pallas_call x4, Pallas kernels, attention_call(): pl.pallas_call(functools.partial(attention_kernel, j, rel), grid_spec=gri...  70.6 us
    pallas_call x1, Pallas kernels, ff_call(): pl.pallas_call(ff_kernel, grid_spec=grid_spec, out_shape=[jax.ShapeDtypeS...  27 us
    ppermute x20, starting transfers between devices, exchange(): return lax.ppermute(a, ('rep', 'opt'), pairs)  26.2 us
    pallas_call x2, Pallas kernels, output_call(): pl.pallas_call(functools.partial(output_kernel, part, parts), grid_spec=g...  25.2 us
    pallas_call x3, Pallas kernels, adam_call(): pl.pallas_call(run, grid_spec=grid_spec, out_shape=outs, input_output_ali...  24.7 us
    pallas_call x1, Pallas kernels, ff_own_call(): pl.pallas_call(ff_own_kernel, grid_spec=grid_spec, out_shape=jax.ShapeDty...  9.85 us
    ppermute x20, waiting for transfers between devices, exchange(): return lax.ppermute(a, ('rep', 'opt'), pairs)  6.98 us
    unnamed x60, local copies, waits for them, and re-layouts  4.97 us
  transfers between devices with their start and end apart: 28, of which 5 were waited for; matrix products, arithmetic and copies ran while one was open for 1% of the time, Pallas kernels for 63%

profile of v4, /device:TPU:0, one launch (start us, length us, event | category | flops | bytes accessed | tf_op | source)
XLA Modules:
  0.0 213.1 jit_solution(2830693138565373509)
XLA Ops:
  0.7 0.6 collective-permute-start.1
  1.2 0.1 collective-permute-start
  1.3 0.7 reshape.135
  2.0 0.7 maximum_bitcast_fusion
  2.7 2.6 %all-gather = bf16[2,26,128]{2,1,0:T(8,128)(2,1)S(1)} all-gather(bf16[1,26,128]{2,1,0:T(8,128)(2,1)S(1)} %maximum_bitcast_fusion), channel_id=1, replica_groups=mesh['rep'=16,'opt'=2] {'opt'}, dimensions={0}, use_global_device_ids=true | all-gather | bytes 19968 | tf_op jit(solution)/shard_map/all_gather | solution.py:764
  5.4 1.6 copy-done.1
  7.0 1.9 norm.1
  9.0 1.2 copy-done.3
  10.2 1.2 copy-done.5
  11.4 27.0 %feed_forward.1 = (bf16[4,64,4096]{2,1,0:T(8,128)(2,1)S(1)}, bf16[2048,2048]{1,0:T(8,128)(2,1)}, bf16[2048,2048]{1,0:T(8,128)(2,1)}, f32[4,1,512]{2,1,0:T(1,128)S(1)}) custom-call(s32[4]{0:T(128)S(1)} %compare_select_fusion.2.meta.meta_ref, bf16[2048,512]{1,0:T(8,128)(2,1)S(1)} %get-tuple-element.122.second_ref, bf16[2048,512]{1,0:T(8,128)(2,1)S(1)} %copy-done, ...), custom_call_target="tpu_custom_call" | custom-call | flops 12884901888 | bytes 20971520 | tf_op jit(solution)/shard_map/feed_forward/pallas_call | solution.py:185
  38.5 0.3 collective-permute-start.2
  38.8 0.2 collective-permute-start.3
  39.0 9.9 %feed_forward_own.1.refs_0_ = bf16[4,64,4096]{2,1,0:T(8,128)(2,1)S(1)} custom-call(s32[4]{0:T(128)S(1)} %compare_select_fusion.2.meta.meta_ref, bf16[2048,512]{1,0:T(8,128)(2,1)S(1)} %get-tuple-element.122.second_ref, bf16[2048,512]{1,0:T(8,128)(2,1)S(1)} %copy-done, bf16[2048,2048]{1,0:T(8,128)(2,1)} %get-tuple-element.125.act_ref, ...), custom_call_target="tpu_custom_call" | custom-call | flops 4294967296 | bytes 16777216 | tf_op jit(solution)/shard_map/feed_forward_own/pallas_call | solution.py:216
  48.8 0.0 copy-start.12
  48.9 0.5 ff_pair.1
  49.4 2.9 %collective-permute-start.5 = (bf16[2,64,4096]{2,1,0:T(8,128)(2,1)S(1)}, bf16[2,64,4096]{2,1,0:T(8,128)(2,1)S(1)}, u32[]{:S(2)}, u32[]{:S(2)}) collective-permute-start(bf16[2,64,4096]{2,1,0:T(8,128)(2,1)S(1)} %get-tuple-element.132), channel_id=1, source_target_pairs={{0,2},{1,5},{2,0},{3,7},{4,6},{5,1},{6,4},{7,3},{8,10},{9,13},{10,... | collective-permute-start | bytes 3145736 | tf_op jit(solution)/shard_map/ppermute | solution.py:616
  52.3 1.5 collective-permute-done.4.ow_ref.refs_9_
  53.8 17.6 %attention_01.1 = (bf16[4,64,384]{2,1,0:T(8,128)(2,1)S(1)}, bf16[4,64,640]{2,1,0:T(8,128)(2,1)S(1)}, bf16[2048,384]{1,0:T(8,128)(2,1)S(1)}, bf16[2048,128]{1,0:T(8,128)(2,1)S(1)}, f32[1,384]{1,0:T(1,128)S(1)}) custom-call(s32[4]{0:T(128)S(1)} %compare_select_fusion.2.meta.meta_ref, bf16[2048,512]{1,0:T(8,128)(2,1)S(1)} %get-tuple-element.129.first_ref, ...), custom_call_target="tpu_custom_call" | custom-call | flops 5368709120 | bytes 6291456 | tf_op jit(solution)/shard_map/attention_01/pallas_call | solution.py:384
  71.4 0.3 ff_sum0.1
  71.6 1.6 collective-permute-start.6
  73.3 17.7 %attention_00.1 = (bf16[4,64,1024]{2,1,0:T(8,128)(2,1)S(1)}, bf16[4,64,1024]{2,1,0:T(8,128)(2,1)S(1)}, bf16[2048,384]{1,0:T(8,128)(2,1)S(1)}, bf16[2048,128]{1,0:T(8,128)(2,1)S(1)}, f32[1,384]{1,0:T(1,128)S(1)}) custom-call(s32[4]{0:T(128)S(1)} %compare_select_fusion.2.meta.meta_ref, bf16[2048,512]{1,0:T(8,128)(2,1)S(1)} %get-tuple-element.129.first_ref, ...), custom_call_target="tpu_custom_call" | custom-call | flops 5368709120 | bytes 6291456 | tf_op jit(solution)/shard_map/attention_00/pallas_call | solution.py:384
  91.0 0.1 collective-permute-start.8
  91.1 0.7 ff_sum1.1
  91.8 1.6 collective-permute-start.7
  93.4 17.6 %attention_11.1 = (bf16[4,64,384]{2,1,0:T(8,128)(2,1)S(1)}, bf16[4,64,640]{2,1,0:T(8,128)(2,1)S(1)}, bf16[2048,384]{1,0:T(8,128)(2,1)S(1)}, bf16[2048,128]{1,0:T(8,128)(2,1)S(1)}, f32[1,384]{1,0:T(1,128)S(1)}) custom-call(s32[4]{0:T(128)S(1)} %compare_select_fusion.2.meta.meta_ref, bf16[2048,512]{1,0:T(8,128)(2,1)S(1)} %get-tuple-element.129.first_ref, ...), custom_call_target="tpu_custom_call" | custom-call | flops 5368709120 | bytes 6291456 | tf_op jit(solution)/shard_map/attention_11/pallas_call | solution.py:384
  111.0 0.1 ff_sum2.1.refs_0_
  111.0 2.6 %collective-permute-start.9 = (bf16[1,32,4096]{2,1,0:T(8,128)(2,1)S(1)}, bf16[1,32,4096]{2,1,0:T(8,128)(2,1)S(1)}, u32[]{:S(2)}, u32[]{:S(2)}) collective-permute-start(bf16[1,32,4096]{2,1,0:T(8,128)(2,1)S(1)} %ff_sum2.1.refs_0_), channel_id=1, source_target_pairs={{0,16},{1,17},{2,18},{3,19},{4,20},{5,21},{6,22},{7,23},{8,24},{9,... | collective-permute-start | bytes 786440 | tf_op jit(solution)/shard_map/ppermute | solution.py:616
  113.7 17.8 %attention_10.1 = (bf16[4,64,1024]{2,1,0:T(8,128)(2,1)S(1)}, bf16[4,64,1024]{2,1,0:T(8,128)(2,1)S(1)}, bf16[2048,384]{1,0:T(8,128)(2,1)S(1)}, bf16[2048,128]{1,0:T(8,128)(2,1)S(1)}, f32[1,384]{1,0:T(1,128)S(1)}) custom-call(s32[4]{0:T(128)S(1)} %compare_select_fusion.2.meta.meta_ref, bf16[2048,512]{1,0:T(8,128)(2,1)S(1)} %get-tuple-element.129.first_ref, ...), custom_call_target="tpu_custom_call" | custom-call | flops 5368709120 | bytes 6291456 | tf_op jit(solution)/shard_map/attention_10/pallas_call | solution.py:384
  131.5 0.1 ff_sum3.1.mine_ref
  131.6 0.1 collective-permute-start.10
  131.7 0.5 collective-permute-start.14
  132.2 1.4 collective-permute-done.10.refs_3_
  133.6 0.3 att_pair.1
  133.8 0.6 collective-permute-start.11
  134.4 1.3 collective-permute-start.12
  135.8 1.6 collective-permute-start.13
  137.4 12.6 %outputs_0.1 = (bf16[2048,512]{1,0:T(8,128)(2,1)}, bf16[2048,512]{1,0:T(8,128)(2,1)}, f32[5,8,512]{2,1,0:T(8,128)S(1)}) custom-call(s32[4]{0:T(128)S(1)} %compare_select_fusion.2.meta.meta_ref, bf16[2048,512]{1,0:T(8,128)(2,1)S(1)} %copy-done.2, bf16[2048,512]{1,0:T(8,128)(2,1)S(1)} %copy-done, bf16[2048,2048]{1,0:T(8,128)(2,1)} %get-tuple-element.125.act_ref, ...), custom_call_target="tpu_custom_call" | custom-call | flops 6442450944 | bytes 20971520 | tf_op jit(solution)/shard_map/outputs_0/pallas_call | solution.py:527
  150.0 0.1 att_sum0.1.refs_0_
  150.1 0.5 collective-permute-start.17
  150.6 0.6 ff_join.1.refs_0_
  151.2 0.6 collective-permute-start.16
  151.9 1.3 collective-permute-start.15
  153.2 12.7 %outputs_1.1 = (bf16[2048,512]{1,0:T(8,128)(2,1)}, bf16[2048,512]{1,0:T(8,128)(2,1)}, f32[32,1,128]{2,1,0:T(1,128)S(1)}, f32[32,1,128]{2,1,0:T(1,128)S(1)}) custom-call(s32[4]{0:T(128)S(1)} %compare_select_fusion.2.meta.meta_ref, bf16[2048,512]{1,0:T(8,128)(2,1)S(1)} %copy-done.2, ...), custom_call_target="tpu_custom_call", output_to_operand_aliasing={{0}: (28, {}), {1}: (29, {})} | custom-call | flops 6442450944 | bytes 20971520 | tf_op jit(solution)/shard_map/outputs_1/pallas_call | solution.py:527
  165.9 0.1 att_sum1.1.refs_0_
  165.9 0.8 collective-permute-start.21
  166.7 0.3 collective-permute-start.20
  167.0 1.2 collective-permute-done.18.refs_1_
  168.3 1.6 collective-permute-start.19
  169.8 10.8 %adam_ff_0.1 = (f32[2,512,512]{2,1,0:T(8,128)}, f32[2,512,512]{2,1,0:T(8,128)}, f32[2,512,512]{2,1,0:T(8,128)}, f32[2,512,512]{2,1,0:T(8,128)}, f32[256,2048]{1,...) custom-call(s32[4]{0:T(128)} %copy-done.11, bf16[1,64,4096]{2,1,0:T(8,128)(2,1)} %copy-done.9, ...), custom_call_target="tpu_custom_call" | custom-call | flops 15728640 | bytes 22020096 | tf_op jit(solution)/shard_map/adam_ff_0/pallas_call | solution.py:716
  180.7 0.1 att_sum2.1.refs_0_
  180.8 1.4 collective-permute-start.26
  182.2 0.6 collective-permute-start.25
  182.8 1.6 collective-permute-start.24
  184.4 0.5 collective-permute-start.22
  184.8 0.8 copy-done.14
  185.6 5.5 %adam_ff_3.1 = (f32[2,512,512]{2,1,0:T(8,128)}, f32[2,512,512]{2,1,0:T(8,128)}, f32[2,512,512]{2,1,0:T(8,128)}, f32[2,512,512]{2,1,0:T(8,128)}, f32[256,2048]{1,...) custom-call(s32[4]{0:T(128)} %copy-done.11, ...), custom_call_target="tpu_custom_call", output_to_operand_aliasing={{0}: (1, {}), {1}: (2, {}), {2}: (3, {}), {3}: (4, {}), {4}... | custom-call | flops 5242880 | bytes 7340032 | tf_op jit(solution)/shard_map/adam_ff_3/pallas_call | solution.py:716
  191.1 4.7 %collective-permute-done.22.refs_1_ = f32[32,1,128]{2,1,0:T(1,128)S(1)} collective-permute-done((f32[32,1,128]{2,1,0:T(1,128)S(1)}, f32[32,1,128]{2,1,0:T(1,128)S(1)}, u32[]{:S(2)}, u32[]{:S(2)}) %collective-permute-start.22) | collective-permute-done | bytes 16416 | tf_op jit(solution)/shard_map/ppermute | solution.py:616
  195.8 1.6 collective-permute-start.23
  197.4 2.2 %collective-permute-done.23.refs_1_ = f32[32,1,128]{2,1,0:T(1,128)S(1)} collective-permute-done((f32[32,1,128]{2,1,0:T(1,128)S(1)}, f32[32,1,128]{2,1,0:T(1,128)S(1)}, u32[]{:S(2)}, u32[]{:S(2)}) %collective-permute-start.23) | collective-permute-done | bytes 16416 | tf_op jit(solution)/shard_map/ppermute | solution.py:616
  199.7 2.6 %collective-permute-start.27 = (f32[32,1,128]{2,1,0:T(1,128)S(1)}, f32[32,1,128]{2,1,0:T(1,128)S(1)}, u32[]{:S(2)}, u32[]{:S(2)}) collective-permute-start(f32[32,1,128]{2,1,0:T(1,128)S(1)} %small_sum.6.refs_0_), channel_id=1, source_target_pairs={{0,16},{1,17},{2,18},{3,19},{4,20},{5,21},{6,22},{7,23},{8,24},{9,... | collective-permute-start | bytes 49160 | tf_op jit(solution)/shard_map/ppermute | solution.py:616
  202.5 8.4 %adam_qkv.1 = (f32[256,1536]{1,0:T(8,128)}, f32[256,1536]{1,0:T(8,128)}, f32[256,1536]{1,0:T(8,128)}, f32[256,1536]{1,0:T(8,128)}, f32[2,128,512]{2,1,0:T(8,128)...) custom-call(s32[4]{0:T(128)} %copy-done.11, bf16[1,64,2048]{2,1,0:T(8,128)(2,1)} %copy-done.10, ...), custom_call_target="tpu_custom_call" | custom-call | flops 10485760 | bytes 14680064 | tf_op jit(solution)/shard_map/adam_qkv/pallas_call | solution.py:716
  211.0 0.6 add_multiply_fusion.1
  211.7 0.6 add_multiply_fusion.2
  212.3 0.6 add_multiply_fusion
  (91 shorter events, 0.4 us)
Async XLA Ops:
  0.7 8.3 %copy-start = (bf16[2048,512]{1,0:T(8,128)(2,1)S(1)}, bf16[2048,512]{1,0:T(8,128)(2,1)}, u32[]{:S(2)}) copy-start(bf16[2048,512]{1,0:T(8,128)(2,1)} %grad_ref.15) | copy-start | bytes 6291460
  0.7 8.3 %collective-permute-start.1 = (bf16[1024,512]{1,0:T(8,128)(2,1)}, bf16[1024,512]{1,0:T(8,128)(2,1)S(1)}, u32[]{:S(2)}, u32[]{:S(2)}) collective-permute-start(bf16[1024,512]{1,0:T(8,128)(2,1)} %refs_10_.3), channel_id=1, source_target_pairs={{0,1},{1,0},{2,3},{3,2},{4,5},{5,4},{6,7},{7,6},{8,9},{9,8},{10,11... | collective-permute-start | bytes 3145736 | tf_op jit(solution)/shard_map/ppermute | solution.py:620
  1.2 7.7 %collective-permute-start = (bf16[256,2048]{1,0:T(8,128)(2,1)}, bf16[256,2048]{1,0:T(8,128)(2,1)}, u32[]{:S(2)}, u32[]{:S(2)}) collective-permute-start(bf16[256,2048]{1,0:T(8,128)(2,1)} %refs_14_.5), channel_id=1, source_target_pairs={{0,1},{1,0},{2,3},{3,2},{4,5},{5,4},{6,7},{7,6},{8,9},{9,8},{10,11... | collective-permute-start | bytes 3145736 | tf_op jit(solution)/shard_map/ppermute | solution.py:620
  5.4 1.6 copy-start.1
  8.9 144.2 %copy-start.11 = (s32[4]{0:T(128)}, s32[4]{0:T(128)S(1)}, u32[]{:S(2)}) copy-start(s32[4]{0:T(128)S(1)} %compare_select_fusion.2.meta.meta_ref) | copy-start | bytes 52
  9.0 1.2 copy-start.3
  10.2 1.2 copy-start.5
  11.4 27.4 %copy-start.7 = (bf16[256,1536]{1,0:T(8,128)(2,1)S(1)}, bf16[256,1536]{1,0:T(8,128)(2,1)}, u32[]{:S(2)}) copy-start(bf16[256,1536]{1,0:T(8,128)(2,1)} %refs_6_.3) | copy-start | bytes 2359300
  38.5 10.4 %collective-permute-start.2 = (bf16[4,64,4096]{2,1,0:T(8,128)(2,1)S(1)}, bf16[4,64,4096]{2,1,0:T(8,128)(2,1)S(1)}, u32[]{:S(2)}, u32[]{:S(2)}) collective-permute-start(bf16[4,64,4096]{2,1,0:T(8,128)(2,1)S(1)} %get-tuple-element.123), channel_id=1, source_target_pairs={{0,1},{1,0},{2,3},{3,2},{4,5},{5,4},{6,7},{7,6},{8,9},{9,8},{10,11... | collective-permute-start | bytes 6291464 | tf_op jit(solution)/shard_map/ppermute | solution.py:620
  38.8 15.0 %collective-permute-start.3 = (bf16[256,1536]{1,0:T(8,128)(2,1)S(1)}, bf16[256,1536]{1,0:T(8,128)(2,1)S(1)}, u32[]{:S(2)}, u32[]{:S(2)}) collective-permute-start(bf16[256,1536]{1,0:T(8,128)(2,1)S(1)} %copy-done.7), channel_id=1, source_target_pairs={{0,1},{1,0},{2,3},{3,2},{4,5},{5,4},{6,7},{7,6},{8,9},{9,8},{10,11... | collective-permute-start | bytes 2359304 | tf_op jit(solution)/shard_map/ppermute | solution.py:620
  48.8 3.4 %copy-start.8 = (bf16[256,512]{1,0:T(8,128)(2,1)S(1)}, bf16[256,512]{1,0:T(8,128)(2,1)}, u32[]{:S(2)}) copy-start(bf16[256,512]{1,0:T(8,128)(2,1)} %refs_8_.4) | copy-start | bytes 786436
  48.8 5.0 %copy-start.12 = (f32[2,8,512]{2,1,0:T(8,128)S(1)}, f32[2,8,512]{2,1,0:T(8,128)}, u32[]{:S(2)}) copy-start(f32[2,8,512]{2,1,0:T(8,128)} %constant.31.clone.trig_ref) | copy-start | bytes 98308
  49.4 22.0 %collective-permute-start.5 = (bf16[2,64,4096]{2,1,0:T(8,128)(2,1)S(1)}, bf16[2,64,4096]{2,1,0:T(8,128)(2,1)S(1)}, u32[]{:S(2)}, u32[]{:S(2)}) collective-permute-start(bf16[2,64,4096]{2,1,0:T(8,128)(2,1)S(1)} %get-tuple-element.132), channel_id=1, source_target_pairs={{0,2},{1,5},{2,0},{3,7},{4,6},{5,1},{6,4},{7,3},{8,10},{9,13},{10,... | collective-permute-start | bytes 3145736 | tf_op jit(solution)/shard_map/ppermute | solution.py:616
  52.3 1.5 collective-permute-start.4
  71.6 19.5 %collective-permute-start.6 = (bf16[1,64,4096]{2,1,0:T(8,128)(2,1)S(1)}, bf16[1,64,4096]{2,1,0:T(8,128)(2,1)S(1)}, u32[]{:S(2)}, u32[]{:S(2)}) collective-permute-start(bf16[1,64,4096]{2,1,0:T(8,128)(2,1)S(1)} %get-tuple-element.140), channel_id=1, source_target_pairs={{0,4},{1,3},{2,6},{3,1},{4,0},{5,7},{6,2},{7,5},{8,12},{9,11},{10,... | collective-permute-start | bytes 1572872 | tf_op jit(solution)/shard_map/ppermute | solution.py:616
  91.0 22.7 %collective-permute-start.8 = (bf16[4,64,1024]{2,1,0:T(8,128)(2,1)S(1)}, bf16[4,64,1024]{2,1,0:T(8,128)(2,1)S(1)}, u32[]{:S(2)}, u32[]{:S(2)}) collective-permute-start(bf16[4,64,1024]{2,1,0:T(8,128)(2,1)S(1)} %get-tuple-element.146), channel_id=1, source_target_pairs={{0,1},{1,0},{2,3},{3,2},{4,5},{5,4},{6,7},{7,6},{8,9},{9,8},{10,11... | collective-permute-start | bytes 1572872 | tf_op jit(solution)/shard_map/ppermute | solution.py:620
  91.8 19.2 %collective-permute-start.7 = (bf16[1,32,4096]{2,1,0:T(8,128)(2,1)S(1)}, bf16[1,32,4096]{2,1,0:T(8,128)(2,1)S(1)}, u32[]{:S(2)}, u32[]{:S(2)}) collective-permute-start(bf16[1,32,4096]{2,1,0:T(8,128)(2,1)S(1)} %get-tuple-element.145), channel_id=1, source_target_pairs={{0,8},{1,9},{2,10},{3,11},{4,12},{5,13},{6,14},{7,15},{8,0},{9,1},... | collective-permute-start | bytes 786440 | tf_op jit(solution)/shard_map/ppermute | solution.py:616
  111.0 20.5 %collective-permute-start.9 = (bf16[1,32,4096]{2,1,0:T(8,128)(2,1)S(1)}, bf16[1,32,4096]{2,1,0:T(8,128)(2,1)S(1)}, u32[]{:S(2)}, u32[]{:S(2)}) collective-permute-start(bf16[1,32,4096]{2,1,0:T(8,128)(2,1)S(1)} %ff_sum2.1.refs_0_), channel_id=1, source_target_pairs={{0,16},{1,17},{2,18},{3,19},{4,20},{5,21},{6,22},{7,23},{8,24},{9,... | collective-permute-start | bytes 786440 | tf_op jit(solution)/shard_map/ppermute | solution.py:616
  113.7 23.7 %copy-start.4 = (bf16[256,2048]{1,0:T(8,128)(2,1)S(1)}, bf16[256,2048]{1,0:T(8,128)(2,1)}, u32[]{:S(2)}) copy-start(bf16[256,2048]{1,0:T(8,128)(2,1)} %refs_14_.5) | copy-start | bytes 3145732
  113.7 23.7 %copy-start.6 = (bf16[1024,512]{1,0:T(8,128)(2,1)S(1)}, bf16[1024,512]{1,0:T(8,128)(2,1)}, u32[]{:S(2)}) copy-start(bf16[1024,512]{1,0:T(8,128)(2,1)} %refs_10_.3) | copy-start | bytes 3145732
  131.5 5.9 %copy-start.2 = (bf16[2048,512]{1,0:T(8,128)(2,1)S(1)}, bf16[2048,512]{1,0:T(8,128)(2,1)}, u32[]{:S(2)}) copy-start(bf16[2048,512]{1,0:T(8,128)(2,1)} %tok_ref.5) | copy-start | bytes 6291460
  131.6 2.0 collective-permute-start.10
  131.7 19.0 %collective-permute-start.14 = (bf16[1,32,4096]{2,1,0:T(8,128)(2,1)S(1)}, bf16[1,32,4096]{2,1,0:T(8,128)(2,1)S(1)}, u32[]{:S(2)}, u32[]{:S(2)}) collective-permute-start(bf16[1,32,4096]{2,1,0:T(8,128)(2,1)S(1)} %ff_sum3.1.mine_ref), channel_id=1, source_target_pairs={{0,8},{1,9},{2,10},{3,11},{4,12},{5,13},{6,14},{7,15},{8,0},{9,1},... | collective-permute-start | bytes 786440 | tf_op jit(solution)/shard_map/ppermute | solution.py:616
  133.8 16.1 %collective-permute-start.11 = (bf16[1,64,2048]{2,1,0:T(8,128)(2,1)S(1)}, bf16[1,64,2048]{2,1,0:T(8,128)(2,1)S(1)}, u32[]{:S(2)}, u32[]{:S(2)}) collective-permute-start(bf16[1,64,2048]{2,1,0:T(8,128)(2,1)S(1)} %get-tuple-element.168), channel_id=1, source_target_pairs={{0,4},{1,3},{2,6},{3,1},{4,0},{5,7},{6,2},{7,5},{8,12},{9,11},{10,... | collective-permute-start | bytes 786440 | tf_op jit(solution)/shard_map/ppermute | solution.py:616
  134.4 15.5 %collective-permute-start.12 = (bf16[1,64,2048]{2,1,0:T(8,128)(2,1)S(1)}, bf16[1,64,2048]{2,1,0:T(8,128)(2,1)S(1)}, u32[]{:S(2)}, u32[]{:S(2)}) collective-permute-start(bf16[1,64,2048]{2,1,0:T(8,128)(2,1)S(1)} %get-tuple-element.169), channel_id=1, source_target_pairs={{0,2},{1,5},{2,0},{3,7},{4,6},{5,1},{6,4},{7,3},{8,10},{9,13},{10,... | collective-permute-start | bytes 786440 | tf_op jit(solution)/shard_map/ppermute | solution.py:616
  135.8 14.2 %collective-permute-start.13 = (bf16[1,64,2048]{2,1,0:T(8,128)(2,1)S(1)}, bf16[1,64,2048]{2,1,0:T(8,128)(2,1)S(1)}, u32[]{:S(2)}, u32[]{:S(2)}) collective-permute-start(bf16[1,64,2048]{2,1,0:T(8,128)(2,1)S(1)} %get-tuple-element.170), channel_id=1, source_target_pairs={{0,6},{1,7},{2,4},{3,5},{4,2},{5,3},{6,0},{7,1},{8,14},{9,15},{10,... | collective-permute-start | bytes 786440 | tf_op jit(solution)/shard_map/ppermute | solution.py:616
  150.1 15.8 %collective-permute-start.17 = (bf16[1,64,2048]{2,1,0:T(8,128)(2,1)S(1)}, bf16[1,64,2048]{2,1,0:T(8,128)(2,1)S(1)}, u32[]{:S(2)}, u32[]{:S(2)}) collective-permute-start(bf16[1,64,2048]{2,1,0:T(8,128)(2,1)S(1)} %att_sum0.1.refs_0_), channel_id=1, source_target_pairs={{0,8},{1,9},{2,10},{3,11},{4,12},{5,13},{6,14},{7,15},{8,0},{9,1},... | collective-permute-start | bytes 786440 | tf_op jit(solution)/shard_map/ppermute | solution.py:616
  151.2 14.6 %copy-start.9 = (bf16[1,64,4096]{2,1,0:T(8,128)(2,1)}, bf16[1,64,4096]{2,1,0:T(8,128)(2,1)S(1)}, u32[]{:S(2)}) copy-start(bf16[1,64,4096]{2,1,0:T(8,128)(2,1)S(1)} %ff_join.1.refs_0_) | copy-start | bytes 1572868
  151.2 14.6 %collective-permute-start.16 = (bf16[1,64,4096]{2,1,0:T(8,128)(2,1)S(1)}, bf16[1,64,4096]{2,1,0:T(8,128)(2,1)}, u32[]{:S(2)}, u32[]{:S(2)}) collective-permute-start(bf16[1,64,4096]{2,1,0:T(8,128)(2,1)S(1)} %ff_join.1.refs_0_), channel_id=1, source_target_pairs={{0,2},{1,5},{2,0},{3,7},{4,6},{5,1},{6,4},{7,3},{8,10},{9,13},{10,... | collective-permute-start | bytes 1572872 | tf_op jit(solution)/shard_map/ppermute | solution.py:616
  151.9 14.0 %collective-permute-start.15 = (bf16[1,64,4096]{2,1,0:T(8,128)(2,1)S(1)}, bf16[1,64,4096]{2,1,0:T(8,128)(2,1)S(1)}, u32[]{:S(2)}, u32[]{:S(2)}) collective-permute-start(bf16[1,64,4096]{2,1,0:T(8,128)(2,1)S(1)} %ff_join.1.refs_0_), channel_id=1, source_target_pairs={{0,4},{1,3},{2,6},{3,1},{4,0},{5,7},{6,2},{7,5},{8,12},{9,11},{10,... | collective-permute-start | bytes 1572872 | tf_op jit(solution)/shard_map/ppermute | solution.py:616
  165.9 2.4 %copy-start.13 = (bf16[1,64,4096]{2,1,0:T(8,128)(2,1)}, bf16[1,64,4096]{2,1,0:T(8,128)(2,1)S(1)}, u32[]{:S(2)}) copy-start(bf16[1,64,4096]{2,1,0:T(8,128)(2,1)S(1)} %collective-permute-done.15.refs_1_) | copy-start | bytes 1572868
  165.9 18.9 %collective-permute-start.21 = (bf16[1,64,4096]{2,1,0:T(8,128)(2,1)}, bf16[1,64,4096]{2,1,0:T(8,128)(2,1)S(1)}, u32[]{:S(2)}, u32[]{:S(2)}) collective-permute-start(bf16[1,64,4096]{2,1,0:T(8,128)(2,1)} %collective-permute-done.16.refs_2_), channel_id=1, source_target_pairs={{0,4},{1,3},{2,6},{3,1},{4,0},{5,7},{6,2},{7,5},{8,12},{9,11},{10,... | collective-permute-start | bytes 1572872 | tf_op jit(solution)/shard_map/ppermute | solution.py:616
  166.7 14.0 %collective-permute-start.20 = (bf16[1,64,2048]{2,1,0:T(8,128)(2,1)S(1)}, bf16[1,64,2048]{2,1,0:T(8,128)(2,1)S(1)}, u32[]{:S(2)}, u32[]{:S(2)}) collective-permute-start(bf16[1,64,2048]{2,1,0:T(8,128)(2,1)S(1)} %att_sum1.1.refs_0_), channel_id=1, source_target_pairs={{0,16},{1,17},{2,18},{3,19},{4,20},{5,21},{6,22},{7,23},{8,24},{9,... | collective-permute-start | bytes 786440 | tf_op jit(solution)/shard_map/ppermute | solution.py:616
  167.0 1.2 collective-permute-start.18
  168.3 12.4 %collective-permute-start.19 = (f32[32,1,128]{2,1,0:T(1,128)S(1)}, f32[32,1,128]{2,1,0:T(1,128)S(1)}, u32[]{:S(2)}, u32[]{:S(2)}) collective-permute-start(f32[32,1,128]{2,1,0:T(1,128)S(1)} %small_pair.1.refs_0_), channel_id=1, source_target_pairs={{0,2},{1,3},{2,0},{3,1},{4,6},{5,7},{6,4},{7,5},{8,10},{9,11},{10,... | collective-permute-start | bytes 49160 | tf_op jit(solution)/shard_map/ppermute | solution.py:616
  180.8 10.3 %copy-start.10 = (bf16[1,64,2048]{2,1,0:T(8,128)(2,1)}, bf16[1,64,2048]{2,1,0:T(8,128)(2,1)S(1)}, u32[]{:S(2)}) copy-start(bf16[1,64,2048]{2,1,0:T(8,128)(2,1)S(1)} %att_sum2.1.refs_0_) | copy-start | bytes 786436
  180.8 18.9 %collective-permute-start.26 = (bf16[1,64,2048]{2,1,0:T(8,128)(2,1)S(1)}, bf16[1,64,2048]{2,1,0:T(8,128)(2,1)S(1)}, u32[]{:S(2)}, u32[]{:S(2)}) collective-permute-start(bf16[1,64,2048]{2,1,0:T(8,128)(2,1)S(1)} %att_sum2.1.refs_0_), channel_id=1, source_target_pairs={{0,6},{1,7},{2,4},{3,5},{4,2},{5,3},{6,0},{7,1},{8,14},{9,15},{10,... | collective-permute-start | bytes 786440 | tf_op jit(solution)/shard_map/ppermute | solution.py:616
  182.2 17.5 %collective-permute-start.25 = (bf16[1,64,2048]{2,1,0:T(8,128)(2,1)S(1)}, bf16[1,64,2048]{2,1,0:T(8,128)(2,1)S(1)}, u32[]{:S(2)}, u32[]{:S(2)}) collective-permute-start(bf16[1,64,2048]{2,1,0:T(8,128)(2,1)S(1)} %att_sum2.1.refs_0_), channel_id=1, source_target_pairs={{0,2},{1,5},{2,0},{3,7},{4,6},{5,1},{6,4},{7,3},{8,10},{9,13},{10,... | collective-permute-start | bytes 786440 | tf_op jit(solution)/shard_map/ppermute | solution.py:616
  182.8 16.9 %collective-permute-start.24 = (bf16[1,64,2048]{2,1,0:T(8,128)(2,1)S(1)}, bf16[1,64,2048]{2,1,0:T(8,128)(2,1)S(1)}, u32[]{:S(2)}, u32[]{:S(2)}) collective-permute-start(bf16[1,64,2048]{2,1,0:T(8,128)(2,1)S(1)} %att_sum2.1.refs_0_), channel_id=1, source_target_pairs={{0,4},{1,3},{2,6},{3,1},{4,0},{5,7},{6,2},{7,5},{8,12},{9,11},{10,... | collective-permute-start | bytes 786440 | tf_op jit(solution)/shard_map/ppermute | solution.py:616
  184.4 11.5 %collective-permute-start.22 = (f32[32,1,128]{2,1,0:T(1,128)S(1)}, f32[32,1,128]{2,1,0:T(1,128)S(1)}, u32[]{:S(2)}, u32[]{:S(2)}) collective-permute-start(f32[32,1,128]{2,1,0:T(1,128)S(1)} %small_sum.4.refs_0_), channel_id=1, source_target_pairs={{0,4},{1,5},{2,6},{3,7},{4,0},{5,1},{6,2},{7,3},{8,12},{9,13},{10,... | collective-permute-start | bytes 49160 | tf_op jit(solution)/shard_map/ppermute | solution.py:616
  184.8 0.8 copy-start.14
  195.8 3.8 %collective-permute-start.23 = (f32[32,1,128]{2,1,0:T(1,128)S(1)}, f32[32,1,128]{2,1,0:T(1,128)S(1)}, u32[]{:S(2)}, u32[]{:S(2)}) collective-permute-start(f32[32,1,128]{2,1,0:T(1,128)S(1)} %small_sum.5.refs_0_), channel_id=1, source_target_pairs={{0,8},{1,9},{2,10},{3,11},{4,12},{5,13},{6,14},{7,15},{8,0},{9,1},... | collective-permute-start | bytes 49160 | tf_op jit(solution)/shard_map/ppermute | solution.py:616
  199.7 2.7 %copy-start.15 = (bf16[1,64,2048]{2,1,0:T(8,128)(2,1)}, bf16[1,64,2048]{2,1,0:T(8,128)(2,1)S(1)}, u32[]{:S(2)}) copy-start(bf16[1,64,2048]{2,1,0:T(8,128)(2,1)S(1)} %collective-permute-done.26.refs_3_) | copy-start | bytes 786436
  199.7 2.7 %copy-start.16 = (bf16[1,64,2048]{2,1,0:T(8,128)(2,1)}, bf16[1,64,2048]{2,1,0:T(8,128)(2,1)S(1)}, u32[]{:S(2)}) copy-start(bf16[1,64,2048]{2,1,0:T(8,128)(2,1)S(1)} %collective-permute-done.25.refs_2_) | copy-start | bytes 786436
  199.7 2.6 %copy-start.17 = (bf16[1,64,2048]{2,1,0:T(8,128)(2,1)}, bf16[1,64,2048]{2,1,0:T(8,128)(2,1)S(1)}, u32[]{:S(2)}) copy-start(bf16[1,64,2048]{2,1,0:T(8,128)(2,1)S(1)} %collective-permute-done.24.refs_1_) | copy-start | bytes 786436
  199.7 11.1 %collective-permute-start.27 = (f32[32,1,128]{2,1,0:T(1,128)S(1)}, f32[32,1,128]{2,1,0:T(1,128)S(1)}, u32[]{:S(2)}, u32[]{:S(2)}) collective-permute-start(f32[32,1,128]{2,1,0:T(1,128)S(1)} %small_sum.6.refs_0_), channel_id=1, source_target_pairs={{0,16},{1,17},{2,18},{3,19},{4,20},{5,21},{6,22},{7,23},{8,24},{9,... | collective-permute-start | bytes 49160 | tf_op jit(solution)/shard_map/ppermute | solution.py:616
  202.4 8.7 %copy-start.24 = (bf16[1024]{0:T(1024)(128)(2,1)S(1)}, bf16[1024]{0:T(1024)(128)(2,1)}, u32[]{:S(2)}) copy-start(bf16[1024]{0:T(1024)(128)(2,1)} %param.31) | copy-start | bytes 6148
  202.4 8.7 %copy-start.26 = (f32[1024]{0:T(1024)S(1)}, f32[1024]{0:T(1024)}, u32[]{:S(2)}) copy-start(f32[1024]{0:T(1024)} %param.38) | copy-start | bytes 12292
  202.4 8.7 %copy-start.27 = (f32[1024]{0:T(1024)S(1)}, f32[1024]{0:T(1024)}, u32[]{:S(2)}) copy-start(f32[1024]{0:T(1024)} %param.45) | copy-start | bytes 12292
  202.4 9.3 %copy-start.25 = (bf16[768]{0:T(1024)(128)(2,1)S(1)}, bf16[768]{0:T(1024)(128)(2,1)}, u32[]{:S(2)}) copy-start(bf16[768]{0:T(1024)(128)(2,1)} %param.28) | copy-start | bytes 4612
  202.4 9.3 %copy-start.28 = (f32[768]{0:T(1024)S(1)}, f32[768]{0:T(1024)}, u32[]{:S(2)}) copy-start(f32[768]{0:T(1024)} %param.35) | copy-start | bytes 9220
  202.4 9.2 %copy-start.29 = (f32[768]{0:T(1024)S(1)}, f32[768]{0:T(1024)}, u32[]{:S(2)}) copy-start(f32[768]{0:T(1024)} %param.42) | copy-start | bytes 9220
  202.4 9.9 %copy-start.21 = (bf16[6,256]{1,0:T(8,128)(2,1)S(1)}, bf16[6,256]{1,0:T(8,128)(2,1)}, u32[]{:S(2)}) copy-start(bf16[6,256]{1,0:T(8,128)(2,1)} %param.26) | copy-start | bytes 9220
  202.4 9.9 %copy-start.22 = (f32[6,256]{1,0:T(8,128)S(1)}, f32[6,256]{1,0:T(8,128)}, u32[]{:S(2)}) copy-start(f32[6,256]{1,0:T(8,128)} %param.33) | copy-start | bytes 18436
  202.5 9.8 %copy-start.23 = (f32[6,256]{1,0:T(8,128)S(1)}, f32[6,256]{1,0:T(8,128)}, u32[]{:S(2)}) copy-start(f32[6,256]{1,0:T(8,128)} %param.40) | copy-start | bytes 18436
  210.9 2.0 copy-start.19
  210.9 2.0 copy-start.20
  211.0 1.9 copy-start.18

commit v5 on v4

--- a/solution.py
+++ b/solution.py
@@ -107,18 +107,21 @@
     fc = fc_ref[...]
     base = o * SMALL_ROWS + 18 + 4 * j
     bias = jnp.concatenate([small_ref[base + k] for k in range(cols // 128)], 1)
-    tile = 256
+    sub, parts = 256, 4
+    tile = sub * parts
 
     def block(i, total):
-        r = pl.ds(pl.multiple_of(i * tile, tile), tile)
-        hidden = dot_nn(second_ref[r, :], fc) + bias
-        act_grad = dot_nt(grad_ref[r, :], proj)
-        phi_cap = 0.5 + 0.5 * lax.erf(hidden * INV_ROOT_TWO)
-        slope = phi_cap + hidden * (jnp.exp(-0.5 * hidden * hidden) * INV_ROOT_TWO_PI)
-        act_ref[r, :] = (hidden * phi_cap).astype(bf16)
-        hg = (act_grad * slope).astype(bf16)
-        hg_ref[r, :] = hg
-        return total + jnp.sum(hg.astype(f32).reshape(tile // 8, 8, cols), 0)
+        at = [pl.ds(pl.multiple_of(i * tile + k * sub, sub), sub) for k in range(parts)]
+        products = [(dot_nn(second_ref[r, :], fc), dot_nt(grad_ref[r, :], proj)) for r in at]
+        for r, (product, act_grad) in zip(at, products):
+            hidden = product + bias
+            phi_cap = 0.5 + 0.5 * lax.erf(hidden * INV_ROOT_TWO)
+            slope = phi_cap + hidden * (jnp.exp(-0.5 * hidden * hidden) * INV_ROOT_TWO_PI)
+            act_ref[r, :] = (hidden * phi_cap).astype(bf16)
+            hg = (act_grad * slope).astype(bf16)
+            hg_ref[r, :] = hg
+            total += jnp.sum(hg.astype(f32).reshape(sub // 8, 8, cols), 0)
+        return total
 
     total = lax.fori_loop(0, rows // tile, block, jnp.zeros((8, cols), f32))
     bias_ref[...] = jnp.sum(total, 0, keepdims=True)[None]
@@ -273,38 +276,44 @@
     col_id = lax.broadcasted_iota(jnp.int32, (hl, hl), 1)
     keep = row_id <= col_id
     zeros = jnp.zeros((64, LEN), bf16)
+    def pad(u, h):
+        return jnp.concatenate([u, zeros], 0) if h == 0 else jnp.concatenate([zeros, u], 0)
+
+    def open_chunk(h, t):
+        hs, ts, n = slice(64 * h, 64 * h + 64), slice(hl * t, hl * t + hl), hl * (t + 1)
+        return dot_nn(k_tok[:n], pad(q_t[hs], h)[:, ts]), dot_nn(v_tok[:n], pad(da_t[hs], h)[:, ts])
+
+    def close_chunk(h, t, score, pg):
+        hs, ts, n = slice(64 * h, 64 * h + 64), slice(hl * t, hl * t + hl), hl * (t + 1)
+        qh, kh, vh, dah = q_t[hs], k_t[hs], v_t[hs], da_t[hs]
+        diag = jnp.where(keep, score[n - hl :], -1e30)
+        score = diag if t == 0 else jnp.concatenate([score[:hl], diag], 0)
+        exps = jnp.exp(score - jnp.max(score, 0, keepdims=True))
+        prob = exps * (1.0 / jnp.sum(exps, 0, keepdims=True))
+        prob_b = prob.astype(bf16)
+        sg = (prob * (pg - jnp.sum(pg * prob, 0, keepdims=True))).astype(bf16)
+        return (
+            dot_nn(vh[:, :n], prob_b),
+            dot_nn(kh[:, :n], sg),
+            dot_nt(dah[:, ts], prob_b),
+            dot_nt(qh[:, ts], sg),
+        )
+
+    chunks = [(h, t) for h in range(2) for t in range(2)]
+    ahead = 4
+    opened = [open_chunk(*k) for k in chunks[:ahead]]
+    closed = {}
+    for i, k in enumerate(chunks):
+        if i + ahead < len(chunks):
+            opened.append(open_chunk(*chunks[i + ahead]))
+        closed[k] = close_chunk(*k, *opened[i])
     att, dq, dk, dv = [], [], [], []
     for h in range(2):
-        hs = slice(64 * h, 64 * h + 64)
-        qh, kh, vh, dah = q_t[hs], k_t[hs], v_t[hs], da_t[hs]
-        pad = (lambda u: jnp.concatenate([u, zeros], 0)) if h == 0 else (lambda u: jnp.concatenate([zeros, u], 0))
-        qz, daz = pad(qh), pad(dah)
-        att_h, dq_h = [], []
-        dk_h = dv_h = None
-        for t in range(2):
-            ts = slice(hl * t, hl * t + hl)
-            n = hl * (t + 1)
-            score = dot_nn(k_tok[:n], qz[:, ts])
-            diag = jnp.where(keep, score[n - hl :], -1e30)
-            score = diag if t == 0 else jnp.concatenate([score[:hl], diag], 0)
-            exps = jnp.exp(score - jnp.max(score, 0, keepdims=True))
-            prob = exps * (1.0 / jnp.sum(exps, 0, keepdims=True))
-            prob_b = prob.astype(bf16)
-            att_h.append(dot_nn(vh[:, :n], prob_b))
-            pg = dot_nn(v_tok[:n], daz[:, ts])
-            sg = (prob * (pg - jnp.sum(pg * prob, 0, keepdims=True))).astype(bf16)
-            dq_h.append(dot_nn(kh[:, :n], sg))
-            dv_t = dot_nt(dah[:, ts], prob_b)
-            dk_t = dot_nt(qh[:, ts], sg)
-            if t == 0:
-                dv_h, dk_h = dv_t, dk_t
-            else:
-                dv_h = jnp.concatenate([dv_h + dv_t[:, :hl], dv_t[:, hl:]], 1)
-                dk_h = jnp.concatenate([dk_h + dk_t[:, :hl], dk_t[:, hl:]], 1)
-        att.append(jnp.concatenate(att_h, 1))
-        dq.append(jnp.concatenate(dq_h, 1) * 0.125)
-        dk.append(dk_h)
-        dv.append(dv_h)
+        (a0, q0, v0, k0), (a1, q1, v1, k1) = closed[h, 0], closed[h, 1]
+        att.append(jnp.concatenate([a0, a1], 1))
+        dq.append(jnp.concatenate([q0, q1], 1) * 0.125)
+        dk.append(jnp.concatenate([k0 + k1[:, :hl], k1[:, hl:]], 1))
+        dv.append(jnp.concatenate([v0 + v1[:, :hl], v1[:, hl:]], 1))
     att_t = jnp.concatenate(att, 0).astype(bf16)
     dq_t = rotate_rows(jnp.concatenate(dq, 0), cosine, -sine)
     dk_t = rotate_rows(jnp.concatenate(dk, 0), cosine, -sine)
@@ -661,39 +670,43 @@
 def adam_ff_kernel(meta, *refs):
     pieces, proj, fc, proj_out, fc_out = refs[:-14], refs[-14:-11], refs[-11:-8], refs[-8:-4], refs[-4:]
     which = pl.program_id(0)
-    quarter = fc[0].shape[0]
+    n = fc[0].shape[0]
+    rows = pl.ds(pl.multiple_of(pl.program_id(1) * n, n), n)
     for j in range(2):
         for k in range(2):
-            at = (j, slice(k * quarter, (k + 1) * quarter), slice(None))
             col = 1024 * j + 512 * k
-            adam_block(pick(pieces, which, slice(col, col + 512)), *proj, *proj_out, at)
+            at = (j, 0, k, slice(None), slice(None))
+            adam_block(pick(pieces, which, slice(col, col + 512), rows), *proj, *proj_out, at)
             at = (slice(None), slice(col, col + 512))
-            adam_block(pick(pieces, which, slice(2048 + col, 2048 + col + 512)), *fc, *fc_out, at)
+            adam_block(pick(pieces, which, slice(2048 + col, 2048 + col + 512), rows), *fc, *fc_out, at)
 
 
 def adam_qkv_kernel(meta, *refs):
     pieces, qkv, out, qkv_out, out_out = refs[:-14], refs[-14:-11], refs[-11:-8], refs[-8:-4], refs[-4:]
     c = meta[0]
     which = pl.program_id(0)
-    quarter = qkv[0].shape[0]
-    hq = quarter // 2
+    sub = pl.program_id(1)
+    n = qkv[0].shape[0]
+    h = out[0].shape[1]
+    rows = pl.ds(pl.multiple_of(sub * n, n), n)
     for j in range(2):
         for slot in range(2):
             for p in range(3):
                 col = 1024 * j + 384 * slot + 128 * p
-                grad = pick(pieces, which, slice(col, col + 128))
+                grad = pick(pieces, which, slice(col, col + 128), rows)
                 lanes = pl.ds(pl.multiple_of((p * 4 + (slot ^ c) * 2 + j) * 128, 128), 128)
                 adam_block(grad, *qkv, *qkv_out, (slice(None), lanes))
         for k in range(2):
             col = 1024 * j + 768
-            grad = pick(pieces, which, slice(col, col + 256), slice(k * hq, (k + 1) * hq))
+            half = pl.ds(pl.multiple_of(k * (pieces[0].shape[1] // 2) + sub * h, h), h)
+            grad = pick(pieces, which, slice(col, col + 256), half)
             adam_block(grad, *out, *out_out, (j, slice(None), slice(256 * k, 256 * k + 256)))
 
 
-def adam_call(kernel, meta, start, pieces, first, second, first_spec, second_spec, name, before=()):
+def adam_call(kernel, meta, start, pieces, first, second, first_spec, second_spec, subs, name, before=()):
     outs = [jax.ShapeDtypeStruct(first[0].shape, f32)] * 4 + [jax.ShapeDtypeStruct(second[0].shape, f32)] * 4
     specs = [
-        pl.BlockSpec(shape, functools.partial(lambda at, i, m: at((start + i) ^ m[1]), at))
+        pl.BlockSpec(shape, functools.partial(lambda at, i, k, m: at((start + i) ^ m[1], k), at))
         for shape, at in (first_spec, second_spec)
     ]
     count = len(before)
@@ -703,7 +716,7 @@
 
     grid_spec = pltpu.PrefetchScalarGridSpec(
         num_scalar_prefetch=1,
-        grid=(len(pieces),),
+        grid=(len(pieces), subs),
         in_specs=[
             *[pl.BlockSpec(memory_space=pl.ANY)] * count,
             *[full_spec(a.shape) for a in pieces],
@@ -846,7 +859,7 @@
     (total,) = sum_call([tie(small_own, att_total), swap(small_send)], 1, "small_pair")
     small_got = exchange(total, reps, 1, 1)
 
-    view = lambda a: a.reshape(2, 512, 512)
+    view = lambda a: a.reshape(2, 4, 2, 64, 512)
     adam_ff = lambda start, pieces, before, *wait: adam_call(
         adam_ff_kernel,
         tie(meta, *wait),
@@ -854,9 +867,24 @@
         pieces,
         [view(a) for a in (mean_proj_weight, square_proj_weight, proj_weight)],
         [mean_fc_weight, square_fc_weight, fc_weight],
-        ((2, 128, 512), lambda q: (0, q, 0)),
-        ((64, 2048), lambda q: (q, 0)),
+        ((2, 1, 2, 64, 512), lambda q, k: (0, q, 0, k, 0)),
+        ((64, 2048), lambda q, k: (q + k, 0)),
+        1,
         f"adam_ff_{start}",
+        before,
+    )
+    view_o = lambda a: a.reshape(2, 128, 512)
+    adam_qkv = lambda start, pieces, before, *wait: adam_call(
+        adam_qkv_kernel,
+        tie(meta, *wait),
+        start,
+        pieces,
+        [mean_qkv_weight, square_qkv_weight, qkv_weight],
+        [view_o(a) for a in (mean_out_weight, square_out_weight, out_weight)],
+        ((64, 1536), lambda q, k: (q + k, 0)),
+        ((2, 32, 512), lambda q, k: (0, q + k, 0)),
+        1,
+        f"adam_qkv_{start}",
         before,
     )
     a_ff = adam_ff(0, ff_pieces[:3], (), total, att_total)
@@ -867,26 +895,17 @@
     att_pieces = [att_total, *crosses([att_total] * 3, reps)]
     a_ff = adam_ff(3, ff_pieces[3:], a_ff, att_total)
     (total,) = sum_call([tie(total, a_ff[4]), small_got], 1, "small_sum")
-    (total,) = sum_call([total, exchange(total, reps, bits[0], bits[0])], 1, "small_sum")
+    small_got = exchange(total, reps, bits[0], bits[0])
+    a_qkv = adam_qkv(0, att_pieces[:1], (), total)
+    (total,) = sum_call([tie(total, a_qkv[0]), small_got], 1, "small_sum")
     mark = tie(total, *att_pieces[1:])
     small_got = exchange(mark, reps, bits[1], bits[1])
 
-    view_o = lambda a: a.reshape(2, 128, 512)
-    qkv_adam = adam_call(
-        adam_qkv_kernel,
-        tie(meta, mark),
-        0,
-        att_pieces,
-        [mean_qkv_weight, square_qkv_weight, qkv_weight],
-        [view_o(a) for a in (mean_out_weight, square_out_weight, out_weight)],
-        ((64, 1536), lambda q: (q, 0)),
-        ((2, 32, 512), lambda q: (0, q, 0)),
-        "adam_qkv",
-    )
+    a_qkv = adam_qkv(1, att_pieces[1:], a_qkv, mark)
     a_proj = [a.reshape(1024, 512) for a in a_ff[:4]]
     a_fc = a_ff[4:]
-    a_qkv = qkv_adam[:4]
-    a_out = [a.reshape(256, 512) for a in qkv_adam[4:]]
+    a_out = [a.reshape(256, 512) for a in a_qkv[4:]]
+    a_qkv = a_qkv[:4]
     (total,) = sum_call([tie(mark, a_out[0]), small_got], 1, "small_sum")
     total = rest(total, 2, "small_sum")
     flat = total.reshape(32, 128)

time: 214 us -> 189 us (0.88)
  Pallas kernels: 162 us -> 139 us
    pallas_call x4, Pallas kernels: 70.6 us -> 46.1 us  [attention_call(): pl.pallas_call(functools.partial(attention_kernel, j, rel), grid_spec=gri...]
    pallas_call x3 -> x4, Pallas kernels: 24.7 us -> 27.5 us  [adam_call(): pl.pallas_call(run, grid_spec=grid_spec, out_shape=outs, input_output_ali...]
  transfers between devices with their start and end apart: 28 -> 28, of which waited for: 5 -> 5; matrix products, arithmetic and copies ran while one was open for 1% -> 1% of each run, Pallas kernels for 63% -> 60%
where the time goes in v5:
time: 189 us
  Pallas kernels  139 us (74%)
  starting transfers between devices  27.5 us (15%)
  waiting for transfers between devices  9.81 us (5%)
  local copies, waits for them, and re-layouts  5.73 us (3%)
  blocking collectives  2.64 us (1%)
  other arithmetic  2.58 us (1%)
    pallas_call x4, Pallas kernels, attention_call(): pl.pallas_call(functools.partial(attention_kernel, j, rel), grid_spec=gri...  46.1 us
    pallas_call x4, Pallas kernels, adam_call(): pl.pallas_call(run, grid_spec=grid_spec, out_shape=outs, input_output_ali...  27.5 us
    ppermute x20, starting transfers between devices, exchange(): return lax.ppermute(a, ('rep', 'opt'), pairs)  26.2 us
    pallas_call x1, Pallas kernels, ff_call(): pl.pallas_call(ff_kernel, grid_spec=grid_spec, out_shape=[jax.ShapeDtypeS...  25.7 us
    pallas_call x2, Pallas kernels, output_call(): pl.pallas_call(functools.partial(output_kernel, part, parts), grid_spec=g...  25.2 us
    pallas_call x1, Pallas kernels, ff_own_call(): pl.pallas_call(ff_own_kernel, grid_spec=grid_spec, out_shape=jax.ShapeDty...  9.86 us
    ppermute x20, waiting for transfers between devices, exchange(): return lax.ppermute(a, ('rep', 'opt'), pairs)  5.26 us
    unnamed x60, local copies, waits for them, and re-layouts  4.97 us
  transfers between devices with their start and end apart: 28, of which 5 were waited for; matrix products, arithmetic and copies ran while one was open for 1% of the time, Pallas kernels for 60%

profile of v5, /device:TPU:0, one launch (start us, length us, event | category | flops | bytes accessed | tf_op | source)
XLA Modules:
  0.0 188.8 jit_solution(12456576809241562353)
XLA Ops:
  0.7 0.6 collective-permute-start.1
  1.2 0.1 collective-permute-start
  1.3 0.7 reshape.138
  2.0 0.7 maximum_bitcast_fusion
  2.7 2.6 %all-gather = bf16[2,26,128]{2,1,0:T(8,128)(2,1)S(1)} all-gather(bf16[1,26,128]{2,1,0:T(8,128)(2,1)S(1)} %maximum_bitcast_fusion), channel_id=1, replica_groups=mesh['rep'=16,'opt'=2] {'opt'}, dimensions={0}, use_global_device_ids=true | all-gather | bytes 19968 | tf_op jit(solution)/shard_map/all_gather | solution.py:777
  5.4 1.6 copy-done.1
  7.0 1.9 %norm.1 = (bf16[2048,512]{1,0:T(8,128)(2,1)S(1)}, bf16[2048,512]{1,0:T(8,128)(2,1)S(1)}) custom-call(bf16[2048,512]{1,0:T(8,128)(2,1)S(1)} %copy-done.1, f32[52,1,128]{2,1,0:T(1,128)S(1)} %reshape.167.small_ref.refs_16_), custom_call_target="tpu_custom_call" | custom-call | flops 20971520 | bytes 6291456 | tf_op jit(solution)/shard_map/norm/pallas_call | solution.py:79
  9.0 1.2 copy-done.3
  10.2 1.2 copy-done.5
  11.4 25.7 %feed_forward.1 = (bf16[4,64,4096]{2,1,0:T(8,128)(2,1)S(1)}, bf16[2048,2048]{1,0:T(8,128)(2,1)}, bf16[2048,2048]{1,0:T(8,128)(2,1)}, f32[4,1,512]{2,1,0:T(1,128)S(1)}) custom-call(s32[4]{0:T(128)S(1)} %compare_select_fusion.2.meta.meta_ref, bf16[2048,512]{1,0:T(8,128)(2,1)S(1)} %get-tuple-element.132.second_ref, bf16[2048,512]{1,0:T(8,128)(2,1)S(1)} %copy-done, ...), custom_call_target="tpu_custom_call" | custom-call | flops 12884901888 | bytes 20971520 | tf_op jit(solution)/shard_map/feed_forward/pallas_call | solution.py:188
  37.2 0.4 collective-permute-start.2
  37.5 0.1 collective-permute-start.3
  37.7 9.9 %feed_forward_own.1.refs_0_ = bf16[4,64,4096]{2,1,0:T(8,128)(2,1)S(1)} custom-call(s32[4]{0:T(128)S(1)} %compare_select_fusion.2.meta.meta_ref, bf16[2048,512]{1,0:T(8,128)(2,1)S(1)} %get-tuple-element.132.second_ref, bf16[2048,512]{1,0:T(8,128)(2,1)S(1)} %copy-done, bf16[2048,2048]{1,0:T(8,128)(2,1)} %get-tuple-element.135.act_ref, ...), custom_call_target="tpu_custom_call" | custom-call | flops 4294967296 | bytes 16777216 | tf_op jit(solution)/shard_map/feed_forward_own/pallas_call | solution.py:219
  47.6 0.5 ff_pair.1
  48.1 2.9 %collective-permute-start.5 = (bf16[2,64,4096]{2,1,0:T(8,128)(2,1)S(1)}, bf16[2,64,4096]{2,1,0:T(8,128)(2,1)S(1)}, u32[]{:S(2)}, u32[]{:S(2)}) collective-permute-start(bf16[2,64,4096]{2,1,0:T(8,128)(2,1)S(1)} %get-tuple-element.142), channel_id=1, source_target_pairs={{0,2},{1,5},{2,0},{3,7},{4,6},{5,1},{6,4},{7,3},{8,10},{9,13},{10,... | collective-permute-start | bytes 3145736 | tf_op jit(solution)/shard_map/ppermute | solution.py:625
  51.0 1.5 collective-permute-done.4.ow_ref.refs_9_
  52.5 11.4 %attention_01.1 = (bf16[4,64,384]{2,1,0:T(8,128)(2,1)S(1)}, bf16[4,64,640]{2,1,0:T(8,128)(2,1)S(1)}, bf16[2048,384]{1,0:T(8,128)(2,1)S(1)}, bf16[2048,128]{1,0:T(8,128)(2,1)S(1)}, f32[1,384]{1,0:T(1,128)S(1)}) custom-call(s32[4]{0:T(128)S(1)} %compare_select_fusion.2.meta.meta_ref, bf16[2048,512]{1,0:T(8,128)(2,1)S(1)} %get-tuple-element.139.first_ref, ...), custom_call_target="tpu_custom_call" | custom-call | flops 5368709120 | bytes 6291456 | tf_op jit(solution)/shard_map/attention_01/pallas_call | solution.py:393
  64.0 0.3 ff_sum0.1
  64.2 1.9 %collective-permute-start.6 = (bf16[1,64,4096]{2,1,0:T(8,128)(2,1)S(1)}, bf16[1,64,4096]{2,1,0:T(8,128)(2,1)S(1)}, u32[]{:S(2)}, u32[]{:S(2)}) collective-permute-start(bf16[1,64,4096]{2,1,0:T(8,128)(2,1)S(1)} %get-tuple-element.150), channel_id=1, source_target_pairs={{0,4},{1,3},{2,6},{3,1},{4,0},{5,7},{6,2},{7,5},{8,12},{9,11},{10,... | collective-permute-start | bytes 1572872 | tf_op jit(solution)/shard_map/ppermute | solution.py:625
  66.1 11.6 %attention_00.1 = (bf16[4,64,1024]{2,1,0:T(8,128)(2,1)S(1)}, bf16[4,64,1024]{2,1,0:T(8,128)(2,1)S(1)}, bf16[2048,384]{1,0:T(8,128)(2,1)S(1)}, bf16[2048,128]{1,0:T(8,128)(2,1)S(1)}, f32[1,384]{1,0:T(1,128)S(1)}) custom-call(s32[4]{0:T(128)S(1)} %compare_select_fusion.2.meta.meta_ref, bf16[2048,512]{1,0:T(8,128)(2,1)S(1)} %get-tuple-element.139.first_ref, ...), custom_call_target="tpu_custom_call" | custom-call | flops 5368709120 | bytes 6291456 | tf_op jit(solution)/shard_map/attention_00/pallas_call | solution.py:393
  77.8 0.1 collective-permute-start.8
  77.9 0.7 ff_sum1.1
  78.5 1.6 collective-permute-start.7
  80.2 11.4 %attention_11.1 = (bf16[4,64,384]{2,1,0:T(8,128)(2,1)S(1)}, bf16[4,64,640]{2,1,0:T(8,128)(2,1)S(1)}, bf16[2048,384]{1,0:T(8,128)(2,1)S(1)}, bf16[2048,128]{1,0:T(8,128)(2,1)S(1)}, f32[1,384]{1,0:T(1,128)S(1)}) custom-call(s32[4]{0:T(128)S(1)} %compare_select_fusion.2.meta.meta_ref, bf16[2048,512]{1,0:T(8,128)(2,1)S(1)} %get-tuple-element.139.first_ref, ...), custom_call_target="tpu_custom_call" | custom-call | flops 5368709120 | bytes 6291456 | tf_op jit(solution)/shard_map/attention_11/pallas_call | solution.py:393
  91.6 0.1 ff_sum2.1.refs_0_
  91.7 2.7 %collective-permute-start.9 = (bf16[1,32,4096]{2,1,0:T(8,128)(2,1)S(1)}, bf16[1,32,4096]{2,1,0:T(8,128)(2,1)S(1)}, u32[]{:S(2)}, u32[]{:S(2)}) collective-permute-start(bf16[1,32,4096]{2,1,0:T(8,128)(2,1)S(1)} %ff_sum2.1.refs_0_), channel_id=1, source_target_pairs={{0,16},{1,17},{2,18},{3,19},{4,20},{5,21},{6,22},{7,23},{8,24},{9,... | collective-permute-start | bytes 786440 | tf_op jit(solution)/shard_map/ppermute | solution.py:625
  94.4 11.7 %attention_10.1 = (bf16[4,64,1024]{2,1,0:T(8,128)(2,1)S(1)}, bf16[4,64,1024]{2,1,0:T(8,128)(2,1)S(1)}, bf16[2048,384]{1,0:T(8,128)(2,1)S(1)}, bf16[2048,128]{1,0:T(8,128)(2,1)S(1)}, f32[1,384]{1,0:T(1,128)S(1)}) custom-call(s32[4]{0:T(128)S(1)} %compare_select_fusion.2.meta.meta_ref, bf16[2048,512]{1,0:T(8,128)(2,1)S(1)} %get-tuple-element.139.first_ref, ...), custom_call_target="tpu_custom_call" | custom-call | flops 5368709120 | bytes 6291456 | tf_op jit(solution)/shard_map/attention_10/pallas_call | solution.py:393
  106.0 0.5 collective-permute-done.9.refs_1_
  106.6 0.1 ff_sum3.1.mine_ref
  106.7 0.1 collective-permute-start.10
  106.8 0.0 collective-permute-start.14
  106.8 1.8 collective-permute-done.10.refs_3_
  108.6 0.3 att_pair.1
  108.9 0.5 collective-permute-start.11
  109.4 1.5 collective-permute-start.12
  111.0 1.5 collective-permute-start.13
  112.5 12.6 %outputs_0.1 = (bf16[2048,512]{1,0:T(8,128)(2,1)}, bf16[2048,512]{1,0:T(8,128)(2,1)}, f32[5,8,512]{2,1,0:T(8,128)S(1)}) custom-call(s32[4]{0:T(128)S(1)} %compare_select_fusion.2.meta.meta_ref, bf16[2048,512]{1,0:T(8,128)(2,1)S(1)} %copy-done.2, bf16[2048,512]{1,0:T(8,128)(2,1)S(1)} %copy-done, bf16[2048,2048]{1,0:T(8,128)(2,1)} %get-tuple-element.135.act_ref, ...), custom_call_target="tpu_custom_call" | custom-call | flops 6442450944 | bytes 20971520 | tf_op jit(solution)/shard_map/outputs_0/pallas_call | solution.py:536
  125.0 0.1 att_sum0.1.refs_0_
  125.2 0.3 collective-permute-start.17
  125.4 0.6 ff_join.1.refs_0_
  126.0 1.6 collective-permute-start.16
  127.6 0.5 collective-permute-start.15
  128.1 12.7 %outputs_1.1 = (bf16[2048,512]{1,0:T(8,128)(2,1)}, bf16[2048,512]{1,0:T(8,128)(2,1)}, f32[32,1,128]{2,1,0:T(1,128)S(1)}, f32[32,1,128]{2,1,0:T(1,128)S(1)}) custom-call(s32[4]{0:T(128)S(1)} %compare_select_fusion.2.meta.meta_ref, bf16[2048,512]{1,0:T(8,128)(2,1)S(1)} %copy-done.2, ...), custom_call_target="tpu_custom_call", output_to_operand_aliasing={{0}: (28, {}), {1}: (29, {})} | custom-call | flops 6442450944 | bytes 20971520 | tf_op jit(solution)/shard_map/outputs_1/pallas_call | solution.py:536
  140.8 0.1 att_sum1.1.refs_0_
  140.9 1.6 collective-permute-start.21
  142.5 3.0 %collective-permute-start.20 = (bf16[1,64,2048]{2,1,0:T(8,128)(2,1)S(1)}, bf16[1,64,2048]{2,1,0:T(8,128)(2,1)S(1)}, u32[]{:S(2)}, u32[]{:S(2)}) collective-permute-start(bf16[1,64,2048]{2,1,0:T(8,128)(2,1)S(1)} %att_sum1.1.refs_0_), channel_id=1, source_target_pairs={{0,16},{1,17},{2,18},{3,19},{4,20},{5,21},{6,22},{7,23},{8,24},{9,... | collective-permute-start | bytes 786440 | tf_op jit(solution)/shard_map/ppermute | solution.py:625
  145.4 1.2 collective-permute-done.18.refs_1_
  146.6 0.6 collective-permute-start.19
  147.2 10.8 %adam_ff_0.1 = (f32[2,4,2,64,512]{4,3,2,1,0:T(8,128)}, f32[2,4,2,64,512]{4,3,2,1,0:T(8,128)}, f32[2,4,2,64,512]{4,3,2,1,0:T(8,128)}, f32[2,4,2,64,512]{4,3,2,1,0...) custom-call(s32[4]{0:T(128)} %copy-done.11, ...), custom_call_target="tpu_custom_call" | custom-call | flops 15728640 | bytes 22020096 | tf_op jit(solution)/shard_map/adam_ff_0/pallas_call | solution.py:729
  158.1 0.1 att_sum2.1.refs_0_
  158.2 1.5 collective-permute-start.26
  159.7 0.5 collective-permute-start.25
  160.2 1.5 collective-permute-start.24
  161.7 0.5 collective-permute-start.22
  162.3 0.8 copy-done.14
  163.1 5.5 %adam_ff_3.1 = (f32[2,4,2,64,512]{4,3,2,1,0:T(8,128)}, f32[2,4,2,64,512]{4,3,2,1,0:T(8,128)}, f32[2,4,2,64,512]{4,3,2,1,0:T(8,128)}, f32[2,4,2,64,512]{4,3,2,1,0...) custom-call(s32[4]{0:T(128)} %copy-done.11, ...), custom_call_target="tpu_custom_call", output_to_operand_aliasing={{0}: (1, {}), {1}: (2, {}), {2}: (3, {}), {3}: (4, {}), {4}... | custom-call | flops 5242880 | bytes 7340032 | tf_op jit(solution)/shard_map/adam_ff_3/pallas_call | solution.py:729
  168.5 4.7 %collective-permute-done.22.refs_1_ = f32[32,1,128]{2,1,0:T(1,128)S(1)} collective-permute-done((f32[32,1,128]{2,1,0:T(1,128)S(1)}, f32[32,1,128]{2,1,0:T(1,128)S(1)}, u32[]{:S(2)}, u32[]{:S(2)}) %collective-permute-start.22) | collective-permute-done | bytes 16416 | tf_op jit(solution)/shard_map/ppermute | solution.py:625
  173.2 0.3 collective-permute-start.23
  173.5 3.8 %adam_qkv_0.1 = (f32[256,1536]{1,0:T(8,128)}, f32[256,1536]{1,0:T(8,128)}, f32[256,1536]{1,0:T(8,128)}, f32[256,1536]{1,0:T(8,128)}, f32[2,128,512]{2,1,0:T(8,12...) custom-call(s32[4]{0:T(128)} %copy-done.11, bf16[1,64,2048]{2,1,0:T(8,128)(2,1)} %copy-done.10, ...), custom_call_target="tpu_custom_call" | custom-call | flops 2621440 | bytes 3670016 | tf_op jit(solution)/shard_map/adam_qkv_0/pallas_call | solution.py:729
  177.4 1.7 collective-permute-start.27
  179.2 7.4 %adam_qkv_1.1 = (f32[256,1536]{1,0:T(8,128)}, f32[256,1536]{1,0:T(8,128)}, f32[256,1536]{1,0:T(8,128)}, f32[256,1536]{1,0:T(8,128)}, f32[2,128,512]{2,1,0:T(8,12...) custom-call(s32[4]{0:T(128)} %copy-done.11, ...), custom_call_target="tpu_custom_call", output_to_operand_aliasing={{0}: (1, {}), {1}: (2, {}), {2}: (3, {}), {3}: (4, {}), {4}... | custom-call | flops 7864320 | bytes 11010048 | tf_op jit(solution)/shard_map/adam_qkv_1/pallas_call | solution.py:729
  186.7 0.6 add_multiply_fusion.1
  187.3 0.6 add_multiply_fusion.2
  188.0 0.6 add_multiply_fusion
  (92 shorter events, 0.4 us)
Async XLA Ops:
  0.7 8.3 %copy-start = (bf16[2048,512]{1,0:T(8,128)(2,1)S(1)}, bf16[2048,512]{1,0:T(8,128)(2,1)}, u32[]{:S(2)}) copy-start(bf16[2048,512]{1,0:T(8,128)(2,1)} %grad_ref.15) | copy-start | bytes 6291460
  0.7 8.3 %collective-permute-start.1 = (bf16[1024,512]{1,0:T(8,128)(2,1)}, bf16[1024,512]{1,0:T(8,128)(2,1)S(1)}, u32[]{:S(2)}, u32[]{:S(2)}) collective-permute-start(bf16[1024,512]{1,0:T(8,128)(2,1)} %refs_10_.3), channel_id=1, source_target_pairs={{0,1},{1,0},{2,3},{3,2},{4,5},{5,4},{6,7},{7,6},{8,9},{9,8},{10,11... | collective-permute-start | bytes 3145736 | tf_op jit(solution)/shard_map/ppermute | solution.py:629
  1.2 7.7 %collective-permute-start = (bf16[256,2048]{1,0:T(8,128)(2,1)}, bf16[256,2048]{1,0:T(8,128)(2,1)}, u32[]{:S(2)}, u32[]{:S(2)}) collective-permute-start(bf16[256,2048]{1,0:T(8,128)(2,1)} %refs_14_.5), channel_id=1, source_target_pairs={{0,1},{1,0},{2,3},{3,2},{4,5},{5,4},{6,7},{7,6},{8,9},{9,8},{10,11... | collective-permute-start | bytes 3145736 | tf_op jit(solution)/shard_map/ppermute | solution.py:629
  5.4 1.6 copy-start.1
  8.9 119.2 %copy-start.11 = (s32[4]{0:T(128)}, s32[4]{0:T(128)S(1)}, u32[]{:S(2)}) copy-start(s32[4]{0:T(128)S(1)} %compare_select_fusion.2.meta.meta_ref) | copy-start | bytes 52
  9.0 1.2 copy-start.3
  10.2 1.2 copy-start.5
  11.4 26.1 %copy-start.7 = (bf16[256,1536]{1,0:T(8,128)(2,1)S(1)}, bf16[256,1536]{1,0:T(8,128)(2,1)}, u32[]{:S(2)}) copy-start(bf16[256,1536]{1,0:T(8,128)(2,1)} %refs_13_.3) | copy-start | bytes 2359300
  37.2 10.4 %collective-permute-start.2 = (bf16[4,64,4096]{2,1,0:T(8,128)(2,1)S(1)}, bf16[4,64,4096]{2,1,0:T(8,128)(2,1)S(1)}, u32[]{:S(2)}, u32[]{:S(2)}) collective-permute-start(bf16[4,64,4096]{2,1,0:T(8,128)(2,1)S(1)} %get-tuple-element.133), channel_id=1, source_target_pairs={{0,1},{1,0},{2,3},{3,2},{4,5},{5,4},{6,7},{7,6},{8,9},{9,8},{10,11... | collective-permute-start | bytes 6291464 | tf_op jit(solution)/shard_map/ppermute | solution.py:629
  37.5 15.0 %collective-permute-start.3 = (bf16[256,1536]{1,0:T(8,128)(2,1)S(1)}, bf16[256,1536]{1,0:T(8,128)(2,1)S(1)}, u32[]{:S(2)}, u32[]{:S(2)}) collective-permute-start(bf16[256,1536]{1,0:T(8,128)(2,1)S(1)} %copy-done.7), channel_id=1, source_target_pairs={{0,1},{1,0},{2,3},{3,2},{4,5},{5,4},{6,7},{7,6},{8,9},{9,8},{10,11... | collective-permute-start | bytes 2359304 | tf_op jit(solution)/shard_map/ppermute | solution.py:629
  47.5 3.4 %copy-start.8 = (bf16[256,512]{1,0:T(8,128)(2,1)S(1)}, bf16[256,512]{1,0:T(8,128)(2,1)}, u32[]{:S(2)}) copy-start(bf16[256,512]{1,0:T(8,128)(2,1)} %refs_8_.4) | copy-start | bytes 786436
  47.5 5.0 %copy-start.12 = (f32[2,8,512]{2,1,0:T(8,128)S(1)}, f32[2,8,512]{2,1,0:T(8,128)}, u32[]{:S(2)}) copy-start(f32[2,8,512]{2,1,0:T(8,128)} %constant.31.clone.trig_ref) | copy-start | bytes 98308
  48.1 15.9 %collective-permute-start.5 = (bf16[2,64,4096]{2,1,0:T(8,128)(2,1)S(1)}, bf16[2,64,4096]{2,1,0:T(8,128)(2,1)S(1)}, u32[]{:S(2)}, u32[]{:S(2)}) collective-permute-start(bf16[2,64,4096]{2,1,0:T(8,128)(2,1)S(1)} %get-tuple-element.142), channel_id=1, source_target_pairs={{0,2},{1,5},{2,0},{3,7},{4,6},{5,1},{6,4},{7,3},{8,10},{9,13},{10,... | collective-permute-start | bytes 3145736 | tf_op jit(solution)/shard_map/ppermute | solution.py:625
  51.0 1.5 collective-permute-start.4
  64.2 13.6 %collective-permute-start.6 = (bf16[1,64,4096]{2,1,0:T(8,128)(2,1)S(1)}, bf16[1,64,4096]{2,1,0:T(8,128)(2,1)S(1)}, u32[]{:S(2)}, u32[]{:S(2)}) collective-permute-start(bf16[1,64,4096]{2,1,0:T(8,128)(2,1)S(1)} %get-tuple-element.150), channel_id=1, source_target_pairs={{0,4},{1,3},{2,6},{3,1},{4,0},{5,7},{6,2},{7,5},{8,12},{9,11},{10,... | collective-permute-start | bytes 1572872 | tf_op jit(solution)/shard_map/ppermute | solution.py:625
  77.8 16.6 %collective-permute-start.8 = (bf16[4,64,1024]{2,1,0:T(8,128)(2,1)S(1)}, bf16[4,64,1024]{2,1,0:T(8,128)(2,1)S(1)}, u32[]{:S(2)}, u32[]{:S(2)}) collective-permute-start(bf16[4,64,1024]{2,1,0:T(8,128)(2,1)S(1)} %get-tuple-element.156), channel_id=1, source_target_pairs={{0,1},{1,0},{2,3},{3,2},{4,5},{5,4},{6,7},{7,6},{8,9},{9,8},{10,11... | collective-permute-start | bytes 1572872 | tf_op jit(solution)/shard_map/ppermute | solution.py:629
  78.5 13.1 %collective-permute-start.7 = (bf16[1,32,4096]{2,1,0:T(8,128)(2,1)S(1)}, bf16[1,32,4096]{2,1,0:T(8,128)(2,1)S(1)}, u32[]{:S(2)}, u32[]{:S(2)}) collective-permute-start(bf16[1,32,4096]{2,1,0:T(8,128)(2,1)S(1)} %get-tuple-element.155), channel_id=1, source_target_pairs={{0,8},{1,9},{2,10},{3,11},{4,12},{5,13},{6,14},{7,15},{8,0},{9,1},... | collective-permute-start | bytes 786440 | tf_op jit(solution)/shard_map/ppermute | solution.py:625
  91.7 14.9 %collective-permute-start.9 = (bf16[1,32,4096]{2,1,0:T(8,128)(2,1)S(1)}, bf16[1,32,4096]{2,1,0:T(8,128)(2,1)S(1)}, u32[]{:S(2)}, u32[]{:S(2)}) collective-permute-start(bf16[1,32,4096]{2,1,0:T(8,128)(2,1)S(1)} %ff_sum2.1.refs_0_), channel_id=1, source_target_pairs={{0,16},{1,17},{2,18},{3,19},{4,20},{5,21},{6,22},{7,23},{8,24},{9,... | collective-permute-start | bytes 786440 | tf_op jit(solution)/shard_map/ppermute | solution.py:625
  94.4 18.1 %copy-start.4 = (bf16[256,2048]{1,0:T(8,128)(2,1)S(1)}, bf16[256,2048]{1,0:T(8,128)(2,1)}, u32[]{:S(2)}) copy-start(bf16[256,2048]{1,0:T(8,128)(2,1)} %refs_14_.5) | copy-start | bytes 3145732
  94.4 18.1 %copy-start.6 = (bf16[1024,512]{1,0:T(8,128)(2,1)S(1)}, bf16[1024,512]{1,0:T(8,128)(2,1)}, u32[]{:S(2)}) copy-start(bf16[1024,512]{1,0:T(8,128)(2,1)} %refs_10_.3) | copy-start | bytes 3145732
  106.0 6.4 %copy-start.2 = (bf16[2048,512]{1,0:T(8,128)(2,1)S(1)}, bf16[2048,512]{1,0:T(8,128)(2,1)}, u32[]{:S(2)}) copy-start(bf16[2048,512]{1,0:T(8,128)(2,1)} %tok_ref.5) | copy-start | bytes 6291460
  106.7 2.0 %collective-permute-start.10 = (bf16[4,64,1024]{2,1,0:T(8,128)(2,1)S(1)}, bf16[4,64,1024]{2,1,0:T(8,128)(2,1)S(1)}, u32[]{:S(2)}, u32[]{:S(2)}) collective-permute-start(bf16[4,64,1024]{2,1,0:T(8,128)(2,1)S(1)} %get-tuple-element.164), channel_id=1, source_target_pairs={{0,1},{1,0},{2,3},{3,2},{4,5},{5,4},{6,7},{7,6},{8,9},{9,8},{10,11... | collective-permute-start | bytes 1572872 | tf_op jit(solution)/shard_map/ppermute | solution.py:629
  106.8 18.7 %collective-permute-start.14 = (bf16[1,32,4096]{2,1,0:T(8,128)(2,1)S(1)}, bf16[1,32,4096]{2,1,0:T(8,128)(2,1)S(1)}, u32[]{:S(2)}, u32[]{:S(2)}) collective-permute-start(bf16[1,32,4096]{2,1,0:T(8,128)(2,1)S(1)} %ff_sum3.1.mine_ref), channel_id=1, source_target_pairs={{0,8},{1,9},{2,10},{3,11},{4,12},{5,13},{6,14},{7,15},{8,0},{9,1},... | collective-permute-start | bytes 786440 | tf_op jit(solution)/shard_map/ppermute | solution.py:625
  108.9 16.1 %collective-permute-start.11 = (bf16[1,64,2048]{2,1,0:T(8,128)(2,1)S(1)}, bf16[1,64,2048]{2,1,0:T(8,128)(2,1)S(1)}, u32[]{:S(2)}, u32[]{:S(2)}) collective-permute-start(bf16[1,64,2048]{2,1,0:T(8,128)(2,1)S(1)} %get-tuple-element.178), channel_id=1, source_target_pairs={{0,4},{1,3},{2,6},{3,1},{4,0},{5,7},{6,2},{7,5},{8,12},{9,11},{10,... | collective-permute-start | bytes 786440 | tf_op jit(solution)/shard_map/ppermute | solution.py:625
  109.4 15.6 %collective-permute-start.12 = (bf16[1,64,2048]{2,1,0:T(8,128)(2,1)S(1)}, bf16[1,64,2048]{2,1,0:T(8,128)(2,1)S(1)}, u32[]{:S(2)}, u32[]{:S(2)}) collective-permute-start(bf16[1,64,2048]{2,1,0:T(8,128)(2,1)S(1)} %get-tuple-element.179), channel_id=1, source_target_pairs={{0,2},{1,5},{2,0},{3,7},{4,6},{5,1},{6,4},{7,3},{8,10},{9,13},{10,... | collective-permute-start | bytes 786440 | tf_op jit(solution)/shard_map/ppermute | solution.py:625
  111.0 14.1 %collective-permute-start.13 = (bf16[1,64,2048]{2,1,0:T(8,128)(2,1)S(1)}, bf16[1,64,2048]{2,1,0:T(8,128)(2,1)S(1)}, u32[]{:S(2)}, u32[]{:S(2)}) collective-permute-start(bf16[1,64,2048]{2,1,0:T(8,128)(2,1)S(1)} %get-tuple-element.180), channel_id=1, source_target_pairs={{0,6},{1,7},{2,4},{3,5},{4,2},{5,3},{6,0},{7,1},{8,14},{9,15},{10,... | collective-permute-start | bytes 786440 | tf_op jit(solution)/shard_map/ppermute | solution.py:625
  125.2 15.6 %collective-permute-start.17 = (bf16[1,64,2048]{2,1,0:T(8,128)(2,1)S(1)}, bf16[1,64,2048]{2,1,0:T(8,128)(2,1)S(1)}, u32[]{:S(2)}, u32[]{:S(2)}) collective-permute-start(bf16[1,64,2048]{2,1,0:T(8,128)(2,1)S(1)} %att_sum0.1.refs_0_), channel_id=1, source_target_pairs={{0,8},{1,9},{2,10},{3,11},{4,12},{5,13},{6,14},{7,15},{8,0},{9,1},... | collective-permute-start | bytes 786440 | tf_op jit(solution)/shard_map/ppermute | solution.py:625
  126.0 14.8 %copy-start.9 = (bf16[1,64,4096]{2,1,0:T(8,128)(2,1)}, bf16[1,64,4096]{2,1,0:T(8,128)(2,1)S(1)}, u32[]{:S(2)}) copy-start(bf16[1,64,4096]{2,1,0:T(8,128)(2,1)S(1)} %ff_join.1.refs_0_) | copy-start | bytes 1572868
  126.0 14.7 %collective-permute-start.16 = (bf16[1,64,4096]{2,1,0:T(8,128)(2,1)S(1)}, bf16[1,64,4096]{2,1,0:T(8,128)(2,1)}, u32[]{:S(2)}, u32[]{:S(2)}) collective-permute-start(bf16[1,64,4096]{2,1,0:T(8,128)(2,1)S(1)} %ff_join.1.refs_0_), channel_id=1, source_target_pairs={{0,2},{1,5},{2,0},{3,7},{4,6},{5,1},{6,4},{7,3},{8,10},{9,13},{10,... | collective-permute-start | bytes 1572872 | tf_op jit(solution)/shard_map/ppermute | solution.py:625
  127.6 13.2 %collective-permute-start.15 = (bf16[1,64,4096]{2,1,0:T(8,128)(2,1)S(1)}, bf16[1,64,4096]{2,1,0:T(8,128)(2,1)S(1)}, u32[]{:S(2)}, u32[]{:S(2)}) collective-permute-start(bf16[1,64,4096]{2,1,0:T(8,128)(2,1)S(1)} %ff_join.1.refs_0_), channel_id=1, source_target_pairs={{0,4},{1,3},{2,6},{3,1},{4,0},{5,7},{6,2},{7,5},{8,12},{9,11},{10,... | collective-permute-start | bytes 1572872 | tf_op jit(solution)/shard_map/ppermute | solution.py:625
  140.8 5.8 %copy-start.13 = (bf16[1,64,4096]{2,1,0:T(8,128)(2,1)}, bf16[1,64,4096]{2,1,0:T(8,128)(2,1)S(1)}, u32[]{:S(2)}) copy-start(bf16[1,64,4096]{2,1,0:T(8,128)(2,1)S(1)} %collective-permute-done.15.refs_1_) | copy-start | bytes 1572868
  140.9 21.4 %collective-permute-start.21 = (bf16[1,64,4096]{2,1,0:T(8,128)(2,1)}, bf16[1,64,4096]{2,1,0:T(8,128)(2,1)S(1)}, u32[]{:S(2)}, u32[]{:S(2)}) collective-permute-start(bf16[1,64,4096]{2,1,0:T(8,128)(2,1)} %collective-permute-done.16.refs_2_), channel_id=1, source_target_pairs={{0,4},{1,3},{2,6},{3,1},{4,0},{5,7},{6,2},{7,5},{8,12},{9,11},{10,... | collective-permute-start | bytes 1572872 | tf_op jit(solution)/shard_map/ppermute | solution.py:625
  142.5 15.6 %collective-permute-start.20 = (bf16[1,64,2048]{2,1,0:T(8,128)(2,1)S(1)}, bf16[1,64,2048]{2,1,0:T(8,128)(2,1)S(1)}, u32[]{:S(2)}, u32[]{:S(2)}) collective-permute-start(bf16[1,64,2048]{2,1,0:T(8,128)(2,1)S(1)} %att_sum1.1.refs_0_), channel_id=1, source_target_pairs={{0,16},{1,17},{2,18},{3,19},{4,20},{5,21},{6,22},{7,23},{8,24},{9,... | collective-permute-start | bytes 786440 | tf_op jit(solution)/shard_map/ppermute | solution.py:625
  145.4 1.2 collective-permute-start.18
  146.6 11.4 %collective-permute-start.19 = (f32[32,1,128]{2,1,0:T(1,128)S(1)}, f32[32,1,128]{2,1,0:T(1,128)S(1)}, u32[]{:S(2)}, u32[]{:S(2)}) collective-permute-start(f32[32,1,128]{2,1,0:T(1,128)S(1)} %small_pair.1.refs_0_), channel_id=1, source_target_pairs={{0,2},{1,3},{2,0},{3,1},{4,6},{5,7},{6,4},{7,5},{8,10},{9,11},{10,... | collective-permute-start | bytes 49160 | tf_op jit(solution)/shard_map/ppermute | solution.py:625
  158.2 10.4 %copy-start.10 = (bf16[1,64,2048]{2,1,0:T(8,128)(2,1)}, bf16[1,64,2048]{2,1,0:T(8,128)(2,1)S(1)}, u32[]{:S(2)}) copy-start(bf16[1,64,2048]{2,1,0:T(8,128)(2,1)S(1)} %att_sum2.1.refs_0_) | copy-start | bytes 786436
  158.2 19.1 %collective-permute-start.26 = (bf16[1,64,2048]{2,1,0:T(8,128)(2,1)S(1)}, bf16[1,64,2048]{2,1,0:T(8,128)(2,1)S(1)}, u32[]{:S(2)}, u32[]{:S(2)}) collective-permute-start(bf16[1,64,2048]{2,1,0:T(8,128)(2,1)S(1)} %att_sum2.1.refs_0_), channel_id=1, source_target_pairs={{0,6},{1,7},{2,4},{3,5},{4,2},{5,3},{6,0},{7,1},{8,14},{9,15},{10,... | collective-permute-start | bytes 786440 | tf_op jit(solution)/shard_map/ppermute | solution.py:625
  159.7 17.7 %collective-permute-start.25 = (bf16[1,64,2048]{2,1,0:T(8,128)(2,1)S(1)}, bf16[1,64,2048]{2,1,0:T(8,128)(2,1)S(1)}, u32[]{:S(2)}, u32[]{:S(2)}) collective-permute-start(bf16[1,64,2048]{2,1,0:T(8,128)(2,1)S(1)} %att_sum2.1.refs_0_), channel_id=1, source_target_pairs={{0,2},{1,5},{2,0},{3,7},{4,6},{5,1},{6,4},{7,3},{8,10},{9,13},{10,... | collective-permute-start | bytes 786440 | tf_op jit(solution)/shard_map/ppermute | solution.py:625
  160.2 17.1 %collective-permute-start.24 = (bf16[1,64,2048]{2,1,0:T(8,128)(2,1)S(1)}, bf16[1,64,2048]{2,1,0:T(8,128)(2,1)S(1)}, u32[]{:S(2)}, u32[]{:S(2)}) collective-permute-start(bf16[1,64,2048]{2,1,0:T(8,128)(2,1)S(1)} %att_sum2.1.refs_0_), channel_id=1, source_target_pairs={{0,4},{1,3},{2,6},{3,1},{4,0},{5,7},{6,2},{7,5},{8,12},{9,11},{10,... | collective-permute-start | bytes 786440 | tf_op jit(solution)/shard_map/ppermute | solution.py:625
  161.7 11.5 %collective-permute-start.22 = (f32[32,1,128]{2,1,0:T(1,128)S(1)}, f32[32,1,128]{2,1,0:T(1,128)S(1)}, u32[]{:S(2)}, u32[]{:S(2)}) collective-permute-start(f32[32,1,128]{2,1,0:T(1,128)S(1)} %small_sum.4.refs_0_), channel_id=1, source_target_pairs={{0,4},{1,5},{2,6},{3,7},{4,0},{5,1},{6,2},{7,3},{8,12},{9,13},{10,... | collective-permute-start | bytes 49160 | tf_op jit(solution)/shard_map/ppermute | solution.py:625
  162.3 0.8 copy-start.14
  173.2 4.1 %collective-permute-start.23 = (f32[32,1,128]{2,1,0:T(1,128)S(1)}, f32[32,1,128]{2,1,0:T(1,128)S(1)}, u32[]{:S(2)}, u32[]{:S(2)}) collective-permute-start(f32[32,1,128]{2,1,0:T(1,128)S(1)} %small_sum.5.refs_0_), channel_id=1, source_target_pairs={{0,8},{1,9},{2,10},{3,11},{4,12},{5,13},{6,14},{7,15},{8,0},{9,1},... | collective-permute-start | bytes 49160 | tf_op jit(solution)/shard_map/ppermute | solution.py:625
  177.3 1.7 copy-start.15
  177.3 1.7 copy-start.16
  177.4 1.7 copy-start.17
  177.4 9.2 %collective-permute-start.27 = (f32[32,1,128]{2,1,0:T(1,128)S(1)}, f32[32,1,128]{2,1,0:T(1,128)S(1)}, u32[]{:S(2)}, u32[]{:S(2)}) collective-permute-start(f32[32,1,128]{2,1,0:T(1,128)S(1)} %small_sum.6.refs_0_), channel_id=1, source_target_pairs={{0,16},{1,17},{2,18},{3,19},{4,20},{5,21},{6,22},{7,23},{8,24},{9,... | collective-permute-start | bytes 49160 | tf_op jit(solution)/shard_map/ppermute | solution.py:625
  179.1 7.6 %copy-start.24 = (bf16[1024]{0:T(1024)(128)(2,1)S(1)}, bf16[1024]{0:T(1024)(128)(2,1)}, u32[]{:S(2)}) copy-start(bf16[1024]{0:T(1024)(128)(2,1)} %param.31) | copy-start | bytes 6148
  179.1 7.6 %copy-start.26 = (f32[1024]{0:T(1024)S(1)}, f32[1024]{0:T(1024)}, u32[]{:S(2)}) copy-start(f32[1024]{0:T(1024)} %param.38) | copy-start | bytes 12292
  179.1 7.6 %copy-start.27 = (f32[1024]{0:T(1024)S(1)}, f32[1024]{0:T(1024)}, u32[]{:S(2)}) copy-start(f32[1024]{0:T(1024)} %param.45) | copy-start | bytes 12292
  179.1 8.3 %copy-start.25 = (bf16[768]{0:T(1024)(128)(2,1)S(1)}, bf16[768]{0:T(1024)(128)(2,1)}, u32[]{:S(2)}) copy-start(bf16[768]{0:T(1024)(128)(2,1)} %param.28) | copy-start | bytes 4612
  179.1 8.2 %copy-start.28 = (f32[768]{0:T(1024)S(1)}, f32[768]{0:T(1024)}, u32[]{:S(2)}) copy-start(f32[768]{0:T(1024)} %param.35) | copy-start | bytes 9220
  179.1 8.2 %copy-start.29 = (f32[768]{0:T(1024)S(1)}, f32[768]{0:T(1024)}, u32[]{:S(2)}) copy-start(f32[768]{0:T(1024)} %param.42) | copy-start | bytes 9220
  179.1 8.8 %copy-start.21 = (bf16[6,256]{1,0:T(8,128)(2,1)S(1)}, bf16[6,256]{1,0:T(8,128)(2,1)}, u32[]{:S(2)}) copy-start(bf16[6,256]{1,0:T(8,128)(2,1)} %param.26) | copy-start | bytes 9220
  179.1 8.8 %copy-start.22 = (f32[6,256]{1,0:T(8,128)S(1)}, f32[6,256]{1,0:T(8,128)}, u32[]{:S(2)}) copy-start(f32[6,256]{1,0:T(8,128)} %param.33) | copy-start | bytes 18436
  179.1 8.8 %copy-start.23 = (f32[6,256]{1,0:T(8,128)S(1)}, f32[6,256]{1,0:T(8,128)}, u32[]{:S(2)}) copy-start(f32[6,256]{1,0:T(8,128)} %param.40) | copy-start | bytes 18436
  186.6 2.0 %copy-start.19 = (f32[6,128]{1,0:T(8,128)}, f32[6,128]{1,0:T(8,128)S(1)}, u32[]{:S(2)}) copy-start(f32[6,128]{1,0:T(8,128)S(1)} %slice_reduce_fusion.1) | copy-start | bytes 9220
  186.6 2.0 %copy-start.20 = (f32[8,1,128]{2,1,0:T(1,128)}, f32[8,1,128]{2,1,0:T(1,128)S(1)}, u32[]{:S(2)}) copy-start(f32[8,1,128]{2,1,0:T(1,128)S(1)} %slice.17) | copy-start | bytes 12292
  186.7 1.9 %copy-start.18 = (f32[6,256]{1,0:T(8,128)}, f32[6,256]{1,0:T(8,128)S(1)}, u32[]{:S(2)}) copy-start(f32[6,256]{1,0:T(8,128)S(1)} %reshape.150) | copy-start | bytes 18436

commit v6 on v5

--- a/solution.py
+++ b/solution.py
@@ -889,17 +889,17 @@
     )
     a_ff = adam_ff(0, ff_pieces[:3], (), total, att_total)
     (total,) = sum_call([tie(total, a_ff[4]), small_got], 1, "small_sum")
-    small_got = exchange(total, reps, 2, 2)
+    small_got = exchange(total, reps, bits[0], bits[0])
     (att_total,) = sum_call([tie(att_total, total), got], 1, "att_sum2")
     att_total = rest(att_total, 2, "att_sum3")
     att_pieces = [att_total, *crosses([att_total] * 3, reps)]
     a_ff = adam_ff(3, ff_pieces[3:], a_ff, att_total)
     (total,) = sum_call([tie(total, a_ff[4]), small_got], 1, "small_sum")
-    small_got = exchange(total, reps, bits[0], bits[0])
+    small_got = exchange(total, reps, bits[1], bits[1])
     a_qkv = adam_qkv(0, att_pieces[:1], (), total)
     (total,) = sum_call([tie(total, a_qkv[0]), small_got], 1, "small_sum")
     mark = tie(total, *att_pieces[1:])
-    small_got = exchange(mark, reps, bits[1], bits[1])
+    small_got = exchange(mark, reps, 2, 2)
 
     a_qkv = adam_qkv(1, att_pieces[1:], a_qkv, mark)
     a_proj = [a.reshape(1024, 512) for a in a_ff[:4]]

time: 189 us -> 185 us (0.979)
  waiting for transfers between devices: 9.81 us -> 5.13 us
    ppermute x20, waiting for transfers between devices: 5.26 us -> 0.58 us  [exchange(): return lax.ppermute(a, ('rep', 'opt'), pairs)]
  transfers between devices with their start and end apart: 28 -> 28, of which waited for: 5 -> 4; matrix products, arithmetic and copies ran while one was open for 1% -> 1% of each run, Pallas kernels for 60% -> 61%
where the time goes in v6:
time: 185 us; the launch traced here: 184 us
  Pallas kernels  139 us (75%)
  starting transfers between devices  27.5 us (15%)
  local copies, waits for them, and re-layouts  6.05 us (3%)
  waiting for transfers between devices  5.13 us (3%)
  blocking collectives  2.64 us (1%)
  other arithmetic  2.58 us (1%)
    pallas_call x4, Pallas kernels, attention_call(): pl.pallas_call(functools.partial(attention_kernel, j, rel), grid_spec=gri...  46.1 us
    pallas_call x4, Pallas kernels, adam_call(): pl.pallas_call(run, grid_spec=grid_spec, out_shape=outs, input_output_ali...  27.5 us
    ppermute x20, starting transfers between devices, exchange(): return lax.ppermute(a, ('rep', 'opt'), pairs)  26.1 us
    pallas_call x1, Pallas kernels, ff_call(): pl.pallas_call(ff_kernel, grid_spec=grid_spec, out_shape=[jax.ShapeDtypeS...  25.7 us
    pallas_call x2, Pallas kernels, output_call(): pl.pallas_call(functools.partial(output_kernel, part, parts), grid_spec=g...  25.2 us
    pallas_call x1, Pallas kernels, ff_own_call(): pl.pallas_call(ff_own_kernel, grid_spec=grid_spec, out_shape=jax.ShapeDty...  9.86 us
    unnamed x60, local copies, waits for them, and re-layouts  5.29 us
    ppermute x8, waiting for transfers between devices, swap(): return lax.ppermute(a, 'opt', [(0, 1), (1, 0)])  4.54 us
  transfers between devices with their start and end apart: 28, of which 4 were waited for; matrix products, arithmetic and copies ran while one was open for 1% of the time, Pallas kernels for 61%

profile of v6, /device:TPU:0, one launch (start us, length us, event | category | flops | bytes accessed | tf_op | source)
XLA Modules:
  0.0 184.4 jit_solution(10521398701478369608)
XLA Ops:
  0.7 0.6 collective-permute-start.1
  1.2 0.1 collective-permute-start
  1.3 0.7 reshape.138
  2.0 0.7 maximum_bitcast_fusion
  2.7 2.6 %all-gather = bf16[2,26,128]{2,1,0:T(8,128)(2,1)S(1)} all-gather(bf16[1,26,128]{2,1,0:T(8,128)(2,1)S(1)} %maximum_bitcast_fusion), channel_id=1, replica_groups=mesh['rep'=16,'opt'=2] {'opt'}, dimensions={0}, use_global_device_ids=true | all-gather | bytes 19968 | tf_op jit(solution)/shard_map/all_gather | solution.py:777
  5.4 1.6 copy-done.1
  7.0 1.9 %norm.1 = (bf16[2048,512]{1,0:T(8,128)(2,1)S(1)}, bf16[2048,512]{1,0:T(8,128)(2,1)S(1)}) custom-call(bf16[2048,512]{1,0:T(8,128)(2,1)S(1)} %copy-done.1, f32[52,1,128]{2,1,0:T(1,128)S(1)} %reshape.167.small_ref.refs_16_), custom_call_target="tpu_custom_call" | custom-call | flops 20971520 | bytes 6291456 | tf_op jit(solution)/shard_map/norm/pallas_call | solution.py:79
  9.0 1.2 copy-done.3
  10.2 1.2 copy-done.5
  11.4 25.7 %feed_forward.1 = (bf16[4,64,4096]{2,1,0:T(8,128)(2,1)S(1)}, bf16[2048,2048]{1,0:T(8,128)(2,1)}, bf16[2048,2048]{1,0:T(8,128)(2,1)}, f32[4,1,512]{2,1,0:T(1,128)S(1)}) custom-call(s32[4]{0:T(128)S(1)} %compare_select_fusion.2.meta.meta_ref, bf16[2048,512]{1,0:T(8,128)(2,1)S(1)} %get-tuple-element.132.second_ref, bf16[2048,512]{1,0:T(8,128)(2,1)S(1)} %copy-done, ...), custom_call_target="tpu_custom_call" | custom-call | flops 12884901888 | bytes 20971520 | tf_op jit(solution)/shard_map/feed_forward/pallas_call | solution.py:188
  37.2 0.4 collective-permute-start.2
  37.5 0.1 collective-permute-start.3
  37.7 9.9 %feed_forward_own.1.refs_0_ = bf16[4,64,4096]{2,1,0:T(8,128)(2,1)S(1)} custom-call(s32[4]{0:T(128)S(1)} %compare_select_fusion.2.meta.meta_ref, bf16[2048,512]{1,0:T(8,128)(2,1)S(1)} %get-tuple-element.132.second_ref, bf16[2048,512]{1,0:T(8,128)(2,1)S(1)} %copy-done, bf16[2048,2048]{1,0:T(8,128)(2,1)} %get-tuple-element.135.act_ref, ...), custom_call_target="tpu_custom_call" | custom-call | flops 4294967296 | bytes 16777216 | tf_op jit(solution)/shard_map/feed_forward_own/pallas_call | solution.py:219
  47.6 0.5 ff_pair.1
  48.1 2.9 %collective-permute-start.5 = (bf16[2,64,4096]{2,1,0:T(8,128)(2,1)S(1)}, bf16[2,64,4096]{2,1,0:T(8,128)(2,1)S(1)}, u32[]{:S(2)}, u32[]{:S(2)}) collective-permute-start(bf16[2,64,4096]{2,1,0:T(8,128)(2,1)S(1)} %get-tuple-element.142), channel_id=1, source_target_pairs={{0,2},{1,5},{2,0},{3,7},{4,6},{5,1},{6,4},{7,3},{8,10},{9,13},{10,... | collective-permute-start | bytes 3145736 | tf_op jit(solution)/shard_map/ppermute | solution.py:625
  51.0 1.5 collective-permute-done.4.ow_ref.refs_9_
  52.5 11.4 %attention_01.1 = (bf16[4,64,384]{2,1,0:T(8,128)(2,1)S(1)}, bf16[4,64,640]{2,1,0:T(8,128)(2,1)S(1)}, bf16[2048,384]{1,0:T(8,128)(2,1)S(1)}, bf16[2048,128]{1,0:T(8,128)(2,1)S(1)}, f32[1,384]{1,0:T(1,128)S(1)}) custom-call(s32[4]{0:T(128)S(1)} %compare_select_fusion.2.meta.meta_ref, bf16[2048,512]{1,0:T(8,128)(2,1)S(1)} %get-tuple-element.139.first_ref, ...), custom_call_target="tpu_custom_call" | custom-call | flops 5368709120 | bytes 6291456 | tf_op jit(solution)/shard_map/attention_01/pallas_call | solution.py:393
  64.0 0.3 ff_sum0.1
  64.2 1.9 %collective-permute-start.6 = (bf16[1,64,4096]{2,1,0:T(8,128)(2,1)S(1)}, bf16[1,64,4096]{2,1,0:T(8,128)(2,1)S(1)}, u32[]{:S(2)}, u32[]{:S(2)}) collective-permute-start(bf16[1,64,4096]{2,1,0:T(8,128)(2,1)S(1)} %get-tuple-element.150), channel_id=1, source_target_pairs={{0,4},{1,3},{2,6},{3,1},{4,0},{5,7},{6,2},{7,5},{8,12},{9,11},{10,... | collective-permute-start | bytes 1572872 | tf_op jit(solution)/shard_map/ppermute | solution.py:625
  66.1 11.6 %attention_00.1 = (bf16[4,64,1024]{2,1,0:T(8,128)(2,1)S(1)}, bf16[4,64,1024]{2,1,0:T(8,128)(2,1)S(1)}, bf16[2048,384]{1,0:T(8,128)(2,1)S(1)}, bf16[2048,128]{1,0:T(8,128)(2,1)S(1)}, f32[1,384]{1,0:T(1,128)S(1)}) custom-call(s32[4]{0:T(128)S(1)} %compare_select_fusion.2.meta.meta_ref, bf16[2048,512]{1,0:T(8,128)(2,1)S(1)} %get-tuple-element.139.first_ref, ...), custom_call_target="tpu_custom_call" | custom-call | flops 5368709120 | bytes 6291456 | tf_op jit(solution)/shard_map/attention_00/pallas_call | solution.py:393
  77.8 0.1 collective-permute-start.8
  77.9 0.7 ff_sum1.1
  78.5 1.6 collective-permute-start.7
  80.2 11.4 %attention_11.1 = (bf16[4,64,384]{2,1,0:T(8,128)(2,1)S(1)}, bf16[4,64,640]{2,1,0:T(8,128)(2,1)S(1)}, bf16[2048,384]{1,0:T(8,128)(2,1)S(1)}, bf16[2048,128]{1,0:T(8,128)(2,1)S(1)}, f32[1,384]{1,0:T(1,128)S(1)}) custom-call(s32[4]{0:T(128)S(1)} %compare_select_fusion.2.meta.meta_ref, bf16[2048,512]{1,0:T(8,128)(2,1)S(1)} %get-tuple-element.139.first_ref, ...), custom_call_target="tpu_custom_call" | custom-call | flops 5368709120 | bytes 6291456 | tf_op jit(solution)/shard_map/attention_11/pallas_call | solution.py:393
  91.6 0.1 ff_sum2.1.refs_0_
  91.7 2.7 %collective-permute-start.9 = (bf16[1,32,4096]{2,1,0:T(8,128)(2,1)S(1)}, bf16[1,32,4096]{2,1,0:T(8,128)(2,1)S(1)}, u32[]{:S(2)}, u32[]{:S(2)}) collective-permute-start(bf16[1,32,4096]{2,1,0:T(8,128)(2,1)S(1)} %ff_sum2.1.refs_0_), channel_id=1, source_target_pairs={{0,16},{1,17},{2,18},{3,19},{4,20},{5,21},{6,22},{7,23},{8,24},{9,... | collective-permute-start | bytes 786440 | tf_op jit(solution)/shard_map/ppermute | solution.py:625
  94.4 11.7 %attention_10.1 = (bf16[4,64,1024]{2,1,0:T(8,128)(2,1)S(1)}, bf16[4,64,1024]{2,1,0:T(8,128)(2,1)S(1)}, bf16[2048,384]{1,0:T(8,128)(2,1)S(1)}, bf16[2048,128]{1,0:T(8,128)(2,1)S(1)}, f32[1,384]{1,0:T(1,128)S(1)}) custom-call(s32[4]{0:T(128)S(1)} %compare_select_fusion.2.meta.meta_ref, bf16[2048,512]{1,0:T(8,128)(2,1)S(1)} %get-tuple-element.139.first_ref, ...), custom_call_target="tpu_custom_call" | custom-call | flops 5368709120 | bytes 6291456 | tf_op jit(solution)/shard_map/attention_10/pallas_call | solution.py:393
  106.0 0.5 collective-permute-done.9.refs_1_
  106.6 0.1 ff_sum3.1.mine_ref
  106.7 0.1 collective-permute-start.10
  106.8 1.8 collective-permute-done.10.refs_3_
  108.6 0.3 att_pair.1
  108.9 0.5 collective-permute-start.11
  109.4 1.5 collective-permute-start.12
  111.0 1.5 collective-permute-start.13
  112.5 12.6 %outputs_0.1 = (bf16[2048,512]{1,0:T(8,128)(2,1)}, bf16[2048,512]{1,0:T(8,128)(2,1)}, f32[5,8,512]{2,1,0:T(8,128)S(1)}) custom-call(s32[4]{0:T(128)S(1)} %compare_select_fusion.2.meta.meta_ref, bf16[2048,512]{1,0:T(8,128)(2,1)S(1)} %copy-done.2, bf16[2048,512]{1,0:T(8,128)(2,1)S(1)} %copy-done, bf16[2048,2048]{1,0:T(8,128)(2,1)} %get-tuple-element.135.act_ref, ...), custom_call_target="tpu_custom_call" | custom-call | flops 6442450944 | bytes 20971520 | tf_op jit(solution)/shard_map/outputs_0/pallas_call | solution.py:536
  125.0 0.1 att_sum0.1.refs_0_
  125.2 0.3 collective-permute-start.17
  125.4 0.6 ff_join.1.refs_0_
  126.0 1.6 collective-permute-start.16
  127.6 0.5 collective-permute-start.15
  128.1 12.7 %outputs_1.1 = (bf16[2048,512]{1,0:T(8,128)(2,1)}, bf16[2048,512]{1,0:T(8,128)(2,1)}, f32[32,1,128]{2,1,0:T(1,128)S(1)}, f32[32,1,128]{2,1,0:T(1,128)S(1)}) custom-call(s32[4]{0:T(128)S(1)} %compare_select_fusion.2.meta.meta_ref, bf16[2048,512]{1,0:T(8,128)(2,1)S(1)} %copy-done.2, ...), custom_call_target="tpu_custom_call", output_to_operand_aliasing={{0}: (28, {}), {1}: (29, {})} | custom-call | flops 6442450944 | bytes 20971520 | tf_op jit(solution)/shard_map/outputs_1/pallas_call | solution.py:536
  140.9 1.6 collective-permute-start.21
  142.5 3.0 %collective-permute-start.20 = (bf16[1,64,2048]{2,1,0:T(8,128)(2,1)S(1)}, bf16[1,64,2048]{2,1,0:T(8,128)(2,1)S(1)}, u32[]{:S(2)}, u32[]{:S(2)}) collective-permute-start(bf16[1,64,2048]{2,1,0:T(8,128)(2,1)S(1)} %att_sum1.1.refs_0_), channel_id=1, source_target_pairs={{0,16},{1,17},{2,18},{3,19},{4,20},{5,21},{6,22},{7,23},{8,24},{9,... | collective-permute-start | bytes 786440 | tf_op jit(solution)/shard_map/ppermute | solution.py:625
  145.4 1.2 collective-permute-done.18.refs_1_
  146.6 0.6 collective-permute-start.19
  147.2 10.8 %adam_ff_0.1 = (f32[2,4,2,64,512]{4,3,2,1,0:T(8,128)}, f32[2,4,2,64,512]{4,3,2,1,0:T(8,128)}, f32[2,4,2,64,512]{4,3,2,1,0:T(8,128)}, f32[2,4,2,64,512]{4,3,2,1,0...) custom-call(s32[4]{0:T(128)} %copy-done.11, ...), custom_call_target="tpu_custom_call" | custom-call | flops 15728640 | bytes 22020096 | tf_op jit(solution)/shard_map/adam_ff_0/pallas_call | solution.py:729
  158.1 0.1 att_sum2.1.refs_0_
  158.2 1.5 collective-permute-start.26
  159.7 0.5 collective-permute-start.25
  160.2 1.5 collective-permute-start.24
  161.7 0.2 collective-permute-start.22
  162.0 0.8 copy-done.14
  162.7 5.5 %adam_ff_3.1 = (f32[2,4,2,64,512]{4,3,2,1,0:T(8,128)}, f32[2,4,2,64,512]{4,3,2,1,0:T(8,128)}, f32[2,4,2,64,512]{4,3,2,1,0:T(8,128)}, f32[2,4,2,64,512]{4,3,2,1,0...) custom-call(s32[4]{0:T(128)} %copy-done.11, ...), custom_call_target="tpu_custom_call", output_to_operand_aliasing={{0}: (1, {}), {1}: (2, {}), {2}: (3, {}), {3}: (4, {}), {4}... | custom-call | flops 5242880 | bytes 7340032 | tf_op jit(solution)/shard_map/adam_ff_3/pallas_call | solution.py:729
  168.3 1.7 collective-permute-start.23
  169.9 3.8 %adam_qkv_0.1 = (f32[256,1536]{1,0:T(8,128)}, f32[256,1536]{1,0:T(8,128)}, f32[256,1536]{1,0:T(8,128)}, f32[256,1536]{1,0:T(8,128)}, f32[2,128,512]{2,1,0:T(8,12...) custom-call(s32[4]{0:T(128)} %copy-done.11, bf16[1,64,2048]{2,1,0:T(8,128)(2,1)} %copy-done.10, ...), custom_call_target="tpu_custom_call" | custom-call | flops 2621440 | bytes 3670016 | tf_op jit(solution)/shard_map/adam_qkv_0/pallas_call | solution.py:729
  173.8 0.5 collective-permute-start.27
  174.3 0.1 copy-done.15
  174.4 0.1 copy-done.16
  174.6 0.1 copy-done.17
  174.7 7.4 %adam_qkv_1.1 = (f32[256,1536]{1,0:T(8,128)}, f32[256,1536]{1,0:T(8,128)}, f32[256,1536]{1,0:T(8,128)}, f32[256,1536]{1,0:T(8,128)}, f32[2,128,512]{2,1,0:T(8,12...) custom-call(s32[4]{0:T(128)} %copy-done.11, ...), custom_call_target="tpu_custom_call", output_to_operand_aliasing={{0}: (1, {}), {1}: (2, {}), {2}: (3, {}), {3}: (4, {}), {4}... | custom-call | flops 7864320 | bytes 11010048 | tf_op jit(solution)/shard_map/adam_qkv_1/pallas_call | solution.py:729
  182.3 0.6 add_multiply_fusion.1
  182.9 0.6 add_multiply_fusion.2
  183.6 0.6 add_multiply_fusion
  (92 shorter events, 0.5 us)
Async XLA Ops:
  0.7 8.3 %copy-start = (bf16[2048,512]{1,0:T(8,128)(2,1)S(1)}, bf16[2048,512]{1,0:T(8,128)(2,1)}, u32[]{:S(2)}) copy-start(bf16[2048,512]{1,0:T(8,128)(2,1)} %grad_ref.15) | copy-start | bytes 6291460
  0.7 8.3 %collective-permute-start.1 = (bf16[1024,512]{1,0:T(8,128)(2,1)}, bf16[1024,512]{1,0:T(8,128)(2,1)S(1)}, u32[]{:S(2)}, u32[]{:S(2)}) collective-permute-start(bf16[1024,512]{1,0:T(8,128)(2,1)} %refs_10_.3), channel_id=1, source_target_pairs={{0,1},{1,0},{2,3},{3,2},{4,5},{5,4},{6,7},{7,6},{8,9},{9,8},{10,11... | collective-permute-start | bytes 3145736 | tf_op jit(solution)/shard_map/ppermute | solution.py:629
  1.2 7.7 %collective-permute-start = (bf16[256,2048]{1,0:T(8,128)(2,1)}, bf16[256,2048]{1,0:T(8,128)(2,1)}, u32[]{:S(2)}, u32[]{:S(2)}) collective-permute-start(bf16[256,2048]{1,0:T(8,128)(2,1)} %refs_14_.5), channel_id=1, source_target_pairs={{0,1},{1,0},{2,3},{3,2},{4,5},{5,4},{6,7},{7,6},{8,9},{9,8},{10,11... | collective-permute-start | bytes 3145736 | tf_op jit(solution)/shard_map/ppermute | solution.py:629
  5.4 1.6 copy-start.1
  8.9 119.2 %copy-start.11 = (s32[4]{0:T(128)}, s32[4]{0:T(128)S(1)}, u32[]{:S(2)}) copy-start(s32[4]{0:T(128)S(1)} %compare_select_fusion.2.meta.meta_ref) | copy-start | bytes 52
  9.0 1.2 copy-start.3
  10.2 1.2 copy-start.5
  11.4 26.1 %copy-start.7 = (bf16[256,1536]{1,0:T(8,128)(2,1)S(1)}, bf16[256,1536]{1,0:T(8,128)(2,1)}, u32[]{:S(2)}) copy-start(bf16[256,1536]{1,0:T(8,128)(2,1)} %refs_13_.3) | copy-start | bytes 2359300
  37.2 10.4 %collective-permute-start.2 = (bf16[4,64,4096]{2,1,0:T(8,128)(2,1)S(1)}, bf16[4,64,4096]{2,1,0:T(8,128)(2,1)S(1)}, u32[]{:S(2)}, u32[]{:S(2)}) collective-permute-start(bf16[4,64,4096]{2,1,0:T(8,128)(2,1)S(1)} %get-tuple-element.133), channel_id=1, source_target_pairs={{0,1},{1,0},{2,3},{3,2},{4,5},{5,4},{6,7},{7,6},{8,9},{9,8},{10,11... | collective-permute-start | bytes 6291464 | tf_op jit(solution)/shard_map/ppermute | solution.py:629
  37.5 15.0 %collective-permute-start.3 = (bf16[256,1536]{1,0:T(8,128)(2,1)S(1)}, bf16[256,1536]{1,0:T(8,128)(2,1)S(1)}, u32[]{:S(2)}, u32[]{:S(2)}) collective-permute-start(bf16[256,1536]{1,0:T(8,128)(2,1)S(1)} %copy-done.7), channel_id=1, source_target_pairs={{0,1},{1,0},{2,3},{3,2},{4,5},{5,4},{6,7},{7,6},{8,9},{9,8},{10,11... | collective-permute-start | bytes 2359304 | tf_op jit(solution)/shard_map/ppermute | solution.py:629
  47.5 3.4 %copy-start.8 = (bf16[256,512]{1,0:T(8,128)(2,1)S(1)}, bf16[256,512]{1,0:T(8,128)(2,1)}, u32[]{:S(2)}) copy-start(bf16[256,512]{1,0:T(8,128)(2,1)} %refs_8_.4) | copy-start | bytes 786436
  47.5 5.0 %copy-start.12 = (f32[2,8,512]{2,1,0:T(8,128)S(1)}, f32[2,8,512]{2,1,0:T(8,128)}, u32[]{:S(2)}) copy-start(f32[2,8,512]{2,1,0:T(8,128)} %constant.31.clone.trig_ref) | copy-start | bytes 98308
  48.1 15.9 %collective-permute-start.5 = (bf16[2,64,4096]{2,1,0:T(8,128)(2,1)S(1)}, bf16[2,64,4096]{2,1,0:T(8,128)(2,1)S(1)}, u32[]{:S(2)}, u32[]{:S(2)}) collective-permute-start(bf16[2,64,4096]{2,1,0:T(8,128)(2,1)S(1)} %get-tuple-element.142), channel_id=1, source_target_pairs={{0,2},{1,5},{2,0},{3,7},{4,6},{5,1},{6,4},{7,3},{8,10},{9,13},{10,... | collective-permute-start | bytes 3145736 | tf_op jit(solution)/shard_map/ppermute | solution.py:625
  51.0 1.5 collective-permute-start.4
  64.2 13.6 %collective-permute-start.6 = (bf16[1,64,4096]{2,1,0:T(8,128)(2,1)S(1)}, bf16[1,64,4096]{2,1,0:T(8,128)(2,1)S(1)}, u32[]{:S(2)}, u32[]{:S(2)}) collective-permute-start(bf16[1,64,4096]{2,1,0:T(8,128)(2,1)S(1)} %get-tuple-element.150), channel_id=1, source_target_pairs={{0,4},{1,3},{2,6},{3,1},{4,0},{5,7},{6,2},{7,5},{8,12},{9,11},{10,... | collective-permute-start | bytes 1572872 | tf_op jit(solution)/shard_map/ppermute | solution.py:625
  77.8 16.6 %collective-permute-start.8 = (bf16[4,64,1024]{2,1,0:T(8,128)(2,1)S(1)}, bf16[4,64,1024]{2,1,0:T(8,128)(2,1)S(1)}, u32[]{:S(2)}, u32[]{:S(2)}) collective-permute-start(bf16[4,64,1024]{2,1,0:T(8,128)(2,1)S(1)} %get-tuple-element.156), channel_id=1, source_target_pairs={{0,1},{1,0},{2,3},{3,2},{4,5},{5,4},{6,7},{7,6},{8,9},{9,8},{10,11... | collective-permute-start | bytes 1572872 | tf_op jit(solution)/shard_map/ppermute | solution.py:629
  78.5 13.1 %collective-permute-start.7 = (bf16[1,32,4096]{2,1,0:T(8,128)(2,1)S(1)}, bf16[1,32,4096]{2,1,0:T(8,128)(2,1)S(1)}, u32[]{:S(2)}, u32[]{:S(2)}) collective-permute-start(bf16[1,32,4096]{2,1,0:T(8,128)(2,1)S(1)} %get-tuple-element.155), channel_id=1, source_target_pairs={{0,8},{1,9},{2,10},{3,11},{4,12},{5,13},{6,14},{7,15},{8,0},{9,1},... | collective-permute-start | bytes 786440 | tf_op jit(solution)/shard_map/ppermute | solution.py:625
  91.7 14.9 %collective-permute-start.9 = (bf16[1,32,4096]{2,1,0:T(8,128)(2,1)S(1)}, bf16[1,32,4096]{2,1,0:T(8,128)(2,1)S(1)}, u32[]{:S(2)}, u32[]{:S(2)}) collective-permute-start(bf16[1,32,4096]{2,1,0:T(8,128)(2,1)S(1)} %ff_sum2.1.refs_0_), channel_id=1, source_target_pairs={{0,16},{1,17},{2,18},{3,19},{4,20},{5,21},{6,22},{7,23},{8,24},{9,... | collective-permute-start | bytes 786440 | tf_op jit(solution)/shard_map/ppermute | solution.py:625
  94.4 18.1 %copy-start.4 = (bf16[256,2048]{1,0:T(8,128)(2,1)S(1)}, bf16[256,2048]{1,0:T(8,128)(2,1)}, u32[]{:S(2)}) copy-start(bf16[256,2048]{1,0:T(8,128)(2,1)} %refs_14_.5) | copy-start | bytes 3145732
  94.4 18.1 %copy-start.6 = (bf16[1024,512]{1,0:T(8,128)(2,1)S(1)}, bf16[1024,512]{1,0:T(8,128)(2,1)}, u32[]{:S(2)}) copy-start(bf16[1024,512]{1,0:T(8,128)(2,1)} %refs_10_.3) | copy-start | bytes 3145732
  106.0 6.4 %copy-start.2 = (bf16[2048,512]{1,0:T(8,128)(2,1)S(1)}, bf16[2048,512]{1,0:T(8,128)(2,1)}, u32[]{:S(2)}) copy-start(bf16[2048,512]{1,0:T(8,128)(2,1)} %tok_ref.5) | copy-start | bytes 6291460
  106.7 2.0 %collective-permute-start.10 = (bf16[4,64,1024]{2,1,0:T(8,128)(2,1)S(1)}, bf16[4,64,1024]{2,1,0:T(8,128)(2,1)S(1)}, u32[]{:S(2)}, u32[]{:S(2)}) collective-permute-start(bf16[4,64,1024]{2,1,0:T(8,128)(2,1)S(1)} %get-tuple-element.164), channel_id=1, source_target_pairs={{0,1},{1,0},{2,3},{3,2},{4,5},{5,4},{6,7},{7,6},{8,9},{9,8},{10,11... | collective-permute-start | bytes 1572872 | tf_op jit(solution)/shard_map/ppermute | solution.py:629
  106.8 18.7 %collective-permute-start.14 = (bf16[1,32,4096]{2,1,0:T(8,128)(2,1)S(1)}, bf16[1,32,4096]{2,1,0:T(8,128)(2,1)S(1)}, u32[]{:S(2)}, u32[]{:S(2)}) collective-permute-start(bf16[1,32,4096]{2,1,0:T(8,128)(2,1)S(1)} %ff_sum3.1.mine_ref), channel_id=1, source_target_pairs={{0,8},{1,9},{2,10},{3,11},{4,12},{5,13},{6,14},{7,15},{8,0},{9,1},... | collective-permute-start | bytes 786440 | tf_op jit(solution)/shard_map/ppermute | solution.py:625
  108.9 16.1 %collective-permute-start.11 = (bf16[1,64,2048]{2,1,0:T(8,128)(2,1)S(1)}, bf16[1,64,2048]{2,1,0:T(8,128)(2,1)S(1)}, u32[]{:S(2)}, u32[]{:S(2)}) collective-permute-start(bf16[1,64,2048]{2,1,0:T(8,128)(2,1)S(1)} %get-tuple-element.178), channel_id=1, source_target_pairs={{0,4},{1,3},{2,6},{3,1},{4,0},{5,7},{6,2},{7,5},{8,12},{9,11},{10,... | collective-permute-start | bytes 786440 | tf_op jit(solution)/shard_map/ppermute | solution.py:625
  109.4 15.6 %collective-permute-start.12 = (bf16[1,64,2048]{2,1,0:T(8,128)(2,1)S(1)}, bf16[1,64,2048]{2,1,0:T(8,128)(2,1)S(1)}, u32[]{:S(2)}, u32[]{:S(2)}) collective-permute-start(bf16[1,64,2048]{2,1,0:T(8,128)(2,1)S(1)} %get-tuple-element.179), channel_id=1, source_target_pairs={{0,2},{1,5},{2,0},{3,7},{4,6},{5,1},{6,4},{7,3},{8,10},{9,13},{10,... | collective-permute-start | bytes 786440 | tf_op jit(solution)/shard_map/ppermute | solution.py:625
  111.0 14.1 %collective-permute-start.13 = (bf16[1,64,2048]{2,1,0:T(8,128)(2,1)S(1)}, bf16[1,64,2048]{2,1,0:T(8,128)(2,1)S(1)}, u32[]{:S(2)}, u32[]{:S(2)}) collective-permute-start(bf16[1,64,2048]{2,1,0:T(8,128)(2,1)S(1)} %get-tuple-element.180), channel_id=1, source_target_pairs={{0,6},{1,7},{2,4},{3,5},{4,2},{5,3},{6,0},{7,1},{8,14},{9,15},{10,... | collective-permute-start | bytes 786440 | tf_op jit(solution)/shard_map/ppermute | solution.py:625
  125.2 15.6 %collective-permute-start.17 = (bf16[1,64,2048]{2,1,0:T(8,128)(2,1)S(1)}, bf16[1,64,2048]{2,1,0:T(8,128)(2,1)S(1)}, u32[]{:S(2)}, u32[]{:S(2)}) collective-permute-start(bf16[1,64,2048]{2,1,0:T(8,128)(2,1)S(1)} %att_sum0.1.refs_0_), channel_id=1, source_target_pairs={{0,8},{1,9},{2,10},{3,11},{4,12},{5,13},{6,14},{7,15},{8,0},{9,1},... | collective-permute-start | bytes 786440 | tf_op jit(solution)/shard_map/ppermute | solution.py:625
  126.0 14.8 %copy-start.9 = (bf16[1,64,4096]{2,1,0:T(8,128)(2,1)}, bf16[1,64,4096]{2,1,0:T(8,128)(2,1)S(1)}, u32[]{:S(2)}) copy-start(bf16[1,64,4096]{2,1,0:T(8,128)(2,1)S(1)} %ff_join.1.refs_0_) | copy-start | bytes 1572868
  126.0 14.7 %collective-permute-start.16 = (bf16[1,64,4096]{2,1,0:T(8,128)(2,1)S(1)}, bf16[1,64,4096]{2,1,0:T(8,128)(2,1)}, u32[]{:S(2)}, u32[]{:S(2)}) collective-permute-start(bf16[1,64,4096]{2,1,0:T(8,128)(2,1)S(1)} %ff_join.1.refs_0_), channel_id=1, source_target_pairs={{0,2},{1,5},{2,0},{3,7},{4,6},{5,1},{6,4},{7,3},{8,10},{9,13},{10,... | collective-permute-start | bytes 1572872 | tf_op jit(solution)/shard_map/ppermute | solution.py:625
  127.6 13.2 %collective-permute-start.15 = (bf16[1,64,4096]{2,1,0:T(8,128)(2,1)S(1)}, bf16[1,64,4096]{2,1,0:T(8,128)(2,1)S(1)}, u32[]{:S(2)}, u32[]{:S(2)}) collective-permute-start(bf16[1,64,4096]{2,1,0:T(8,128)(2,1)S(1)} %ff_join.1.refs_0_), channel_id=1, source_target_pairs={{0,4},{1,3},{2,6},{3,1},{4,0},{5,7},{6,2},{7,5},{8,12},{9,11},{10,... | collective-permute-start | bytes 1572872 | tf_op jit(solution)/shard_map/ppermute | solution.py:625
  140.8 5.8 %copy-start.13 = (bf16[1,64,4096]{2,1,0:T(8,128)(2,1)}, bf16[1,64,4096]{2,1,0:T(8,128)(2,1)S(1)}, u32[]{:S(2)}) copy-start(bf16[1,64,4096]{2,1,0:T(8,128)(2,1)S(1)} %collective-permute-done.15.refs_1_) | copy-start | bytes 1572868
  140.9 21.1 %collective-permute-start.21 = (bf16[1,64,4096]{2,1,0:T(8,128)(2,1)}, bf16[1,64,4096]{2,1,0:T(8,128)(2,1)S(1)}, u32[]{:S(2)}, u32[]{:S(2)}) collective-permute-start(bf16[1,64,4096]{2,1,0:T(8,128)(2,1)} %collective-permute-done.16.refs_2_), channel_id=1, source_target_pairs={{0,4},{1,3},{2,6},{3,1},{4,0},{5,7},{6,2},{7,5},{8,12},{9,11},{10,... | collective-permute-start | bytes 1572872 | tf_op jit(solution)/shard_map/ppermute | solution.py:625
  142.5 15.6 %collective-permute-start.20 = (bf16[1,64,2048]{2,1,0:T(8,128)(2,1)S(1)}, bf16[1,64,2048]{2,1,0:T(8,128)(2,1)S(1)}, u32[]{:S(2)}, u32[]{:S(2)}) collective-permute-start(bf16[1,64,2048]{2,1,0:T(8,128)(2,1)S(1)} %att_sum1.1.refs_0_), channel_id=1, source_target_pairs={{0,16},{1,17},{2,18},{3,19},{4,20},{5,21},{6,22},{7,23},{8,24},{9,... | collective-permute-start | bytes 786440 | tf_op jit(solution)/shard_map/ppermute | solution.py:625
  145.4 1.2 collective-permute-start.18
  146.6 11.4 %collective-permute-start.19 = (f32[32,1,128]{2,1,0:T(1,128)S(1)}, f32[32,1,128]{2,1,0:T(1,128)S(1)}, u32[]{:S(2)}, u32[]{:S(2)}) collective-permute-start(f32[32,1,128]{2,1,0:T(1,128)S(1)} %small_pair.1.refs_0_), channel_id=1, source_target_pairs={{0,2},{1,3},{2,0},{3,1},{4,6},{5,7},{6,4},{7,5},{8,10},{9,11},{10,... | collective-permute-start | bytes 49160 | tf_op jit(solution)/shard_map/ppermute | solution.py:625
  158.2 10.0 %copy-start.10 = (bf16[1,64,2048]{2,1,0:T(8,128)(2,1)}, bf16[1,64,2048]{2,1,0:T(8,128)(2,1)S(1)}, u32[]{:S(2)}) copy-start(bf16[1,64,2048]{2,1,0:T(8,128)(2,1)S(1)} %att_sum2.1.refs_0_) | copy-start | bytes 786436
  158.2 15.5 %collective-permute-start.26 = (bf16[1,64,2048]{2,1,0:T(8,128)(2,1)S(1)}, bf16[1,64,2048]{2,1,0:T(8,128)(2,1)S(1)}, u32[]{:S(2)}, u32[]{:S(2)}) collective-permute-start(bf16[1,64,2048]{2,1,0:T(8,128)(2,1)S(1)} %att_sum2.1.refs_0_), channel_id=1, source_target_pairs={{0,6},{1,7},{2,4},{3,5},{4,2},{5,3},{6,0},{7,1},{8,14},{9,15},{10,... | collective-permute-start | bytes 786440 | tf_op jit(solution)/shard_map/ppermute | solution.py:625
  159.7 14.1 %collective-permute-start.25 = (bf16[1,64,2048]{2,1,0:T(8,128)(2,1)S(1)}, bf16[1,64,2048]{2,1,0:T(8,128)(2,1)S(1)}, u32[]{:S(2)}, u32[]{:S(2)}) collective-permute-start(bf16[1,64,2048]{2,1,0:T(8,128)(2,1)S(1)} %att_sum2.1.refs_0_), channel_id=1, source_target_pairs={{0,2},{1,5},{2,0},{3,7},{4,6},{5,1},{6,4},{7,3},{8,10},{9,13},{10,... | collective-permute-start | bytes 786440 | tf_op jit(solution)/shard_map/ppermute | solution.py:625
  160.2 13.5 %collective-permute-start.24 = (bf16[1,64,2048]{2,1,0:T(8,128)(2,1)S(1)}, bf16[1,64,2048]{2,1,0:T(8,128)(2,1)S(1)}, u32[]{:S(2)}, u32[]{:S(2)}) collective-permute-start(bf16[1,64,2048]{2,1,0:T(8,128)(2,1)S(1)} %att_sum2.1.refs_0_), channel_id=1, source_target_pairs={{0,4},{1,3},{2,6},{3,1},{4,0},{5,7},{6,2},{7,5},{8,12},{9,11},{10,... | collective-permute-start | bytes 786440 | tf_op jit(solution)/shard_map/ppermute | solution.py:625
  161.7 6.5 %collective-permute-start.22 = (f32[32,1,128]{2,1,0:T(1,128)S(1)}, f32[32,1,128]{2,1,0:T(1,128)S(1)}, u32[]{:S(2)}, u32[]{:S(2)}) collective-permute-start(f32[32,1,128]{2,1,0:T(1,128)S(1)} %small_sum.4.refs_0_), channel_id=1, source_target_pairs={{0,8},{1,9},{2,10},{3,11},{4,12},{5,13},{6,14},{7,15},{8,0},{9,1},... | collective-permute-start | bytes 49160 | tf_op jit(solution)/shard_map/ppermute | solution.py:625
  161.9 0.8 copy-start.14
  168.3 5.5 %collective-permute-start.23 = (f32[32,1,128]{2,1,0:T(1,128)S(1)}, f32[32,1,128]{2,1,0:T(1,128)S(1)}, u32[]{:S(2)}, u32[]{:S(2)}) collective-permute-start(f32[32,1,128]{2,1,0:T(1,128)S(1)} %small_sum.5.refs_0_), channel_id=1, source_target_pairs={{0,16},{1,17},{2,18},{3,19},{4,20},{5,21},{6,22},{7,23},{8,24},{9,... | collective-permute-start | bytes 49160 | tf_op jit(solution)/shard_map/ppermute | solution.py:625
  173.7 0.7 copy-start.15
  173.8 0.8 copy-start.16
  173.8 0.9 copy-start.17
  173.8 8.3 %collective-permute-start.27 = (f32[32,1,128]{2,1,0:T(1,128)S(1)}, f32[32,1,128]{2,1,0:T(1,128)S(1)}, u32[]{:S(2)}, u32[]{:S(2)}) collective-permute-start(f32[32,1,128]{2,1,0:T(1,128)S(1)} %small_sum.6.refs_0_), channel_id=1, source_target_pairs={{0,4},{1,5},{2,6},{3,7},{4,0},{5,1},{6,2},{7,3},{8,12},{9,13},{10,... | collective-permute-start | bytes 49160 | tf_op jit(solution)/shard_map/ppermute | solution.py:625
  174.7 7.6 %copy-start.24 = (bf16[1024]{0:T(1024)(128)(2,1)S(1)}, bf16[1024]{0:T(1024)(128)(2,1)}, u32[]{:S(2)}) copy-start(bf16[1024]{0:T(1024)(128)(2,1)} %param.31) | copy-start | bytes 6148
  174.7 7.6 %copy-start.26 = (f32[1024]{0:T(1024)S(1)}, f32[1024]{0:T(1024)}, u32[]{:S(2)}) copy-start(f32[1024]{0:T(1024)} %param.38) | copy-start | bytes 12292
  174.7 7.6 %copy-start.27 = (f32[1024]{0:T(1024)S(1)}, f32[1024]{0:T(1024)}, u32[]{:S(2)}) copy-start(f32[1024]{0:T(1024)} %param.45) | copy-start | bytes 12292
  174.7 8.2 %copy-start.25 = (bf16[768]{0:T(1024)(128)(2,1)S(1)}, bf16[768]{0:T(1024)(128)(2,1)}, u32[]{:S(2)}) copy-start(bf16[768]{0:T(1024)(128)(2,1)} %param.28) | copy-start | bytes 4612
  174.7 8.2 %copy-start.28 = (f32[768]{0:T(1024)S(1)}, f32[768]{0:T(1024)}, u32[]{:S(2)}) copy-start(f32[768]{0:T(1024)} %param.35) | copy-start | bytes 9220
  174.7 8.2 %copy-start.29 = (f32[768]{0:T(1024)S(1)}, f32[768]{0:T(1024)}, u32[]{:S(2)}) copy-start(f32[768]{0:T(1024)} %param.42) | copy-start | bytes 9220
  174.7 8.8 %copy-start.21 = (bf16[6,256]{1,0:T(8,128)(2,1)S(1)}, bf16[6,256]{1,0:T(8,128)(2,1)}, u32[]{:S(2)}) copy-start(bf16[6,256]{1,0:T(8,128)(2,1)} %param.26) | copy-start | bytes 9220
  174.7 8.8 %copy-start.22 = (f32[6,256]{1,0:T(8,128)S(1)}, f32[6,256]{1,0:T(8,128)}, u32[]{:S(2)}) copy-start(f32[6,256]{1,0:T(8,128)} %param.33) | copy-start | bytes 18436
  174.7 8.8 %copy-start.23 = (f32[6,256]{1,0:T(8,128)S(1)}, f32[6,256]{1,0:T(8,128)}, u32[]{:S(2)}) copy-start(f32[6,256]{1,0:T(8,128)} %param.40) | copy-start | bytes 18436
  182.2 2.0 %copy-start.19 = (f32[6,128]{1,0:T(8,128)}, f32[6,128]{1,0:T(8,128)S(1)}, u32[]{:S(2)}) copy-start(f32[6,128]{1,0:T(8,128)S(1)} %slice_reduce_fusion.1) | copy-start | bytes 9220
  182.2 2.0 %copy-start.20 = (f32[8,1,128]{2,1,0:T(1,128)}, f32[8,1,128]{2,1,0:T(1,128)S(1)}, u32[]{:S(2)}) copy-start(f32[8,1,128]{2,1,0:T(1,128)S(1)} %slice.17) | copy-start | bytes 12292
  182.2 1.9 %copy-start.18 = (f32[6,256]{1,0:T(8,128)}, f32[6,256]{1,0:T(8,128)S(1)}, u32[]{:S(2)}) copy-start(f32[6,256]{1,0:T(8,128)S(1)} %reshape.150) | copy-start | bytes 18436

commit v7 on v6

--- a/solution.py
+++ b/solution.py
@@ -774,9 +774,11 @@
     packed = jnp.concatenate(
         [vectors.reshape(12, 128), qkv_bias.reshape(6, 128), fc_bias.reshape(8, 128)], 0
     )
-    small = lax.all_gather(packed, "opt", axis=0, tiled=True).astype(f32).reshape(2 * SMALL_ROWS, 1, 128)
-    fc_far = swap(fc_weight)
-    proj_far = swap(proj_weight)
+    packed_far = swap(packed)
+    small = jnp.stack([jnp.where(c == 0, packed, packed_far), jnp.where(c == 0, packed_far, packed)])
+    small = small.astype(f32).reshape(2 * SMALL_ROWS, 1, 128)
+    fc_far = swap(tie(fc_weight, packed_far))
+    proj_far = swap(tie(proj_weight, packed_far))
     qkv_far = swap(qkv_weight)
     out_far = swap(out_weight)
 

time: 185 us -> 184 us (level)
  blocking collectives: 2.64 us -> 0 us
    all_gather x1 -> x0, blocking collectives: 2.64 us -> none  [body(): lax.all_gather(packed, 'opt', axis=0, tiled=True).astype(f32)]
    ppermute x8 -> x9, waiting for transfers between devices: 4.54 us -> 5.37 us  [swap(): return lax.ppermute(a, 'opt', [(0, 1), (1, 0)])]
  transfers between devices with their start and end apart: 28 -> 29, of which waited for: 4 -> 5; matrix products, arithmetic and copies ran while one was open for 1% -> 0% of each run, Pallas kernels for 61% -> 61%
where the time goes in v7:
time: 184 us
  Pallas kernels  139 us (76%)
  starting transfers between devices  27.8 us (15%)
  local copies, waits for them, and re-layouts  6.22 us (3%)
  waiting for transfers between devices  5.99 us (3%)
  other arithmetic  3.3 us (2%)
    pallas_call x4, Pallas kernels, attention_call(): pl.pallas_call(functools.partial(attention_kernel, j, rel), grid_spec=gri...  46.1 us
    pallas_call x4, Pallas kernels, adam_call(): pl.pallas_call(run, grid_spec=grid_spec, out_shape=outs, input_output_ali...  27.5 us
    ppermute x20, starting transfers between devices, exchange(): return lax.ppermute(a, ('rep', 'opt'), pairs)  26.1 us
    pallas_call x1, Pallas kernels, ff_call(): pl.pallas_call(ff_kernel, grid_spec=grid_spec, out_shape=[jax.ShapeDtypeS...  25.8 us
    pallas_call x2, Pallas kernels, output_call(): pl.pallas_call(functools.partial(output_kernel, part, parts), grid_spec=g...  25.2 us
    pallas_call x1, Pallas kernels, ff_own_call(): pl.pallas_call(ff_own_kernel, grid_spec=grid_spec, out_shape=jax.ShapeDty...  9.86 us
    ppermute x9, waiting for transfers between devices, swap(): return lax.ppermute(a, 'opt', [(0, 1), (1, 0)])  5.37 us
    unnamed x60, local copies, waits for them, and re-layouts  5.31 us
  transfers between devices with their start and end apart: 29, of which 5 were waited for; matrix products, arithmetic and copies ran while one was open for 0% of the time, Pallas kernels for 61%

profile of v7, /device:TPU:0, one launch (start us, length us, event | category | flops | bytes accessed | tf_op | source)
XLA Modules:
  0.0 183.8 jit_solution(5750668928874556967)
XLA Ops:
  0.7 0.8 reshape.146
  1.5 0.7 pad_maximum_fusion
  2.2 0.5 collective-permute-start
  2.8 0.8 collective-permute-done
  3.6 0.3 collective-permute-start.2
  4.0 0.2 collective-permute-start.1
  4.1 0.7 select_bitcast_fusion.1
  4.9 1.6 copy-done.1
  6.5 1.9 %norm.1 = (bf16[2048,512]{1,0:T(8,128)(2,1)S(1)}, bf16[2048,512]{1,0:T(8,128)(2,1)S(1)}) custom-call(bf16[2048,512]{1,0:T(8,128)(2,1)S(1)} %copy-done.1, f32[52,1,128]{2,1,0:T(1,128)S(1)} %reshape.167.small_ref.refs_16_), custom_call_target="tpu_custom_call" | custom-call | flops 20971520 | bytes 6291456 | tf_op jit(solution)/shard_map/norm/pallas_call | solution.py:79
  8.4 1.2 copy-done.3
  9.7 1.2 copy-done.5
  10.9 25.8 %feed_forward.1 = (bf16[4,64,4096]{2,1,0:T(8,128)(2,1)S(1)}, bf16[2048,2048]{1,0:T(8,128)(2,1)}, bf16[2048,2048]{1,0:T(8,128)(2,1)}, f32[4,1,512]{2,1,0:T(1,128)S(1)}) custom-call(s32[4]{0:T(128)S(1)} %compare_select_fusion.2.meta.meta_ref, bf16[2048,512]{1,0:T(8,128)(2,1)S(1)} %get-tuple-element.134.second_ref, bf16[2048,512]{1,0:T(8,128)(2,1)S(1)} %copy-done, ...), custom_call_target="tpu_custom_call" | custom-call | flops 12884901888 | bytes 20971520 | tf_op jit(solution)/shard_map/feed_forward/pallas_call | solution.py:188
  36.6 0.3 collective-permute-start.3
  36.9 0.2 collective-permute-start.4
  37.1 9.9 %feed_forward_own.1.refs_0_ = bf16[4,64,4096]{2,1,0:T(8,128)(2,1)S(1)} custom-call(s32[4]{0:T(128)S(1)} %compare_select_fusion.2.meta.meta_ref, bf16[2048,512]{1,0:T(8,128)(2,1)S(1)} %get-tuple-element.134.second_ref, bf16[2048,512]{1,0:T(8,128)(2,1)S(1)} %copy-done, bf16[2048,2048]{1,0:T(8,128)(2,1)} %get-tuple-element.139.act_ref, ...), custom_call_target="tpu_custom_call" | custom-call | flops 4294967296 | bytes 16777216 | tf_op jit(solution)/shard_map/feed_forward_own/pallas_call | solution.py:219
  47.0 0.5 ff_pair.1
  47.5 2.9 %collective-permute-start.6 = (bf16[2,64,4096]{2,1,0:T(8,128)(2,1)S(1)}, bf16[2,64,4096]{2,1,0:T(8,128)(2,1)S(1)}, u32[]{:S(2)}, u32[]{:S(2)}) collective-permute-start(bf16[2,64,4096]{2,1,0:T(8,128)(2,1)S(1)} %get-tuple-element.146), channel_id=1, source_target_pairs={{0,2},{1,5},{2,0},{3,7},{4,6},{5,1},{6,4},{7,3},{8,10},{9,13},{10,... | collective-permute-start | bytes 3145736 | tf_op jit(solution)/shard_map/ppermute | solution.py:625
  50.4 1.5 collective-permute-done.5.ow_ref.refs_9_
  52.0 11.4 %attention_01.1 = (bf16[4,64,384]{2,1,0:T(8,128)(2,1)S(1)}, bf16[4,64,640]{2,1,0:T(8,128)(2,1)S(1)}, bf16[2048,384]{1,0:T(8,128)(2,1)S(1)}, bf16[2048,128]{1,0:T(8,128)(2,1)S(1)}, f32[1,384]{1,0:T(1,128)S(1)}) custom-call(s32[4]{0:T(128)S(1)} %compare_select_fusion.2.meta.meta_ref, bf16[2048,512]{1,0:T(8,128)(2,1)S(1)} %get-tuple-element.143.first_ref, ...), custom_call_target="tpu_custom_call" | custom-call | flops 5368709120 | bytes 6291456 | tf_op jit(solution)/shard_map/attention_01/pallas_call | solution.py:393
  63.4 0.3 ff_sum0.1
  63.7 1.9 %collective-permute-start.7 = (bf16[1,64,4096]{2,1,0:T(8,128)(2,1)S(1)}, bf16[1,64,4096]{2,1,0:T(8,128)(2,1)S(1)}, u32[]{:S(2)}, u32[]{:S(2)}) collective-permute-start(bf16[1,64,4096]{2,1,0:T(8,128)(2,1)S(1)} %get-tuple-element.154), channel_id=1, source_target_pairs={{0,4},{1,3},{2,6},{3,1},{4,0},{5,7},{6,2},{7,5},{8,12},{9,11},{10,... | collective-permute-start | bytes 1572872 | tf_op jit(solution)/shard_map/ppermute | solution.py:625
  65.6 11.6 %attention_00.1 = (bf16[4,64,1024]{2,1,0:T(8,128)(2,1)S(1)}, bf16[4,64,1024]{2,1,0:T(8,128)(2,1)S(1)}, bf16[2048,384]{1,0:T(8,128)(2,1)S(1)}, bf16[2048,128]{1,0:T(8,128)(2,1)S(1)}, f32[1,384]{1,0:T(1,128)S(1)}) custom-call(s32[4]{0:T(128)S(1)} %compare_select_fusion.2.meta.meta_ref, bf16[2048,512]{1,0:T(8,128)(2,1)S(1)} %get-tuple-element.143.first_ref, ...), custom_call_target="tpu_custom_call" | custom-call | flops 5368709120 | bytes 6291456 | tf_op jit(solution)/shard_map/attention_00/pallas_call | solution.py:393
  77.2 0.1 collective-permute-start.9
  77.3 0.7 ff_sum1.1
  78.0 1.6 collective-permute-start.8
  79.6 11.4 %attention_11.1 = (bf16[4,64,384]{2,1,0:T(8,128)(2,1)S(1)}, bf16[4,64,640]{2,1,0:T(8,128)(2,1)S(1)}, bf16[2048,384]{1,0:T(8,128)(2,1)S(1)}, bf16[2048,128]{1,0:T(8,128)(2,1)S(1)}, f32[1,384]{1,0:T(1,128)S(1)}) custom-call(s32[4]{0:T(128)S(1)} %compare_select_fusion.2.meta.meta_ref, bf16[2048,512]{1,0:T(8,128)(2,1)S(1)} %get-tuple-element.143.first_ref, ...), custom_call_target="tpu_custom_call" | custom-call | flops 5368709120 | bytes 6291456 | tf_op jit(solution)/shard_map/attention_11/pallas_call | solution.py:393
  91.1 2.7 %collective-permute-start.10 = (bf16[1,32,4096]{2,1,0:T(8,128)(2,1)S(1)}, bf16[1,32,4096]{2,1,0:T(8,128)(2,1)S(1)}, u32[]{:S(2)}, u32[]{:S(2)}) collective-permute-start(bf16[1,32,4096]{2,1,0:T(8,128)(2,1)S(1)} %ff_sum2.1.refs_0_), channel_id=1, source_target_pairs={{0,16},{1,17},{2,18},{3,19},{4,20},{5,21},{6,22},{7,23},{8,24},{9,... | collective-permute-start | bytes 786440 | tf_op jit(solution)/shard_map/ppermute | solution.py:625
  93.8 11.6 %attention_10.1 = (bf16[4,64,1024]{2,1,0:T(8,128)(2,1)S(1)}, bf16[4,64,1024]{2,1,0:T(8,128)(2,1)S(1)}, bf16[2048,384]{1,0:T(8,128)(2,1)S(1)}, bf16[2048,128]{1,0:T(8,128)(2,1)S(1)}, f32[1,384]{1,0:T(1,128)S(1)}) custom-call(s32[4]{0:T(128)S(1)} %compare_select_fusion.2.meta.meta_ref, bf16[2048,512]{1,0:T(8,128)(2,1)S(1)} %get-tuple-element.143.first_ref, ...), custom_call_target="tpu_custom_call" | custom-call | flops 5368709120 | bytes 6291456 | tf_op jit(solution)/shard_map/attention_10/pallas_call | solution.py:393
  105.5 0.6 collective-permute-done.10.refs_1_
  106.0 0.1 ff_sum3.1.mine_ref
  106.1 0.1 collective-permute-start.11
  106.3 1.8 collective-permute-done.11.refs_3_
  108.1 0.3 att_pair.1
  108.3 0.5 collective-permute-start.12
  108.8 1.5 collective-permute-start.13
  110.4 1.5 collective-permute-start.14
  111.9 12.6 %outputs_0.1 = (bf16[2048,512]{1,0:T(8,128)(2,1)}, bf16[2048,512]{1,0:T(8,128)(2,1)}, f32[5,8,512]{2,1,0:T(8,128)S(1)}) custom-call(s32[4]{0:T(128)S(1)} %compare_select_fusion.2.meta.meta_ref, bf16[2048,512]{1,0:T(8,128)(2,1)S(1)} %copy-done.2, bf16[2048,512]{1,0:T(8,128)(2,1)S(1)} %copy-done, bf16[2048,2048]{1,0:T(8,128)(2,1)} %get-tuple-element.139.act_ref, ...), custom_call_target="tpu_custom_call" | custom-call | flops 6442450944 | bytes 20971520 | tf_op jit(solution)/shard_map/outputs_0/pallas_call | solution.py:536
  124.5 0.1 att_sum0.1.refs_0_
  124.6 0.3 collective-permute-start.18
  124.9 0.6 ff_join.1.refs_0_
  125.5 1.6 collective-permute-start.17
  127.0 0.5 collective-permute-start.16
  127.5 12.7 %outputs_1.1 = (bf16[2048,512]{1,0:T(8,128)(2,1)}, bf16[2048,512]{1,0:T(8,128)(2,1)}, f32[32,1,128]{2,1,0:T(1,128)S(1)}, f32[32,1,128]{2,1,0:T(1,128)S(1)}) custom-call(s32[4]{0:T(128)S(1)} %compare_select_fusion.2.meta.meta_ref, bf16[2048,512]{1,0:T(8,128)(2,1)S(1)} %copy-done.2, ...), custom_call_target="tpu_custom_call", output_to_operand_aliasing={{0}: (28, {}), {1}: (29, {})} | custom-call | flops 6442450944 | bytes 20971520 | tf_op jit(solution)/shard_map/outputs_1/pallas_call | solution.py:536
  140.3 1.6 collective-permute-start.22
  141.9 3.0 %collective-permute-start.21 = (bf16[1,64,2048]{2,1,0:T(8,128)(2,1)S(1)}, bf16[1,64,2048]{2,1,0:T(8,128)(2,1)S(1)}, u32[]{:S(2)}, u32[]{:S(2)}) collective-permute-start(bf16[1,64,2048]{2,1,0:T(8,128)(2,1)S(1)} %att_sum1.1.refs_0_), channel_id=1, source_target_pairs={{0,16},{1,17},{2,18},{3,19},{4,20},{5,21},{6,22},{7,23},{8,24},{9,... | collective-permute-start | bytes 786440 | tf_op jit(solution)/shard_map/ppermute | solution.py:625
  144.9 1.2 collective-permute-done.19.refs_1_
  146.1 0.6 collective-permute-start.20
  146.7 10.8 %adam_ff_0.1 = (f32[2,4,2,64,512]{4,3,2,1,0:T(8,128)}, f32[2,4,2,64,512]{4,3,2,1,0:T(8,128)}, f32[2,4,2,64,512]{4,3,2,1,0:T(8,128)}, f32[2,4,2,64,512]{4,3,2,1,0...) custom-call(s32[4]{0:T(128)} %copy-done.11, ...), custom_call_target="tpu_custom_call" | custom-call | flops 15728640 | bytes 22020096 | tf_op jit(solution)/shard_map/adam_ff_0/pallas_call | solution.py:729
  157.6 1.5 collective-permute-start.27
  159.1 0.5 collective-permute-start.26
  159.7 1.5 collective-permute-start.25
  161.2 0.2 collective-permute-start.23
  161.4 0.8 copy-done.14
  162.2 5.5 %adam_ff_3.1 = (f32[2,4,2,64,512]{4,3,2,1,0:T(8,128)}, f32[2,4,2,64,512]{4,3,2,1,0:T(8,128)}, f32[2,4,2,64,512]{4,3,2,1,0:T(8,128)}, f32[2,4,2,64,512]{4,3,2,1,0...) custom-call(s32[4]{0:T(128)} %copy-done.11, ...), custom_call_target="tpu_custom_call", output_to_operand_aliasing={{0}: (1, {}), {1}: (2, {}), {2}: (3, {}), {3}: (4, {}), {4}... | custom-call | flops 5242880 | bytes 7340032 | tf_op jit(solution)/shard_map/adam_ff_3/pallas_call | solution.py:729
  167.7 1.7 collective-permute-start.24
  169.4 3.8 %adam_qkv_0.1 = (f32[256,1536]{1,0:T(8,128)}, f32[256,1536]{1,0:T(8,128)}, f32[256,1536]{1,0:T(8,128)}, f32[256,1536]{1,0:T(8,128)}, f32[2,128,512]{2,1,0:T(8,12...) custom-call(s32[4]{0:T(128)} %copy-done.11, bf16[1,64,2048]{2,1,0:T(8,128)(2,1)} %copy-done.10, ...), custom_call_target="tpu_custom_call" | custom-call | flops 2621440 | bytes 3670016 | tf_op jit(solution)/shard_map/adam_qkv_0/pallas_call | solution.py:729
  173.2 0.5 collective-permute-start.28
  173.8 0.1 copy-done.15
  173.9 0.1 copy-done.16
  174.0 0.1 copy-done.17
  174.2 7.4 %adam_qkv_1.1 = (f32[256,1536]{1,0:T(8,128)}, f32[256,1536]{1,0:T(8,128)}, f32[256,1536]{1,0:T(8,128)}, f32[256,1536]{1,0:T(8,128)}, f32[2,128,512]{2,1,0:T(8,12...) custom-call(s32[4]{0:T(128)} %copy-done.11, ...), custom_call_target="tpu_custom_call", output_to_operand_aliasing={{0}: (1, {}), {1}: (2, {}), {2}: (3, {}), {3}: (4, {}), {4}... | custom-call | flops 7864320 | bytes 11010048 | tf_op jit(solution)/shard_map/adam_qkv_1/pallas_call | solution.py:729
  181.8 0.6 add_multiply_fusion.1
  182.4 0.6 add_multiply_fusion.2
  183.0 0.6 add_multiply_fusion
  (95 shorter events, 0.6 us)
Async XLA Ops:
  0.7 7.7 %copy-start = (bf16[2048,512]{1,0:T(8,128)(2,1)S(1)}, bf16[2048,512]{1,0:T(8,128)(2,1)}, u32[]{:S(2)}) copy-start(bf16[2048,512]{1,0:T(8,128)(2,1)} %grad_ref.15) | copy-start | bytes 6291460
  2.2 1.4 collective-permute-start
  3.6 4.8 %collective-permute-start.2 = (bf16[1024,512]{1,0:T(8,128)(2,1)}, bf16[1024,512]{1,0:T(8,128)(2,1)S(1)}, u32[]{:S(2)}, u32[]{:S(2)}) collective-permute-start(bf16[1024,512]{1,0:T(8,128)(2,1)} %refs_10_.3), channel_id=1, source_target_pairs={{0,1},{1,0},{2,3},{3,2},{4,5},{5,4},{6,7},{7,6},{8,9},{9,8},{10,11... | collective-permute-start | bytes 3145736 | tf_op jit(solution)/shard_map/ppermute | solution.py:629
  4.0 4.5 %collective-permute-start.1 = (bf16[256,2048]{1,0:T(8,128)(2,1)}, bf16[256,2048]{1,0:T(8,128)(2,1)}, u32[]{:S(2)}, u32[]{:S(2)}) collective-permute-start(bf16[256,2048]{1,0:T(8,128)(2,1)} %refs_14_.5), channel_id=1, source_target_pairs={{0,1},{1,0},{2,3},{3,2},{4,5},{5,4},{6,7},{7,6},{8,9},{9,8},{10,11... | collective-permute-start | bytes 3145736 | tf_op jit(solution)/shard_map/ppermute | solution.py:629
  4.1 123.4 %copy-start.11 = (s32[4]{0:T(128)}, s32[4]{0:T(128)S(1)}, u32[]{:S(2)}) copy-start(s32[4]{0:T(128)S(1)} %compare_select_fusion.2.meta.meta_ref) | copy-start | bytes 52
  4.9 1.6 copy-start.1
  8.4 1.2 copy-start.3
  9.6 1.2 copy-start.5
  10.9 26.0 %copy-start.7 = (bf16[256,1536]{1,0:T(8,128)(2,1)S(1)}, bf16[256,1536]{1,0:T(8,128)(2,1)}, u32[]{:S(2)}) copy-start(bf16[256,1536]{1,0:T(8,128)(2,1)} %refs_13_.3) | copy-start | bytes 2359300
  36.6 10.4 %collective-permute-start.3 = (bf16[4,64,4096]{2,1,0:T(8,128)(2,1)S(1)}, bf16[4,64,4096]{2,1,0:T(8,128)(2,1)S(1)}, u32[]{:S(2)}, u32[]{:S(2)}) collective-permute-start(bf16[4,64,4096]{2,1,0:T(8,128)(2,1)S(1)} %get-tuple-element.137), channel_id=1, source_target_pairs={{0,1},{1,0},{2,3},{3,2},{4,5},{5,4},{6,7},{7,6},{8,9},{9,8},{10,11... | collective-permute-start | bytes 6291464 | tf_op jit(solution)/shard_map/ppermute | solution.py:629
  36.9 15.0 %collective-permute-start.4 = (bf16[256,1536]{1,0:T(8,128)(2,1)S(1)}, bf16[256,1536]{1,0:T(8,128)(2,1)S(1)}, u32[]{:S(2)}, u32[]{:S(2)}) collective-permute-start(bf16[256,1536]{1,0:T(8,128)(2,1)S(1)} %copy-done.7), channel_id=1, source_target_pairs={{0,1},{1,0},{2,3},{3,2},{4,5},{5,4},{6,7},{7,6},{8,9},{9,8},{10,11... | collective-permute-start | bytes 2359304 | tf_op jit(solution)/shard_map/ppermute | solution.py:629
  47.0 3.4 %copy-start.8 = (bf16[256,512]{1,0:T(8,128)(2,1)S(1)}, bf16[256,512]{1,0:T(8,128)(2,1)}, u32[]{:S(2)}) copy-start(bf16[256,512]{1,0:T(8,128)(2,1)} %refs_8_.4) | copy-start | bytes 786436
  47.0 4.9 %copy-start.12 = (f32[2,8,512]{2,1,0:T(8,128)S(1)}, f32[2,8,512]{2,1,0:T(8,128)}, u32[]{:S(2)}) copy-start(f32[2,8,512]{2,1,0:T(8,128)} %constant.31.clone.trig_ref) | copy-start | bytes 98308
  47.5 15.9 %collective-permute-start.6 = (bf16[2,64,4096]{2,1,0:T(8,128)(2,1)S(1)}, bf16[2,64,4096]{2,1,0:T(8,128)(2,1)S(1)}, u32[]{:S(2)}, u32[]{:S(2)}) collective-permute-start(bf16[2,64,4096]{2,1,0:T(8,128)(2,1)S(1)} %get-tuple-element.146), channel_id=1, source_target_pairs={{0,2},{1,5},{2,0},{3,7},{4,6},{5,1},{6,4},{7,3},{8,10},{9,13},{10,... | collective-permute-start | bytes 3145736 | tf_op jit(solution)/shard_map/ppermute | solution.py:625
  50.4 1.5 collective-permute-start.5
  63.7 13.6 %collective-permute-start.7 = (bf16[1,64,4096]{2,1,0:T(8,128)(2,1)S(1)}, bf16[1,64,4096]{2,1,0:T(8,128)(2,1)S(1)}, u32[]{:S(2)}, u32[]{:S(2)}) collective-permute-start(bf16[1,64,4096]{2,1,0:T(8,128)(2,1)S(1)} %get-tuple-element.154), channel_id=1, source_target_pairs={{0,4},{1,3},{2,6},{3,1},{4,0},{5,7},{6,2},{7,5},{8,12},{9,11},{10,... | collective-permute-start | bytes 1572872 | tf_op jit(solution)/shard_map/ppermute | solution.py:625
  77.2 16.6 %collective-permute-start.9 = (bf16[4,64,1024]{2,1,0:T(8,128)(2,1)S(1)}, bf16[4,64,1024]{2,1,0:T(8,128)(2,1)S(1)}, u32[]{:S(2)}, u32[]{:S(2)}) collective-permute-start(bf16[4,64,1024]{2,1,0:T(8,128)(2,1)S(1)} %get-tuple-element.160), channel_id=1, source_target_pairs={{0,1},{1,0},{2,3},{3,2},{4,5},{5,4},{6,7},{7,6},{8,9},{9,8},{10,11... | collective-permute-start | bytes 1572872 | tf_op jit(solution)/shard_map/ppermute | solution.py:629
  78.0 13.1 %collective-permute-start.8 = (bf16[1,32,4096]{2,1,0:T(8,128)(2,1)S(1)}, bf16[1,32,4096]{2,1,0:T(8,128)(2,1)S(1)}, u32[]{:S(2)}, u32[]{:S(2)}) collective-permute-start(bf16[1,32,4096]{2,1,0:T(8,128)(2,1)S(1)} %get-tuple-element.159), channel_id=1, source_target_pairs={{0,8},{1,9},{2,10},{3,11},{4,12},{5,13},{6,14},{7,15},{8,0},{9,1},... | collective-permute-start | bytes 786440 | tf_op jit(solution)/shard_map/ppermute | solution.py:625
  91.1 14.9 %collective-permute-start.10 = (bf16[1,32,4096]{2,1,0:T(8,128)(2,1)S(1)}, bf16[1,32,4096]{2,1,0:T(8,128)(2,1)S(1)}, u32[]{:S(2)}, u32[]{:S(2)}) collective-permute-start(bf16[1,32,4096]{2,1,0:T(8,128)(2,1)S(1)} %ff_sum2.1.refs_0_), channel_id=1, source_target_pairs={{0,16},{1,17},{2,18},{3,19},{4,20},{5,21},{6,22},{7,23},{8,24},{9,... | collective-permute-start | bytes 786440 | tf_op jit(solution)/shard_map/ppermute | solution.py:625
  93.8 18.1 %copy-start.4 = (bf16[256,2048]{1,0:T(8,128)(2,1)S(1)}, bf16[256,2048]{1,0:T(8,128)(2,1)}, u32[]{:S(2)}) copy-start(bf16[256,2048]{1,0:T(8,128)(2,1)} %refs_14_.5) | copy-start | bytes 3145732
  93.8 18.1 %copy-start.6 = (bf16[1024,512]{1,0:T(8,128)(2,1)S(1)}, bf16[1024,512]{1,0:T(8,128)(2,1)}, u32[]{:S(2)}) copy-start(bf16[1024,512]{1,0:T(8,128)(2,1)} %refs_10_.3) | copy-start | bytes 3145732
  105.5 6.4 %copy-start.2 = (bf16[2048,512]{1,0:T(8,128)(2,1)S(1)}, bf16[2048,512]{1,0:T(8,128)(2,1)}, u32[]{:S(2)}) copy-start(bf16[2048,512]{1,0:T(8,128)(2,1)} %tok_ref.5) | copy-start | bytes 6291460
  106.1 2.0 %collective-permute-start.11 = (bf16[4,64,1024]{2,1,0:T(8,128)(2,1)S(1)}, bf16[4,64,1024]{2,1,0:T(8,128)(2,1)S(1)}, u32[]{:S(2)}, u32[]{:S(2)}) collective-permute-start(bf16[4,64,1024]{2,1,0:T(8,128)(2,1)S(1)} %get-tuple-element.168), channel_id=1, source_target_pairs={{0,1},{1,0},{2,3},{3,2},{4,5},{5,4},{6,7},{7,6},{8,9},{9,8},{10,11... | collective-permute-start | bytes 1572872 | tf_op jit(solution)/shard_map/ppermute | solution.py:629
  106.2 18.7 %collective-permute-start.15 = (bf16[1,32,4096]{2,1,0:T(8,128)(2,1)S(1)}, bf16[1,32,4096]{2,1,0:T(8,128)(2,1)S(1)}, u32[]{:S(2)}, u32[]{:S(2)}) collective-permute-start(bf16[1,32,4096]{2,1,0:T(8,128)(2,1)S(1)} %ff_sum3.1.mine_ref), channel_id=1, source_target_pairs={{0,8},{1,9},{2,10},{3,11},{4,12},{5,13},{6,14},{7,15},{8,0},{9,1},... | collective-permute-start | bytes 786440 | tf_op jit(solution)/shard_map/ppermute | solution.py:625
  108.3 16.1 %collective-permute-start.12 = (bf16[1,64,2048]{2,1,0:T(8,128)(2,1)S(1)}, bf16[1,64,2048]{2,1,0:T(8,128)(2,1)S(1)}, u32[]{:S(2)}, u32[]{:S(2)}) collective-permute-start(bf16[1,64,2048]{2,1,0:T(8,128)(2,1)S(1)} %get-tuple-element.182), channel_id=1, source_target_pairs={{0,4},{1,3},{2,6},{3,1},{4,0},{5,7},{6,2},{7,5},{8,12},{9,11},{10,... | collective-permute-start | bytes 786440 | tf_op jit(solution)/shard_map/ppermute | solution.py:625
  108.8 15.6 %collective-permute-start.13 = (bf16[1,64,2048]{2,1,0:T(8,128)(2,1)S(1)}, bf16[1,64,2048]{2,1,0:T(8,128)(2,1)S(1)}, u32[]{:S(2)}, u32[]{:S(2)}) collective-permute-start(bf16[1,64,2048]{2,1,0:T(8,128)(2,1)S(1)} %get-tuple-element.183), channel_id=1, source_target_pairs={{0,2},{1,5},{2,0},{3,7},{4,6},{5,1},{6,4},{7,3},{8,10},{9,13},{10,... | collective-permute-start | bytes 786440 | tf_op jit(solution)/shard_map/ppermute | solution.py:625
  110.4 14.1 %collective-permute-start.14 = (bf16[1,64,2048]{2,1,0:T(8,128)(2,1)S(1)}, bf16[1,64,2048]{2,1,0:T(8,128)(2,1)S(1)}, u32[]{:S(2)}, u32[]{:S(2)}) collective-permute-start(bf16[1,64,2048]{2,1,0:T(8,128)(2,1)S(1)} %get-tuple-element.184), channel_id=1, source_target_pairs={{0,6},{1,7},{2,4},{3,5},{4,2},{5,3},{6,0},{7,1},{8,14},{9,15},{10,... | collective-permute-start | bytes 786440 | tf_op jit(solution)/shard_map/ppermute | solution.py:625
  124.6 15.6 %collective-permute-start.18 = (bf16[1,64,2048]{2,1,0:T(8,128)(2,1)S(1)}, bf16[1,64,2048]{2,1,0:T(8,128)(2,1)S(1)}, u32[]{:S(2)}, u32[]{:S(2)}) collective-permute-start(bf16[1,64,2048]{2,1,0:T(8,128)(2,1)S(1)} %att_sum0.1.refs_0_), channel_id=1, source_target_pairs={{0,8},{1,9},{2,10},{3,11},{4,12},{5,13},{6,14},{7,15},{8,0},{9,1},... | collective-permute-start | bytes 786440 | tf_op jit(solution)/shard_map/ppermute | solution.py:625
  125.5 14.7 %copy-start.9 = (bf16[1,64,4096]{2,1,0:T(8,128)(2,1)}, bf16[1,64,4096]{2,1,0:T(8,128)(2,1)S(1)}, u32[]{:S(2)}) copy-start(bf16[1,64,4096]{2,1,0:T(8,128)(2,1)S(1)} %ff_join.1.refs_0_) | copy-start | bytes 1572868
  125.5 14.7 %collective-permute-start.17 = (bf16[1,64,4096]{2,1,0:T(8,128)(2,1)S(1)}, bf16[1,64,4096]{2,1,0:T(8,128)(2,1)}, u32[]{:S(2)}, u32[]{:S(2)}) collective-permute-start(bf16[1,64,4096]{2,1,0:T(8,128)(2,1)S(1)} %ff_join.1.refs_0_), channel_id=1, source_target_pairs={{0,2},{1,5},{2,0},{3,7},{4,6},{5,1},{6,4},{7,3},{8,10},{9,13},{10,... | collective-permute-start | bytes 1572872 | tf_op jit(solution)/shard_map/ppermute | solution.py:625
  127.0 13.2 %collective-permute-start.16 = (bf16[1,64,4096]{2,1,0:T(8,128)(2,1)S(1)}, bf16[1,64,4096]{2,1,0:T(8,128)(2,1)S(1)}, u32[]{:S(2)}, u32[]{:S(2)}) collective-permute-start(bf16[1,64,4096]{2,1,0:T(8,128)(2,1)S(1)} %ff_join.1.refs_0_), channel_id=1, source_target_pairs={{0,4},{1,3},{2,6},{3,1},{4,0},{5,7},{6,2},{7,5},{8,12},{9,11},{10,... | collective-permute-start | bytes 1572872 | tf_op jit(solution)/shard_map/ppermute | solution.py:625
  140.2 5.9 %copy-start.13 = (bf16[1,64,4096]{2,1,0:T(8,128)(2,1)}, bf16[1,64,4096]{2,1,0:T(8,128)(2,1)S(1)}, u32[]{:S(2)}) copy-start(bf16[1,64,4096]{2,1,0:T(8,128)(2,1)S(1)} %collective-permute-done.16.refs_1_) | copy-start | bytes 1572868
  140.3 21.1 %collective-permute-start.22 = (bf16[1,64,4096]{2,1,0:T(8,128)(2,1)}, bf16[1,64,4096]{2,1,0:T(8,128)(2,1)S(1)}, u32[]{:S(2)}, u32[]{:S(2)}) collective-permute-start(bf16[1,64,4096]{2,1,0:T(8,128)(2,1)} %collective-permute-done.17.refs_2_), channel_id=1, source_target_pairs={{0,4},{1,3},{2,6},{3,1},{4,0},{5,7},{6,2},{7,5},{8,12},{9,11},{10,... | collective-permute-start | bytes 1572872 | tf_op jit(solution)/shard_map/ppermute | solution.py:625
  141.9 15.6 %collective-permute-start.21 = (bf16[1,64,2048]{2,1,0:T(8,128)(2,1)S(1)}, bf16[1,64,2048]{2,1,0:T(8,128)(2,1)S(1)}, u32[]{:S(2)}, u32[]{:S(2)}) collective-permute-start(bf16[1,64,2048]{2,1,0:T(8,128)(2,1)S(1)} %att_sum1.1.refs_0_), channel_id=1, source_target_pairs={{0,16},{1,17},{2,18},{3,19},{4,20},{5,21},{6,22},{7,23},{8,24},{9,... | collective-permute-start | bytes 786440 | tf_op jit(solution)/shard_map/ppermute | solution.py:625
  144.9 1.2 collective-permute-start.19
  146.1 11.4 %collective-permute-start.20 = (f32[32,1,128]{2,1,0:T(1,128)S(1)}, f32[32,1,128]{2,1,0:T(1,128)S(1)}, u32[]{:S(2)}, u32[]{:S(2)}) collective-permute-start(f32[32,1,128]{2,1,0:T(1,128)S(1)} %small_pair.1.refs_0_), channel_id=1, source_target_pairs={{0,2},{1,3},{2,0},{3,1},{4,6},{5,7},{6,4},{7,5},{8,10},{9,11},{10,... | collective-permute-start | bytes 49160 | tf_op jit(solution)/shard_map/ppermute | solution.py:625
  157.6 10.0 %copy-start.10 = (bf16[1,64,2048]{2,1,0:T(8,128)(2,1)}, bf16[1,64,2048]{2,1,0:T(8,128)(2,1)S(1)}, u32[]{:S(2)}) copy-start(bf16[1,64,2048]{2,1,0:T(8,128)(2,1)S(1)} %att_sum2.1.refs_0_) | copy-start | bytes 786436
  157.6 15.6 %collective-permute-start.27 = (bf16[1,64,2048]{2,1,0:T(8,128)(2,1)S(1)}, bf16[1,64,2048]{2,1,0:T(8,128)(2,1)S(1)}, u32[]{:S(2)}, u32[]{:S(2)}) collective-permute-start(bf16[1,64,2048]{2,1,0:T(8,128)(2,1)S(1)} %att_sum2.1.refs_0_), channel_id=1, source_target_pairs={{0,6},{1,7},{2,4},{3,5},{4,2},{5,3},{6,0},{7,1},{8,14},{9,15},{10,... | collective-permute-start | bytes 786440 | tf_op jit(solution)/shard_map/ppermute | solution.py:625
  159.1 14.1 %collective-permute-start.26 = (bf16[1,64,2048]{2,1,0:T(8,128)(2,1)S(1)}, bf16[1,64,2048]{2,1,0:T(8,128)(2,1)S(1)}, u32[]{:S(2)}, u32[]{:S(2)}) collective-permute-start(bf16[1,64,2048]{2,1,0:T(8,128)(2,1)S(1)} %att_sum2.1.refs_0_), channel_id=1, source_target_pairs={{0,2},{1,5},{2,0},{3,7},{4,6},{5,1},{6,4},{7,3},{8,10},{9,13},{10,... | collective-permute-start | bytes 786440 | tf_op jit(solution)/shard_map/ppermute | solution.py:625
  159.7 13.6 %collective-permute-start.25 = (bf16[1,64,2048]{2,1,0:T(8,128)(2,1)S(1)}, bf16[1,64,2048]{2,1,0:T(8,128)(2,1)S(1)}, u32[]{:S(2)}, u32[]{:S(2)}) collective-permute-start(bf16[1,64,2048]{2,1,0:T(8,128)(2,1)S(1)} %att_sum2.1.refs_0_), channel_id=1, source_target_pairs={{0,4},{1,3},{2,6},{3,1},{4,0},{5,7},{6,2},{7,5},{8,12},{9,11},{10,... | collective-permute-start | bytes 786440 | tf_op jit(solution)/shard_map/ppermute | solution.py:625
  161.2 6.5 %collective-permute-start.23 = (f32[32,1,128]{2,1,0:T(1,128)S(1)}, f32[32,1,128]{2,1,0:T(1,128)S(1)}, u32[]{:S(2)}, u32[]{:S(2)}) collective-permute-start(f32[32,1,128]{2,1,0:T(1,128)S(1)} %small_sum.4.refs_0_), channel_id=1, source_target_pairs={{0,8},{1,9},{2,10},{3,11},{4,12},{5,13},{6,14},{7,15},{8,0},{9,1},... | collective-permute-start | bytes 49160 | tf_op jit(solution)/shard_map/ppermute | solution.py:625
  161.4 0.8 copy-start.14
  167.7 5.5 %collective-permute-start.24 = (f32[32,1,128]{2,1,0:T(1,128)S(1)}, f32[32,1,128]{2,1,0:T(1,128)S(1)}, u32[]{:S(2)}, u32[]{:S(2)}) collective-permute-start(f32[32,1,128]{2,1,0:T(1,128)S(1)} %small_sum.5.refs_0_), channel_id=1, source_target_pairs={{0,16},{1,17},{2,18},{3,19},{4,20},{5,21},{6,22},{7,23},{8,24},{9,... | collective-permute-start | bytes 49160 | tf_op jit(solution)/shard_map/ppermute | solution.py:625
  173.2 0.7 copy-start.15
  173.2 0.8 copy-start.16
  173.2 0.9 copy-start.17
  173.2 8.3 %collective-permute-start.28 = (f32[32,1,128]{2,1,0:T(1,128)S(1)}, f32[32,1,128]{2,1,0:T(1,128)S(1)}, u32[]{:S(2)}, u32[]{:S(2)}) collective-permute-start(f32[32,1,128]{2,1,0:T(1,128)S(1)} %small_sum.6.refs_0_), channel_id=1, source_target_pairs={{0,4},{1,5},{2,6},{3,7},{4,0},{5,1},{6,2},{7,3},{8,12},{9,13},{10,... | collective-permute-start | bytes 49160 | tf_op jit(solution)/shard_map/ppermute | solution.py:625
  174.1 7.6 %copy-start.19 = (bf16[1024]{0:T(1024)(128)(2,1)S(1)}, bf16[1024]{0:T(1024)(128)(2,1)}, u32[]{:S(2)}) copy-start(bf16[1024]{0:T(1024)(128)(2,1)} %param.31) | copy-start | bytes 6148
  174.1 7.6 %copy-start.26 = (f32[1024]{0:T(1024)S(1)}, f32[1024]{0:T(1024)}, u32[]{:S(2)}) copy-start(f32[1024]{0:T(1024)} %param.38) | copy-start | bytes 12292
  174.1 7.6 %copy-start.27 = (f32[1024]{0:T(1024)S(1)}, f32[1024]{0:T(1024)}, u32[]{:S(2)}) copy-start(f32[1024]{0:T(1024)} %param.45) | copy-start | bytes 12292
  174.1 8.2 %copy-start.20 = (bf16[768]{0:T(1024)(128)(2,1)S(1)}, bf16[768]{0:T(1024)(128)(2,1)}, u32[]{:S(2)}) copy-start(bf16[768]{0:T(1024)(128)(2,1)} %param.28) | copy-start | bytes 4612
  174.1 8.2 %copy-start.28 = (f32[768]{0:T(1024)S(1)}, f32[768]{0:T(1024)}, u32[]{:S(2)}) copy-start(f32[768]{0:T(1024)} %param.35) | copy-start | bytes 9220
  174.1 8.2 %copy-start.29 = (f32[768]{0:T(1024)S(1)}, f32[768]{0:T(1024)}, u32[]{:S(2)}) copy-start(f32[768]{0:T(1024)} %param.42) | copy-start | bytes 9220
  174.2 8.8 %copy-start.23 = (bf16[6,256]{1,0:T(8,128)(2,1)S(1)}, bf16[6,256]{1,0:T(8,128)(2,1)}, u32[]{:S(2)}) copy-start(bf16[6,256]{1,0:T(8,128)(2,1)} %param.26) | copy-start | bytes 9220
  174.2 8.8 %copy-start.24 = (f32[6,256]{1,0:T(8,128)S(1)}, f32[6,256]{1,0:T(8,128)}, u32[]{:S(2)}) copy-start(f32[6,256]{1,0:T(8,128)} %param.33) | copy-start | bytes 18436
  174.2 8.8 %copy-start.25 = (f32[6,256]{1,0:T(8,128)S(1)}, f32[6,256]{1,0:T(8,128)}, u32[]{:S(2)}) copy-start(f32[6,256]{1,0:T(8,128)} %param.40) | copy-start | bytes 18436
  181.6 2.0 %copy-start.21 = (f32[6,128]{1,0:T(8,128)}, f32[6,128]{1,0:T(8,128)S(1)}, u32[]{:S(2)}) copy-start(f32[6,128]{1,0:T(8,128)S(1)} %slice_reduce_fusion.1) | copy-start | bytes 9220
  181.7 2.0 %copy-start.22 = (f32[8,1,128]{2,1,0:T(1,128)}, f32[8,1,128]{2,1,0:T(1,128)S(1)}, u32[]{:S(2)}) copy-start(f32[8,1,128]{2,1,0:T(1,128)S(1)} %slice.17) | copy-start | bytes 12292
  181.7 1.9 %copy-start.18 = (f32[6,256]{1,0:T(8,128)}, f32[6,256]{1,0:T(8,128)S(1)}, u32[]{:S(2)}) copy-start(f32[6,256]{1,0:T(8,128)S(1)} %reshape.156) | copy-start | bytes 18436
